TPU v7x, 512 devices: a whole 4x4x16 slice. The times are simulated.
512 devices in a mesh: clip: 4 (over y), row: 8 (over x, core), tm: 16 (over z).
Axes of the slice: x: 4, y: 4, z: 16, core: 2. Of those that a mesh axis runs over, the one named last changes fastest.
Arguments:
- clip_input: bfloat16 [4, 32, 16, 48, 192], P('clip', 'tm', 'row'), may hold values from -6 to 6
- out_grad: bfloat16 [4, 64, 16, 48, 192], P('clip', 'tm', 'row'), may hold values from -6 to 6
- weight_one: bfloat16 [3, 3, 3, 192, 192], replicated, may hold values from -0.078125 to 0.078125
- weight_two: bfloat16 [3, 3, 3, 192, 192], replicated, may hold values from -0.078125 to 0.078125
- lengths: int32 [4], P('clip'), may hold values from 2 to 32, as said below
Outputs:
- input_grad: float32 [4, 32, 16, 48, 192], P('clip', 'tm', 'row')
- kernel_grad: float32 [5184, 192], P(('clip', 'tm'), 'row')
Inputs may be any that keep to these rules, and one draw needn't show every extreme that they name: `lengths`: every clip has at least 2 frames; one clip has all 32 frames in every draw.
All inputs are finite; a program needn't handle non-finite values.
Results may differ from a plain program's by a relative error of at most 0.0065.
Values may be sent and summed in bfloat16 or wider, within the bound.
No kernel may reach another device: no remote copies, remote signals or barrier semaphores. Data moves between devices by JAX's collectives and lax.ppermute only.
A program may use at most 64 MiB of HBM per device.

v0:
```python
import math

import jax
import jax.numpy as jnp
from jax import lax
from jax.sharding import PartitionSpec as P


def shifted(block, axis, distance):
    devices = range(lax.axis_size(axis))
    route = [(i - distance, i) for i in devices if i - distance in devices]
    return lax.ppermute(block, axis, route)


def extended_2(value, sides, width):
    for axis, dim in sides:
        peers, length = (lax.axis_size(axis), value.shape[dim])
        up = [(i, (i + 1) % peers) for i in range(peers - 1)]
        down = [(j, i) for i, j in up]
        last = lax.slice_in_dim(value, length - width, length, axis=dim)
        initial = lax.slice_in_dim(value, 0, width, axis=dim)
        before = lax.ppermute(last, axis, up)
        after = lax.ppermute(initial, axis, down)
        value = jnp.concatenate([before, value, after], axis=dim)
    return value


def forward_patches(source, frames, rows, cols):
    chan = source.shape[-1]
    pieces = []
    for i in range(3):
        for j in range(3):
            for k in range(3):
                pieces.append(
                    source[2 - i : 2 - i + frames, j : j + rows, k : k + cols].reshape(-1, chan)
                )
    return jnp.concatenate(pieces, axis=1)


def backward_patches(source, frames, rows, cols):
    chan = source.shape[-1]
    pieces = []
    for i in range(3):
        for j in range(3):
            for k in range(3):
                pieces.append(
                    source[i : i + frames, 2 - j : 2 - j + rows, 2 - k : 2 - k + cols].reshape(
                        -1, chan
                    )
                )
    return jnp.concatenate(pieces, axis=1)


def widen(field):
    return jnp.pad(field, ((0, 0), (0, 0), (1, 1), (0, 0)))


def local(clip_input, out_grad, weight_one, weight_two, lengths):
    frames_in, rows, cols, chan = clip_input.shape[1:]
    frames_out = 2 * frames_in
    inputs = clip_input[0]
    block_pos = lax.axis_index("tm")
    frame_ids = block_pos * frames_out + jnp.arange(frames_out, dtype=jnp.int32)
    keep = frame_ids < 2 * lengths[0]
    masked = jnp.where(keep[:, None, None, None], out_grad[0], jnp.zeros_like(out_grad[0]))
    flat_one = weight_one.reshape(-1, chan)
    back_one = jnp.swapaxes(weight_one, 3, 4).reshape(-1, chan)
    back_two = jnp.swapaxes(weight_two, 3, 4).reshape(-1, chan)
    earlier = shifted(inputs, "tm", 1)
    extended = jnp.concatenate([earlier, inputs], axis=0)
    extended = widen(extended_2(extended, (("row", 1),), 1))
    hidden = jnp.dot(
        forward_patches(extended, frames_in, rows, cols),
        flat_one,
        preferred_element_type=jnp.float32,
    )
    act = jax.nn.silu(hidden).astype(jnp.bfloat16).reshape(frames_in, rows, cols, chan)
    act_before = shifted(act[frames_in - 1 :], "tm", 1)
    act_ext = jnp.concatenate([act_before, act], axis=0)
    act_ext = extended_2(act_ext, (("row", 1),), 1)
    upsampled = widen(jnp.repeat(act_ext, 2, axis=0))
    up_columns = forward_patches(upsampled, frames_out, rows, cols)
    masked_flat = masked.reshape(-1, chan)
    kernel_part = lax.psum_scatter(
        lax.dot_general(
            up_columns, masked_flat, (((0,), (0,)), ((), ())), preferred_element_type=jnp.float32
        ),
        ("clip", "tm"),
        scatter_dimension=0,
        tiled=True,
    )
    kernel_sum = lax.psum_scatter(kernel_part, "row", scatter_dimension=1, tiled=True)
    cells_all = (
        lax.axis_size("clip")
        * frames_out
        * lax.axis_size("tm")
        * rows
        * lax.axis_size("row")
        * cols
    )
    kernel_grad = kernel_sum * (1.0 / math.sqrt(cells_all))
    grad_band = widen(extended_2(masked, (("row", 1),), 1))
    source = jnp.pad(grad_band, ((2, 2), (0, 0), (0, 0), (0, 0)))
    whole = jnp.dot(
        backward_patches(source, frames_out + 2, rows, cols),
        back_two,
        preferred_element_type=jnp.float32,
    )
    whole = whole.reshape(frames_out + 2, rows, cols, chan)
    returned = shifted(whole[:2], "tm", -1)
    up_grad = jnp.concatenate([whole[2:frames_out], whole[frames_out:] + returned], axis=0)
    hidden_four = hidden.reshape(frames_in, rows, cols, chan)
    sigma = jax.nn.sigmoid(hidden_four)
    pair_sum = up_grad.reshape(frames_in, 2, rows, cols, chan).sum(axis=1)
    hidden_grad = (pair_sum * sigma * (1.0 + hidden_four * (1.0 - sigma))).astype(jnp.bfloat16)
    hidden_band = widen(extended_2(hidden_grad, (("row", 1),), 1))
    source_h = jnp.pad(hidden_band, ((2, 2), (0, 0), (0, 0), (0, 0)))
    whole_h = jnp.dot(
        backward_patches(source_h, frames_in + 2, rows, cols),
        back_one,
        preferred_element_type=jnp.float32,
    )
    whole_h = whole_h.reshape(frames_in + 2, rows, cols, chan)
    returned_h = shifted(whole_h[:2], "tm", -1)
    input_grad = jnp.concatenate([whole_h[2:frames_in], whole_h[frames_in:] + returned_h], axis=0)
    return (input_grad[None], kernel_grad)


def solution(mesh):
    return jax.shard_map(
        local,
        mesh=mesh,
        in_specs=(
            P("clip", "tm", "row", None, None),
            P("clip", "tm", "row", None, None),
            P(),
            P(),
            P("clip"),
        ),
        out_specs=(P("clip", "tm", "row", None, None), P(("clip", "tm"), "row")),
        check_vma=False,
    )
```

profile of v0, /device:TPU:24, one launch (start us, length us, event | category | flops | bytes accessed | tf_op | source)
XLA Modules:
  0.0 355.1 jit_solution(9688802781732440877)
XLA Ops:
  1.3 1.0 bitcast_select_fusion.1
  2.3 1.7 collective-permute-start
  4.1 1.3 collective-permute-start.1
  5.4 3.8 %collective-permute-start.3 = (bf16[2,2,48,192]{3,2,1,0:T(8,128)(2,1)}, bf16[2,2,48,192]{3,2,1,0:T(8,128)(2,1)S(1)}, u32[]{:S(2)}, u32[]{:S(2)}) collective-permute-start(bf16[2,2,48,192]{3,2,1,0:T(8,128)(2,1)} %bitcast.153), channel_id=1, source_target_pairs={{0,1},{1,2},{2,3},{3,4},{4,5},{5,6},{6,7},{7,8},{8,9},{9,10},{10,1... | collective-permute-start | bytes 221192 | tf_op jit(solution)/shard_map/ppermute | solution.py:12
  9.4 4.2 %copy.18 = bf16[3,3,3,192,192]{4,3,2,1,0:T(8,128)(2,1)S(1)} copy(bf16[3,3,3,192,192]{3,4,2,1,0:T(8,128)(2,1)} %bitcast.150) | data formatting | bytes 3981312 | tf_op jit(solution)/shard_map/transpose | solution.py:68
  13.8 2.9 pad_slice_fusion.27
  16.8 1.6 pad_slice_fusion.28
  19.1 4.0 %collective-permute-start.4 = (bf16[4,1,48,192]{3,2,1,0:T(8,128)(2,1)}, bf16[4,1,48,192]{3,2,1,0:T(8,128)(2,1)S(1)}, u32[]{:S(2)}, u32[]{:S(2)}) collective-permute-start(bf16[4,1,48,192]{3,2,1,0:T(8,128)(2,1)} %get-tuple-element.122), channel_id=1, source_target_pairs={{0,16},{16,32},{32,48},{48,64},{64,80},{80,96},{96,112},{1,17},{17... | collective-permute-start | bytes 221192 | tf_op jit(solution)/shard_map/ppermute | solution.py:22
  23.1 1.3 collective-permute-start.5
  24.4 11.4 %concatenate.44 = bf16[576,5184]{1,0:T(8,128)(2,1)} concatenate(bf16[576,192]{1,0:T(8,128)(2,1)} %bitcast.186, bf16[576,192]{1,0:T(8,128)(2,1)S(1)} %bitcast.161, bf16[576,192]{1,0:T(8,128)(2,1)} %bitcast.162, bf16[576,192]{1,0:T(8,128)(2,1)} %bitcast.163, bf16[576,192]{1,0:T(8,128)(2,1)} %bitcast.164, bf16[576,192]{1,0:T(8,128)(2,1)} %bitcast.165, bf16[576,192]{1,0:T(8,128)(2,1)} %bitcast.166, ...), dimensions={1} | concatenate | bytes 11943936 | tf_op jit(solution)/shard_map/concatenate | solution.py:51
  35.8 5.0 %fusion.20 = f32[576,192]{0,1:T(8,128)S(1)} fusion(bf16[576,5184]{1,0:T(8,128)(2,1)} %concatenate.44, bf16[5184,192]{1,0:T(8,128)(2,1)S(1)} %bitcast.149), kind=kOutput, calls=%fused_computation.121 | convolution fusion | flops 1146617856 | bytes 8404992 | tf_op jit(solution)/shard_map/dot_general | solution.py:104
  41.7 1.3 collective-permute-start.2
  44.2 1.1 select_maximum_fusion
  45.3 1.1 fusion.14
  46.4 1.2 pad_maximum_fusion.1
  47.6 0.8 fusion.16
  48.5 4.5 %concatenate.50 = bf16[192,5184]{1,0:T(8,128)(2,1)} concatenate(bf16[192,192]{1,0:T(8,128)(2,1)} %bitcast.263, bf16[192,192]{1,0:T(8,128)(2,1)} %bitcast.267, bf16[192,192]{1,0:T(8,128)(2,1)} %bitcast.262, bf16[192,192]{1,0:T(8,128)(2,1)} %bitcast.261, bf16[192,192]{1,0:T(8,128)(2,1)S(1)} %bitcast.158, bf16[192,192]{1,0:T(8,128)(2,1)} %bitcast.260, bf16[192,192]{1,0:T(8,128)(2,1)} %bitcast.259, ...), dimensions={1} | concatenate | bytes 3981312 | tf_op jit(solution)/shard_map/concatenate | solution.py:37
  53.0 3.0 multiply_convert_fusion
  56.0 4.5 %collective-permute-start.9 = (bf16[1,2,48,192]{3,2,1,0:T(8,128)(2,1)S(1)}, bf16[1,2,48,192]{3,2,1,0:T(8,128)(2,1)S(1)}, u32[]{:S(2)}, u32[]{:S(2)}) collective-permute-start(bf16[1,2,48,192]{3,2,1,0:T(8,128)(2,1)S(1)} %bitcast.273), channel_id=1, source_target_pairs={{0,1},{1,2},{2,3},{3,4},{4,5},{5,6},{6,7},{7,8},{8,9},{9,10},{10,1... | collective-permute-start | bytes 110600 | tf_op jit(solution)/shard_map/ppermute | solution.py:12
  61.4 1.3 dynamic-slice.6
  62.6 4.2 %copy.22 = bf16[3,3,3,192,192]{4,3,2,1,0:T(8,128)(2,1)S(1)} copy(bf16[3,3,3,192,192]{3,4,2,1,0:T(8,128)(2,1)} %bitcast.151) | data formatting | bytes 3981312 | tf_op jit(solution)/shard_map/transpose | solution.py:67
  67.5 1.3 dynamic-slice.2
  69.7 4.2 %collective-permute-start.10 = (bf16[3,1,48,192]{3,2,1,0:T(8,128)(2,1)S(1)}, bf16[3,1,48,192]{3,2,1,0:T(8,128)(2,1)S(1)}, u32[]{:S(2)}, u32[]{:S(2)}) collective-permute-start(bf16[3,1,48,192]{3,2,1,0:T(8,128)(2,1)S(1)} %get-tuple-element.124), channel_id=1, source_target_pairs={{0,16},{16,32},{32,48},{48,64},{64,80},{80,96},{96,112},{1,17},{17... | collective-permute-start | bytes 165896 | tf_op jit(solution)/shard_map/ppermute | solution.py:22
  73.9 1.3 collective-permute-start.11
  75.2 1.0 add.44
  76.2 1.0 multiply_convert_fusion.1
  77.9 5.3 %collective-permute-start.6 = (bf16[2,1,48,192]{3,2,1,0:T(8,128)(2,1)}, bf16[2,1,48,192]{3,2,1,0:T(8,128)(2,1)}, u32[]{:S(2)}, u32[]{:S(2)}) collective-permute-start(bf16[2,1,48,192]{3,2,1,0:T(8,128)(2,1)} %get-tuple-element.126), channel_id=1, source_target_pairs={{0,16},{16,32},{32,48},{48,64},{64,80},{80,96},{96,112},{1,17},{17... | collective-permute-start | bytes 110600 | tf_op jit(solution)/shard_map/ppermute | solution.py:22
  83.1 1.3 collective-permute-start.7
  84.6 1.9 pad_slice_fusion.60
  86.5 1.2 fusion.12
  87.7 7.9 %concatenate.55 = bf16[384,5184]{1,0:T(8,128)(2,1)} concatenate(bf16[384,192]{1,0:T(8,128)(2,1)} %bitcast.216, bf16[384,192]{1,0:T(8,128)(2,1)} %bitcast.215, bf16[384,192]{1,0:T(8,128)(2,1)S(1)} %bitcast.188, bf16[384,192]{1,0:T(8,128)(2,1)S(1)} %bitcast.189, bf16[384,192]{1,0:T(8,128)(2,1)} %bitcast.214, bf16[384,192]{1,0:T(8,128)(2,1)S(1)} %bitcast.190, ...), dimensions={1} | concatenate | bytes 7962624 | tf_op jit(solution)/shard_map/concatenate | solution.py:37
  95.5 6.1 %fusion.22 = f32[5184,192]{1,0:T(8,128)} fusion(bf16[384,5184]{1,0:T(8,128)(2,1)} %concatenate.55, bf16[384,192]{1,0:T(8,128)(2,1)} %bitcast_select_fusion), kind=kOutput, calls=%fused_computation.123 | convolution fusion | flops 764411904 | bytes 8110080 | tf_op jit(solution)/shard_map/dot_general | solution.py:85
  101.6 159.4 %fusion = f32[88,192]{1,0:T(8,128)S(1)} fusion(f32[5184,192]{1,0:T(8,128)} %fusion.22), kind=kCustom, calls=%all-reduce-scatter | all-reduce-scatter fusion | flops 1081345 | bytes 4050944
  261.1 1.9 collective-permute-start.12
  263.0 1.9 collective-permute-start.13
  264.9 6.4 %collective-permute-start.14 = (f32[88,192]{1,0:T(8,128)S(1)}, f32[88,192]{1,0:T(8,128)}, u32[]{:S(2)}, u32[]{:S(2)}) collective-permute-start(f32[88,192]{1,0:T(8,128)S(1)} %fusion), channel_id=1, source_target_pairs={{0,3},{1,4},{2,5},{3,6},{4,7},{5,8},{6,9},{7,10},{8,11},{9,12},{10... | collective-permute-start | bytes 202760
  271.4 14.6 %collective-permute-start.15 = (f32[88,192]{1,0:T(8,128)S(1)}, f32[88,192]{1,0:T(8,128)}, u32[]{:S(2)}, u32[]{:S(2)}) collective-permute-start(f32[88,192]{1,0:T(8,128)S(1)} %fusion), channel_id=1, source_target_pairs={{0,4},{1,5},{2,6},{3,7},{4,8},{5,9},{6,10},{7,11},{8,12},{9,13},{1... | collective-permute-start | bytes 202760
  286.0 8.3 %collective-permute-start.17 = (f32[1,192]{1,0:T(1,128)S(1)}, f32[1,192]{1,0:T(1,128)S(1)}, u32[]{:S(2)}, u32[]{:S(2)}) collective-permute-start(f32[1,192]{1,0:T(1,128)S(1)} %slice.582), channel_id=1, source_target_pairs={{0,6},{1,7},{2,8},{3,9},{4,10},{5,11},{6,12},{7,13},{8,14},{9,15},... | collective-permute-start | bytes 2312
  294.3 0.9 fusion.8
  295.2 2.1 pad_slice_fusion
  297.4 1.0 pad_slice_fusion.1
  298.4 7.8 %concatenate.52 = bf16[384,5184]{1,0:T(8,128)(2,1)} concatenate(bf16[384,192]{1,0:T(8,128)(2,1)} %bitcast.224, bf16[384,192]{1,0:T(8,128)(2,1)} %bitcast.226, bf16[384,192]{1,0:T(8,128)(2,1)} %bitcast.227, bf16[384,192]{1,0:T(8,128)(2,1)} %bitcast.228, bf16[384,192]{1,0:T(8,128)(2,1)} %bitcast.229, bf16[384,192]{1,0:T(8,128)(2,1)} %bitcast.230, bf16[384,192]{1,0:T(8,128)(2,1)} %bitcast.231, ...), dimensions={1} | concatenate | bytes 7962624 | tf_op jit(solution)/shard_map/concatenate | solution.py:51
  306.2 3.6 %fusion.21 = f32[384,192]{0,1:T(8,128)S(1)} fusion(bf16[384,5184]{1,0:T(8,128)(2,1)} %concatenate.52, bf16[5184,192]{1,0:T(8,128)(2,1)S(1)} %bitcast.148), kind=kOutput, calls=%fused_computation.122 | convolution fusion | flops 764411904 | bytes 6266880 | tf_op jit(solution)/shard_map/dot_general | solution.py:118
  309.8 3.1 collective-permute-start.16
  313.3 1.3 collective-permute-start.8
  314.6 8.5 %collective-permute-done.16 = f32[88,192]{1,0:T(8,128)S(1)} collective-permute-done((f32[88,192]{1,0:T(8,128)S(1)}, f32[88,192]{1,0:T(8,128)S(1)}, u32[]{:S(2)}, u32[]{:S(2)}) %collective-permute-start.16) | collective-permute-done | bytes 67616
  323.2 4.0 %concatenate.56 = f32[529,192]{1,0:T(8,128)S(1)} concatenate(f32[1,192]{1,0:T(1,128)S(1)} %collective-permute-done.17, f32[88,192]{1,0:T(8,128)S(1)} %collective-permute-done.16, f32[88,192]{1,0:T(8,128)} %collective-permute-done.15, f32[88,192]{1,0:T(8,128)} %collective-permute-done.14, f32[88,192]{1,0:T(8,128)} %collective-permute-done.13, f32[88,192]{1,0:T(8,128)} %collective-permute-done.12, ...), dimensions={0} | concatenate | bytes 812544
  327.2 26.4 %all-reduce.7 = f32[81,192]{1,0:T(8,128)S(1)} all-reduce(f32[81,192]{1,0:T(8,128)S(1)} %constant_dynamic-slice_fusion), channel_id=3, replica_groups=mesh['clip'=4,'row'=8,'tm'=16] {'row'}, use_global_device_ids=true, to_apply=%region_2.3.clone | all-reduce | flops 15552 | bytes 124416
  (51 shorter events, 7.0 us)
Async XLA Ops:
  2.3 11.3 %collective-permute-start = (bf16[4,1,48,192]{3,2,1,0:T(8,128)(2,1)S(1)}, bf16[4,1,48,192]{3,2,1,0:T(8,128)(2,1)S(1)}, u32[]{:S(2)}, u32[]{:S(2)}) collective-permute-start(bf16[4,1,48,192]{3,2,1,0:T(8,128)(2,1)S(1)} %get-tuple-element.118), channel_id=1, source_target_pairs={{0,16},{16,32},{32,48},{48,64},{64,80},{80,96},{96,112},{1,17},{17... | collective-permute-start | bytes 221192 | tf_op jit(solution)/shard_map/ppermute | solution.py:22
  4.1 9.6 %collective-permute-start.1 = (bf16[4,1,48,192]{3,2,1,0:T(8,128)(2,1)S(1)}, bf16[4,1,48,192]{3,2,1,0:T(8,128)(2,1)S(1)}, u32[]{:S(2)}, u32[]{:S(2)}) collective-permute-start(bf16[4,1,48,192]{3,2,1,0:T(8,128)(2,1)S(1)} %get-tuple-element.119), channel_id=1, source_target_pairs={{16,0},{32,16},{48,32},{64,48},{80,64},{96,80},{112,96},{17,1},{33... | collective-permute-start | bytes 221192 | tf_op jit(solution)/shard_map/ppermute | solution.py:23
  5.4 13.0 %collective-permute-start.3 = (bf16[2,2,48,192]{3,2,1,0:T(8,128)(2,1)}, bf16[2,2,48,192]{3,2,1,0:T(8,128)(2,1)S(1)}, u32[]{:S(2)}, u32[]{:S(2)}) collective-permute-start(bf16[2,2,48,192]{3,2,1,0:T(8,128)(2,1)} %bitcast.153), channel_id=1, source_target_pairs={{0,1},{1,2},{2,3},{3,4},{4,5},{5,6},{6,7},{7,8},{8,9},{9,10},{10,1... | collective-permute-start | bytes 221192 | tf_op jit(solution)/shard_map/ppermute | solution.py:12
  13.8 4.6 %copy-start.1 = (bf16[1,2,2,48,192]{4,3,2,1,0:T(8,128)(2,1)S(1)}, bf16[1,2,2,48,192]{4,3,2,1,0:T(8,128)(2,1)}, u32[]{:S(2)}) copy-start(bf16[1,2,2,48,192]{4,3,2,1,0:T(8,128)(2,1)} %param.5) | copy-start | bytes 221188
  19.1 24.5 %collective-permute-start.4 = (bf16[4,1,48,192]{3,2,1,0:T(8,128)(2,1)}, bf16[4,1,48,192]{3,2,1,0:T(8,128)(2,1)S(1)}, u32[]{:S(2)}, u32[]{:S(2)}) collective-permute-start(bf16[4,1,48,192]{3,2,1,0:T(8,128)(2,1)} %get-tuple-element.122), channel_id=1, source_target_pairs={{0,16},{16,32},{32,48},{48,64},{64,80},{80,96},{96,112},{1,17},{17... | collective-permute-start | bytes 221192 | tf_op jit(solution)/shard_map/ppermute | solution.py:22
  23.1 20.5 %collective-permute-start.5 = (bf16[4,1,48,192]{3,2,1,0:T(8,128)(2,1)}, bf16[4,1,48,192]{3,2,1,0:T(8,128)(2,1)}, u32[]{:S(2)}, u32[]{:S(2)}) collective-permute-start(bf16[4,1,48,192]{3,2,1,0:T(8,128)(2,1)} %get-tuple-element.123), channel_id=1, source_target_pairs={{16,0},{32,16},{48,32},{64,48},{80,64},{96,80},{112,96},{17,1},{33... | collective-permute-start | bytes 221192 | tf_op jit(solution)/shard_map/ppermute | solution.py:23
  41.7 33.6 %collective-permute-start.2 = (f32[2,2,48,192]{3,2,1,0:T(8,128)}, f32[2,2,48,192]{3,2,1,0:T(8,128)}, u32[]{:S(2)}, u32[]{:S(2)}) collective-permute-start(f32[2,2,48,192]{3,2,1,0:T(8,128)} %bitcast.33), channel_id=1, source_target_pairs={{1,0},{2,1},{3,2},{4,3},{5,4},{6,5},{7,6},{8,7},{9,8},{10,9},{11,1... | collective-permute-start | bytes 442376 | tf_op jit(solution)/shard_map/ppermute | solution.py:12
  43.6 0.6 copy-start.3
  46.4 6.6 %copy-start = (bf16[3,3,3,192,192]{4,3,2,1,0:T(8,128)(2,1)S(1)}, bf16[3,3,3,192,192]{4,3,2,1,0:T(8,128)(2,1)}, u32[]{:S(2)}) copy-start(bf16[3,3,3,192,192]{4,3,2,1,0:T(8,128)(2,1)} %param.7) | copy-start | bytes 5971972
  53.0 7.6 %copy-start.2 = (bf16[1,4,2,48,192]{4,3,2,1,0:T(8,128)(2,1)S(1)}, bf16[1,4,2,48,192]{4,3,2,1,0:T(8,128)(2,1)}, u32[]{:S(2)}) copy-start(bf16[1,4,2,48,192]{4,3,2,1,0:T(8,128)(2,1)} %param.6) | copy-start | bytes 442372
  56.0 13.7 %collective-permute-start.9 = (bf16[1,2,48,192]{3,2,1,0:T(8,128)(2,1)S(1)}, bf16[1,2,48,192]{3,2,1,0:T(8,128)(2,1)S(1)}, u32[]{:S(2)}, u32[]{:S(2)}) collective-permute-start(bf16[1,2,48,192]{3,2,1,0:T(8,128)(2,1)S(1)} %bitcast.273), channel_id=1, source_target_pairs={{0,1},{1,2},{2,3},{3,4},{4,5},{5,6},{6,7},{7,8},{8,9},{9,10},{10,1... | collective-permute-start | bytes 110600 | tf_op jit(solution)/shard_map/ppermute | solution.py:12
  69.7 14.7 %collective-permute-start.10 = (bf16[3,1,48,192]{3,2,1,0:T(8,128)(2,1)S(1)}, bf16[3,1,48,192]{3,2,1,0:T(8,128)(2,1)S(1)}, u32[]{:S(2)}, u32[]{:S(2)}) collective-permute-start(bf16[3,1,48,192]{3,2,1,0:T(8,128)(2,1)S(1)} %get-tuple-element.124), channel_id=1, source_target_pairs={{0,16},{16,32},{32,48},{48,64},{64,80},{80,96},{96,112},{1,17},{17... | collective-permute-start | bytes 165896 | tf_op jit(solution)/shard_map/ppermute | solution.py:22
  73.9 10.5 %collective-permute-start.11 = (bf16[3,1,48,192]{3,2,1,0:T(8,128)(2,1)S(1)}, bf16[3,1,48,192]{3,2,1,0:T(8,128)(2,1)S(1)}, u32[]{:S(2)}, u32[]{:S(2)}) collective-permute-start(bf16[3,1,48,192]{3,2,1,0:T(8,128)(2,1)S(1)} %get-tuple-element.125), channel_id=1, source_target_pairs={{16,0},{32,16},{48,32},{64,48},{80,64},{96,80},{112,96},{17,1},{33... | collective-permute-start | bytes 165896 | tf_op jit(solution)/shard_map/ppermute | solution.py:23
  77.9 193.5 %collective-permute-start.6 = (bf16[2,1,48,192]{3,2,1,0:T(8,128)(2,1)}, bf16[2,1,48,192]{3,2,1,0:T(8,128)(2,1)}, u32[]{:S(2)}, u32[]{:S(2)}) collective-permute-start(bf16[2,1,48,192]{3,2,1,0:T(8,128)(2,1)} %get-tuple-element.126), channel_id=1, source_target_pairs={{0,16},{16,32},{32,48},{48,64},{64,80},{80,96},{96,112},{1,17},{17... | collective-permute-start | bytes 110600 | tf_op jit(solution)/shard_map/ppermute | solution.py:22
  83.1 202.8 %collective-permute-start.7 = (bf16[2,1,48,192]{3,2,1,0:T(8,128)(2,1)}, bf16[2,1,48,192]{3,2,1,0:T(8,128)(2,1)}, u32[]{:S(2)}, u32[]{:S(2)}) collective-permute-start(bf16[2,1,48,192]{3,2,1,0:T(8,128)(2,1)} %get-tuple-element.127), channel_id=1, source_target_pairs={{16,0},{32,16},{48,32},{64,48},{80,64},{96,80},{112,96},{17,1},{33... | collective-permute-start | bytes 110600 | tf_op jit(solution)/shard_map/ppermute | solution.py:23
  261.1 52.2 %collective-permute-start.12 = (f32[88,192]{1,0:T(8,128)S(1)}, f32[88,192]{1,0:T(8,128)}, u32[]{:S(2)}, u32[]{:S(2)}) collective-permute-start(f32[88,192]{1,0:T(8,128)S(1)} %fusion), channel_id=1, source_target_pairs={{0,1},{1,2},{2,3},{3,4},{4,5},{5,6},{6,7},{7,8},{8,9},{9,10},{10,1... | collective-permute-start | bytes 202760
  263.0 51.6 %collective-permute-start.13 = (f32[88,192]{1,0:T(8,128)S(1)}, f32[88,192]{1,0:T(8,128)}, u32[]{:S(2)}, u32[]{:S(2)}) collective-permute-start(f32[88,192]{1,0:T(8,128)S(1)} %fusion), channel_id=1, source_target_pairs={{0,2},{1,3},{2,4},{3,5},{4,6},{5,7},{6,8},{7,9},{8,10},{9,11},{10,... | collective-permute-start | bytes 202760
  264.9 49.7 %collective-permute-start.14 = (f32[88,192]{1,0:T(8,128)S(1)}, f32[88,192]{1,0:T(8,128)}, u32[]{:S(2)}, u32[]{:S(2)}) collective-permute-start(f32[88,192]{1,0:T(8,128)S(1)} %fusion), channel_id=1, source_target_pairs={{0,3},{1,4},{2,5},{3,6},{4,7},{5,8},{6,9},{7,10},{8,11},{9,12},{10... | collective-permute-start | bytes 202760
  271.4 43.2 %collective-permute-start.15 = (f32[88,192]{1,0:T(8,128)S(1)}, f32[88,192]{1,0:T(8,128)}, u32[]{:S(2)}, u32[]{:S(2)}) collective-permute-start(f32[88,192]{1,0:T(8,128)S(1)} %fusion), channel_id=1, source_target_pairs={{0,4},{1,5},{2,6},{3,7},{4,8},{5,9},{6,10},{7,11},{8,12},{9,13},{1... | collective-permute-start | bytes 202760
  286.0 23.8 %collective-permute-start.17 = (f32[1,192]{1,0:T(1,128)S(1)}, f32[1,192]{1,0:T(1,128)S(1)}, u32[]{:S(2)}, u32[]{:S(2)}) collective-permute-start(f32[1,192]{1,0:T(1,128)S(1)} %slice.582), channel_id=1, source_target_pairs={{0,6},{1,7},{2,8},{3,9},{4,10},{5,11},{6,12},{7,13},{8,14},{9,15},... | collective-permute-start | bytes 2312
  309.8 13.3 %collective-permute-start.16 = (f32[88,192]{1,0:T(8,128)S(1)}, f32[88,192]{1,0:T(8,128)S(1)}, u32[]{:S(2)}, u32[]{:S(2)}) collective-permute-start(f32[88,192]{1,0:T(8,128)S(1)} %fusion), channel_id=1, source_target_pairs={{0,5},{1,6},{2,7},{3,8},{4,9},{5,10},{6,11},{7,12},{8,13},{9,14},{... | collective-permute-start | bytes 202760
  313.3 41.1 %collective-permute-start.8 = (f32[2,2,48,192]{3,2,1,0:T(8,128)S(1)}, f32[2,2,48,192]{3,2,1,0:T(8,128)S(1)}, u32[]{:S(2)}, u32[]{:S(2)}) collective-permute-start(f32[2,2,48,192]{3,2,1,0:T(8,128)S(1)} %bitcast.271), channel_id=1, source_target_pairs={{1,0},{2,1},{3,2},{4,3},{5,4},{6,5},{7,6},{8,7},{9,8},{10,9},{11,1... | collective-permute-start | bytes 442376 | tf_op jit(solution)/shard_map/ppermute | solution.py:12
where the time goes:
time: 359 us; the launch traced here: 355 us
  blocking collectives  186 us (52%)
  starting transfers between devices  67.6 us (19%)
  local copies, waits for them, and re-layouts  63 us (18%)
  matrix products  17.6 us (5%)
  other arithmetic  9.37 us (3%)
  waiting for transfers between devices  8.58 us (2%)
    unnamed x2, blocking collectives  186 us
    unnamed x6, starting transfers between devices  36.3 us
    concatenate x2, local copies, waits for them, and re-layouts, backward_patches(): return jnp.concatenate(pieces, axis=1)  19.2 us
    ppermute x4, starting transfers between devices, extended_2(): before = lax.ppermute(last, axis, up)  15.2 us
    concatenate x2, local copies, waits for them, and re-layouts, forward_patches(): return jnp.concatenate(pieces, axis=1)  12.4 us
    ppermute x4, starting transfers between devices, shifted(): return lax.ppermute(block, axis, route)  10.9 us
    unnamed x6, waiting for transfers between devices  8.55 us
    unnamed x14, local copies, waits for them, and re-layouts  7.89 us
  transfers between devices with their start and end apart: 18, of which 1 were waited for; matrix products, arithmetic and copies ran while one was open for 69% of the time, Pallas kernels for 0%

commit v1 on v0

v1 whole, which is shorter than its diff:
```python
import functools
import math

import jax
import jax.numpy as jnp
from jax import lax
from jax.experimental import pallas as pl
from jax.experimental.pallas import tpu as pltpu
from jax.sharding import PartitionSpec as P

BF = jnp.bfloat16
F32 = jnp.float32
EDGE = 16
PITCH = 64
WIDE = 72
VMEM_LIMIT = 56 * 1024 * 1024


def route(sizes, steps):
    total = math.prod(sizes)
    pairs = []
    for source in range(total):
        index, rest = [], source
        for size in reversed(sizes):
            index.append(rest % size)
            rest //= size
        index = index[::-1]
        there = [a + b for a, b in zip(index, steps)]
        if all(0 <= a < size for a, size in zip(there, sizes)):
            target = 0
            for a, size in zip(there, sizes):
                target = target * size + a
            pairs.append((source, target))
    return pairs


def move(value, axes, steps):
    sizes = [lax.axis_size(axis) for axis in axes]
    return lax.ppermute(value, axes if len(axes) > 1 else axes[0], route(sizes, steps))


def spread(ref, index, cols, value):
    ref[index, EDGE : EDGE + cols, :] = value.astype(F32)


def clear_edges(ref, cols):
    blocks, width, chan = ref.shape
    ref[:, 0:EDGE, :] = jnp.zeros((blocks, EDGE, chan), F32)
    ref[:, EDGE + cols :, :] = jnp.zeros((blocks, width - EDGE - cols, chan), F32)


def transposed_dot(a, b):
    return lax.dot_general(a, b, (((1,), (1,)), ((), ())), preferred_element_type=F32)


def first_kernel(
    lengths, x, g, above, below, xprev, gnext, w1, w2,
    pay, hg, hg_top, hg_bot,
    xs, ps, xk, pk,
):
    frames, rows, cols, chan = x.shape
    cells = frames * rows * cols
    peers = pay.shape[0]
    width = chan // peers
    block = lax.axis_index("tm")
    clear_edges(xs, cols)
    clear_edges(ps, cols)
    for f in range(2):
        for r in range(4):
            spread(xs, f * 4 + r, cols, xprev[f, r])
        for r in range(2):
            spread(xs, (2 + f) * 4 + 1 + r, cols, x[f, r])
        spread(xs, (2 + f) * 4, cols, above[f])
        spread(xs, (2 + f) * 4 + 3, cols, below[f])
    for k in range(3):
        xk[k] = xs[:, EDGE - 1 + k : EDGE - 1 + k + cols, :].astype(BF)
    hidden = jnp.zeros((cells, chan), F32)
    for i in range(3):
        for j in range(3):
            for k in range(3):
                part = [xk[k, (f + 2 - i) * 4 + j : (f + 2 - i) * 4 + j + 2] for f in range(2)]
                patch = jnp.concatenate(part, axis=0).reshape(cells, chan)
                hidden += jnp.dot(patch, w1[i * 9 + j * 3 + k], preferred_element_type=F32)
    sigma = 1.0 / (1.0 + jnp.exp(-hidden))
    act = (hidden * sigma).astype(BF)
    limit = 2 * lengths[0] - 2 * frames * block

    def cotangent(f, r):
        if f >= 2 * frames:
            value = gnext[f - 2 * frames, r]
        elif r == 0:
            value = above[frames + f]
        elif r == 3:
            value = below[frames + f]
        else:
            value = g[f, r - 1]
        value = value.astype(F32)
        return jnp.where(f < limit, value, jnp.zeros_like(value))

    for r in range(4):
        field = [cotangent(f, r) for f in range(6)]
        for a in range(5):
            spread(ps, a * 4 + r, cols, field[a] + field[a + 1])
    for k in range(3):
        pk[k] = ps[:, EDGE + 1 - k : EDGE + 1 - k + cols, :].astype(BF)
    pair = jnp.zeros((cells, chan), F32)
    for i in range(3):
        for j in range(3):
            for k in range(3):
                part = [pk[k, (2 * t + i) * 4 + 2 - j : (2 * t + i) * 4 + 4 - j] for t in range(2)]
                patch = jnp.concatenate(part, axis=0).reshape(cells, chan)
                pair += transposed_dot(patch, w2[i * 9 + j * 3 + k])
    grad = (pair * sigma * (1.0 + hidden * (1.0 - sigma))).astype(BF)
    grad = grad.reshape(frames, rows, cols, chan)
    hg[...] = grad
    hg_top[...] = grad[:, 0]
    hg_bot[...] = grad[:, 1]
    half = cells // 2
    wide = act.astype(F32)
    low = wide[:, :128].astype(BF)
    high = jnp.concatenate([wide[:half, 128:], wide[half:, 128:]], axis=1).astype(BF)
    turned = [
        jnp.transpose(ps[a * 4 + 1 : a * 4 + 3, 0:PITCH, :].reshape(2 * PITCH, chan))
        for a in range(5)
    ]
    for p in range(peers):
        pay[p, 0:cells, :] = low
        pay[p, cells : cells + half, :] = high
        mine = jnp.concatenate([v[p * width : (p + 1) * width] for v in turned], axis=0)
        pay[p, cells + half :, :] = mine.astype(BF)


def second_kernel(got, out, field, left, prod):
    peers = got.shape[0]
    cells = field.shape[0] // peers // (4 * PITCH) * 192
    half = cells // 2
    chan = field.shape[1]
    width = chan // peers
    cols = 48
    blocks, _, lanes = out.shape
    span = 27 * chan // blocks
    field[...] = jnp.zeros(field.shape, BF)
    low_lane = lax.broadcasted_iota(jnp.int32, (width, 128), 1) < PITCH
    for q in range(peers):
        low = got[q, 0:cells, :]
        high = got[q, cells : cells + half, :].astype(F32)
        high = [high[:, 0:64].astype(BF), high[:, 64:128].astype(BF)]
        for t in range(2):
            for r in range(2):
                at = ((t * peers + q) * 2 + r) * PITCH + EDGE
                field[at : at + cols, 0:128] = low[(t * 2 + r) * cols : (t * 2 + r + 1) * cols]
                field[at : at + cols, 128:192] = high[t][r * cols : (r + 1) * cols]
    base = cells + half
    for a in range(5):
        plain = [
            got[q, base + a * width : base + (a + 1) * width, :].astype(F32) for q in range(peers)
        ]
        swapped = [pltpu.roll(v, PITCH, 1) for v in plain]
        zero = jnp.zeros((width, 128), F32)
        ring = [zero] + swapped + [zero]
        for q in range(peers):
            rows_of = [
                jnp.where(low_lane, ring[q + 1], ring[q + 2]),
                plain[q],
                jnp.where(low_lane, ring[q], ring[q + 1]),
            ]
            for j in range(3):
                for k in range(3):
                    value = rows_of[j]
                    if k != 1:
                        value = pltpu.roll(value, 127 if k == 0 else 1, 1)
                    for t in range(2):
                        i = a - 2 * t
                        if 0 <= i < 3:
                            tap = i * 9 + j * 3 + k
                            at = (t * peers + q) * 128
                            left[tap * width : (tap + 1) * width, at : at + 128] = value
    prod[:, 192:256] = jnp.zeros((prod.shape[0], 64), F32)
    for i in range(3):
        rows = slice(i * 9 * width, (i + 1) * 9 * width)
        prod[rows, 0:192] = jnp.dot(
            left[rows, :].astype(BF), field[...], preferred_element_type=F32
        )
    lane = lax.broadcasted_iota(jnp.int32, (width, 256), 1)
    for b in range(blocks):
        pieces = []
        done = 0
        while done < span:
            tap, start = divmod(b * span + done, chan)
            size = min(span - done, chan - start)
            pieces.append((tap, start, size, done))
            done += size
        for chunk in range(0, lanes, 128):
            value = None
            for tap, start, size, at in pieces:
                if at + size <= chunk or at >= chunk + 128:
                    continue
                shift = (at - chunk - start) % 256
                part = prod[tap * width : (tap + 1) * width, :]
                if shift:
                    part = pltpu.roll(part, shift, 1)
                part = part[:, :128]
                if value is None:
                    value = part
                else:
                    value = jnp.where(lane[:, :128] < at - chunk, value, part)
            if value is None:
                value = jnp.zeros((width, 128), F32)
            out[b, :, chunk : chunk + 128] = value.astype(BF)


def clip_kernel(got, out):
    total = got[0].astype(F32)
    for p in range(1, got.shape[0]):
        total += got[p].astype(F32)
    out[...] = total.astype(BF)


def last_kernel(scale, got, out):
    total = got[0].astype(F32)
    for p in range(1, got.shape[0]):
        total += got[p].astype(F32)
    out[...] = jnp.transpose(total * scale)[: out.shape[0], :]


def grad_kernel(hg, top, bot, nxt, nxt_top, nxt_bot, w1, out, hs, hk):
    frames, rows, cols, chan = hg.shape
    cells = frames * rows * cols
    clear_edges(hs, cols)
    for f in range(2):
        spread(hs, f * 4, cols, top[f])
        spread(hs, f * 4 + 3, cols, bot[f])
        spread(hs, (2 + f) * 4, cols, nxt_top[f])
        spread(hs, (2 + f) * 4 + 3, cols, nxt_bot[f])
        for r in range(2):
            spread(hs, f * 4 + 1 + r, cols, hg[f, r])
            spread(hs, (2 + f) * 4 + 1 + r, cols, nxt[f, r])
    for k in range(3):
        hk[k] = hs[:, EDGE + 1 - k : EDGE + 1 - k + cols, :].astype(BF)
    total = jnp.zeros((cells, chan), F32)
    for i in range(3):
        for j in range(3):
            for k in range(3):
                part = [hk[k, (f + i) * 4 + 2 - j : (f + i) * 4 + 4 - j] for f in range(2)]
                patch = jnp.concatenate(part, axis=0).reshape(cells, chan)
                total += transposed_dot(patch, w1[i * 9 + j * 3 + k])
    out[...] = total.reshape(frames, rows, cols, chan)


def in_vmem(count):
    return [pl.BlockSpec(memory_space=pltpu.VMEM)] * count


def call(body, name, shapes, args, scratch, scalars=()):
    specs = [pl.BlockSpec(memory_space=pltpu.SMEM)] * len(scalars) + in_vmem(len(args))
    outs = [jax.ShapeDtypeStruct(shape, kind) for shape, kind in shapes]
    return pl.pallas_call(
        body,
        name=name,
        out_shape=outs,
        in_specs=specs,
        out_specs=in_vmem(len(outs)),
        scratch_shapes=[pltpu.VMEM(shape, kind) for shape, kind in scratch],
        compiler_params=pltpu.CompilerParams(vmem_limit_bytes=VMEM_LIMIT),
    )(*scalars, *args)


def local(clip_input, out_grad, weight_one, weight_two, lengths):
    frames, rows, cols, chan = clip_input.shape[1:]
    cells = frames * rows * cols
    peers = lax.axis_size("row")
    clips = lax.axis_size("clip")
    steps = lax.axis_size("tm")
    width = chan // peers
    x = clip_input[0]
    g = out_grad[0]
    w1 = weight_one.reshape(27, chan, chan)
    w2 = weight_two.reshape(27, chan, chan)

    top = jnp.concatenate([x[:, 0], g[:, 0]], axis=0)
    bot = jnp.concatenate([x[:, 1], g[:, 1]], axis=0)
    above = move(bot, ("row",), (1,))
    below = move(top, ("row",), (-1,))
    x_tall = jnp.stack([above[:2], x[:, 0], x[:, 1], below[:2]], axis=1)
    g_tall = jnp.stack([above[2:4], g[:2, 0], g[:2, 1], below[2:4]], axis=1)
    xprev = move(x_tall, ("tm",), (1,))
    gnext = move(g_tall, ("tm",), (-1,))

    edge = (frames, cols, chan)
    pay, hg, hg_top, hg_bot = call(
        first_kernel,
        "hidden_and_pairs",
        [
            ((peers, cells + cells // 2 + 5 * width, 128), BF),
            ((frames, rows, cols, chan), BF),
            (edge, BF),
            (edge, BF),
        ],
        (x, g, above, below, xprev, gnext, w1, w2),
        [
            ((16, WIDE, chan), F32),
            ((20, WIDE, chan), F32),
            ((3, 16, cols, chan), BF),
            ((3, 20, cols, chan), BF),
        ],
        scalars=(lengths,),
    )
    got = lax.all_to_all(pay, "row", 0, 0)
    above_h = move(hg_bot, ("row",), (1,))
    below_h = move(hg_top, ("row",), (-1,))
    next_h = move(hg, ("tm",), (-1,))
    next_above = move(hg_bot, ("row", "tm"), (1, -1))
    next_below = move(hg_top, ("row", "tm"), (-1, -1))

    blocks = clips * steps
    span = 27 * chan // blocks
    lanes = (span + 127) // 128 * 128
    (part,) = call(
        second_kernel,
        "kernel_grad_part",
        [((blocks, width, lanes), BF)],
        (got,),
        [
            ((2 * peers * 2 * PITCH, chan), BF),
            ((27 * width, 2 * peers * 128), F32),
            ((27 * width, 256), F32),
        ],
    )
    by_clip = lax.all_to_all(part.reshape(clips, steps * width, lanes), "clip", 0, 0)
    (summed,) = call(clip_kernel, "clip_sum", [((steps * width, lanes), BF)], (by_clip,), [])
    by_step = lax.all_to_all(summed.reshape(steps, width, lanes), "tm", 0, 0)
    total = clips * 2 * frames * steps * rows * peers * cols
    (kernel_grad,) = call(
        functools.partial(last_kernel, 1.0 / math.sqrt(total)),
        "kernel_grad_sum",
        [((span, width), F32)],
        (by_step,),
        [],
    )
    (input_grad,) = call(
        grad_kernel,
        "input_grad",
        [((frames, rows, cols, chan), F32)],
        (hg, above_h, below_h, next_h, next_above, next_below, w1),
        [((16, WIDE, chan), F32), ((3, 16, cols, chan), BF)],
    )
    return (input_grad[None], kernel_grad)


def solution(mesh):
    return jax.shard_map(
        local,
        mesh=mesh,
        in_specs=(
            P("clip", "tm", "row", None, None),
            P("clip", "tm", "row", None, None),
            P(),
            P(),
            P("clip"),
        ),
        out_specs=(P("clip", "tm", "row", None, None), P(("clip", "tm"), "row")),
        check_vma=False,
    )
```

time: 359 us -> 106 us (0.30)
  the two profiles are of different devices: /device:TPU:24 before, /device:TPU:97 now
where the time goes in v1:
time: 106 us; the launch traced here: 105 us
  starting transfers between devices  36.4 us (34%)
  blocking collectives  31.2 us (29%)
  Pallas kernels  16.2 us (15%)
  waiting for transfers between devices  11.9 us (11%)
  local copies, waits for them, and re-layouts  7.51 us (7%)
  between operations  1.51 us (1%)
    ppermute x9, starting transfers between devices, move(): lax.ppermute(value, axes if len(axes) > 1 else axes[0], route(sizes, steps))  25.2 us
    all_to_all x1, blocking collectives, local(): got = lax.all_to_all(pay, 'row', 0, 0)  19.7 us
    pallas_call x5, Pallas kernels, call(): pl.pallas_call(body, name=name, out_shape=outs, in_specs=specs, out_specs...  16.2 us
    ppermute x9, waiting for transfers between devices, move(): lax.ppermute(value, axes if len(axes) > 1 else axes[0], route(sizes, steps))  11.9 us
    all_to_all x1, blocking collectives, local(): lax.all_to_all(part.reshape(clips, steps * width, lanes), 'clip', 0, 0)  11.5 us
    all_to_all x1, starting transfers between devices, local(): by_step = lax.all_to_all(summed.reshape(steps, width, lanes), 'tm', 0, 0)  11.2 us
    unnamed x27, local copies, waits for them, and re-layouts  5.88 us
  transfers between devices with their start and end apart: 10, of which 4 were waited for; matrix products, arithmetic and copies ran while one was open for 2% of the time, Pallas kernels for 3%

profile of v1, /device:TPU:97, one launch (start us, length us, event | category | flops | bytes accessed | tf_op | source)
XLA Modules:
  0.0 104.9 jit_solution(10058851856127588689)
XLA Ops:
  0.6 0.9 copy.19
  1.5 0.9 copy.18
  2.5 3.7 %collective-permute-start = (bf16[6,48,192]{2,1,0:T(8,128)(2,1)S(1)}, bf16[6,48,192]{2,1,0:T(8,128)(2,1)S(1)}, u32[]{:S(2)}, u32[]{:S(2)}) collective-permute-start(bf16[6,48,192]{2,1,0:T(8,128)(2,1)S(1)} %pad_maximum_fusion.2), channel_id=1, source_target_pairs={{0,16},{16,32},{32,48},{48,64},{64,80},{80,96},{96,112},{1,17},{17... | collective-permute-start | bytes 331784 | tf_op jit(solution)/shard_map/ppermute | solution.py:39
  6.3 1.9 %collective-permute-start.1 = (bf16[6,48,192]{2,1,0:T(8,128)(2,1)S(1)}, bf16[6,48,192]{2,1,0:T(8,128)(2,1)S(1)}, u32[]{:S(2)}, u32[]{:S(2)}) collective-permute-start(bf16[6,48,192]{2,1,0:T(8,128)(2,1)S(1)} %pad_maximum_fusion.3), channel_id=1, source_target_pairs={{16,0},{32,16},{48,32},{64,48},{80,64},{96,80},{112,96},{17,1},{33... | collective-permute-start | bytes 331784 | tf_op jit(solution)/shard_map/ppermute | solution.py:39
  8.2 0.9 slice_bitcast_fusion.2
  9.1 0.0 collective-permute-done.above
  9.1 0.0 copy-start
  9.1 3.6 %collective-permute-done.1.below = bf16[6,48,192]{2,1,0:T(8,128)(2,1)S(1)} collective-permute-done((bf16[6,48,192]{2,1,0:T(8,128)(2,1)S(1)}, bf16[6,48,192]{2,1,0:T(8,128)(2,1)S(1)}, u32[]{:S(2)}, u32[]{:S(2)}) %collective-permute-start.1) | collective-permute-done | bytes 110624 | tf_op jit(solution)/shard_map/ppermute | solution.py:39
  12.8 4.8 %collective-permute-start.2 = (bf16[2,4,48,192]{3,2,0,1:T(8,128)(2,1)S(1)}, bf16[2,4,48,192]{3,2,0,1:T(8,128)(2,1)S(1)}, u32[]{:S(2)}, u32[]{:S(2)}) collective-permute-start(bf16[2,4,48,192]{3,2,0,1:T(8,128)(2,1)S(1)} %pad_maximum_fusion), channel_id=1, source_target_pairs={{0,1},{1,2},{2,3},{3,4},{4,5},{5,6},{6,7},{7,8},{8,9},{9,10},{10,1... | collective-permute-start | bytes 442376 | tf_op jit(solution)/shard_map/ppermute | solution.py:39
  17.6 1.9 %collective-permute-start.3 = (bf16[2,4,48,192]{3,2,1,0:T(8,128)(2,1)S(1)}, bf16[2,4,48,192]{3,2,1,0:T(8,128)(2,1)S(1)}, u32[]{:S(2)}, u32[]{:S(2)}) collective-permute-start(bf16[2,4,48,192]{3,2,1,0:T(8,128)(2,1)S(1)} %pad_maximum_fusion.1), channel_id=1, source_target_pairs={{1,0},{2,1},{3,2},{4,3},{5,4},{6,5},{7,6},{8,7},{9,8},{10,9},{11,1... | collective-permute-start | bytes 442376 | tf_op jit(solution)/shard_map/ppermute | solution.py:39
  20.2 0.0 collective-permute-done.2
  20.2 0.7 copy.12.xprev
  20.9 4.3 %collective-permute-done.3.gnext = bf16[2,4,48,192]{3,2,1,0:T(8,128)(2,1)S(1)} collective-permute-done((bf16[2,4,48,192]{3,2,1,0:T(8,128)(2,1)S(1)}, bf16[2,4,48,192]{3,2,1,0:T(8,128)(2,1)S(1)}, u32[]{:S(2)}, u32[]{:S(2)}) %collective-permute-start.3) | collective-permute-done | bytes 147488 | tf_op jit(solution)/shard_map/ppermute | solution.py:39
  25.2 0.0 copy-done
  25.2 0.0 copy-done.1
  25.2 0.7 copy-done.3
  25.9 5.8 %hidden_and_pairs.1 = (bf16[8,408,128]{2,1,0:T(8,128)(2,1)}, bf16[2,2,48,192]{3,2,1,0:T(8,128)(2,1)}, bf16[2,48,192]{2,1,0:T(8,128)(2,1)}, bf16[2,48,192]{2,1,0:T(8,128)(2,1)}) custom-call(s32[1]{0:T(128)S(6)} %copy.20.lengths, bf16[2,2,48,192]{3,2,1,0:T(8,128)(2,1)} %bitcast.42, bf16[4,2,48,192]{3,2,1,0:T(8,128)(2,1)} %bitcast.37, ...), custom_call_target="tpu_custom_call" | custom-call | tf_op jit(solution)/shard_map/hidden_and_pairs/pallas_call | solution.py:257
  31.7 0.0 copy-start.10
  31.7 19.7 %all_to_all.15.got = bf16[8,408,128]{2,1,0:T(8,128)(2,1)} all-to-all(bf16[8,408,128]{2,1,0:T(8,128)(2,1)} %get-tuple-element.9), channel_id=1, replica_groups=mesh['clip'=4,'row'=8,'tm'=16] {'row'}, dimensions={0} | all-to-all | bytes 1671168 | tf_op jit(solution)/shard_map/all_to_all | solution.py:308
  51.5 3.6 %kernel_grad_part.1 = bf16[64,24,128]{2,1,0:T(8,128)(2,1)} custom-call(bf16[8,408,128]{2,1,0:T(8,128)(2,1)} %all_to_all.15.got), custom_call_target="tpu_custom_call" | custom-call | tf_op jit(solution)/shard_map/kernel_grad_part/pallas_call | solution.py:257
  55.0 11.5 %all_to_all.16.got = bf16[4,384,128]{2,1,0:T(8,128)(2,1)} all-to-all(bf16[4,384,128]{2,1,0:T(8,128)(2,1)} %bitcast.36), channel_id=1, replica_groups=mesh['clip'=4,'row'=8,'tm'=16] {'clip'}, dimensions={0} | all-to-all | bytes 786432 | tf_op jit(solution)/shard_map/all_to_all | solution.py:329
  66.5 1.7 %clip_sum.1 = bf16[384,128]{1,0:T(8,128)(2,1)} custom-call(bf16[4,384,128]{2,1,0:T(8,128)(2,1)} %all_to_all.16.got), custom_call_target="tpu_custom_call" | custom-call | tf_op jit(solution)/shard_map/clip_sum/pallas_call | solution.py:257
  68.2 11.2 %all-to-all-start.2 = ((bf16[16,24,128]{2,1,0:T(8,128)(2,1)}), bf16[16,24,128]{2,1,0:T(8,128)(2,1)S(1)}, u32[]{:S(2)}, u32[]{:S(2)}) async-start(bf16[16,24,128]{2,1,0:T(8,128)(2,1)} %bitcast.41), calls=%async_computation.2 | async-start | bytes 196608 | tf_op jit(solution)/shard_map/all_to_all | solution.py:331
  79.4 0.0 copy-done.4
  79.4 2.2 %collective-permute-start.6 = (bf16[2,2,48,192]{3,2,1,0:T(8,128)(2,1)S(1)}, bf16[2,2,48,192]{3,2,1,0:T(8,128)(2,1)S(1)}, u32[]{:S(2)}, u32[]{:S(2)}) collective-permute-start(bf16[2,2,48,192]{3,2,1,0:T(8,128)(2,1)S(1)} %copy-done.4), channel_id=1, source_target_pairs={{1,0},{2,1},{3,2},{4,3},{5,4},{6,5},{7,6},{8,7},{9,8},{10,9},{11,1... | collective-permute-start | bytes 221192 | tf_op jit(solution)/shard_map/ppermute | solution.py:39
  81.6 0.0 copy-done.11
  81.6 4.8 %collective-permute-start.7 = (bf16[2,48,192]{2,1,0:T(8,128)(2,1)S(1)}, bf16[2,48,192]{2,1,0:T(8,128)(2,1)S(1)}, u32[]{:S(2)}, u32[]{:S(2)}) collective-permute-start(bf16[2,48,192]{2,1,0:T(8,128)(2,1)S(1)} %copy-done.11), channel_id=1, source_target_pairs={{1,16},{2,17},{3,18},{4,19},{5,20},{6,21},{7,22},{8,23},{9,24},{10... | collective-permute-start | bytes 110600 | tf_op jit(solution)/shard_map/ppermute | solution.py:39
  86.3 1.9 %collective-permute-start.4 = (bf16[2,48,192]{2,1,0:T(8,128)(2,1)S(1)}, bf16[2,48,192]{2,1,0:T(8,128)(2,1)S(1)}, u32[]{:S(2)}, u32[]{:S(2)}) collective-permute-start(bf16[2,48,192]{2,1,0:T(8,128)(2,1)S(1)} %copy-done.11), channel_id=1, source_target_pairs={{0,16},{16,32},{32,48},{48,64},{64,80},{80,96},{96,112},{1,17},{17... | collective-permute-start | bytes 110600 | tf_op jit(solution)/shard_map/ppermute | solution.py:39
  88.3 0.0 copy-done.10
  88.3 2.1 %collective-permute-start.8 = (bf16[2,48,192]{2,1,0:T(8,128)(2,1)S(1)}, bf16[2,48,192]{2,1,0:T(8,128)(2,1)S(1)}, u32[]{:S(2)}, u32[]{:S(2)}) collective-permute-start(bf16[2,48,192]{2,1,0:T(8,128)(2,1)S(1)} %copy-done.10), channel_id=1, source_target_pairs={{17,0},{18,1},{19,2},{20,3},{21,4},{22,5},{23,6},{24,7},{25,8},{26... | collective-permute-start | bytes 110600 | tf_op jit(solution)/shard_map/ppermute | solution.py:39
  90.4 1.9 %collective-permute-start.5 = (bf16[2,48,192]{2,1,0:T(8,128)(2,1)S(1)}, bf16[2,48,192]{2,1,0:T(8,128)(2,1)S(1)}, u32[]{:S(2)}, u32[]{:S(2)}) collective-permute-start(bf16[2,48,192]{2,1,0:T(8,128)(2,1)S(1)} %copy-done.10), channel_id=1, source_target_pairs={{16,0},{32,16},{48,32},{64,48},{80,64},{96,80},{112,96},{17,1},{33... | collective-permute-start | bytes 110600 | tf_op jit(solution)/shard_map/ppermute | solution.py:39
  92.3 0.0 collective-permute-done.7.nxt_top
  92.3 0.0 copy-start.6
  92.4 0.0 collective-permute-done.4.top
  92.4 0.0 copy-start.7
  92.4 3.5 %collective-permute-done.8.nxt_bot = bf16[2,48,192]{2,1,0:T(8,128)(2,1)S(1)} collective-permute-done((bf16[2,48,192]{2,1,0:T(8,128)(2,1)S(1)}, bf16[2,48,192]{2,1,0:T(8,128)(2,1)S(1)}, u32[]{:S(2)}, u32[]{:S(2)}) %collective-permute-start.8) | collective-permute-done | bytes 36896 | tf_op jit(solution)/shard_map/ppermute | solution.py:39
  95.9 0.5 collective-permute-done.5.bot
  96.3 0.0 collective-permute-done.6.nxt
  96.3 0.0 copy-done.6
  96.3 0.0 copy-done.7
  96.4 0.1 copy-done.8
  96.5 0.5 copy-done.9
  97.0 0.6 copy-done.5
  97.6 3.6 %input_grad.1 = f32[2,2,48,192]{3,2,1,0:T(8,128)} custom-call(bf16[2,2,48,192]{3,2,1,0:T(8,128)(2,1)} %get-tuple-element.6.hg, bf16[2,48,192]{2,1,0:T(8,128)(2,1)} %copy-done.7, bf16[2,48,192]{2,1,0:T(8,128)(2,1)} %copy-done.9, bf16[2,2,48,192]{3,2,1,0:T(8,128)(2,1)} %copy-done.5, bf16[2,48,192]{2,1,0:T(8,128)(2,1)} %copy-done.6, ...), custom_call_target="tpu_custom_call" | custom-call | tf_op jit(solution)/shard_map/input_grad/pallas_call | solution.py:257
  101.2 0.0 all-to-all-done.2.got
  101.2 0.6 copy-done.2
  101.8 1.6 %kernel_grad_sum.1 = f32[81,24]{1,0:T(8,128)} custom-call(bf16[16,24,128]{2,1,0:T(8,128)(2,1)} %copy-done.2), custom_call_target="tpu_custom_call" | custom-call | tf_op jit(solution)/shard_map/kernel_grad_sum/pallas_call | solution.py:257
  103.4 1.5 %copy.13 = f32[81,24]{0,1:T(8,128)} copy(f32[81,24]{1,0:T(8,128)} %kernel_grad_sum.1) | data formatting | bytes 15552
  (16 shorter events, 0.2 us)
Async XLA Ops:
  2.5 6.6 %collective-permute-start = (bf16[6,48,192]{2,1,0:T(8,128)(2,1)S(1)}, bf16[6,48,192]{2,1,0:T(8,128)(2,1)S(1)}, u32[]{:S(2)}, u32[]{:S(2)}) collective-permute-start(bf16[6,48,192]{2,1,0:T(8,128)(2,1)S(1)} %pad_maximum_fusion.2), channel_id=1, source_target_pairs={{0,16},{16,32},{32,48},{48,64},{64,80},{80,96},{96,112},{1,17},{17... | collective-permute-start | bytes 331784 | tf_op jit(solution)/shard_map/ppermute | solution.py:39
  6.3 6.5 %collective-permute-start.1 = (bf16[6,48,192]{2,1,0:T(8,128)(2,1)S(1)}, bf16[6,48,192]{2,1,0:T(8,128)(2,1)S(1)}, u32[]{:S(2)}, u32[]{:S(2)}) collective-permute-start(bf16[6,48,192]{2,1,0:T(8,128)(2,1)S(1)} %pad_maximum_fusion.3), channel_id=1, source_target_pairs={{16,0},{32,16},{48,32},{64,48},{80,64},{96,80},{112,96},{17,1},{33... | collective-permute-start | bytes 331784 | tf_op jit(solution)/shard_map/ppermute | solution.py:39
  9.1 16.1 %copy-start = (bf16[6,48,192]{2,1,0:T(8,128)(2,1)}, bf16[6,48,192]{2,1,0:T(8,128)(2,1)S(1)}, u32[]{:S(2)}) copy-start(bf16[6,48,192]{2,1,0:T(8,128)(2,1)S(1)} %collective-permute-done.above) | copy-start | bytes 331780
  12.7 12.5 %copy-start.1 = (bf16[6,48,192]{2,1,0:T(8,128)(2,1)}, bf16[6,48,192]{2,1,0:T(8,128)(2,1)S(1)}, u32[]{:S(2)}) copy-start(bf16[6,48,192]{2,1,0:T(8,128)(2,1)S(1)} %collective-permute-done.1.below) | copy-start | bytes 331780
  12.8 7.4 %collective-permute-start.2 = (bf16[2,4,48,192]{3,2,0,1:T(8,128)(2,1)S(1)}, bf16[2,4,48,192]{3,2,0,1:T(8,128)(2,1)S(1)}, u32[]{:S(2)}, u32[]{:S(2)}) collective-permute-start(bf16[2,4,48,192]{3,2,0,1:T(8,128)(2,1)S(1)} %pad_maximum_fusion), channel_id=1, source_target_pairs={{0,1},{1,2},{2,3},{3,4},{4,5},{5,6},{6,7},{7,8},{8,9},{9,10},{10,1... | collective-permute-start | bytes 442376 | tf_op jit(solution)/shard_map/ppermute | solution.py:39
  17.6 7.6 %collective-permute-start.3 = (bf16[2,4,48,192]{3,2,1,0:T(8,128)(2,1)S(1)}, bf16[2,4,48,192]{3,2,1,0:T(8,128)(2,1)S(1)}, u32[]{:S(2)}, u32[]{:S(2)}) collective-permute-start(bf16[2,4,48,192]{3,2,1,0:T(8,128)(2,1)S(1)} %pad_maximum_fusion.1), channel_id=1, source_target_pairs={{1,0},{2,1},{3,2},{4,3},{5,4},{6,5},{7,6},{8,7},{9,8},{10,9},{11,1... | collective-permute-start | bytes 442376 | tf_op jit(solution)/shard_map/ppermute | solution.py:39
  25.2 0.7 copy-start.3
  31.7 47.6 %copy-start.4 = (bf16[2,2,48,192]{3,2,1,0:T(8,128)(2,1)S(1)}, bf16[2,2,48,192]{3,2,1,0:T(8,128)(2,1)}, u32[]{:S(2)}) copy-start(bf16[2,2,48,192]{3,2,1,0:T(8,128)(2,1)} %get-tuple-element.6.hg) | copy-start | bytes 221188
  31.7 49.8 %copy-start.11 = (bf16[2,48,192]{2,1,0:T(8,128)(2,1)S(1)}, bf16[2,48,192]{2,1,0:T(8,128)(2,1)}, u32[]{:S(2)}) copy-start(bf16[2,48,192]{2,1,0:T(8,128)(2,1)} %get-tuple-element.7) | copy-start | bytes 110596
  31.7 56.5 %copy-start.10 = (bf16[2,48,192]{2,1,0:T(8,128)(2,1)S(1)}, bf16[2,48,192]{2,1,0:T(8,128)(2,1)}, u32[]{:S(2)}) copy-start(bf16[2,48,192]{2,1,0:T(8,128)(2,1)} %get-tuple-element.8) | copy-start | bytes 110596
  68.2 33.0 %all-to-all-start.2 = ((bf16[16,24,128]{2,1,0:T(8,128)(2,1)}), bf16[16,24,128]{2,1,0:T(8,128)(2,1)S(1)}, u32[]{:S(2)}, u32[]{:S(2)}) async-start(bf16[16,24,128]{2,1,0:T(8,128)(2,1)} %bitcast.41), calls=%async_computation.2 | async-start | bytes 196608 | tf_op jit(solution)/shard_map/all_to_all | solution.py:331
  79.4 17.0 %collective-permute-start.6 = (bf16[2,2,48,192]{3,2,1,0:T(8,128)(2,1)S(1)}, bf16[2,2,48,192]{3,2,1,0:T(8,128)(2,1)S(1)}, u32[]{:S(2)}, u32[]{:S(2)}) collective-permute-start(bf16[2,2,48,192]{3,2,1,0:T(8,128)(2,1)S(1)} %copy-done.4), channel_id=1, source_target_pairs={{1,0},{2,1},{3,2},{4,3},{5,4},{6,5},{7,6},{8,7},{9,8},{10,9},{11,1... | collective-permute-start | bytes 221192 | tf_op jit(solution)/shard_map/ppermute | solution.py:39
  81.6 10.8 %collective-permute-start.7 = (bf16[2,48,192]{2,1,0:T(8,128)(2,1)S(1)}, bf16[2,48,192]{2,1,0:T(8,128)(2,1)S(1)}, u32[]{:S(2)}, u32[]{:S(2)}) collective-permute-start(bf16[2,48,192]{2,1,0:T(8,128)(2,1)S(1)} %copy-done.11), channel_id=1, source_target_pairs={{1,16},{2,17},{3,18},{4,19},{5,20},{6,21},{7,22},{8,23},{9,24},{10... | collective-permute-start | bytes 110600 | tf_op jit(solution)/shard_map/ppermute | solution.py:39
  86.3 6.0 %collective-permute-start.4 = (bf16[2,48,192]{2,1,0:T(8,128)(2,1)S(1)}, bf16[2,48,192]{2,1,0:T(8,128)(2,1)S(1)}, u32[]{:S(2)}, u32[]{:S(2)}) collective-permute-start(bf16[2,48,192]{2,1,0:T(8,128)(2,1)S(1)} %copy-done.11), channel_id=1, source_target_pairs={{0,16},{16,32},{32,48},{48,64},{64,80},{80,96},{96,112},{1,17},{17... | collective-permute-start | bytes 110600 | tf_op jit(solution)/shard_map/ppermute | solution.py:39
  88.3 7.6 %collective-permute-start.8 = (bf16[2,48,192]{2,1,0:T(8,128)(2,1)S(1)}, bf16[2,48,192]{2,1,0:T(8,128)(2,1)S(1)}, u32[]{:S(2)}, u32[]{:S(2)}) collective-permute-start(bf16[2,48,192]{2,1,0:T(8,128)(2,1)S(1)} %copy-done.10), channel_id=1, source_target_pairs={{17,0},{18,1},{19,2},{20,3},{21,4},{22,5},{23,6},{24,7},{25,8},{26... | collective-permute-start | bytes 110600 | tf_op jit(solution)/shard_map/ppermute | solution.py:39
  90.4 5.9 %collective-permute-start.5 = (bf16[2,48,192]{2,1,0:T(8,128)(2,1)S(1)}, bf16[2,48,192]{2,1,0:T(8,128)(2,1)S(1)}, u32[]{:S(2)}, u32[]{:S(2)}) collective-permute-start(bf16[2,48,192]{2,1,0:T(8,128)(2,1)S(1)} %copy-done.10), channel_id=1, source_target_pairs={{16,0},{32,16},{48,32},{64,48},{80,64},{96,80},{112,96},{17,1},{33... | collective-permute-start | bytes 110600 | tf_op jit(solution)/shard_map/ppermute | solution.py:39
  92.3 4.0 %copy-start.6 = (bf16[2,48,192]{2,1,0:T(8,128)(2,1)}, bf16[2,48,192]{2,1,0:T(8,128)(2,1)S(1)}, u32[]{:S(2)}) copy-start(bf16[2,48,192]{2,1,0:T(8,128)(2,1)S(1)} %collective-permute-done.7.nxt_top) | copy-start | bytes 110596
  92.4 4.0 %copy-start.7 = (bf16[2,48,192]{2,1,0:T(8,128)(2,1)}, bf16[2,48,192]{2,1,0:T(8,128)(2,1)S(1)}, u32[]{:S(2)}) copy-start(bf16[2,48,192]{2,1,0:T(8,128)(2,1)S(1)} %collective-permute-done.4.top) | copy-start | bytes 110596
  95.9 0.6 copy-start.8
  96.3 0.6 copy-start.9
  97.0 0.6 copy-start.5
  101.2 0.6 copy-start.2

commit v2 on v1

--- a/solution.py
+++ b/solution.py
@@ -13,7 +13,7 @@
 EDGE = 16
 PITCH = 64
 WIDE = 72
-VMEM_LIMIT = 56 * 1024 * 1024
+MIB = 1024 * 1024
 
 
 def route(sizes, steps):
@@ -53,11 +53,36 @@
     return lax.dot_general(a, b, (((1,), (1,)), ((), ())), preferred_element_type=F32)
 
 
+def edges_kernel(x, g, xprev, gnext, top, bot, sem):
+    nx, ng = x.shape[0], g.shape[0]
+    copies = []
+    for row, out in ((0, top), (1, bot)):
+        for source, at in ((x, 0), (g, 2 * nx)):
+            target = out.at[at : at + source.shape[0]]
+            copies.append(pltpu.make_async_copy(source.at[:, row], target, sem.at[len(copies)]))
+    for copy in copies:
+        copy.start()
+    for row, out in ((0, top), (1, bot)):
+        for f in range(nx):
+            out[nx + f] = xprev[f, row]
+            out[2 * nx + ng + f] = gnext[f, row]
+    for copy in copies:
+        copy.wait()
+
+
+def packed(width, span):
+    return (width, span) == (24, 81)
+
+
 def first_kernel(
-    lengths, x, g, above, below, xprev, gnext, w1, w2,
+    lengths, x_far, g_far, w1_far, w2_far, above, below, xprev, gnext,
     pay, hg, hg_top, hg_bot,
-    xs, ps, xk, pk,
+    xs, ps, xk, pk, x, g, w1, w2, sem,
 ):
+    pairs = ((x_far, x), (w1_far, w1), (g_far, g), (w2_far, w2))
+    copies = [pltpu.make_async_copy(a, b, sem.at[n]) for n, (a, b) in enumerate(pairs)]
+    for copy in copies:
+        copy.start()
     frames, rows, cols, chan = x.shape
     cells = frames * rows * cols
     peers = pay.shape[0]
@@ -65,15 +90,18 @@
     block = lax.axis_index("tm")
     clear_edges(xs, cols)
     clear_edges(ps, cols)
+    copies[0].wait()
     for f in range(2):
-        for r in range(4):
-            spread(xs, f * 4 + r, cols, xprev[f, r])
         for r in range(2):
+            spread(xs, f * 4 + 1 + r, cols, xprev[f, r])
             spread(xs, (2 + f) * 4 + 1 + r, cols, x[f, r])
+        spread(xs, f * 4, cols, above[2 + f])
+        spread(xs, f * 4 + 3, cols, below[2 + f])
         spread(xs, (2 + f) * 4, cols, above[f])
         spread(xs, (2 + f) * 4 + 3, cols, below[f])
     for k in range(3):
         xk[k] = xs[:, EDGE - 1 + k : EDGE - 1 + k + cols, :].astype(BF)
+    copies[1].wait()
     hidden = jnp.zeros((cells, chan), F32)
     for i in range(3):
         for j in range(3):
@@ -86,23 +114,25 @@
     limit = 2 * lengths[0] - 2 * frames * block
 
     def cotangent(f, r):
-        if f >= 2 * frames:
-            value = gnext[f - 2 * frames, r]
-        elif r == 0:
-            value = above[frames + f]
+        if r == 0:
+            value = above[2 * frames + f]
         elif r == 3:
-            value = below[frames + f]
+            value = below[2 * frames + f]
+        elif f >= 2 * frames:
+            value = gnext[f - 2 * frames, r - 1]
         else:
             value = g[f, r - 1]
         value = value.astype(F32)
         return jnp.where(f < limit, value, jnp.zeros_like(value))
 
+    copies[2].wait()
     for r in range(4):
         field = [cotangent(f, r) for f in range(6)]
         for a in range(5):
             spread(ps, a * 4 + r, cols, field[a] + field[a + 1])
     for k in range(3):
         pk[k] = ps[:, EDGE + 1 - k : EDGE + 1 - k + cols, :].astype(BF)
+    copies[3].wait()
     pair = jnp.zeros((cells, chan), F32)
     for i in range(3):
         for j in range(3):
@@ -130,7 +160,14 @@
         pay[p, cells + half :, :] = mine.astype(BF)
 
 
-def second_kernel(got, out, field, left, prod):
+def tall_kernel(hg, above, below, tall):
+    tall[:, 0] = above[...]
+    tall[:, 1] = hg[:, 0]
+    tall[:, 2] = hg[:, 1]
+    tall[:, 3] = below[...]
+
+
+def second_kernel(span, got, out, field, left, prod):
     peers = got.shape[0]
     cells = field.shape[0] // peers // (4 * PITCH) * 192
     half = cells // 2
@@ -138,7 +175,6 @@
     width = chan // peers
     cols = 48
     blocks, _, lanes = out.shape
-    span = 27 * chan // blocks
     field[...] = jnp.zeros(field.shape, BF)
     low_lane = lax.broadcasted_iota(jnp.int32, (width, 128), 1) < PITCH
     for q in range(peers):
@@ -206,6 +242,10 @@
                     value = jnp.where(lane[:, :128] < at - chunk, value, part)
             if value is None:
                 value = jnp.zeros((width, 128), F32)
+            if packed(width, span):
+                tail = value[16:24]
+                tail = jnp.concatenate([pltpu.roll(tail, 81, 1), pltpu.roll(tail, 40, 1)], axis=0)
+                value = jnp.where(lane[:16, :128] < span, value[:16], tail)
             out[b, :, chunk : chunk + 128] = value.astype(BF)
 
 
@@ -216,53 +256,57 @@
     out[...] = total.astype(BF)
 
 
-def last_kernel(scale, got, out):
+def last_kernel(scale, w1_far, got, tall, after, out, grad, hs, hk, w1, sem):
+    copy = pltpu.make_async_copy(w1_far, w1, sem.at[0])
+    copy.start()
+    width, span = out.shape
     total = got[0].astype(F32)
     for p in range(1, got.shape[0]):
         total += got[p].astype(F32)
-    out[...] = jnp.transpose(total * scale)[: out.shape[0], :]
-
-
-def grad_kernel(hg, top, bot, nxt, nxt_top, nxt_bot, w1, out, hs, hk):
-    frames, rows, cols, chan = hg.shape
+    total = total * scale
+    if packed(width, span):
+        lane = lax.broadcasted_iota(jnp.int32, (8, 128), 1)
+        tail = jnp.where(lane < 41, pltpu.roll(total[:8], 47, 1), pltpu.roll(total[8:], 88, 1))
+        out[:16] = total[:, :span]
+        out[16:] = tail[:, :span]
+    else:
+        out[...] = total[:, :span]
+    frames, rows, cols, chan = grad.shape
     cells = frames * rows * cols
     clear_edges(hs, cols)
     for f in range(2):
-        spread(hs, f * 4, cols, top[f])
-        spread(hs, f * 4 + 3, cols, bot[f])
-        spread(hs, (2 + f) * 4, cols, nxt_top[f])
-        spread(hs, (2 + f) * 4 + 3, cols, nxt_bot[f])
-        for r in range(2):
-            spread(hs, f * 4 + 1 + r, cols, hg[f, r])
-            spread(hs, (2 + f) * 4 + 1 + r, cols, nxt[f, r])
+        for r in range(4):
+            spread(hs, f * 4 + r, cols, tall[f, r])
+            spread(hs, (2 + f) * 4 + r, cols, after[f, r])
     for k in range(3):
         hk[k] = hs[:, EDGE + 1 - k : EDGE + 1 - k + cols, :].astype(BF)
-    total = jnp.zeros((cells, chan), F32)
+    copy.wait()
+    acc = jnp.zeros((cells, chan), F32)
     for i in range(3):
         for j in range(3):
             for k in range(3):
                 part = [hk[k, (f + i) * 4 + 2 - j : (f + i) * 4 + 4 - j] for f in range(2)]
                 patch = jnp.concatenate(part, axis=0).reshape(cells, chan)
-                total += transposed_dot(patch, w1[i * 9 + j * 3 + k])
-    out[...] = total.reshape(frames, rows, cols, chan)
-
-
-def in_vmem(count):
-    return [pl.BlockSpec(memory_space=pltpu.VMEM)] * count
-
-
-def call(body, name, shapes, args, scratch, scalars=()):
-    specs = [pl.BlockSpec(memory_space=pltpu.SMEM)] * len(scalars) + in_vmem(len(args))
+                acc += transposed_dot(patch, w1[i * 9 + j * 3 + k])
+    grad[...] = acc.reshape(frames, rows, cols, chan)
+
+
+def call(body, name, limit, shapes, args, scratch, far=(), scalars=(), sems=0):
+    spaces = [pltpu.SMEM] * len(scalars) + [pltpu.HBM] * len(far) + [pltpu.VMEM] * len(args)
+    far = [pltpu.with_memory_space_constraint(value, pltpu.HBM) for value in far]
     outs = [jax.ShapeDtypeStruct(shape, kind) for shape, kind in shapes]
+    buffers = [pltpu.VMEM(shape, kind) for shape, kind in scratch]
+    if sems:
+        buffers.append(pltpu.SemaphoreType.DMA((sems,)))
     return pl.pallas_call(
         body,
         name=name,
         out_shape=outs,
-        in_specs=specs,
-        out_specs=in_vmem(len(outs)),
-        scratch_shapes=[pltpu.VMEM(shape, kind) for shape, kind in scratch],
-        compiler_params=pltpu.CompilerParams(vmem_limit_bytes=VMEM_LIMIT),
-    )(*scalars, *args)
+        in_specs=[pl.BlockSpec(memory_space=space) for space in spaces],
+        out_specs=[pl.BlockSpec(memory_space=pltpu.VMEM)] * len(outs),
+        scratch_shapes=buffers,
+        compiler_params=pltpu.CompilerParams(vmem_limit_bytes=limit * MIB),
+    )(*scalars, *far, *args)
 
 
 def local(clip_input, out_grad, weight_one, weight_two, lengths):
@@ -277,48 +321,71 @@
     w1 = weight_one.reshape(27, chan, chan)
     w2 = weight_two.reshape(27, chan, chan)
 
-    top = jnp.concatenate([x[:, 0], g[:, 0]], axis=0)
-    bot = jnp.concatenate([x[:, 1], g[:, 1]], axis=0)
+    xprev = move(x, ("tm",), (1,))
+    gnext = move(g[:frames], ("tm",), (-1,))
+    band = (5 * frames, cols, chan)
+    top, bot = call(
+        edges_kernel,
+        "edge_rows",
+        4,
+        [(band, BF), (band, BF)],
+        (xprev, gnext),
+        [],
+        far=(x, g),
+        sems=4,
+    )
     above = move(bot, ("row",), (1,))
     below = move(top, ("row",), (-1,))
-    x_tall = jnp.stack([above[:2], x[:, 0], x[:, 1], below[:2]], axis=1)
-    g_tall = jnp.stack([above[2:4], g[:2, 0], g[:2, 1], below[2:4]], axis=1)
-    xprev = move(x_tall, ("tm",), (1,))
-    gnext = move(g_tall, ("tm",), (-1,))
 
     edge = (frames, cols, chan)
     pay, hg, hg_top, hg_bot = call(
         first_kernel,
         "hidden_and_pairs",
+        20,
         [
             ((peers, cells + cells // 2 + 5 * width, 128), BF),
             ((frames, rows, cols, chan), BF),
             (edge, BF),
             (edge, BF),
         ],
-        (x, g, above, below, xprev, gnext, w1, w2),
+        (above, below, xprev, gnext),
         [
             ((16, WIDE, chan), F32),
             ((20, WIDE, chan), F32),
             ((3, 16, cols, chan), BF),
             ((3, 20, cols, chan), BF),
+            (x.shape, BF),
+            (g.shape, BF),
+            (w1.shape, BF),
+            (w2.shape, BF),
         ],
+        far=(x, g, w1, w2),
         scalars=(lengths,),
-    )
-    got = lax.all_to_all(pay, "row", 0, 0)
+        sems=4,
+    )
     above_h = move(hg_bot, ("row",), (1,))
     below_h = move(hg_top, ("row",), (-1,))
-    next_h = move(hg, ("tm",), (-1,))
-    next_above = move(hg_bot, ("row", "tm"), (1, -1))
-    next_below = move(hg_top, ("row", "tm"), (-1, -1))
+    pay, above_h, below_h = lax.optimization_barrier((pay, above_h, below_h))
+    got = lax.all_to_all(pay, "row", 0, 0)
+    got, hg, above_h, below_h = lax.optimization_barrier((got, hg, above_h, below_h))
+    (tall,) = call(
+        tall_kernel,
+        "tall_band",
+        4,
+        [((frames, rows + 2, cols, chan), BF)],
+        (hg, above_h, below_h),
+        [],
+    )
+    after = move(tall, ("tm",), (-1,))
 
     blocks = clips * steps
     span = 27 * chan // blocks
-    lanes = (span + 127) // 128 * 128
+    shape = (16, 128) if packed(width, span) else (width, (span + 127) // 128 * 128)
     (part,) = call(
-        second_kernel,
+        functools.partial(second_kernel, span),
         "kernel_grad_part",
-        [((blocks, width, lanes), BF)],
+        16,
+        [((blocks,) + shape, BF)],
         (got,),
         [
             ((2 * peers * 2 * PITCH, chan), BF),
@@ -326,25 +393,29 @@
             ((27 * width, 256), F32),
         ],
     )
-    by_clip = lax.all_to_all(part.reshape(clips, steps * width, lanes), "clip", 0, 0)
-    (summed,) = call(clip_kernel, "clip_sum", [((steps * width, lanes), BF)], (by_clip,), [])
-    by_step = lax.all_to_all(summed.reshape(steps, width, lanes), "tm", 0, 0)
+    part, after = lax.optimization_barrier((part, after))
+    by_clip = lax.all_to_all(part.reshape((clips, steps * shape[0], shape[1])), "clip", 0, 0)
+    (summed,) = call(
+        clip_kernel,
+        "clip_sum",
+        4,
+        [((steps * shape[0], shape[1]), BF)],
+        (by_clip,),
+        [],
+    )
+    by_step = lax.all_to_all(summed.reshape((steps,) + shape), "tm", 0, 0)
     total = clips * 2 * frames * steps * rows * peers * cols
-    (kernel_grad,) = call(
+    kernel_grad, input_grad = call(
         functools.partial(last_kernel, 1.0 / math.sqrt(total)),
-        "kernel_grad_sum",
-        [((span, width), F32)],
-        (by_step,),
-        [],
-    )
-    (input_grad,) = call(
-        grad_kernel,
-        "input_grad",
-        [((frames, rows, cols, chan), F32)],
-        (hg, above_h, below_h, next_h, next_above, next_below, w1),
-        [((16, WIDE, chan), F32), ((3, 16, cols, chan), BF)],
-    )
-    return (input_grad[None], kernel_grad)
+        "both_grads",
+        16,
+        [((width, span), F32), ((frames, rows, cols, chan), F32)],
+        (by_step, tall, after),
+        [((16, WIDE, chan), F32), ((3, 16, cols, chan), BF), (w1.shape, BF)],
+        far=(w1,),
+        sems=1,
+    )
+    return (input_grad[None], kernel_grad.T)
 
 
 def solution(mesh):

time: 106 us -> 104 us (0.981)
  the two profiles are of different devices: /device:TPU:97 before, /device:TPU:2 now
where the time goes in v2:
time: 104 us; the launch traced here: 103 us
  blocking collectives  57.7 us (55%)
  starting transfers between devices  18.4 us (18%)
  waiting for transfers between devices  13.4 us (13%)
  Pallas kernels  11.5 us (11%)
  between operations  1.37 us (1%)
    all_to_all x1, blocking collectives, local(): by_step = lax.all_to_all(summed.reshape((steps,) + shape), 'tm', 0, 0)  28.9 us
    ppermute x7, starting transfers between devices, move(): lax.ppermute(value, axes if len(axes) > 1 else axes[0], route(sizes, steps))  18.4 us
    all_to_all x1, blocking collectives, local(): got = lax.all_to_all(pay, 'row', 0, 0)  17.9 us
    ppermute x7, waiting for transfers between devices, move(): lax.ppermute(value, axes if len(axes) > 1 else axes[0], route(sizes, steps))  13.4 us
    pallas_call x6, Pallas kernels, call(): pl.pallas_call(body, name=name, out_shape=outs, in_specs=[pl.BlockSpec(me...  11.5 us
    all_to_all x1, blocking collectives, local(): lax.all_to_all(part.reshape((clips, steps * shape[0], shape[1])), 'clip',...  10.9 us
  transfers between devices with their start and end apart: 7, of which 6 were waited for; matrix products, arithmetic and copies ran while one was open for 0% of the time, Pallas kernels for 2%

profile of v2, /device:TPU:2, one launch (start us, length us, event | category | flops | bytes accessed | tf_op | source)
XLA Modules:
  0.0 103.2 jit_solution(6223411994318848911)
XLA Ops:
  0.6 0.9 slice_bitcast_fusion
  1.5 1.3 %collective-permute-start.1 = (bf16[2,2,48,192]{3,2,1,0:T(8,128)(2,1)S(1)}, bf16[2,2,48,192]{3,2,1,0:T(8,128)(2,1)S(1)}, u32[]{:S(2)}, u32[]{:S(2)}) collective-permute-start(bf16[2,2,48,192]{3,2,1,0:T(8,128)(2,1)S(1)} %slice_bitcast_fusion), channel_id=1, source_target_pairs={{1,0},{2,1},{3,2},{4,3},{5,4},{6,5},{7,6},{8,7},{9,8},{10,9},{11,1... | collective-permute-start | bytes 221192 | tf_op jit(solution)/shard_map/ppermute | solution.py:39
  2.8 4.6 %collective-permute-start = (bf16[2,2,48,192]{3,2,1,0:T(8,128)(2,1)}, bf16[2,2,48,192]{3,2,1,0:T(8,128)(2,1)S(1)}, u32[]{:S(2)}, u32[]{:S(2)}) collective-permute-start(bf16[2,2,48,192]{3,2,1,0:T(8,128)(2,1)} %bitcast.17), channel_id=1, source_target_pairs={{0,1},{1,2},{2,3},{3,4},{4,5},{5,6},{6,7},{7,8},{8,9},{9,10},{10,1... | collective-permute-start | bytes 221192 | tf_op jit(solution)/shard_map/ppermute | solution.py:39
  7.4 0.8 collective-permute-done.1.gnext
  8.1 1.8 %collective-permute-done.xprev = bf16[2,2,48,192]{3,2,1,0:T(8,128)(2,1)S(1)} collective-permute-done((bf16[2,2,48,192]{3,2,1,0:T(8,128)(2,1)}, bf16[2,2,48,192]{3,2,1,0:T(8,128)(2,1)S(1)}, u32[]{:S(2)}, u32[]{:S(2)}) %collective-permute-start) | collective-permute-done | bytes 73760 | tf_op jit(solution)/shard_map/ppermute | solution.py:39
  9.9 1.0 edge_rows.1
  10.9 1.9 %collective-permute-start.2 = (bf16[10,48,192]{2,1,0:T(8,128)(2,1)S(1)}, bf16[10,48,192]{2,1,0:T(8,128)(2,1)S(1)}, u32[]{:S(2)}, u32[]{:S(2)}) collective-permute-start(bf16[10,48,192]{2,1,0:T(8,128)(2,1)S(1)} %get-tuple-element.19), channel_id=1, source_target_pairs={{0,16},{16,32},{32,48},{48,64},{64,80},{80,96},{96,112},{1,17},{17... | collective-permute-start | bytes 552968 | tf_op jit(solution)/shard_map/ppermute | solution.py:39
  12.9 3.6 %collective-permute-start.3 = (bf16[10,48,192]{2,1,0:T(8,128)(2,1)S(1)}, bf16[10,48,192]{2,1,0:T(8,128)(2,1)S(1)}, u32[]{:S(2)}, u32[]{:S(2)}) collective-permute-start(bf16[10,48,192]{2,1,0:T(8,128)(2,1)S(1)} %get-tuple-element.20), channel_id=1, source_target_pairs={{16,0},{32,16},{48,32},{64,48},{80,64},{96,80},{112,96},{17,1},{33... | collective-permute-start | bytes 552968 | tf_op jit(solution)/shard_map/ppermute | solution.py:39
  17.1 1.3 %collective-permute-done.2.above = bf16[10,48,192]{2,1,0:T(8,128)(2,1)S(1)} collective-permute-done((bf16[10,48,192]{2,1,0:T(8,128)(2,1)S(1)}, bf16[10,48,192]{2,1,0:T(8,128)(2,1)S(1)}, u32[]{:S(2)}, u32[]{:S(2)}) %collective-permute-start.2) | collective-permute-done | bytes 184352 | tf_op jit(solution)/shard_map/ppermute | solution.py:39
  18.4 1.8 %collective-permute-done.3.below = bf16[10,48,192]{2,1,0:T(8,128)(2,1)S(1)} collective-permute-done((bf16[10,48,192]{2,1,0:T(8,128)(2,1)S(1)}, bf16[10,48,192]{2,1,0:T(8,128)(2,1)S(1)}, u32[]{:S(2)}, u32[]{:S(2)}) %collective-permute-start.3) | collective-permute-done | bytes 184352 | tf_op jit(solution)/shard_map/ppermute | solution.py:39
  20.2 5.4 %hidden_and_pairs.1 = (bf16[8,408,128]{2,1,0:T(8,128)(2,1)S(1)}, bf16[2,2,48,192]{3,2,1,0:T(8,128)(2,1)S(1)}, bf16[2,48,192]{2,1,0:T(8,128)(2,1)S(1)}, bf16[2,48,192]{2,1,0:T(8,128)(2,1)S(1)}) custom-call(s32[1]{0:T(128)S(6)} %copy.7.lengths, bf16[2,2,48,192]{3,2,1,0:T(8,128)(2,1)} %bitcast.19, bf16[4,2,48,192]{3,2,1,0:T(8,128)(2,1)} %bitcast.16, ...), custom_call_target="tpu_custom_call" | custom-call | tf_op jit(solution)/shard_map/hidden_and_pairs/pallas_call | solution.py:301
  25.6 3.7 %collective-permute-start.4 = (bf16[2,48,192]{2,1,0:T(8,128)(2,1)S(1)}, bf16[2,48,192]{2,1,0:T(8,128)(2,1)S(1)}, u32[]{:S(2)}, u32[]{:S(2)}) collective-permute-start(bf16[2,48,192]{2,1,0:T(8,128)(2,1)S(1)} %get-tuple-element.22), channel_id=1, source_target_pairs={{0,16},{16,32},{32,48},{48,64},{64,80},{80,96},{96,112},{1,17},{17... | collective-permute-start | bytes 110600 | tf_op jit(solution)/shard_map/ppermute | solution.py:39
  29.3 2.1 %collective-permute-start.5 = (bf16[2,48,192]{2,1,0:T(8,128)(2,1)S(1)}, bf16[2,48,192]{2,1,0:T(8,128)(2,1)S(1)}, u32[]{:S(2)}, u32[]{:S(2)}) collective-permute-start(bf16[2,48,192]{2,1,0:T(8,128)(2,1)S(1)} %get-tuple-element.23), channel_id=1, source_target_pairs={{16,0},{32,16},{48,32},{64,48},{80,64},{96,80},{112,96},{17,1},{33... | collective-permute-start | bytes 110600 | tf_op jit(solution)/shard_map/ppermute | solution.py:39
  31.3 0.0 collective-permute-done.4.above
  31.4 1.7 %collective-permute-done.5.below = bf16[2,48,192]{2,1,0:T(8,128)(2,1)S(1)} collective-permute-done((bf16[2,48,192]{2,1,0:T(8,128)(2,1)S(1)}, bf16[2,48,192]{2,1,0:T(8,128)(2,1)S(1)}, u32[]{:S(2)}, u32[]{:S(2)}) %collective-permute-start.5) | collective-permute-done | bytes 36896 | tf_op jit(solution)/shard_map/ppermute | solution.py:39
  33.1 17.9 %all_to_all.15.got = bf16[8,408,128]{2,1,0:T(8,128)(2,1)S(1)} all-to-all(bf16[8,408,128]{2,1,0:T(8,128)(2,1)S(1)} %get-tuple-element.24), channel_id=1, replica_groups=mesh['clip'=4,'row'=8,'tm'=16] {'row'}, dimensions={0} | all-to-all | bytes 1671168 | tf_op jit(solution)/shard_map/all_to_all | solution.py:369
  51.0 1.3 %collective-permute-start.6 = (bf16[2,4,48,192]{3,2,1,0:T(8,128)(2,1)S(1)}, bf16[2,4,48,192]{3,2,1,0:T(8,128)(2,1)S(1)}, u32[]{:S(2)}, u32[]{:S(2)}) collective-permute-start(bf16[2,4,48,192]{3,2,1,0:T(8,128)(2,1)S(1)} %tall_band.1.tall), channel_id=1, source_target_pairs={{1,0},{2,1},{3,2},{4,3},{5,4},{6,5},{7,6},{8,7},{9,8},{10,9},{11,1... | collective-permute-start | bytes 442376 | tf_op jit(solution)/shard_map/ppermute | solution.py:39
  52.3 1.7 %kernel_grad_part.1 = bf16[64,16,128]{2,1,0:T(8,128)(2,1)S(1)} custom-call(bf16[8,408,128]{2,1,0:T(8,128)(2,1)S(1)} %all_to_all.15.got), custom_call_target="tpu_custom_call" | custom-call | tf_op jit(solution)/shard_map/kernel_grad_part/pallas_call | solution.py:301
  54.0 6.1 %collective-permute-done.6.after = bf16[2,4,48,192]{3,2,1,0:T(8,128)(2,1)S(1)} collective-permute-done((bf16[2,4,48,192]{3,2,1,0:T(8,128)(2,1)S(1)}, bf16[2,4,48,192]{3,2,1,0:T(8,128)(2,1)S(1)}, u32[]{:S(2)}, u32[]{:S(2)}) %collective-permute-start.6) | collective-permute-done | bytes 147488 | tf_op jit(solution)/shard_map/ppermute | solution.py:39
  60.1 10.9 %all_to_all.16.got = bf16[4,256,128]{2,1,0:T(8,128)(2,1)S(1)} all-to-all(bf16[4,256,128]{2,1,0:T(8,128)(2,1)S(1)} %bitcast.10), channel_id=1, replica_groups=mesh['clip'=4,'row'=8,'tm'=16] {'clip'}, dimensions={0} | all-to-all | bytes 524288 | tf_op jit(solution)/shard_map/all_to_all | solution.py:397
  71.0 28.9 %all_to_all.17.got = bf16[16,16,128]{2,1,0:T(8,128)(2,1)S(1)} all-to-all(bf16[16,16,128]{2,1,0:T(8,128)(2,1)S(1)} %bitcast.11), channel_id=1, replica_groups=mesh['clip'=4,'row'=8,'tm'=16] {'tm'}, dimensions={0} | all-to-all | bytes 131072 | tf_op jit(solution)/shard_map/all_to_all | solution.py:406
  99.9 3.3 %both_grads.1 = (f32[24,81]{1,0:T(8,128)}, f32[2,2,48,192]{3,2,1,0:T(8,128)}) custom-call(bf16[27,192,192]{2,1,0:T(8,128)(2,1)} %bitcast.13, bf16[16,16,128]{2,1,0:T(8,128)(2,1)S(1)} %all_to_all.17.got, bf16[2,4,48,192]{3,2,1,0:T(8,128)(2,1)S(1)} %tall_band.1.tall, bf16[2,4,48,192]{3,2,1,0:T(8,128)(2,1)S(1)} %collective-permute-done.6.after), custom_call_target="tpu_custom_call" | custom-call | tf_op jit(solution)/shard_map/both_grads/pallas_call | solution.py:301
  (2 shorter events, 0.0 us)
Async XLA Ops:
  1.5 6.6 %collective-permute-start.1 = (bf16[2,2,48,192]{3,2,1,0:T(8,128)(2,1)S(1)}, bf16[2,2,48,192]{3,2,1,0:T(8,128)(2,1)S(1)}, u32[]{:S(2)}, u32[]{:S(2)}) collective-permute-start(bf16[2,2,48,192]{3,2,1,0:T(8,128)(2,1)S(1)} %slice_bitcast_fusion), channel_id=1, source_target_pairs={{1,0},{2,1},{3,2},{4,3},{5,4},{6,5},{7,6},{8,7},{9,8},{10,9},{11,1... | collective-permute-start | bytes 221192 | tf_op jit(solution)/shard_map/ppermute | solution.py:39
  2.8 7.1 %collective-permute-start = (bf16[2,2,48,192]{3,2,1,0:T(8,128)(2,1)}, bf16[2,2,48,192]{3,2,1,0:T(8,128)(2,1)S(1)}, u32[]{:S(2)}, u32[]{:S(2)}) collective-permute-start(bf16[2,2,48,192]{3,2,1,0:T(8,128)(2,1)} %bitcast.17), channel_id=1, source_target_pairs={{0,1},{1,2},{2,3},{3,4},{4,5},{5,6},{6,7},{7,8},{8,9},{9,10},{10,1... | collective-permute-start | bytes 221192 | tf_op jit(solution)/shard_map/ppermute | solution.py:39
  10.9 7.5 %collective-permute-start.2 = (bf16[10,48,192]{2,1,0:T(8,128)(2,1)S(1)}, bf16[10,48,192]{2,1,0:T(8,128)(2,1)S(1)}, u32[]{:S(2)}, u32[]{:S(2)}) collective-permute-start(bf16[10,48,192]{2,1,0:T(8,128)(2,1)S(1)} %get-tuple-element.19), channel_id=1, source_target_pairs={{0,16},{16,32},{32,48},{48,64},{64,80},{80,96},{96,112},{1,17},{17... | collective-permute-start | bytes 552968 | tf_op jit(solution)/shard_map/ppermute | solution.py:39
  12.9 7.3 %collective-permute-start.3 = (bf16[10,48,192]{2,1,0:T(8,128)(2,1)S(1)}, bf16[10,48,192]{2,1,0:T(8,128)(2,1)S(1)}, u32[]{:S(2)}, u32[]{:S(2)}) collective-permute-start(bf16[10,48,192]{2,1,0:T(8,128)(2,1)S(1)} %get-tuple-element.20), channel_id=1, source_target_pairs={{16,0},{32,16},{48,32},{64,48},{80,64},{96,80},{112,96},{17,1},{33... | collective-permute-start | bytes 552968 | tf_op jit(solution)/shard_map/ppermute | solution.py:39
  25.6 5.8 %collective-permute-start.4 = (bf16[2,48,192]{2,1,0:T(8,128)(2,1)S(1)}, bf16[2,48,192]{2,1,0:T(8,128)(2,1)S(1)}, u32[]{:S(2)}, u32[]{:S(2)}) collective-permute-start(bf16[2,48,192]{2,1,0:T(8,128)(2,1)S(1)} %get-tuple-element.22), channel_id=1, source_target_pairs={{0,16},{16,32},{32,48},{48,64},{64,80},{80,96},{96,112},{1,17},{17... | collective-permute-start | bytes 110600 | tf_op jit(solution)/shard_map/ppermute | solution.py:39
  29.3 3.8 %collective-permute-start.5 = (bf16[2,48,192]{2,1,0:T(8,128)(2,1)S(1)}, bf16[2,48,192]{2,1,0:T(8,128)(2,1)S(1)}, u32[]{:S(2)}, u32[]{:S(2)}) collective-permute-start(bf16[2,48,192]{2,1,0:T(8,128)(2,1)S(1)} %get-tuple-element.23), channel_id=1, source_target_pairs={{16,0},{32,16},{48,32},{64,48},{80,64},{96,80},{112,96},{17,1},{33... | collective-permute-start | bytes 110600 | tf_op jit(solution)/shard_map/ppermute | solution.py:39
  51.0 9.1 %collective-permute-start.6 = (bf16[2,4,48,192]{3,2,1,0:T(8,128)(2,1)S(1)}, bf16[2,4,48,192]{3,2,1,0:T(8,128)(2,1)S(1)}, u32[]{:S(2)}, u32[]{:S(2)}) collective-permute-start(bf16[2,4,48,192]{3,2,1,0:T(8,128)(2,1)S(1)} %tall_band.1.tall), channel_id=1, source_target_pairs={{1,0},{2,1},{3,2},{4,3},{5,4},{6,5},{7,6},{8,7},{9,8},{10,9},{11,1... | collective-permute-start | bytes 442376 | tf_op jit(solution)/shard_map/ppermute | solution.py:39

commit v3 on v2

--- a/solution.py
+++ b/solution.py
@@ -53,19 +53,16 @@
     return lax.dot_general(a, b, (((1,), (1,)), ((), ())), preferred_element_type=F32)
 
 
-def edges_kernel(x, g, xprev, gnext, top, bot, sem):
+def band_kernel(x, g, xprev, gnext, band, sem):
     nx, ng = x.shape[0], g.shape[0]
-    copies = []
-    for row, out in ((0, top), (1, bot)):
-        for source, at in ((x, 0), (g, 2 * nx)):
-            target = out.at[at : at + source.shape[0]]
-            copies.append(pltpu.make_async_copy(source.at[:, row], target, sem.at[len(copies)]))
+    copies = [
+        pltpu.make_async_copy(x, band.at[0:nx], sem.at[0]),
+        pltpu.make_async_copy(g, band.at[2 * nx : 2 * nx + ng], sem.at[1]),
+    ]
     for copy in copies:
         copy.start()
-    for row, out in ((0, top), (1, bot)):
-        for f in range(nx):
-            out[nx + f] = xprev[f, row]
-            out[2 * nx + ng + f] = gnext[f, row]
+    band[nx : 2 * nx] = xprev[...]
+    band[2 * nx + ng :] = gnext[...]
     for copy in copies:
         copy.wait()
 
@@ -76,7 +73,7 @@
 
 def first_kernel(
     lengths, x_far, g_far, w1_far, w2_far, above, below, xprev, gnext,
-    pay, hg, hg_top, hg_bot,
+    pay, tall,
     xs, ps, xk, pk, x, g, w1, w2, sem,
 ):
     pairs = ((x_far, x), (w1_far, w1), (g_far, g), (w2_far, w2))
@@ -85,6 +82,7 @@
         copy.start()
     frames, rows, cols, chan = x.shape
     cells = frames * rows * cols
+    reach = 2 * cells
     peers = pay.shape[0]
     width = chan // peers
     block = lax.axis_index("tm")
@@ -93,64 +91,66 @@
     copies[0].wait()
     for f in range(2):
         for r in range(2):
-            spread(xs, f * 4 + 1 + r, cols, xprev[f, r])
-            spread(xs, (2 + f) * 4 + 1 + r, cols, x[f, r])
-        spread(xs, f * 4, cols, above[2 + f])
-        spread(xs, f * 4 + 3, cols, below[2 + f])
-        spread(xs, (2 + f) * 4, cols, above[f])
-        spread(xs, (2 + f) * 4 + 3, cols, below[f])
+            spread(xs, f * 6 + r, cols, above[2 + f, r])
+            spread(xs, f * 6 + 2 + r, cols, xprev[f, r])
+            spread(xs, f * 6 + 4 + r, cols, below[2 + f, r])
+            spread(xs, (2 + f) * 6 + r, cols, above[f, r])
+            spread(xs, (2 + f) * 6 + 2 + r, cols, x[f, r])
+            spread(xs, (2 + f) * 6 + 4 + r, cols, below[f, r])
     for k in range(3):
         xk[k] = xs[:, EDGE - 1 + k : EDGE - 1 + k + cols, :].astype(BF)
     copies[1].wait()
-    hidden = jnp.zeros((cells, chan), F32)
+    hidden = jnp.zeros((reach, chan), F32)
     for i in range(3):
         for j in range(3):
             for k in range(3):
-                part = [xk[k, (f + 2 - i) * 4 + j : (f + 2 - i) * 4 + j + 2] for f in range(2)]
-                patch = jnp.concatenate(part, axis=0).reshape(cells, chan)
+                part = [xk[k, (f + 2 - i) * 6 + j : (f + 2 - i) * 6 + j + 4] for f in range(2)]
+                patch = jnp.concatenate(part, axis=0).reshape(reach, chan)
                 hidden += jnp.dot(patch, w1[i * 9 + j * 3 + k], preferred_element_type=F32)
     sigma = 1.0 / (1.0 + jnp.exp(-hidden))
-    act = (hidden * sigma).astype(BF)
+    act = (hidden * sigma).reshape(frames, rows + 2, cols, chan)[:, 1 : 1 + rows]
+    act = act.reshape(cells, chan).astype(BF)
     limit = 2 * lengths[0] - 2 * frames * block
 
     def cotangent(f, r):
-        if r == 0:
-            value = above[2 * frames + f]
-        elif r == 3:
-            value = below[2 * frames + f]
+        if r < 2:
+            value = above[2 * frames + f, r]
+        elif r > 3:
+            value = below[2 * frames + f, r - 4]
         elif f >= 2 * frames:
-            value = gnext[f - 2 * frames, r - 1]
+            value = gnext[f - 2 * frames, r - 2]
         else:
-            value = g[f, r - 1]
+            value = g[f, r - 2]
         value = value.astype(F32)
         return jnp.where(f < limit, value, jnp.zeros_like(value))
 
     copies[2].wait()
-    for r in range(4):
+    for r in range(6):
         field = [cotangent(f, r) for f in range(6)]
         for a in range(5):
-            spread(ps, a * 4 + r, cols, field[a] + field[a + 1])
+            spread(ps, a * 6 + r, cols, field[a] + field[a + 1])
     for k in range(3):
         pk[k] = ps[:, EDGE + 1 - k : EDGE + 1 - k + cols, :].astype(BF)
     copies[3].wait()
-    pair = jnp.zeros((cells, chan), F32)
+    pair = jnp.zeros((reach, chan), F32)
     for i in range(3):
         for j in range(3):
             for k in range(3):
-                part = [pk[k, (2 * t + i) * 4 + 2 - j : (2 * t + i) * 4 + 4 - j] for t in range(2)]
-                patch = jnp.concatenate(part, axis=0).reshape(cells, chan)
+                part = [pk[k, (2 * t + i) * 6 + 2 - j : (2 * t + i) * 6 + 6 - j] for t in range(2)]
+                patch = jnp.concatenate(part, axis=0).reshape(reach, chan)
                 pair += transposed_dot(patch, w2[i * 9 + j * 3 + k])
-    grad = (pair * sigma * (1.0 + hidden * (1.0 - sigma))).astype(BF)
-    grad = grad.reshape(frames, rows, cols, chan)
-    hg[...] = grad
-    hg_top[...] = grad[:, 0]
-    hg_bot[...] = grad[:, 1]
+    grad = (pair * sigma * (1.0 + hidden * (1.0 - sigma))).reshape(frames, rows + 2, cols, chan)
+    band = lax.axis_index("row")
+    none = jnp.zeros((frames, cols, chan), F32)
+    tall[:, 0] = jnp.where(band > 0, grad[:, 0], none).astype(BF)
+    tall[:, 1 : 1 + rows] = grad[:, 1 : 1 + rows].astype(BF)
+    tall[:, 1 + rows] = jnp.where(band < peers - 1, grad[:, 1 + rows], none).astype(BF)
     half = cells // 2
     wide = act.astype(F32)
     low = wide[:, :128].astype(BF)
     high = jnp.concatenate([wide[:half, 128:], wide[half:, 128:]], axis=1).astype(BF)
     turned = [
-        jnp.transpose(ps[a * 4 + 1 : a * 4 + 3, 0:PITCH, :].reshape(2 * PITCH, chan))
+        jnp.transpose(ps[a * 6 + 2 : a * 6 + 4, 0:PITCH, :].reshape(2 * PITCH, chan))
         for a in range(5)
     ]
     for p in range(peers):
@@ -158,13 +158,6 @@
         pay[p, cells : cells + half, :] = high
         mine = jnp.concatenate([v[p * width : (p + 1) * width] for v in turned], axis=0)
         pay[p, cells + half :, :] = mine.astype(BF)
-
-
-def tall_kernel(hg, above, below, tall):
-    tall[:, 0] = above[...]
-    tall[:, 1] = hg[:, 0]
-    tall[:, 2] = hg[:, 1]
-    tall[:, 3] = below[...]
 
 
 def second_kernel(span, got, out, field, left, prod):
@@ -256,9 +249,7 @@
     out[...] = total.astype(BF)
 
 
-def last_kernel(scale, w1_far, got, tall, after, out, grad, hs, hk, w1, sem):
-    copy = pltpu.make_async_copy(w1_far, w1, sem.at[0])
-    copy.start()
+def last_kernel(scale, got, out):
     width, span = out.shape
     total = got[0].astype(F32)
     for p in range(1, got.shape[0]):
@@ -271,6 +262,11 @@
         out[16:] = tail[:, :span]
     else:
         out[...] = total[:, :span]
+
+
+def grad_kernel(w1_far, tall, after, grad, hs, hk, w1, sem):
+    copy = pltpu.make_async_copy(w1_far, w1, sem.at[0])
+    copy.start()
     frames, rows, cols, chan = grad.shape
     cells = frames * rows * cols
     clear_edges(hs, cols)
@@ -323,37 +319,33 @@
 
     xprev = move(x, ("tm",), (1,))
     gnext = move(g[:frames], ("tm",), (-1,))
-    band = (5 * frames, cols, chan)
-    top, bot = call(
-        edges_kernel,
-        "edge_rows",
+    (band,) = call(
+        band_kernel,
+        "band",
         4,
-        [(band, BF), (band, BF)],
+        [((5 * frames, rows, cols, chan), BF)],
         (xprev, gnext),
         [],
         far=(x, g),
-        sems=4,
-    )
-    above = move(bot, ("row",), (1,))
-    below = move(top, ("row",), (-1,))
-
-    edge = (frames, cols, chan)
-    pay, hg, hg_top, hg_bot = call(
+        sems=2,
+    )
+    above = move(band, ("row",), (1,))
+    below = move(band, ("row",), (-1,))
+
+    pay, tall = call(
         first_kernel,
         "hidden_and_pairs",
-        20,
+        28,
         [
             ((peers, cells + cells // 2 + 5 * width, 128), BF),
-            ((frames, rows, cols, chan), BF),
-            (edge, BF),
-            (edge, BF),
+            ((frames, rows + 2, cols, chan), BF),
         ],
         (above, below, xprev, gnext),
         [
-            ((16, WIDE, chan), F32),
-            ((20, WIDE, chan), F32),
-            ((3, 16, cols, chan), BF),
-            ((3, 20, cols, chan), BF),
+            ((24, WIDE, chan), F32),
+            ((30, WIDE, chan), F32),
+            ((3, 24, cols, chan), BF),
+            ((3, 30, cols, chan), BF),
             (x.shape, BF),
             (g.shape, BF),
             (w1.shape, BF),
@@ -363,20 +355,9 @@
         scalars=(lengths,),
         sems=4,
     )
-    above_h = move(hg_bot, ("row",), (1,))
-    below_h = move(hg_top, ("row",), (-1,))
-    pay, above_h, below_h = lax.optimization_barrier((pay, above_h, below_h))
+    after = move(tall, ("tm",), (-1,))
     got = lax.all_to_all(pay, "row", 0, 0)
-    got, hg, above_h, below_h = lax.optimization_barrier((got, hg, above_h, below_h))
-    (tall,) = call(
-        tall_kernel,
-        "tall_band",
-        4,
-        [((frames, rows + 2, cols, chan), BF)],
-        (hg, above_h, below_h),
-        [],
-    )
-    after = move(tall, ("tm",), (-1,))
+    got, after = lax.optimization_barrier((got, after))
 
     blocks = clips * steps
     span = 27 * chan // blocks
@@ -393,7 +374,6 @@
             ((27 * width, 256), F32),
         ],
     )
-    part, after = lax.optimization_barrier((part, after))
     by_clip = lax.all_to_all(part.reshape((clips, steps * shape[0], shape[1])), "clip", 0, 0)
     (summed,) = call(
         clip_kernel,
@@ -405,12 +385,20 @@
     )
     by_step = lax.all_to_all(summed.reshape((steps,) + shape), "tm", 0, 0)
     total = clips * 2 * frames * steps * rows * peers * cols
-    kernel_grad, input_grad = call(
+    (kernel_grad,) = call(
         functools.partial(last_kernel, 1.0 / math.sqrt(total)),
-        "both_grads",
+        "kernel_grad_sum",
+        4,
+        [((width, span), F32)],
+        (by_step,),
+        [],
+    )
+    (input_grad,) = call(
+        grad_kernel,
+        "input_grad",
         16,
-        [((width, span), F32), ((frames, rows, cols, chan), F32)],
-        (by_step, tall, after),
+        [((frames, rows, cols, chan), F32)],
+        (tall, after),
         [((16, WIDE, chan), F32), ((3, 16, cols, chan), BF), (w1.shape, BF)],
         far=(w1,),
         sems=1,

time: 104 us -> 93.5 us (0.90)
  blocking collectives: 57.7 us -> 9.14 us
  waiting for transfers between devices: 13.4 us -> 34.2 us
  starting transfers between devices: 18.4 us -> 30.8 us
  Pallas kernels: 11.5 us -> 16.6 us
    all_to_all x2 -> x0, blocking collectives: 46.8 us -> none  [the longest x1 28.9 us: local(): by_step = lax.all_to_all(summed.reshape((steps,) + shape), 'tm', 0, 0)]
    all_to_all x0 -> x2, starting transfers between devices: none -> 19.4 us  [the longest x1 15.8 us: local(): by_step = lax.all_to_all(summed.reshape((steps,) + shape), 'tm', 0, 0)]
    all_to_all x0 -> x2, waiting for transfers between devices: none -> 12.4 us  [the longest x1 9.61 us: local(): by_step = lax.all_to_all(summed.reshape((steps,) + shape), 'tm', 0, 0)]
    ppermute x7 -> x5, waiting for transfers between devices: 13.4 us -> 21.8 us  [move(): lax.ppermute(value, axes if len(axes) > 1 else axes[0], route(sizes, steps))]
    ppermute x7 -> x5, starting transfers between devices: 18.4 us -> 11.5 us  [move(): lax.ppermute(value, axes if len(axes) > 1 else axes[0], route(sizes, steps))]
    pallas_call x6, Pallas kernels: 11.5 us -> 16.6 us  [call(): pl.pallas_call(body, name=name, out_shape=outs, in_specs=[pl.BlockSpec(me...]
    all_to_all x1, blocking collectives: 10.9 us -> 9.14 us  [local(): lax.all_to_all(part.reshape((clips, steps * shape[0], shape[1])), 'clip',...]
  transfers between devices with their start and end apart: 7 -> 7, of which waited for: 6 -> 7; matrix products, arithmetic and copies ran while one was open for 0% -> 0% of each run, Pallas kernels for 2% -> 4%
where the time goes in v3:
time: 93.5 us; the launch traced here: 93 us
  waiting for transfers between devices  34.2 us (37%)
  starting transfers between devices  30.8 us (33%)
  Pallas kernels  16.6 us (18%)
  blocking collectives  9.14 us (10%)
  between operations  1.37 us (1%)
    ppermute x5, waiting for transfers between devices, move(): lax.ppermute(value, axes if len(axes) > 1 else axes[0], route(sizes, steps))  21.8 us
    pallas_call x6, Pallas kernels, call(): pl.pallas_call(body, name=name, out_shape=outs, in_specs=[pl.BlockSpec(me...  16.6 us
    all_to_all x1, starting transfers between devices, local(): by_step = lax.all_to_all(summed.reshape((steps,) + shape), 'tm', 0, 0)  15.8 us
    ppermute x5, starting transfers between devices, move(): lax.ppermute(value, axes if len(axes) > 1 else axes[0], route(sizes, steps))  11.5 us
    all_to_all x1, waiting for transfers between devices, local(): by_step = lax.all_to_all(summed.reshape((steps,) + shape), 'tm', 0, 0)  9.61 us
    all_to_all x1, blocking collectives, local(): lax.all_to_all(part.reshape((clips, steps * shape[0], shape[1])), 'clip',...  9.14 us
    all_to_all x1, starting transfers between devices, local(): got = lax.all_to_all(pay, 'row', 0, 0)  3.51 us
    all_to_all x1, waiting for transfers between devices, local(): got = lax.all_to_all(pay, 'row', 0, 0)  2.82 us
  transfers between devices with their start and end apart: 7, of which 7 were waited for; matrix products, arithmetic and copies ran while one was open for 0% of the time, Pallas kernels for 4%

profile of v3, /device:TPU:2, one launch (start us, length us, event | category | flops | bytes accessed | tf_op | source)
XLA Modules:
  0.0 93.0 jit_solution(18078146055970315365)
XLA Ops:
  0.6 0.9 slice_bitcast_fusion
  1.5 1.3 %collective-permute-start.1 = (bf16[2,2,48,192]{3,2,1,0:T(8,128)(2,1)S(1)}, bf16[2,2,48,192]{3,2,1,0:T(8,128)(2,1)S(1)}, u32[]{:S(2)}, u32[]{:S(2)}) collective-permute-start(bf16[2,2,48,192]{3,2,1,0:T(8,128)(2,1)S(1)} %slice_bitcast_fusion), channel_id=1, source_target_pairs={{1,0},{2,1},{3,2},{4,3},{5,4},{6,5},{7,6},{8,7},{9,8},{10,9},{11,1... | collective-permute-start | bytes 221192 | tf_op jit(solution)/shard_map/ppermute | solution.py:39
  2.8 4.6 %collective-permute-start = (bf16[2,2,48,192]{3,2,1,0:T(8,128)(2,1)}, bf16[2,2,48,192]{3,2,1,0:T(8,128)(2,1)S(1)}, u32[]{:S(2)}, u32[]{:S(2)}) collective-permute-start(bf16[2,2,48,192]{3,2,1,0:T(8,128)(2,1)} %bitcast.16), channel_id=1, source_target_pairs={{0,1},{1,2},{2,3},{3,4},{4,5},{5,6},{6,7},{7,8},{8,9},{9,10},{10,1... | collective-permute-start | bytes 221192 | tf_op jit(solution)/shard_map/ppermute | solution.py:39
  7.4 0.8 collective-permute-done.1.gnext
  8.1 1.8 %collective-permute-done.xprev = bf16[2,2,48,192]{3,2,1,0:T(8,128)(2,1)S(1)} collective-permute-done((bf16[2,2,48,192]{3,2,1,0:T(8,128)(2,1)}, bf16[2,2,48,192]{3,2,1,0:T(8,128)(2,1)S(1)}, u32[]{:S(2)}, u32[]{:S(2)}) %collective-permute-start) | collective-permute-done | bytes 73760 | tf_op jit(solution)/shard_map/ppermute | solution.py:39
  9.9 1.0 %band.1 = bf16[10,2,48,192]{3,2,1,0:T(8,128)(2,1)S(1)} custom-call(bf16[2,2,48,192]{3,2,1,0:T(8,128)(2,1)} %bitcast.17, bf16[4,2,48,192]{3,2,1,0:T(8,128)(2,1)} %bitcast.14, bf16[2,2,48,192]{3,2,1,0:T(8,128)(2,1)S(1)} %collective-permute-done.xprev, bf16[2,2,48,192]{3,2,1,0:T(8,128)(2,1)S(1)} %collective-permute-done.1.gnext), custom_call_target="tpu_custom_call" | custom-call | tf_op jit(solution)/shard_map/band/pallas_call | solution.py:297
  10.9 1.9 %collective-permute-start.3 = (bf16[10,2,48,192]{3,2,1,0:T(8,128)(2,1)S(1)}, bf16[10,2,48,192]{3,2,1,0:T(8,128)(2,1)S(1)}, u32[]{:S(2)}, u32[]{:S(2)}) collective-permute-start(bf16[10,2,48,192]{3,2,1,0:T(8,128)(2,1)S(1)} %band.1), channel_id=1, source_target_pairs={{16,0},{32,16},{48,32},{64,48},{80,64},{96,80},{112,96},{17,1},{33... | collective-permute-start | bytes 1105928 | tf_op jit(solution)/shard_map/ppermute | solution.py:39
  12.8 2.4 %collective-permute-start.2 = (bf16[10,2,48,192]{3,2,1,0:T(8,128)(2,1)S(1)}, bf16[10,2,48,192]{3,2,1,0:T(8,128)(2,1)S(1)}, u32[]{:S(2)}, u32[]{:S(2)}) collective-permute-start(bf16[10,2,48,192]{3,2,1,0:T(8,128)(2,1)S(1)} %band.1), channel_id=1, source_target_pairs={{0,16},{16,32},{32,48},{48,64},{64,80},{80,96},{96,112},{1,17},{17... | collective-permute-start | bytes 1105928 | tf_op jit(solution)/shard_map/ppermute | solution.py:39
  15.9 3.3 %collective-permute-done.3.below = bf16[10,2,48,192]{3,2,1,0:T(8,128)(2,1)S(1)} collective-permute-done((bf16[10,2,48,192]{3,2,1,0:T(8,128)(2,1)S(1)}, bf16[10,2,48,192]{3,2,1,0:T(8,128)(2,1)S(1)}, u32[]{:S(2)}, u32[]{:S(2)}) %collective-permute-start.3) | collective-permute-done | bytes 368672 | tf_op jit(solution)/shard_map/ppermute | solution.py:39
  19.1 8.1 %collective-permute-done.2.above = bf16[10,2,48,192]{3,2,1,0:T(8,128)(2,1)S(1)} collective-permute-done((bf16[10,2,48,192]{3,2,1,0:T(8,128)(2,1)S(1)}, bf16[10,2,48,192]{3,2,1,0:T(8,128)(2,1)S(1)}, u32[]{:S(2)}, u32[]{:S(2)}) %collective-permute-start.2) | collective-permute-done | bytes 368672 | tf_op jit(solution)/shard_map/ppermute | solution.py:39
  27.2 9.2 %hidden_and_pairs.1 = (bf16[8,408,128]{2,1,0:T(8,128)(2,1)}, bf16[2,4,48,192]{3,2,1,0:T(8,128)(2,1)S(1)}) custom-call(s32[1]{0:T(128)S(6)} %copy.7.lengths, bf16[2,2,48,192]{3,2,1,0:T(8,128)(2,1)} %bitcast.18, bf16[4,2,48,192]{3,2,1,0:T(8,128)(2,1)} %bitcast.15, bf16[27,192,192]{2,1,0:T(8,128)(2,1)} %bitcast.11, bf16[27,192,192]{2,1,0:T(8,128)(2,1)} %bitcast.13, ...), custom_call_target="tpu_custom_call" | custom-call | tf_op jit(solution)/shard_map/hidden_and_pairs/pallas_call | solution.py:297
  36.5 3.5 %all-to-all-start = ((bf16[8,408,128]{2,1,0:T(8,128)(2,1)}), bf16[8,408,128]{2,1,0:T(8,128)(2,1)S(1)}, u32[]{:S(2)}, u32[]{:S(2)}) async-start(bf16[8,408,128]{2,1,0:T(8,128)(2,1)} %get-tuple-element.7), calls=%async_computation | async-start | bytes 1671168 | tf_op jit(solution)/shard_map/all_to_all | solution.py:359
  40.0 1.3 %collective-permute-start.4 = (bf16[2,4,48,192]{3,2,1,0:T(8,128)(2,1)S(1)}, bf16[2,4,48,192]{3,2,1,0:T(8,128)(2,1)S(1)}, u32[]{:S(2)}, u32[]{:S(2)}) collective-permute-start(bf16[2,4,48,192]{3,2,1,0:T(8,128)(2,1)S(1)} %get-tuple-element.6.tall), channel_id=1, source_target_pairs={{1,0},{2,1},{3,2},{4,3},{5,4},{6,5},{7,6},{8,7},{9,8},{10,9},{11,1... | collective-permute-start | bytes 442376 | tf_op jit(solution)/shard_map/ppermute | solution.py:39
  41.3 7.9 %collective-permute-done.4.after = bf16[2,4,48,192]{3,2,1,0:T(8,128)(2,1)S(1)} collective-permute-done((bf16[2,4,48,192]{3,2,1,0:T(8,128)(2,1)S(1)}, bf16[2,4,48,192]{3,2,1,0:T(8,128)(2,1)S(1)}, u32[]{:S(2)}, u32[]{:S(2)}) %collective-permute-start.4) | collective-permute-done | bytes 147488 | tf_op jit(solution)/shard_map/ppermute | solution.py:39
  49.2 2.8 %all-to-all-done.got = bf16[8,408,128]{2,1,0:T(8,128)(2,1)S(1)} async-done(((bf16[8,408,128]{2,1,0:T(8,128)(2,1)}), bf16[8,408,128]{2,1,0:T(8,128)(2,1)S(1)}, u32[]{:S(2)}, u32[]{:S(2)}) %all-to-all-start) | async-done | bytes 835616 | tf_op jit(solution)/shard_map/all_to_all | solution.py:359
  52.0 1.7 %kernel_grad_part.1 = bf16[64,16,128]{2,1,0:T(8,128)(2,1)S(1)} custom-call(bf16[8,408,128]{2,1,0:T(8,128)(2,1)S(1)} %all-to-all-done.got), custom_call_target="tpu_custom_call" | custom-call | tf_op jit(solution)/shard_map/kernel_grad_part/pallas_call | solution.py:297
  53.7 9.1 %all_to_all.15.got = bf16[4,256,128]{2,1,0:T(8,128)(2,1)S(1)} all-to-all(bf16[4,256,128]{2,1,0:T(8,128)(2,1)S(1)} %bitcast.10), channel_id=1, replica_groups=mesh['clip'=4,'row'=8,'tm'=16] {'clip'}, dimensions={0} | all-to-all | bytes 524288 | tf_op jit(solution)/shard_map/all_to_all | solution.py:377
  62.9 0.7 clip_sum.1
  63.5 15.8 %all-to-all-start.2 = ((bf16[16,16,128]{2,1,0:T(8,128)(2,1)}), bf16[16,16,128]{2,1,0:T(8,128)(2,1)S(1)}, u32[]{:S(2)}, u32[]{:S(2)}) async-start(bf16[16,16,128]{2,1,0:T(8,128)(2,1)} %bitcast.7), calls=%async_computation.2 | async-start | bytes 131072 | tf_op jit(solution)/shard_map/all_to_all | solution.py:386
  79.4 3.3 %input_grad.1 = f32[2,2,48,192]{3,2,1,0:T(8,128)} custom-call(bf16[27,192,192]{2,1,0:T(8,128)(2,1)} %bitcast.12, bf16[2,4,48,192]{3,2,1,0:T(8,128)(2,1)S(1)} %get-tuple-element.6.tall, bf16[2,4,48,192]{3,2,1,0:T(8,128)(2,1)S(1)} %collective-permute-done.4.after), custom_call_target="tpu_custom_call" | custom-call | tf_op jit(solution)/shard_map/input_grad/pallas_call | solution.py:297
  82.7 9.6 %all-to-all-done.2.got = bf16[16,16,128]{2,1,0:T(8,128)(2,1)S(1)} async-done(((bf16[16,16,128]{2,1,0:T(8,128)(2,1)}), bf16[16,16,128]{2,1,0:T(8,128)(2,1)S(1)}, u32[]{:S(2)}, u32[]{:S(2)}) %all-to-all-start.2) | async-done | bytes 65568 | tf_op jit(solution)/shard_map/all_to_all | solution.py:386
  92.3 0.7 kernel_grad_sum.1
Async XLA Ops:
  1.5 6.6 %collective-permute-start.1 = (bf16[2,2,48,192]{3,2,1,0:T(8,128)(2,1)S(1)}, bf16[2,2,48,192]{3,2,1,0:T(8,128)(2,1)S(1)}, u32[]{:S(2)}, u32[]{:S(2)}) collective-permute-start(bf16[2,2,48,192]{3,2,1,0:T(8,128)(2,1)S(1)} %slice_bitcast_fusion), channel_id=1, source_target_pairs={{1,0},{2,1},{3,2},{4,3},{5,4},{6,5},{7,6},{8,7},{9,8},{10,9},{11,1... | collective-permute-start | bytes 221192 | tf_op jit(solution)/shard_map/ppermute | solution.py:39
  2.8 7.1 %collective-permute-start = (bf16[2,2,48,192]{3,2,1,0:T(8,128)(2,1)}, bf16[2,2,48,192]{3,2,1,0:T(8,128)(2,1)S(1)}, u32[]{:S(2)}, u32[]{:S(2)}) collective-permute-start(bf16[2,2,48,192]{3,2,1,0:T(8,128)(2,1)} %bitcast.16), channel_id=1, source_target_pairs={{0,1},{1,2},{2,3},{3,4},{4,5},{5,6},{6,7},{7,8},{8,9},{9,10},{10,1... | collective-permute-start | bytes 221192 | tf_op jit(solution)/shard_map/ppermute | solution.py:39
  10.9 8.3 %collective-permute-start.3 = (bf16[10,2,48,192]{3,2,1,0:T(8,128)(2,1)S(1)}, bf16[10,2,48,192]{3,2,1,0:T(8,128)(2,1)S(1)}, u32[]{:S(2)}, u32[]{:S(2)}) collective-permute-start(bf16[10,2,48,192]{3,2,1,0:T(8,128)(2,1)S(1)} %band.1), channel_id=1, source_target_pairs={{16,0},{32,16},{48,32},{64,48},{80,64},{96,80},{112,96},{17,1},{33... | collective-permute-start | bytes 1105928 | tf_op jit(solution)/shard_map/ppermute | solution.py:39
  12.8 14.4 %collective-permute-start.2 = (bf16[10,2,48,192]{3,2,1,0:T(8,128)(2,1)S(1)}, bf16[10,2,48,192]{3,2,1,0:T(8,128)(2,1)S(1)}, u32[]{:S(2)}, u32[]{:S(2)}) collective-permute-start(bf16[10,2,48,192]{3,2,1,0:T(8,128)(2,1)S(1)} %band.1), channel_id=1, source_target_pairs={{0,16},{16,32},{32,48},{48,64},{64,80},{80,96},{96,112},{1,17},{17... | collective-permute-start | bytes 1105928 | tf_op jit(solution)/shard_map/ppermute | solution.py:39
  36.5 15.5 %all-to-all-start = ((bf16[8,408,128]{2,1,0:T(8,128)(2,1)}), bf16[8,408,128]{2,1,0:T(8,128)(2,1)S(1)}, u32[]{:S(2)}, u32[]{:S(2)}) async-start(bf16[8,408,128]{2,1,0:T(8,128)(2,1)} %get-tuple-element.7), calls=%async_computation | async-start | bytes 1671168 | tf_op jit(solution)/shard_map/all_to_all | solution.py:359
  40.0 9.2 %collective-permute-start.4 = (bf16[2,4,48,192]{3,2,1,0:T(8,128)(2,1)S(1)}, bf16[2,4,48,192]{3,2,1,0:T(8,128)(2,1)S(1)}, u32[]{:S(2)}, u32[]{:S(2)}) collective-permute-start(bf16[2,4,48,192]{3,2,1,0:T(8,128)(2,1)S(1)} %get-tuple-element.6.tall), channel_id=1, source_target_pairs={{1,0},{2,1},{3,2},{4,3},{5,4},{6,5},{7,6},{8,7},{9,8},{10,9},{11,1... | collective-permute-start | bytes 442376 | tf_op jit(solution)/shard_map/ppermute | solution.py:39
  63.5 28.8 %all-to-all-start.2 = ((bf16[16,16,128]{2,1,0:T(8,128)(2,1)}), bf16[16,16,128]{2,1,0:T(8,128)(2,1)S(1)}, u32[]{:S(2)}, u32[]{:S(2)}) async-start(bf16[16,16,128]{2,1,0:T(8,128)(2,1)} %bitcast.7), calls=%async_computation.2 | async-start | bytes 131072 | tf_op jit(solution)/shard_map/all_to_all | solution.py:386

commit v4 on v3

--- a/solution.py
+++ b/solution.py
@@ -37,6 +37,31 @@
 def move(value, axes, steps):
     sizes = [lax.axis_size(axis) for axis in axes]
     return lax.ppermute(value, axes if len(axes) > 1 else axes[0], route(sizes, steps))
+
+
+def digits(size):
+    stages, stride = [], size
+    while stride > 1:
+        radix = 4 if stride % 4 == 0 else stride
+        stride //= radix
+        stages.append((stride, radix))
+    return stages
+
+
+def rotate(value, axis, stride, radix, by):
+    pairs = []
+    for source in range(lax.axis_size(axis)):
+        digit = source // stride % radix
+        pairs.append((source, source + ((digit + by) % radix - digit) * stride))
+    return lax.ppermute(value, axis, pairs)
+
+
+def exchange(parts, axis, stride, radix):
+    return [parts[0]] + [rotate(parts[d], axis, stride, radix, d) for d in range(1, radix)]
+
+
+def digit_of(axis, stride, radix):
+    return lax.rem(lax.div(lax.axis_index(axis), stride), radix)
 
 
 def spread(ref, index, cols, value):
@@ -160,7 +185,8 @@
         pay[p, cells + half :, :] = mine.astype(BF)
 
 
-def second_kernel(span, got, out, field, left, prod):
+def second_kernel(span, got, *refs):
+    *outs, out, field, left, prod = refs
     peers = got.shape[0]
     cells = field.shape[0] // peers // (4 * PITCH) * 192
     half = cells // 2
@@ -240,20 +266,34 @@
                 tail = jnp.concatenate([pltpu.roll(tail, 81, 1), pltpu.roll(tail, 40, 1)], axis=0)
                 value = jnp.where(lane[:16, :128] < span, value[:16], tail)
             out[b, :, chunk : chunk + 128] = value.astype(BF)
-
-
-def clip_kernel(got, out):
-    total = got[0].astype(F32)
-    for p in range(1, got.shape[0]):
-        total += got[p].astype(F32)
-    out[...] = total.astype(BF)
-
-
-def last_kernel(scale, got, out):
+    send(out, outs, "clip", 1)
+
+
+def send(source, outs, axis, stride):
+    digit = digit_of(axis, stride, len(outs))
+    size = source.shape[0] // len(outs)
+    for d, out in enumerate(outs):
+        at = lax.rem(digit + d, len(outs)) * size
+        out[...] = source[pl.ds(at, size)]
+
+
+def summed(refs):
+    total = refs[0][...].astype(F32)
+    for ref in refs[1:]:
+        total += ref[...].astype(F32)
+    return total
+
+
+def sum_kernel(count, stride, *refs):
+    total = refs[-1]
+    total[...] = summed(refs[:count]).astype(BF)
+    send(total, refs[count:-1], "tm", stride)
+
+
+def last_kernel(scale, *refs):
+    out = refs[-1]
     width, span = out.shape
-    total = got[0].astype(F32)
-    for p in range(1, got.shape[0]):
-        total += got[p].astype(F32)
+    total = summed(refs[:-1])[0]
     total = total * scale
     if packed(width, span):
         lane = lax.broadcasted_iota(jnp.int32, (8, 128), 1)
@@ -362,35 +402,39 @@
     blocks = clips * steps
     span = 27 * chan // blocks
     shape = (16, 128) if packed(width, span) else (width, (span + 127) // 128 * 128)
-    (part,) = call(
+    parts = call(
         functools.partial(second_kernel, span),
         "kernel_grad_part",
-        16,
-        [((blocks,) + shape, BF)],
+        20,
+        [((steps,) + shape, BF)] * clips,
         (got,),
         [
+            ((blocks,) + shape, BF),
             ((2 * peers * 2 * PITCH, chan), BF),
             ((27 * width, 2 * peers * 128), F32),
             ((27 * width, 256), F32),
         ],
     )
-    by_clip = lax.all_to_all(part.reshape((clips, steps * shape[0], shape[1])), "clip", 0, 0)
-    (summed,) = call(
-        clip_kernel,
-        "clip_sum",
-        4,
-        [((steps * shape[0], shape[1]), BF)],
-        (by_clip,),
-        [],
-    )
-    by_step = lax.all_to_all(summed.reshape((steps,) + shape), "tm", 0, 0)
+    parts = exchange(parts, "clip", 1, clips)
+    held = steps
+    for stride, radix in digits(steps):
+        parts = call(
+            functools.partial(sum_kernel, len(parts), stride),
+            f"sum_before_{stride}",
+            4,
+            [((held // radix,) + shape, BF)] * radix,
+            parts,
+            [((held,) + shape, BF)],
+        )
+        parts = exchange(parts, "tm", stride, radix)
+        held //= radix
     total = clips * 2 * frames * steps * rows * peers * cols
     (kernel_grad,) = call(
         functools.partial(last_kernel, 1.0 / math.sqrt(total)),
         "kernel_grad_sum",
         4,
         [((width, span), F32)],
-        (by_step,),
+        parts,
         [],
     )
     (input_grad,) = call(

time: 93.5 us -> 114 us (1.22)
  the two profiles are of different devices: /device:TPU:2 before, /device:TPU:24 now
where the time goes in v4:
time: 114 us; the launch traced here: 113 us
  starting transfers between devices  68.1 us (60%)
  waiting for transfers between devices  26.5 us (23%)
  Pallas kernels  16 us (14%)
  between operations  1.48 us (1%)
    ppermute x9, starting transfers between devices, rotate(): return lax.ppermute(value, axis, pairs)  46 us
    pallas_call x7, Pallas kernels, call(): pl.pallas_call(body, name=name, out_shape=outs, in_specs=[pl.BlockSpec(me...  16 us
    ppermute x5, waiting for transfers between devices, move(): lax.ppermute(value, axes if len(axes) > 1 else axes[0], route(sizes, steps))  11.8 us
    ppermute x5, starting transfers between devices, move(): lax.ppermute(value, axes if len(axes) > 1 else axes[0], route(sizes, steps))  11.5 us
    ppermute x9, waiting for transfers between devices, rotate(): return lax.ppermute(value, axis, pairs)  10.8 us
    all_to_all x1, starting transfers between devices, local(): got = lax.all_to_all(pay, 'row', 0, 0)  10.6 us
    all_to_all x1, waiting for transfers between devices, local(): got = lax.all_to_all(pay, 'row', 0, 0)  3.93 us
  transfers between devices with their start and end apart: 15, of which 8 were waited for; matrix products, arithmetic and copies ran while one was open for 0% of the time, Pallas kernels for 3%

profile of v4, /device:TPU:24, one launch (start us, length us, event | category | flops | bytes accessed | tf_op | source)
XLA Modules:
  0.0 112.9 jit_solution(4888807945051690837)
XLA Ops:
  0.6 0.9 slice_bitcast_fusion
  1.5 1.3 %collective-permute-start.1 = (bf16[2,2,48,192]{3,2,1,0:T(8,128)(2,1)S(1)}, bf16[2,2,48,192]{3,2,1,0:T(8,128)(2,1)S(1)}, u32[]{:S(2)}, u32[]{:S(2)}) collective-permute-start(bf16[2,2,48,192]{3,2,1,0:T(8,128)(2,1)S(1)} %slice_bitcast_fusion), channel_id=1, source_target_pairs={{1,0},{2,1},{3,2},{4,3},{5,4},{6,5},{7,6},{8,7},{9,8},{10,9},{11,1... | collective-permute-start | bytes 221192 | tf_op jit(solution)/shard_map/ppermute | solution.py:39
  2.8 4.6 %collective-permute-start = (bf16[2,2,48,192]{3,2,1,0:T(8,128)(2,1)}, bf16[2,2,48,192]{3,2,1,0:T(8,128)(2,1)S(1)}, u32[]{:S(2)}, u32[]{:S(2)}) collective-permute-start(bf16[2,2,48,192]{3,2,1,0:T(8,128)(2,1)} %bitcast.13), channel_id=1, source_target_pairs={{0,1},{1,2},{2,3},{3,4},{4,5},{5,6},{6,7},{7,8},{8,9},{9,10},{10,1... | collective-permute-start | bytes 221192 | tf_op jit(solution)/shard_map/ppermute | solution.py:39
  7.4 0.8 collective-permute-done.1.gnext
  8.1 1.8 %collective-permute-done.xprev = bf16[2,2,48,192]{3,2,1,0:T(8,128)(2,1)S(1)} collective-permute-done((bf16[2,2,48,192]{3,2,1,0:T(8,128)(2,1)}, bf16[2,2,48,192]{3,2,1,0:T(8,128)(2,1)S(1)}, u32[]{:S(2)}, u32[]{:S(2)}) %collective-permute-start) | collective-permute-done | bytes 73760 | tf_op jit(solution)/shard_map/ppermute | solution.py:39
  9.9 1.0 band.1
  10.9 1.3 %collective-permute-start.3 = (bf16[10,2,48,192]{3,2,1,0:T(8,128)(2,1)S(1)}, bf16[10,2,48,192]{3,2,1,0:T(8,128)(2,1)S(1)}, u32[]{:S(2)}, u32[]{:S(2)}) collective-permute-start(bf16[10,2,48,192]{3,2,1,0:T(8,128)(2,1)S(1)} %band.1), channel_id=1, source_target_pairs={{16,0},{32,16},{48,32},{64,48},{80,64},{96,80},{112,96},{17,1},{33... | collective-permute-start | bytes 1105928 | tf_op jit(solution)/shard_map/ppermute | solution.py:39
  12.2 3.1 %collective-permute-start.2 = (bf16[10,2,48,192]{3,2,1,0:T(8,128)(2,1)S(1)}, bf16[10,2,48,192]{3,2,1,0:T(8,128)(2,1)S(1)}, u32[]{:S(2)}, u32[]{:S(2)}) collective-permute-start(bf16[10,2,48,192]{3,2,1,0:T(8,128)(2,1)S(1)} %band.1), channel_id=1, source_target_pairs={{0,16},{16,32},{32,48},{48,64},{64,80},{80,96},{96,112},{1,17},{17... | collective-permute-start | bytes 1105928 | tf_op jit(solution)/shard_map/ppermute | solution.py:39
  15.9 0.0 collective-permute-done.3.below
  15.9 0.8 collective-permute-done.2.above
  16.7 9.2 %hidden_and_pairs.1 = (bf16[8,408,128]{2,1,0:T(8,128)(2,1)}, bf16[2,4,48,192]{3,2,1,0:T(8,128)(2,1)S(1)}) custom-call(s32[1]{0:T(128)S(6)} %copy.7.lengths, bf16[2,2,48,192]{3,2,1,0:T(8,128)(2,1)} %bitcast.15, bf16[4,2,48,192]{3,2,1,0:T(8,128)(2,1)} %bitcast.12, bf16[27,192,192]{2,1,0:T(8,128)(2,1)} %bitcast.8, bf16[27,192,192]{2,1,0:T(8,128)(2,1)} %bitcast.10, ...), custom_call_target="tpu_custom_call" | custom-call | tf_op jit(solution)/shard_map/hidden_and_pairs/pallas_call | solution.py:337
  25.9 10.6 %all-to-all-start = ((bf16[8,408,128]{2,1,0:T(8,128)(2,1)}), bf16[8,408,128]{2,1,0:T(8,128)(2,1)S(1)}, u32[]{:S(2)}, u32[]{:S(2)}) async-start(bf16[8,408,128]{2,1,0:T(8,128)(2,1)} %get-tuple-element.19), calls=%async_computation | async-start | bytes 1671168 | tf_op jit(solution)/shard_map/all_to_all | solution.py:399
  36.5 1.3 %collective-permute-start.4 = (bf16[2,4,48,192]{3,2,1,0:T(8,128)(2,1)S(1)}, bf16[2,4,48,192]{3,2,1,0:T(8,128)(2,1)S(1)}, u32[]{:S(2)}, u32[]{:S(2)}) collective-permute-start(bf16[2,4,48,192]{3,2,1,0:T(8,128)(2,1)S(1)} %get-tuple-element.18.tall), channel_id=1, source_target_pairs={{1,0},{2,1},{3,2},{4,3},{5,4},{6,5},{7,6},{8,7},{9,8},{10,9},{11,1... | collective-permute-start | bytes 442376 | tf_op jit(solution)/shard_map/ppermute | solution.py:39
  37.8 8.5 %collective-permute-done.4.after = bf16[2,4,48,192]{3,2,1,0:T(8,128)(2,1)S(1)} collective-permute-done((bf16[2,4,48,192]{3,2,1,0:T(8,128)(2,1)S(1)}, bf16[2,4,48,192]{3,2,1,0:T(8,128)(2,1)S(1)}, u32[]{:S(2)}, u32[]{:S(2)}) %collective-permute-start.4) | collective-permute-done | bytes 147488 | tf_op jit(solution)/shard_map/ppermute | solution.py:39
  46.3 3.9 %all-to-all-done.got = bf16[8,408,128]{2,1,0:T(8,128)(2,1)S(1)} async-done(((bf16[8,408,128]{2,1,0:T(8,128)(2,1)}), bf16[8,408,128]{2,1,0:T(8,128)(2,1)S(1)}, u32[]{:S(2)}, u32[]{:S(2)}) %all-to-all-start) | async-done | bytes 835616 | tf_op jit(solution)/shard_map/all_to_all | solution.py:399
  50.2 1.8 %kernel_grad_part.1 = (bf16[16,16,128]{2,1,0:T(8,128)(2,1)S(1)}, bf16[16,16,128]{2,1,0:T(8,128)(2,1)S(1)}, bf16[16,16,128]{2,1,0:T(8,128)(2,1)S(1)}, bf16[16,16,128]{2,1,0:T(8,128)(2,1)S(1)}) custom-call(bf16[8,408,128]{2,1,0:T(8,128)(2,1)S(1)} %all-to-all-done.got), custom_call_target="tpu_custom_call" | custom-call | tf_op jit(solution)/shard_map/kernel_grad_part/pallas_call | solution.py:337
  52.0 4.9 %collective-permute-start.5 = (bf16[16,16,128]{2,1,0:T(8,128)(2,1)S(1)}, bf16[16,16,128]{2,1,0:T(8,128)(2,1)S(1)}, u32[]{:S(2)}, u32[]{:S(2)}) collective-permute-start(bf16[16,16,128]{2,1,0:T(8,128)(2,1)S(1)} %get-tuple-element.23), channel_id=1, source_target_pairs={{0,128},{128,256},{256,384},{384,0},{1,129},{129,257},{257,385},{3... | collective-permute-start | bytes 196616 | tf_op jit(solution)/shard_map/ppermute | solution.py:56
  56.8 1.9 %collective-permute-start.6 = (bf16[16,16,128]{2,1,0:T(8,128)(2,1)S(1)}, bf16[16,16,128]{2,1,0:T(8,128)(2,1)S(1)}, u32[]{:S(2)}, u32[]{:S(2)}) collective-permute-start(bf16[16,16,128]{2,1,0:T(8,128)(2,1)S(1)} %get-tuple-element.24), channel_id=1, source_target_pairs={{0,256},{128,384},{256,0},{384,128},{1,257},{129,385},{257,1},{385... | collective-permute-start | bytes 196616 | tf_op jit(solution)/shard_map/ppermute | solution.py:56
  58.8 2.8 %collective-permute-start.7 = (bf16[16,16,128]{2,1,0:T(8,128)(2,1)S(1)}, bf16[16,16,128]{2,1,0:T(8,128)(2,1)S(1)}, u32[]{:S(2)}, u32[]{:S(2)}) collective-permute-start(bf16[16,16,128]{2,1,0:T(8,128)(2,1)S(1)} %get-tuple-element.25), channel_id=1, source_target_pairs={{0,384},{128,0},{256,128},{384,256},{1,385},{129,1},{257,129},{385... | collective-permute-start | bytes 196616 | tf_op jit(solution)/shard_map/ppermute | solution.py:56
  61.5 0.0 collective-permute-done.5.refs_1_
  61.6 3.3 %collective-permute-done.6.refs_2_ = bf16[16,16,128]{2,1,0:T(8,128)(2,1)S(1)} collective-permute-done((bf16[16,16,128]{2,1,0:T(8,128)(2,1)S(1)}, bf16[16,16,128]{2,1,0:T(8,128)(2,1)S(1)}, u32[]{:S(2)}, u32[]{:S(2)}) %collective-permute-start.6) | collective-permute-done | bytes 65568 | tf_op jit(solution)/shard_map/ppermute | solution.py:56
  64.9 1.3 %collective-permute-done.7.refs_3_ = bf16[16,16,128]{2,1,0:T(8,128)(2,1)S(1)} collective-permute-done((bf16[16,16,128]{2,1,0:T(8,128)(2,1)S(1)}, bf16[16,16,128]{2,1,0:T(8,128)(2,1)S(1)}, u32[]{:S(2)}, u32[]{:S(2)}) %collective-permute-start.7) | collective-permute-done | bytes 65568 | tf_op jit(solution)/shard_map/ppermute | solution.py:56
  66.2 10.5 %collective-permute-start.8 = (bf16[4,16,128]{2,1,0:T(8,128)(2,1)S(1)}, bf16[4,16,128]{2,1,0:T(8,128)(2,1)S(1)}, u32[]{:S(2)}, u32[]{:S(2)}) collective-permute-start(bf16[4,16,128]{2,1,0:T(8,128)(2,1)S(1)} %get-tuple-element.27), channel_id=1, source_target_pairs={{0,4},{1,5},{2,6},{3,7},{4,8},{5,9},{6,10},{7,11},{8,12},{9,13},{1... | collective-permute-start | bytes 49160 | tf_op jit(solution)/shard_map/ppermute | solution.py:56
  76.7 13.0 %collective-permute-start.9 = (bf16[4,16,128]{2,1,0:T(8,128)(2,1)S(1)}, bf16[4,16,128]{2,1,0:T(8,128)(2,1)S(1)}, u32[]{:S(2)}, u32[]{:S(2)}) collective-permute-start(bf16[4,16,128]{2,1,0:T(8,128)(2,1)S(1)} %get-tuple-element.28), channel_id=1, source_target_pairs={{0,8},{1,9},{2,10},{3,11},{4,12},{5,13},{6,14},{7,15},{8,0},{9,1},... | collective-permute-start | bytes 49160 | tf_op jit(solution)/shard_map/ppermute | solution.py:56
  89.8 3.4 %collective-permute-start.10 = (bf16[4,16,128]{2,1,0:T(8,128)(2,1)S(1)}, bf16[4,16,128]{2,1,0:T(8,128)(2,1)S(1)}, u32[]{:S(2)}, u32[]{:S(2)}) collective-permute-start(bf16[4,16,128]{2,1,0:T(8,128)(2,1)S(1)} %get-tuple-element.29), channel_id=1, source_target_pairs={{0,12},{1,13},{2,14},{3,15},{4,0},{5,1},{6,2},{7,3},{8,4},{9,5},{1... | collective-permute-start | bytes 49160 | tf_op jit(solution)/shard_map/ppermute | solution.py:56
  93.1 0.0 collective-permute-done.8.refs_1_
  93.1 0.0 collective-permute-done.9.refs_2_
  93.1 6.2 %collective-permute-done.10.refs_3_ = bf16[4,16,128]{2,1,0:T(8,128)(2,1)S(1)} collective-permute-done((bf16[4,16,128]{2,1,0:T(8,128)(2,1)S(1)}, bf16[4,16,128]{2,1,0:T(8,128)(2,1)S(1)}, u32[]{:S(2)}, u32[]{:S(2)}) %collective-permute-start.10) | collective-permute-done | bytes 16416 | tf_op jit(solution)/shard_map/ppermute | solution.py:56
  99.3 1.9 %collective-permute-start.11 = (bf16[1,16,128]{2,1,0:T(8,128)(2,1)S(1)}, bf16[1,16,128]{2,1,0:T(8,128)(2,1)S(1)}, u32[]{:S(2)}, u32[]{:S(2)}) collective-permute-start(bf16[1,16,128]{2,1,0:T(8,128)(2,1)S(1)} %get-tuple-element.31), channel_id=1, source_target_pairs={{0,1},{1,2},{2,3},{3,0},{4,5},{5,6},{6,7},{7,4},{8,9},{9,10},{10,1... | collective-permute-start | bytes 12296 | tf_op jit(solution)/shard_map/ppermute | solution.py:56
  101.3 2.0 %collective-permute-start.12 = (bf16[1,16,128]{2,1,0:T(8,128)(2,1)S(1)}, bf16[1,16,128]{2,1,0:T(8,128)(2,1)S(1)}, u32[]{:S(2)}, u32[]{:S(2)}) collective-permute-start(bf16[1,16,128]{2,1,0:T(8,128)(2,1)S(1)} %get-tuple-element.32), channel_id=1, source_target_pairs={{0,2},{1,3},{2,0},{3,1},{4,6},{5,7},{6,4},{7,5},{8,10},{9,11},{10,... | collective-permute-start | bytes 12296 | tf_op jit(solution)/shard_map/ppermute | solution.py:56
  103.2 5.7 %collective-permute-start.13 = (bf16[1,16,128]{2,1,0:T(8,128)(2,1)S(1)}, bf16[1,16,128]{2,1,0:T(8,128)(2,1)S(1)}, u32[]{:S(2)}, u32[]{:S(2)}) collective-permute-start(bf16[1,16,128]{2,1,0:T(8,128)(2,1)S(1)} %get-tuple-element.33), channel_id=1, source_target_pairs={{0,3},{1,0},{2,1},{3,2},{4,7},{5,4},{6,5},{7,6},{8,11},{9,8},{10,9... | collective-permute-start | bytes 12296 | tf_op jit(solution)/shard_map/ppermute | solution.py:56
  108.9 3.3 %input_grad.1 = f32[2,2,48,192]{3,2,1,0:T(8,128)} custom-call(bf16[27,192,192]{2,1,0:T(8,128)(2,1)} %bitcast.9, bf16[2,4,48,192]{3,2,1,0:T(8,128)(2,1)S(1)} %get-tuple-element.18.tall, bf16[2,4,48,192]{3,2,1,0:T(8,128)(2,1)S(1)} %collective-permute-done.4.after), custom_call_target="tpu_custom_call" | custom-call | tf_op jit(solution)/shard_map/input_grad/pallas_call | solution.py:337
  112.2 0.0 collective-permute-done.11.refs_1_
  112.2 0.0 collective-permute-done.12.refs_2_
  112.2 0.0 collective-permute-done.13.refs_3_
  112.3 0.7 kernel_grad_sum.1
  (2 shorter events, 0.1 us)
Async XLA Ops:
  1.5 6.6 %collective-permute-start.1 = (bf16[2,2,48,192]{3,2,1,0:T(8,128)(2,1)S(1)}, bf16[2,2,48,192]{3,2,1,0:T(8,128)(2,1)S(1)}, u32[]{:S(2)}, u32[]{:S(2)}) collective-permute-start(bf16[2,2,48,192]{3,2,1,0:T(8,128)(2,1)S(1)} %slice_bitcast_fusion), channel_id=1, source_target_pairs={{1,0},{2,1},{3,2},{4,3},{5,4},{6,5},{7,6},{8,7},{9,8},{10,9},{11,1... | collective-permute-start | bytes 221192 | tf_op jit(solution)/shard_map/ppermute | solution.py:39
  2.8 7.1 %collective-permute-start = (bf16[2,2,48,192]{3,2,1,0:T(8,128)(2,1)}, bf16[2,2,48,192]{3,2,1,0:T(8,128)(2,1)S(1)}, u32[]{:S(2)}, u32[]{:S(2)}) collective-permute-start(bf16[2,2,48,192]{3,2,1,0:T(8,128)(2,1)} %bitcast.13), channel_id=1, source_target_pairs={{0,1},{1,2},{2,3},{3,4},{4,5},{5,6},{6,7},{7,8},{8,9},{9,10},{10,1... | collective-permute-start | bytes 221192 | tf_op jit(solution)/shard_map/ppermute | solution.py:39
  10.9 5.0 %collective-permute-start.3 = (bf16[10,2,48,192]{3,2,1,0:T(8,128)(2,1)S(1)}, bf16[10,2,48,192]{3,2,1,0:T(8,128)(2,1)S(1)}, u32[]{:S(2)}, u32[]{:S(2)}) collective-permute-start(bf16[10,2,48,192]{3,2,1,0:T(8,128)(2,1)S(1)} %band.1), channel_id=1, source_target_pairs={{16,0},{32,16},{48,32},{64,48},{80,64},{96,80},{112,96},{17,1},{33... | collective-permute-start | bytes 1105928 | tf_op jit(solution)/shard_map/ppermute | solution.py:39
  12.2 4.5 %collective-permute-start.2 = (bf16[10,2,48,192]{3,2,1,0:T(8,128)(2,1)S(1)}, bf16[10,2,48,192]{3,2,1,0:T(8,128)(2,1)S(1)}, u32[]{:S(2)}, u32[]{:S(2)}) collective-permute-start(bf16[10,2,48,192]{3,2,1,0:T(8,128)(2,1)S(1)} %band.1), channel_id=1, source_target_pairs={{0,16},{16,32},{32,48},{48,64},{64,80},{80,96},{96,112},{1,17},{17... | collective-permute-start | bytes 1105928 | tf_op jit(solution)/shard_map/ppermute | solution.py:39
  25.9 24.3 %all-to-all-start = ((bf16[8,408,128]{2,1,0:T(8,128)(2,1)}), bf16[8,408,128]{2,1,0:T(8,128)(2,1)S(1)}, u32[]{:S(2)}, u32[]{:S(2)}) async-start(bf16[8,408,128]{2,1,0:T(8,128)(2,1)} %get-tuple-element.19), calls=%async_computation | async-start | bytes 1671168 | tf_op jit(solution)/shard_map/all_to_all | solution.py:399
  36.5 9.8 %collective-permute-start.4 = (bf16[2,4,48,192]{3,2,1,0:T(8,128)(2,1)S(1)}, bf16[2,4,48,192]{3,2,1,0:T(8,128)(2,1)S(1)}, u32[]{:S(2)}, u32[]{:S(2)}) collective-permute-start(bf16[2,4,48,192]{3,2,1,0:T(8,128)(2,1)S(1)} %get-tuple-element.18.tall), channel_id=1, source_target_pairs={{1,0},{2,1},{3,2},{4,3},{5,4},{6,5},{7,6},{8,7},{9,8},{10,9},{11,1... | collective-permute-start | bytes 442376 | tf_op jit(solution)/shard_map/ppermute | solution.py:39
  52.0 9.6 %collective-permute-start.5 = (bf16[16,16,128]{2,1,0:T(8,128)(2,1)S(1)}, bf16[16,16,128]{2,1,0:T(8,128)(2,1)S(1)}, u32[]{:S(2)}, u32[]{:S(2)}) collective-permute-start(bf16[16,16,128]{2,1,0:T(8,128)(2,1)S(1)} %get-tuple-element.23), channel_id=1, source_target_pairs={{0,128},{128,256},{256,384},{384,0},{1,129},{129,257},{257,385},{3... | collective-permute-start | bytes 196616 | tf_op jit(solution)/shard_map/ppermute | solution.py:56
  56.8 8.0 %collective-permute-start.6 = (bf16[16,16,128]{2,1,0:T(8,128)(2,1)S(1)}, bf16[16,16,128]{2,1,0:T(8,128)(2,1)S(1)}, u32[]{:S(2)}, u32[]{:S(2)}) collective-permute-start(bf16[16,16,128]{2,1,0:T(8,128)(2,1)S(1)} %get-tuple-element.24), channel_id=1, source_target_pairs={{0,256},{128,384},{256,0},{384,128},{1,257},{129,385},{257,1},{385... | collective-permute-start | bytes 196616 | tf_op jit(solution)/shard_map/ppermute | solution.py:56
  58.8 7.4 %collective-permute-start.7 = (bf16[16,16,128]{2,1,0:T(8,128)(2,1)S(1)}, bf16[16,16,128]{2,1,0:T(8,128)(2,1)S(1)}, u32[]{:S(2)}, u32[]{:S(2)}) collective-permute-start(bf16[16,16,128]{2,1,0:T(8,128)(2,1)S(1)} %get-tuple-element.25), channel_id=1, source_target_pairs={{0,384},{128,0},{256,128},{384,256},{1,385},{129,1},{257,129},{385... | collective-permute-start | bytes 196616 | tf_op jit(solution)/shard_map/ppermute | solution.py:56
  66.2 26.9 %collective-permute-start.8 = (bf16[4,16,128]{2,1,0:T(8,128)(2,1)S(1)}, bf16[4,16,128]{2,1,0:T(8,128)(2,1)S(1)}, u32[]{:S(2)}, u32[]{:S(2)}) collective-permute-start(bf16[4,16,128]{2,1,0:T(8,128)(2,1)S(1)} %get-tuple-element.27), channel_id=1, source_target_pairs={{0,4},{1,5},{2,6},{3,7},{4,8},{5,9},{6,10},{7,11},{8,12},{9,13},{1... | collective-permute-start | bytes 49160 | tf_op jit(solution)/shard_map/ppermute | solution.py:56
  76.7 16.4 %collective-permute-start.9 = (bf16[4,16,128]{2,1,0:T(8,128)(2,1)S(1)}, bf16[4,16,128]{2,1,0:T(8,128)(2,1)S(1)}, u32[]{:S(2)}, u32[]{:S(2)}) collective-permute-start(bf16[4,16,128]{2,1,0:T(8,128)(2,1)S(1)} %get-tuple-element.28), channel_id=1, source_target_pairs={{0,8},{1,9},{2,10},{3,11},{4,12},{5,13},{6,14},{7,15},{8,0},{9,1},... | collective-permute-start | bytes 49160 | tf_op jit(solution)/shard_map/ppermute | solution.py:56
  89.8 9.5 %collective-permute-start.10 = (bf16[4,16,128]{2,1,0:T(8,128)(2,1)S(1)}, bf16[4,16,128]{2,1,0:T(8,128)(2,1)S(1)}, u32[]{:S(2)}, u32[]{:S(2)}) collective-permute-start(bf16[4,16,128]{2,1,0:T(8,128)(2,1)S(1)} %get-tuple-element.29), channel_id=1, source_target_pairs={{0,12},{1,13},{2,14},{3,15},{4,0},{5,1},{6,2},{7,3},{8,4},{9,5},{1... | collective-permute-start | bytes 49160 | tf_op jit(solution)/shard_map/ppermute | solution.py:56
  99.3 12.9 %collective-permute-start.11 = (bf16[1,16,128]{2,1,0:T(8,128)(2,1)S(1)}, bf16[1,16,128]{2,1,0:T(8,128)(2,1)S(1)}, u32[]{:S(2)}, u32[]{:S(2)}) collective-permute-start(bf16[1,16,128]{2,1,0:T(8,128)(2,1)S(1)} %get-tuple-element.31), channel_id=1, source_target_pairs={{0,1},{1,2},{2,3},{3,0},{4,5},{5,6},{6,7},{7,4},{8,9},{9,10},{10,1... | collective-permute-start | bytes 12296 | tf_op jit(solution)/shard_map/ppermute | solution.py:56
  101.3 11.0 %collective-permute-start.12 = (bf16[1,16,128]{2,1,0:T(8,128)(2,1)S(1)}, bf16[1,16,128]{2,1,0:T(8,128)(2,1)S(1)}, u32[]{:S(2)}, u32[]{:S(2)}) collective-permute-start(bf16[1,16,128]{2,1,0:T(8,128)(2,1)S(1)} %get-tuple-element.32), channel_id=1, source_target_pairs={{0,2},{1,3},{2,0},{3,1},{4,6},{5,7},{6,4},{7,5},{8,10},{9,11},{10,... | collective-permute-start | bytes 12296 | tf_op jit(solution)/shard_map/ppermute | solution.py:56
  103.2 9.0 %collective-permute-start.13 = (bf16[1,16,128]{2,1,0:T(8,128)(2,1)S(1)}, bf16[1,16,128]{2,1,0:T(8,128)(2,1)S(1)}, u32[]{:S(2)}, u32[]{:S(2)}) collective-permute-start(bf16[1,16,128]{2,1,0:T(8,128)(2,1)S(1)} %get-tuple-element.33), channel_id=1, source_target_pairs={{0,3},{1,0},{2,1},{3,2},{4,7},{5,4},{6,5},{7,6},{8,11},{9,8},{10,9... | collective-permute-start | bytes 12296 | tf_op jit(solution)/shard_map/ppermute | solution.py:56

commit v5 on v3

--- a/solution.py
+++ b/solution.py
@@ -53,16 +53,17 @@
     return lax.dot_general(a, b, (((1,), (1,)), ((), ())), preferred_element_type=F32)
 
 
-def band_kernel(x, g, xprev, gnext, band, sem):
+def band_kernel(x, g, xprev, gnext, band, top, bot, sem):
     nx, ng = x.shape[0], g.shape[0]
-    copies = [
-        pltpu.make_async_copy(x, band.at[0:nx], sem.at[0]),
-        pltpu.make_async_copy(g, band.at[2 * nx : 2 * nx + ng], sem.at[1]),
-    ]
+    pairs = [(x, band.at[0:nx]), (g, band.at[2 * nx : 2 * nx + ng])]
+    pairs += [(x.at[:, row], out.at[0:nx]) for row, out in ((0, top), (1, bot))]
+    copies = [pltpu.make_async_copy(a, b, sem.at[n]) for n, (a, b) in enumerate(pairs)]
     for copy in copies:
         copy.start()
     band[nx : 2 * nx] = xprev[...]
     band[2 * nx + ng :] = gnext[...]
+    top[nx:] = xprev[:, 0]
+    bot[nx:] = xprev[:, 1]
     for copy in copies:
         copy.wait()
 
@@ -71,9 +72,69 @@
     return (width, span) == (24, 81)
 
 
-def first_kernel(
+def silu_kernel(
+    lengths, x_far, g_far, w_far, above, below, xprev, gnext, pay, xs, ps, xk, x, g, w, sem
+):
+    pairs = ((x_far, x), (w_far, w), (g_far, g))
+    copies = [pltpu.make_async_copy(a, b, sem.at[n]) for n, (a, b) in enumerate(pairs)]
+    for copy in copies:
+        copy.start()
+    frames, rows, cols, chan = x.shape
+    cells = frames * rows * cols
+    peers = pay.shape[0]
+    width = chan // peers
+    clear_edges(xs, cols)
+    for f in range(2):
+        for r in range(2):
+            spread(xs, f * 4 + 1 + r, cols, xprev[f, r])
+        spread(xs, f * 4, cols, above[2 + f])
+        spread(xs, f * 4 + 3, cols, below[2 + f])
+        spread(xs, (2 + f) * 4, cols, above[f])
+        spread(xs, (2 + f) * 4 + 3, cols, below[f])
+    copies[0].wait()
+    for f in range(2):
+        for r in range(2):
+            spread(xs, (2 + f) * 4 + 1 + r, cols, x[f, r])
+    for k in range(3):
+        piece = xs[:, EDGE - 1 + k : EDGE - 1 + k + cols, :].astype(BF)
+        xk[:, :, k * chan : (k + 1) * chan] = piece
+    copies[2].wait()
+    limit = 2 * lengths[0] - 2 * frames * lax.axis_index("tm")
+    ps[:, 0:EDGE, :] = jnp.zeros((10, EDGE, chan), F32)
+    for r in range(2):
+        field = masked_frames([g[f, r] for f in range(4)] + [gnext[f, r] for f in range(2)], limit)
+        for a in range(5):
+            ps[a * 2 + r, EDGE : EDGE + cols, :] = field[a] + field[a + 1]
+    turned = [
+        jnp.transpose(ps[2 * a : 2 * a + 2].reshape(2 * PITCH, chan)).astype(BF) for a in range(5)
+    ]
+    copies[1].wait()
+    hidden = jnp.zeros((cells, chan), F32)
+    for i in range(3):
+        for j in range(3):
+            part = [xk[(f + 2 - i) * 4 + j : (f + 2 - i) * 4 + j + 2] for f in range(2)]
+            patch = jnp.concatenate(part, axis=0).reshape(cells, 3 * chan)
+            rows_of = slice((i * 3 + j) * 3 * chan, (i * 3 + j + 1) * 3 * chan)
+            hidden += jnp.dot(patch, w[rows_of, :], preferred_element_type=F32)
+    act = (hidden / (1.0 + jnp.exp(-hidden))).astype(BF)
+    half = cells // 2
+    wide = act.astype(F32)
+    low = wide[:, :128].astype(BF)
+    high = jnp.concatenate([wide[:half, 128:], wide[half:, 128:]], axis=1).astype(BF)
+    for p in range(peers):
+        pay[p, 0:cells, :] = low
+        pay[p, cells : cells + half, :] = high
+        mine = jnp.concatenate([v[p * width : (p + 1) * width] for v in turned], axis=0)
+        pay[p, cells + half :, :] = mine
+
+
+def masked_frames(values, limit):
+    return [jnp.where(f < limit, v.astype(F32), 0.0) for f, v in enumerate(values)]
+
+
+def hidden_grad_kernel(
     lengths, x_far, g_far, w1_far, w2_far, above, below, xprev, gnext,
-    pay, tall,
+    tall,
     xs, ps, xk, pk, x, g, w1, w2, sem,
 ):
     pairs = ((x_far, x), (w1_far, w1), (g_far, g), (w2_far, w2))
@@ -81,11 +142,7 @@
     for copy in copies:
         copy.start()
     frames, rows, cols, chan = x.shape
-    cells = frames * rows * cols
-    reach = 2 * cells
-    peers = pay.shape[0]
-    width = chan // peers
-    block = lax.axis_index("tm")
+    reach = 2 * frames * rows * cols
     clear_edges(xs, cols)
     clear_edges(ps, cols)
     copies[0].wait()
@@ -98,35 +155,28 @@
             spread(xs, (2 + f) * 6 + 2 + r, cols, x[f, r])
             spread(xs, (2 + f) * 6 + 4 + r, cols, below[f, r])
     for k in range(3):
-        xk[k] = xs[:, EDGE - 1 + k : EDGE - 1 + k + cols, :].astype(BF)
+        piece = xs[:, EDGE - 1 + k : EDGE - 1 + k + cols, :].astype(BF)
+        xk[:, :, k * chan : (k + 1) * chan] = piece
     copies[1].wait()
     hidden = jnp.zeros((reach, chan), F32)
     for i in range(3):
         for j in range(3):
-            for k in range(3):
-                part = [xk[k, (f + 2 - i) * 6 + j : (f + 2 - i) * 6 + j + 4] for f in range(2)]
-                patch = jnp.concatenate(part, axis=0).reshape(reach, chan)
-                hidden += jnp.dot(patch, w1[i * 9 + j * 3 + k], preferred_element_type=F32)
+            part = [xk[(f + 2 - i) * 6 + j : (f + 2 - i) * 6 + j + 4] for f in range(2)]
+            patch = jnp.concatenate(part, axis=0).reshape(reach, 3 * chan)
+            rows_of = slice((i * 3 + j) * 3 * chan, (i * 3 + j + 1) * 3 * chan)
+            hidden += jnp.dot(patch, w1[rows_of, :], preferred_element_type=F32)
     sigma = 1.0 / (1.0 + jnp.exp(-hidden))
-    act = (hidden * sigma).reshape(frames, rows + 2, cols, chan)[:, 1 : 1 + rows]
-    act = act.reshape(cells, chan).astype(BF)
-    limit = 2 * lengths[0] - 2 * frames * block
-
-    def cotangent(f, r):
-        if r < 2:
-            value = above[2 * frames + f, r]
-        elif r > 3:
-            value = below[2 * frames + f, r - 4]
-        elif f >= 2 * frames:
-            value = gnext[f - 2 * frames, r - 2]
-        else:
-            value = g[f, r - 2]
-        value = value.astype(F32)
-        return jnp.where(f < limit, value, jnp.zeros_like(value))
-
+    slope = sigma * (1.0 + hidden * (1.0 - sigma))
+    limit = 2 * lengths[0] - 2 * frames * lax.axis_index("tm")
     copies[2].wait()
     for r in range(6):
-        field = [cotangent(f, r) for f in range(6)]
+        if r < 2:
+            values = [above[4 + f, r] for f in range(6)]
+        elif r > 3:
+            values = [below[4 + f, r - 4] for f in range(6)]
+        else:
+            values = [g[f, r - 2] for f in range(4)] + [gnext[f, r - 2] for f in range(2)]
+        field = masked_frames(values, limit)
         for a in range(5):
             spread(ps, a * 6 + r, cols, field[a] + field[a + 1])
     for k in range(3):
@@ -139,25 +189,13 @@
                 part = [pk[k, (2 * t + i) * 6 + 2 - j : (2 * t + i) * 6 + 6 - j] for t in range(2)]
                 patch = jnp.concatenate(part, axis=0).reshape(reach, chan)
                 pair += transposed_dot(patch, w2[i * 9 + j * 3 + k])
-    grad = (pair * sigma * (1.0 + hidden * (1.0 - sigma))).reshape(frames, rows + 2, cols, chan)
+    grad = (pair * slope).reshape(frames, rows + 2, cols, chan)
     band = lax.axis_index("row")
     none = jnp.zeros((frames, cols, chan), F32)
     tall[:, 0] = jnp.where(band > 0, grad[:, 0], none).astype(BF)
     tall[:, 1 : 1 + rows] = grad[:, 1 : 1 + rows].astype(BF)
-    tall[:, 1 + rows] = jnp.where(band < peers - 1, grad[:, 1 + rows], none).astype(BF)
-    half = cells // 2
-    wide = act.astype(F32)
-    low = wide[:, :128].astype(BF)
-    high = jnp.concatenate([wide[:half, 128:], wide[half:, 128:]], axis=1).astype(BF)
-    turned = [
-        jnp.transpose(ps[a * 6 + 2 : a * 6 + 4, 0:PITCH, :].reshape(2 * PITCH, chan))
-        for a in range(5)
-    ]
-    for p in range(peers):
-        pay[p, 0:cells, :] = low
-        pay[p, cells : cells + half, :] = high
-        mine = jnp.concatenate([v[p * width : (p + 1) * width] for v in turned], axis=0)
-        pay[p, cells + half :, :] = mine.astype(BF)
+    last = band == lax.axis_size("row") - 1
+    tall[:, 1 + rows] = jnp.where(last, none, grad[:, 1 + rows]).astype(BF)
 
 
 def second_kernel(span, got, out, field, left, prod):
@@ -319,45 +357,63 @@
 
     xprev = move(x, ("tm",), (1,))
     gnext = move(g[:frames], ("tm",), (-1,))
-    (band,) = call(
+    edge = (2 * frames, cols, chan)
+    band, top, bot = call(
         band_kernel,
         "band",
         4,
-        [((5 * frames, rows, cols, chan), BF)],
+        [((5 * frames, rows, cols, chan), BF), (edge, BF), (edge, BF)],
         (xprev, gnext),
         [],
         far=(x, g),
-        sems=2,
-    )
+        sems=4,
+    )
+    above_edge = move(bot, ("row",), (1,))
+    below_edge = move(top, ("row",), (-1,))
     above = move(band, ("row",), (1,))
     below = move(band, ("row",), (-1,))
-
-    pay, tall = call(
-        first_kernel,
-        "hidden_and_pairs",
+    w1_flat = weight_one.reshape(27 * chan, chan)
+    (pay,) = call(
+        silu_kernel,
+        "hidden_and_act",
+        16,
+        [((peers, cells + cells // 2 + 5 * width, 128), BF)],
+        (above_edge, below_edge, xprev, gnext),
+        [
+            ((16, WIDE, chan), F32),
+            ((10, PITCH, chan), F32),
+            ((16, cols, 3 * chan), BF),
+            (x.shape, BF),
+            (g.shape, BF),
+            (w1_flat.shape, BF),
+        ],
+        far=(x, g, w1_flat),
+        scalars=(lengths,),
+        sems=3,
+    )
+    got = lax.all_to_all(pay, "row", 0, 0)
+    (tall,) = call(
+        hidden_grad_kernel,
+        "hidden_grad",
         28,
-        [
-            ((peers, cells + cells // 2 + 5 * width, 128), BF),
-            ((frames, rows + 2, cols, chan), BF),
-        ],
+        [((frames, rows + 2, cols, chan), BF)],
         (above, below, xprev, gnext),
         [
             ((24, WIDE, chan), F32),
             ((30, WIDE, chan), F32),
-            ((3, 24, cols, chan), BF),
+            ((24, cols, 3 * chan), BF),
             ((3, 30, cols, chan), BF),
             (x.shape, BF),
             (g.shape, BF),
-            (w1.shape, BF),
+            (w1_flat.shape, BF),
             (w2.shape, BF),
         ],
-        far=(x, g, w1, w2),
+        far=(x, g, w1_flat, w2),
         scalars=(lengths,),
         sems=4,
     )
+    got, tall = lax.optimization_barrier((got, tall))
     after = move(tall, ("tm",), (-1,))
-    got = lax.all_to_all(pay, "row", 0, 0)
-    got, after = lax.optimization_barrier((got, after))
 
     blocks = clips * steps
     span = 27 * chan // blocks
@@ -383,6 +439,7 @@
         (by_clip,),
         [],
     )
+    summed, after = lax.optimization_barrier((summed, after))
     by_step = lax.all_to_all(summed.reshape((steps,) + shape), "tm", 0, 0)
     total = clips * 2 * frames * steps * rows * peers * cols
     (kernel_grad,) = call(

time: 93.5 us -> 101 us (1.080)
  the two profiles are of different devices: /device:TPU:2 before, /device:TPU:10 now
where the time goes in v5:
time: 101 us
  starting transfers between devices  44.3 us (44%)
  waiting for transfers between devices  33.8 us (33%)
  Pallas kernels  20.3 us (20%)
  between operations  1.39 us (1%)
    pallas_call x7, Pallas kernels, call(): pl.pallas_call(body, name=name, out_shape=outs, in_specs=[pl.BlockSpec(me...  20.3 us
    ppermute x7, waiting for transfers between devices, move(): lax.ppermute(value, axes if len(axes) > 1 else axes[0], route(sizes, steps))  19.3 us
    ppermute x7, starting transfers between devices, move(): lax.ppermute(value, axes if len(axes) > 1 else axes[0], route(sizes, steps))  17.5 us
    all_to_all x1, starting transfers between devices, local(): by_step = lax.all_to_all(summed.reshape((steps,) + shape), 'tm', 0, 0)  16.1 us
    all_to_all x1, waiting for transfers between devices, local(): by_step = lax.all_to_all(summed.reshape((steps,) + shape), 'tm', 0, 0)  9.43 us
    all_to_all x1, starting transfers between devices, local(): got = lax.all_to_all(pay, 'row', 0, 0)  5.84 us
    all_to_all x1, waiting for transfers between devices, local(): lax.all_to_all(part.reshape((clips, steps * shape[0], shape[1])), 'clip',...  5.09 us
    all_to_all x1, starting transfers between devices, local(): lax.all_to_all(part.reshape((clips, steps * shape[0], shape[1])), 'clip',...  4.91 us
  transfers between devices with their start and end apart: 10, of which 7 were waited for; matrix products, arithmetic and copies ran while one was open for 1% of the time, Pallas kernels for 12%

profile of v5, /device:TPU:10, one launch (start us, length us, event | category | flops | bytes accessed | tf_op | source)
XLA Modules:
  0.0 100.8 jit_solution(5018377042620590386)
XLA Ops:
  0.6 3.8 %collective-permute-start = (bf16[2,2,48,192]{3,2,1,0:T(8,128)(2,1)}, bf16[2,2,48,192]{3,2,1,0:T(8,128)(2,1)S(1)}, u32[]{:S(2)}, u32[]{:S(2)}) collective-permute-start(bf16[2,2,48,192]{3,2,1,0:T(8,128)(2,1)} %bitcast.18), channel_id=1, source_target_pairs={{0,1},{1,2},{2,3},{3,4},{4,5},{5,6},{6,7},{7,8},{8,9},{9,10},{10,1... | collective-permute-start | bytes 221192 | tf_op jit(solution)/shard_map/ppermute | solution.py:39
  4.5 0.9 slice_bitcast_fusion
  5.4 1.3 %collective-permute-start.1 = (bf16[2,2,48,192]{3,2,1,0:T(8,128)(2,1)S(1)}, bf16[2,2,48,192]{3,2,1,0:T(8,128)(2,1)S(1)}, u32[]{:S(2)}, u32[]{:S(2)}) collective-permute-start(bf16[2,2,48,192]{3,2,1,0:T(8,128)(2,1)S(1)} %slice_bitcast_fusion), channel_id=1, source_target_pairs={{1,0},{2,1},{3,2},{4,3},{5,4},{6,5},{7,6},{8,7},{9,8},{10,9},{11,1... | collective-permute-start | bytes 221192 | tf_op jit(solution)/shard_map/ppermute | solution.py:39
  6.7 0.3 collective-permute-done.xprev
  7.0 4.9 %collective-permute-done.1.gnext = bf16[2,2,48,192]{3,2,1,0:T(8,128)(2,1)S(1)} collective-permute-done((bf16[2,2,48,192]{3,2,1,0:T(8,128)(2,1)S(1)}, bf16[2,2,48,192]{3,2,1,0:T(8,128)(2,1)S(1)}, u32[]{:S(2)}, u32[]{:S(2)}) %collective-permute-start.1) | collective-permute-done | bytes 73760 | tf_op jit(solution)/shard_map/ppermute | solution.py:39
  11.9 1.0 %band.1 = (bf16[10,2,48,192]{3,2,1,0:T(8,128)(2,1)S(1)}, bf16[4,48,192]{2,1,0:T(8,128)(2,1)S(1)}, bf16[4,48,192]{2,1,0:T(8,128)(2,1)S(1)}) custom-call(bf16[2,2,48,192]{3,2,1,0:T(8,128)(2,1)} %bitcast.19, bf16[4,2,48,192]{3,2,1,0:T(8,128)(2,1)} %bitcast.15, bf16[2,2,48,192]{3,2,1,0:T(8,128)(2,1)S(1)} %collective-permute-done.xprev, ...), custom_call_target="tpu_custom_call" | custom-call | tf_op jit(solution)/shard_map/band/pallas_call | solution.py:335
  12.9 1.9 %collective-permute-start.2 = (bf16[4,48,192]{2,1,0:T(8,128)(2,1)S(1)}, bf16[4,48,192]{2,1,0:T(8,128)(2,1)S(1)}, u32[]{:S(2)}, u32[]{:S(2)}) collective-permute-start(bf16[4,48,192]{2,1,0:T(8,128)(2,1)S(1)} %get-tuple-element.9), channel_id=1, source_target_pairs={{0,16},{16,32},{32,48},{48,64},{64,80},{80,96},{96,112},{1,17},{17... | collective-permute-start | bytes 221192 | tf_op jit(solution)/shard_map/ppermute | solution.py:39
  14.8 3.6 %collective-permute-start.3 = (bf16[4,48,192]{2,1,0:T(8,128)(2,1)S(1)}, bf16[4,48,192]{2,1,0:T(8,128)(2,1)S(1)}, u32[]{:S(2)}, u32[]{:S(2)}) collective-permute-start(bf16[4,48,192]{2,1,0:T(8,128)(2,1)S(1)} %get-tuple-element.10), channel_id=1, source_target_pairs={{16,0},{32,16},{48,32},{64,48},{80,64},{96,80},{112,96},{17,1},{33... | collective-permute-start | bytes 221192 | tf_op jit(solution)/shard_map/ppermute | solution.py:39
  19.1 0.0 collective-permute-done.2.above
  19.1 1.5 %collective-permute-done.3.below = bf16[4,48,192]{2,1,0:T(8,128)(2,1)S(1)} collective-permute-done((bf16[4,48,192]{2,1,0:T(8,128)(2,1)S(1)}, bf16[4,48,192]{2,1,0:T(8,128)(2,1)S(1)}, u32[]{:S(2)}, u32[]{:S(2)}) %collective-permute-start.3) | collective-permute-done | bytes 73760 | tf_op jit(solution)/shard_map/ppermute | solution.py:39
  20.7 3.8 %hidden_and_act.1 = bf16[8,408,128]{2,1,0:T(8,128)(2,1)} custom-call(s32[1]{0:T(128)S(6)} %copy.7.lengths, bf16[2,2,48,192]{3,2,1,0:T(8,128)(2,1)} %bitcast.20, bf16[4,2,48,192]{3,2,1,0:T(8,128)(2,1)} %bitcast.16, bf16[5184,192]{1,0:T(8,128)(2,1)} %bitcast.11, bf16[4,48,192]{2,1,0:T(8,128)(2,1)S(1)} %collective-permute-done.2.above, ...), custom_call_target="tpu_custom_call" | custom-call | tf_op jit(solution)/shard_map/hidden_and_act/pallas_call | solution.py:335
  24.5 5.8 %all-to-all-start = ((bf16[8,408,128]{2,1,0:T(8,128)(2,1)}), bf16[8,408,128]{2,1,0:T(8,128)(2,1)S(1)}, u32[]{:S(2)}, u32[]{:S(2)}) async-start(bf16[8,408,128]{2,1,0:T(8,128)(2,1)} %hidden_and_act.1), calls=%async_computation | async-start | bytes 1671168 | tf_op jit(solution)/shard_map/all_to_all | solution.py:394
  30.3 2.0 %collective-permute-start.4 = (bf16[10,2,48,192]{3,2,1,0:T(8,128)(2,1)S(1)}, bf16[10,2,48,192]{3,2,1,0:T(8,128)(2,1)S(1)}, u32[]{:S(2)}, u32[]{:S(2)}) collective-permute-start(bf16[10,2,48,192]{3,2,1,0:T(8,128)(2,1)S(1)} %get-tuple-element.11), channel_id=1, source_target_pairs={{0,16},{16,32},{32,48},{48,64},{64,80},{80,96},{96,112},{1,17},{17... | collective-permute-start | bytes 1105928 | tf_op jit(solution)/shard_map/ppermute | solution.py:39
  32.4 3.5 %collective-permute-start.5 = (bf16[10,2,48,192]{3,2,1,0:T(8,128)(2,1)S(1)}, bf16[10,2,48,192]{3,2,1,0:T(8,128)(2,1)S(1)}, u32[]{:S(2)}, u32[]{:S(2)}) collective-permute-start(bf16[10,2,48,192]{3,2,1,0:T(8,128)(2,1)S(1)} %get-tuple-element.11), channel_id=1, source_target_pairs={{16,0},{32,16},{48,32},{64,48},{80,64},{96,80},{112,96},{17,1},{33... | collective-permute-start | bytes 1105928 | tf_op jit(solution)/shard_map/ppermute | solution.py:39
  35.9 10.3 %collective-permute-done.4.above = bf16[10,2,48,192]{3,2,1,0:T(8,128)(2,1)S(1)} collective-permute-done((bf16[10,2,48,192]{3,2,1,0:T(8,128)(2,1)S(1)}, bf16[10,2,48,192]{3,2,1,0:T(8,128)(2,1)S(1)}, u32[]{:S(2)}, u32[]{:S(2)}) %collective-permute-start.4) | collective-permute-done | bytes 368672 | tf_op jit(solution)/shard_map/ppermute | solution.py:39
  46.2 0.0 collective-permute-done.5.below
  46.2 8.4 %hidden_grad.1.tall = bf16[2,4,48,192]{3,2,1,0:T(8,128)(2,1)S(1)} custom-call(s32[1]{0:T(128)S(6)} %copy.7.lengths, bf16[2,2,48,192]{3,2,1,0:T(8,128)(2,1)} %bitcast.21, bf16[4,2,48,192]{3,2,1,0:T(8,128)(2,1)} %bitcast.17, bf16[5184,192]{1,0:T(8,128)(2,1)} %bitcast.12, bf16[27,192,192]{2,1,0:T(8,128)(2,1)} %bitcast.14, ...), custom_call_target="tpu_custom_call" | custom-call | tf_op jit(solution)/shard_map/hidden_grad/pallas_call | solution.py:335
  54.6 0.0 all-to-all-done.got
  54.6 2.4 %kernel_grad_part.1 = bf16[64,16,128]{2,1,0:T(8,128)(2,1)} custom-call(bf16[8,408,128]{2,1,0:T(8,128)(2,1)S(1)} %all-to-all-done.got), custom_call_target="tpu_custom_call" | custom-call | tf_op jit(solution)/shard_map/kernel_grad_part/pallas_call | solution.py:335
  57.0 4.9 %all-to-all-start.1 = ((bf16[4,256,128]{2,1,0:T(8,128)(2,1)}), bf16[4,256,128]{2,1,0:T(8,128)(2,1)S(1)}, u32[]{:S(2)}, u32[]{:S(2)}) async-start(bf16[4,256,128]{2,1,0:T(8,128)(2,1)} %bitcast.6), calls=%async_computation.1 | async-start | bytes 524288 | tf_op jit(solution)/shard_map/all_to_all | solution.py:433
  61.9 1.3 %collective-permute-start.6 = (bf16[2,4,48,192]{3,2,1,0:T(8,128)(2,1)S(1)}, bf16[2,4,48,192]{3,2,1,0:T(8,128)(2,1)S(1)}, u32[]{:S(2)}, u32[]{:S(2)}) collective-permute-start(bf16[2,4,48,192]{3,2,1,0:T(8,128)(2,1)S(1)} %hidden_grad.1.tall), channel_id=1, source_target_pairs={{1,0},{2,1},{3,2},{4,3},{5,4},{6,5},{7,6},{8,7},{9,8},{10,9},{11,1... | collective-permute-start | bytes 442376 | tf_op jit(solution)/shard_map/ppermute | solution.py:39
  63.2 5.1 %all-to-all-done.1.got = bf16[4,256,128]{2,1,0:T(8,128)(2,1)S(1)} async-done(((bf16[4,256,128]{2,1,0:T(8,128)(2,1)}), bf16[4,256,128]{2,1,0:T(8,128)(2,1)S(1)}, u32[]{:S(2)}, u32[]{:S(2)}) %all-to-all-start.1) | async-done | bytes 262176 | tf_op jit(solution)/shard_map/all_to_all | solution.py:433
  68.3 0.7 clip_sum.1
  69.0 2.3 %collective-permute-done.6.after = bf16[2,4,48,192]{3,2,1,0:T(8,128)(2,1)S(1)} collective-permute-done((bf16[2,4,48,192]{3,2,1,0:T(8,128)(2,1)S(1)}, bf16[2,4,48,192]{3,2,1,0:T(8,128)(2,1)S(1)}, u32[]{:S(2)}, u32[]{:S(2)}) %collective-permute-start.6) | collective-permute-done | bytes 147488 | tf_op jit(solution)/shard_map/ppermute | solution.py:39
  71.2 16.1 %all-to-all-start.2 = ((bf16[16,16,128]{2,1,0:T(8,128)(2,1)}), bf16[16,16,128]{2,1,0:T(8,128)(2,1)S(1)}, u32[]{:S(2)}, u32[]{:S(2)}) async-start(bf16[16,16,128]{2,1,0:T(8,128)(2,1)} %bitcast.8), calls=%async_computation.2 | async-start | bytes 131072 | tf_op jit(solution)/shard_map/all_to_all | solution.py:443
  87.3 3.3 %input_grad.1 = f32[2,2,48,192]{3,2,1,0:T(8,128)} custom-call(bf16[27,192,192]{2,1,0:T(8,128)(2,1)} %bitcast.13, bf16[2,4,48,192]{3,2,1,0:T(8,128)(2,1)S(1)} %hidden_grad.1.tall, bf16[2,4,48,192]{3,2,1,0:T(8,128)(2,1)S(1)} %collective-permute-done.6.after), custom_call_target="tpu_custom_call" | custom-call | tf_op jit(solution)/shard_map/input_grad/pallas_call | solution.py:335
  90.6 9.4 %all-to-all-done.2.got = bf16[16,16,128]{2,1,0:T(8,128)(2,1)S(1)} async-done(((bf16[16,16,128]{2,1,0:T(8,128)(2,1)}), bf16[16,16,128]{2,1,0:T(8,128)(2,1)S(1)}, u32[]{:S(2)}, u32[]{:S(2)}) %all-to-all-start.2) | async-done | bytes 65568 | tf_op jit(solution)/shard_map/all_to_all | solution.py:443
  100.1 0.7 kernel_grad_sum.1
Async XLA Ops:
  0.6 6.3 %collective-permute-start = (bf16[2,2,48,192]{3,2,1,0:T(8,128)(2,1)}, bf16[2,2,48,192]{3,2,1,0:T(8,128)(2,1)S(1)}, u32[]{:S(2)}, u32[]{:S(2)}) collective-permute-start(bf16[2,2,48,192]{3,2,1,0:T(8,128)(2,1)} %bitcast.18), channel_id=1, source_target_pairs={{0,1},{1,2},{2,3},{3,4},{4,5},{5,6},{6,7},{7,8},{8,9},{9,10},{10,1... | collective-permute-start | bytes 221192 | tf_op jit(solution)/shard_map/ppermute | solution.py:39
  5.4 6.5 %collective-permute-start.1 = (bf16[2,2,48,192]{3,2,1,0:T(8,128)(2,1)S(1)}, bf16[2,2,48,192]{3,2,1,0:T(8,128)(2,1)S(1)}, u32[]{:S(2)}, u32[]{:S(2)}) collective-permute-start(bf16[2,2,48,192]{3,2,1,0:T(8,128)(2,1)S(1)} %slice_bitcast_fusion), channel_id=1, source_target_pairs={{1,0},{2,1},{3,2},{4,3},{5,4},{6,5},{7,6},{8,7},{9,8},{10,9},{11,1... | collective-permute-start | bytes 221192 | tf_op jit(solution)/shard_map/ppermute | solution.py:39
  12.9 6.2 %collective-permute-start.2 = (bf16[4,48,192]{2,1,0:T(8,128)(2,1)S(1)}, bf16[4,48,192]{2,1,0:T(8,128)(2,1)S(1)}, u32[]{:S(2)}, u32[]{:S(2)}) collective-permute-start(bf16[4,48,192]{2,1,0:T(8,128)(2,1)S(1)} %get-tuple-element.9), channel_id=1, source_target_pairs={{0,16},{16,32},{32,48},{48,64},{64,80},{80,96},{96,112},{1,17},{17... | collective-permute-start | bytes 221192 | tf_op jit(solution)/shard_map/ppermute | solution.py:39
  14.8 5.8 %collective-permute-start.3 = (bf16[4,48,192]{2,1,0:T(8,128)(2,1)S(1)}, bf16[4,48,192]{2,1,0:T(8,128)(2,1)S(1)}, u32[]{:S(2)}, u32[]{:S(2)}) collective-permute-start(bf16[4,48,192]{2,1,0:T(8,128)(2,1)S(1)} %get-tuple-element.10), channel_id=1, source_target_pairs={{16,0},{32,16},{48,32},{64,48},{80,64},{96,80},{112,96},{17,1},{33... | collective-permute-start | bytes 221192 | tf_op jit(solution)/shard_map/ppermute | solution.py:39
  24.5 30.1 %all-to-all-start = ((bf16[8,408,128]{2,1,0:T(8,128)(2,1)}), bf16[8,408,128]{2,1,0:T(8,128)(2,1)S(1)}, u32[]{:S(2)}, u32[]{:S(2)}) async-start(bf16[8,408,128]{2,1,0:T(8,128)(2,1)} %hidden_and_act.1), calls=%async_computation | async-start | bytes 1671168 | tf_op jit(solution)/shard_map/all_to_all | solution.py:394
  30.3 15.8 %collective-permute-start.4 = (bf16[10,2,48,192]{3,2,1,0:T(8,128)(2,1)S(1)}, bf16[10,2,48,192]{3,2,1,0:T(8,128)(2,1)S(1)}, u32[]{:S(2)}, u32[]{:S(2)}) collective-permute-start(bf16[10,2,48,192]{3,2,1,0:T(8,128)(2,1)S(1)} %get-tuple-element.11), channel_id=1, source_target_pairs={{0,16},{16,32},{32,48},{48,64},{64,80},{80,96},{96,112},{1,17},{17... | collective-permute-start | bytes 1105928 | tf_op jit(solution)/shard_map/ppermute | solution.py:39
  32.4 13.8 %collective-permute-start.5 = (bf16[10,2,48,192]{3,2,1,0:T(8,128)(2,1)S(1)}, bf16[10,2,48,192]{3,2,1,0:T(8,128)(2,1)S(1)}, u32[]{:S(2)}, u32[]{:S(2)}) collective-permute-start(bf16[10,2,48,192]{3,2,1,0:T(8,128)(2,1)S(1)} %get-tuple-element.11), channel_id=1, source_target_pairs={{16,0},{32,16},{48,32},{64,48},{80,64},{96,80},{112,96},{17,1},{33... | collective-permute-start | bytes 1105928 | tf_op jit(solution)/shard_map/ppermute | solution.py:39
  57.0 11.3 %all-to-all-start.1 = ((bf16[4,256,128]{2,1,0:T(8,128)(2,1)}), bf16[4,256,128]{2,1,0:T(8,128)(2,1)S(1)}, u32[]{:S(2)}, u32[]{:S(2)}) async-start(bf16[4,256,128]{2,1,0:T(8,128)(2,1)} %bitcast.6), calls=%async_computation.1 | async-start | bytes 524288 | tf_op jit(solution)/shard_map/all_to_all | solution.py:433
  61.9 9.3 %collective-permute-start.6 = (bf16[2,4,48,192]{3,2,1,0:T(8,128)(2,1)S(1)}, bf16[2,4,48,192]{3,2,1,0:T(8,128)(2,1)S(1)}, u32[]{:S(2)}, u32[]{:S(2)}) collective-permute-start(bf16[2,4,48,192]{3,2,1,0:T(8,128)(2,1)S(1)} %hidden_grad.1.tall), channel_id=1, source_target_pairs={{1,0},{2,1},{3,2},{4,3},{5,4},{6,5},{7,6},{8,7},{9,8},{10,9},{11,1... | collective-permute-start | bytes 442376 | tf_op jit(solution)/shard_map/ppermute | solution.py:39
  71.2 28.8 %all-to-all-start.2 = ((bf16[16,16,128]{2,1,0:T(8,128)(2,1)}), bf16[16,16,128]{2,1,0:T(8,128)(2,1)S(1)}, u32[]{:S(2)}, u32[]{:S(2)}) async-start(bf16[16,16,128]{2,1,0:T(8,128)(2,1)} %bitcast.8), calls=%async_computation.2 | async-start | bytes 131072 | tf_op jit(solution)/shard_map/all_to_all | solution.py:443

commit v6 on v5

--- a/solution.py
+++ b/solution.py
@@ -12,7 +12,6 @@
 F32 = jnp.float32
 EDGE = 16
 PITCH = 64
-WIDE = 72
 MIB = 1024 * 1024
 
 
@@ -39,31 +38,53 @@
     return lax.ppermute(value, axes if len(axes) > 1 else axes[0], route(sizes, steps))
 
 
-def spread(ref, index, cols, value):
-    ref[index, EDGE : EDGE + cols, :] = value.astype(F32)
-
-
-def clear_edges(ref, cols):
-    blocks, width, chan = ref.shape
-    ref[:, 0:EDGE, :] = jnp.zeros((blocks, EDGE, chan), F32)
-    ref[:, EDGE + cols :, :] = jnp.zeros((blocks, width - EDGE - cols, chan), F32)
-
-
 def transposed_dot(a, b):
     return lax.dot_general(a, b, (((1,), (1,)), ((), ())), preferred_element_type=F32)
 
 
-def band_kernel(x, g, xprev, gnext, band, top, bot, sem):
-    nx, ng = x.shape[0], g.shape[0]
-    pairs = [(x, band.at[0:nx]), (g, band.at[2 * nx : 2 * nx + ng])]
-    pairs += [(x.at[:, row], out.at[0:nx]) for row, out in ((0, top), (1, bot))]
+def plain_dot(a, b):
+    return jnp.dot(a, b, preferred_element_type=F32)
+
+
+def column_shift(value, by, cols):
+    cells, chan = value.shape
+    moved = pltpu.roll(value, by % cells, 0).reshape(cells // cols, cols, chan)
+    column = lax.broadcasted_iota(jnp.int32, moved.shape, 1)
+    moved = jnp.where(column == (0 if by > 0 else cols - 1), 0.0, moved)
+    return moved.reshape(cells, chan)
+
+
+def conv(patch, weight, dot, first_shift, cols):
+    total = None
+    for k in (1, 0, 2):
+        part = None
+        for i in range(3):
+            for j in range(3):
+                term = dot(patch(i, j), weight[i * 9 + j * 3 + k])
+                part = term if part is None else part + term
+        if k != 1:
+            part = column_shift(part, first_shift if k == 0 else -first_shift, cols)
+        total = part if total is None else total + part
+    return total
+
+
+def blocks_of(ref, starts, count):
+    value = jnp.concatenate([ref[at : at + count] for at in starts], axis=0)
+    return value.reshape(-1, value.shape[-1])
+
+
+def start_copies(pairs, sem):
     copies = [pltpu.make_async_copy(a, b, sem.at[n]) for n, (a, b) in enumerate(pairs)]
     for copy in copies:
         copy.start()
+    return copies
+
+
+def band_kernel(x, g, xprev, gnext, band, sem):
+    nx, ng = x.shape[0], g.shape[0]
+    copies = start_copies(((x, band.at[0:nx]), (g, band.at[2 * nx : 2 * nx + ng])), sem)
     band[nx : 2 * nx] = xprev[...]
     band[2 * nx + ng :] = gnext[...]
-    top[nx:] = xprev[:, 0]
-    bot[nx:] = xprev[:, 1]
     for copy in copies:
         copy.wait()
 
@@ -72,103 +93,72 @@
     return (width, span) == (24, 81)
 
 
+def masked_frames(values, limit):
+    return [jnp.where(f < limit, v.astype(F32), 0.0) for f, v in enumerate(values)]
+
+
 def silu_kernel(
-    lengths, x_far, g_far, w_far, above, below, xprev, gnext, pay, xs, ps, xk, x, g, w, sem
+    lengths, x_far, g_far, w_far, above, below, xprev, gnext, pay, xe, ps, g, w, sem
 ):
-    pairs = ((x_far, x), (w_far, w), (g_far, g))
-    copies = [pltpu.make_async_copy(a, b, sem.at[n]) for n, (a, b) in enumerate(pairs)]
-    for copy in copies:
-        copy.start()
-    frames, rows, cols, chan = x.shape
+    frames, rows, cols, chan = xprev.shape
     cells = frames * rows * cols
     peers = pay.shape[0]
     width = chan // peers
-    clear_edges(xs, cols)
+    pairs = [(g_far, g), (w_far, w)]
+    pairs += [(x_far.at[f], xe.at[(2 + f) * 4 + 1 : (2 + f) * 4 + 3]) for f in range(2)]
+    copies = start_copies(pairs, sem)
     for f in range(2):
-        for r in range(2):
-            spread(xs, f * 4 + 1 + r, cols, xprev[f, r])
-        spread(xs, f * 4, cols, above[2 + f])
-        spread(xs, f * 4 + 3, cols, below[2 + f])
-        spread(xs, (2 + f) * 4, cols, above[f])
-        spread(xs, (2 + f) * 4 + 3, cols, below[f])
-    copies[0].wait()
-    for f in range(2):
-        for r in range(2):
-            spread(xs, (2 + f) * 4 + 1 + r, cols, x[f, r])
-    for k in range(3):
-        piece = xs[:, EDGE - 1 + k : EDGE - 1 + k + cols, :].astype(BF)
-        xk[:, :, k * chan : (k + 1) * chan] = piece
-    copies[2].wait()
+        xe[f * 4] = above[2 + f, 1]
+        xe[f * 4 + 1 : f * 4 + 3] = xprev[f]
+        xe[f * 4 + 3] = below[2 + f, 0]
+        xe[(2 + f) * 4] = above[f, 1]
+        xe[(2 + f) * 4 + 3] = below[f, 0]
     limit = 2 * lengths[0] - 2 * frames * lax.axis_index("tm")
     ps[:, 0:EDGE, :] = jnp.zeros((10, EDGE, chan), F32)
+    copies[0].wait()
     for r in range(2):
         field = masked_frames([g[f, r] for f in range(4)] + [gnext[f, r] for f in range(2)], limit)
         for a in range(5):
             ps[a * 2 + r, EDGE : EDGE + cols, :] = field[a] + field[a + 1]
     turned = [
-        jnp.transpose(ps[2 * a : 2 * a + 2].reshape(2 * PITCH, chan)).astype(BF) for a in range(5)
+        jnp.transpose(ps[2 * a : 2 * a + 2].reshape(2 * PITCH, chan)) for a in range(5)
     ]
-    copies[1].wait()
-    hidden = jnp.zeros((cells, chan), F32)
-    for i in range(3):
-        for j in range(3):
-            part = [xk[(f + 2 - i) * 4 + j : (f + 2 - i) * 4 + j + 2] for f in range(2)]
-            patch = jnp.concatenate(part, axis=0).reshape(cells, 3 * chan)
-            rows_of = slice((i * 3 + j) * 3 * chan, (i * 3 + j + 1) * 3 * chan)
-            hidden += jnp.dot(patch, w[rows_of, :], preferred_element_type=F32)
-    act = (hidden / (1.0 + jnp.exp(-hidden))).astype(BF)
+    for p in range(peers):
+        mine = jnp.concatenate([v[p * width : (p + 1) * width] for v in turned], axis=0)
+        pay[p, cells + cells // 2 :, :] = mine.astype(BF)
+    for copy in copies[1:]:
+        copy.wait()
+
+    def patch(i, j):
+        return blocks_of(xe, [(f + 2 - i) * 4 + j for f in range(2)], 2)
+
+    hidden = conv(patch, w, plain_dot, 1, cols)
+    act = hidden / (1.0 + jnp.exp(-hidden))
     half = cells // 2
-    wide = act.astype(F32)
-    low = wide[:, :128].astype(BF)
-    high = jnp.concatenate([wide[:half, 128:], wide[half:, 128:]], axis=1).astype(BF)
+    low = act[:, :128].astype(BF)
+    high = jnp.concatenate([act[:half, 128:], act[half:, 128:]], axis=1).astype(BF)
     for p in range(peers):
         pay[p, 0:cells, :] = low
         pay[p, cells : cells + half, :] = high
-        mine = jnp.concatenate([v[p * width : (p + 1) * width] for v in turned], axis=0)
-        pay[p, cells + half :, :] = mine
-
-
-def masked_frames(values, limit):
-    return [jnp.where(f < limit, v.astype(F32), 0.0) for f, v in enumerate(values)]
 
 
 def hidden_grad_kernel(
     lengths, x_far, g_far, w1_far, w2_far, above, below, xprev, gnext,
     tall,
-    xs, ps, xk, pk, x, g, w1, w2, sem,
+    xe, pe, g, w1, w2, sem,
 ):
-    pairs = ((x_far, x), (w1_far, w1), (g_far, g), (w2_far, w2))
-    copies = [pltpu.make_async_copy(a, b, sem.at[n]) for n, (a, b) in enumerate(pairs)]
-    for copy in copies:
-        copy.start()
-    frames, rows, cols, chan = x.shape
-    reach = 2 * frames * rows * cols
-    clear_edges(xs, cols)
-    clear_edges(ps, cols)
+    frames, rows, cols, chan = xprev.shape
+    pairs = [(g_far, g), (w1_far, w1), (w2_far, w2)]
+    pairs += [(x_far.at[f], xe.at[(2 + f) * 6 + 2 : (2 + f) * 6 + 4]) for f in range(2)]
+    copies = start_copies(pairs, sem)
+    for f in range(2):
+        xe[f * 6 : f * 6 + 2] = above[2 + f]
+        xe[f * 6 + 2 : f * 6 + 4] = xprev[f]
+        xe[f * 6 + 4 : f * 6 + 6] = below[2 + f]
+        xe[(2 + f) * 6 : (2 + f) * 6 + 2] = above[f]
+        xe[(2 + f) * 6 + 4 : (2 + f) * 6 + 6] = below[f]
+    limit = 2 * lengths[0] - 2 * frames * lax.axis_index("tm")
     copies[0].wait()
-    for f in range(2):
-        for r in range(2):
-            spread(xs, f * 6 + r, cols, above[2 + f, r])
-            spread(xs, f * 6 + 2 + r, cols, xprev[f, r])
-            spread(xs, f * 6 + 4 + r, cols, below[2 + f, r])
-            spread(xs, (2 + f) * 6 + r, cols, above[f, r])
-            spread(xs, (2 + f) * 6 + 2 + r, cols, x[f, r])
-            spread(xs, (2 + f) * 6 + 4 + r, cols, below[f, r])
-    for k in range(3):
-        piece = xs[:, EDGE - 1 + k : EDGE - 1 + k + cols, :].astype(BF)
-        xk[:, :, k * chan : (k + 1) * chan] = piece
-    copies[1].wait()
-    hidden = jnp.zeros((reach, chan), F32)
-    for i in range(3):
-        for j in range(3):
-            part = [xk[(f + 2 - i) * 6 + j : (f + 2 - i) * 6 + j + 4] for f in range(2)]
-            patch = jnp.concatenate(part, axis=0).reshape(reach, 3 * chan)
-            rows_of = slice((i * 3 + j) * 3 * chan, (i * 3 + j + 1) * 3 * chan)
-            hidden += jnp.dot(patch, w1[rows_of, :], preferred_element_type=F32)
-    sigma = 1.0 / (1.0 + jnp.exp(-hidden))
-    slope = sigma * (1.0 + hidden * (1.0 - sigma))
-    limit = 2 * lengths[0] - 2 * frames * lax.axis_index("tm")
-    copies[2].wait()
     for r in range(6):
         if r < 2:
             values = [above[4 + f, r] for f in range(6)]
@@ -178,18 +168,21 @@
             values = [g[f, r - 2] for f in range(4)] + [gnext[f, r - 2] for f in range(2)]
         field = masked_frames(values, limit)
         for a in range(5):
-            spread(ps, a * 6 + r, cols, field[a] + field[a + 1])
-    for k in range(3):
-        pk[k] = ps[:, EDGE + 1 - k : EDGE + 1 - k + cols, :].astype(BF)
-    copies[3].wait()
-    pair = jnp.zeros((reach, chan), F32)
-    for i in range(3):
-        for j in range(3):
-            for k in range(3):
-                part = [pk[k, (2 * t + i) * 6 + 2 - j : (2 * t + i) * 6 + 6 - j] for t in range(2)]
-                patch = jnp.concatenate(part, axis=0).reshape(reach, chan)
-                pair += transposed_dot(patch, w2[i * 9 + j * 3 + k])
-    grad = (pair * slope).reshape(frames, rows + 2, cols, chan)
+            pe[a * 6 + r] = (field[a] + field[a + 1]).astype(BF)
+    for copy in copies[1:]:
+        copy.wait()
+
+    def patch(i, j):
+        return blocks_of(xe, [(f + 2 - i) * 6 + j for f in range(2)], 4)
+
+    def pair_patch(i, j):
+        return blocks_of(pe, [(2 * t + i) * 6 + 2 - j for t in range(2)], 4)
+
+    hidden = conv(patch, w1, plain_dot, 1, cols)
+    pair = conv(pair_patch, w2, transposed_dot, -1, cols)
+    sigma = 1.0 / (1.0 + jnp.exp(-hidden))
+    grad = pair * sigma * (1.0 + hidden * (1.0 - sigma))
+    grad = grad.reshape(frames, rows + 2, cols, chan)
     band = lax.axis_index("row")
     none = jnp.zeros((frames, cols, chan), F32)
     tall[:, 0] = jnp.where(band > 0, grad[:, 0], none).astype(BF)
@@ -302,27 +295,17 @@
         out[...] = total[:, :span]
 
 
-def grad_kernel(w1_far, tall, after, grad, hs, hk, w1, sem):
-    copy = pltpu.make_async_copy(w1_far, w1, sem.at[0])
-    copy.start()
+def grad_kernel(w1_far, tall, after, grad, w1, sem):
+    copies = start_copies([(w1_far, w1)], sem)
     frames, rows, cols, chan = grad.shape
-    cells = frames * rows * cols
-    clear_edges(hs, cols)
-    for f in range(2):
-        for r in range(4):
-            spread(hs, f * 4 + r, cols, tall[f, r])
-            spread(hs, (2 + f) * 4 + r, cols, after[f, r])
-    for k in range(3):
-        hk[k] = hs[:, EDGE + 1 - k : EDGE + 1 - k + cols, :].astype(BF)
-    copy.wait()
-    acc = jnp.zeros((cells, chan), F32)
-    for i in range(3):
-        for j in range(3):
-            for k in range(3):
-                part = [hk[k, (f + i) * 4 + 2 - j : (f + i) * 4 + 4 - j] for f in range(2)]
-                patch = jnp.concatenate(part, axis=0).reshape(cells, chan)
-                acc += transposed_dot(patch, w1[i * 9 + j * 3 + k])
-    grad[...] = acc.reshape(frames, rows, cols, chan)
+    fields = [tall[0], tall[1], after[0], after[1]]
+
+    def patch(i, j):
+        value = jnp.concatenate([fields[f + i][2 - j : 4 - j] for f in range(2)], axis=0)
+        return value.reshape(-1, chan)
+
+    copies[0].wait()
+    grad[...] = conv(patch, w1, transposed_dot, -1, cols).reshape(grad.shape)
 
 
 def call(body, name, limit, shapes, args, scratch, far=(), scalars=(), sems=0):
@@ -357,39 +340,33 @@
 
     xprev = move(x, ("tm",), (1,))
     gnext = move(g[:frames], ("tm",), (-1,))
-    edge = (2 * frames, cols, chan)
-    band, top, bot = call(
+    (band,) = call(
         band_kernel,
         "band",
         4,
-        [((5 * frames, rows, cols, chan), BF), (edge, BF), (edge, BF)],
+        [((5 * frames, rows, cols, chan), BF)],
         (xprev, gnext),
         [],
         far=(x, g),
-        sems=4,
-    )
-    above_edge = move(bot, ("row",), (1,))
-    below_edge = move(top, ("row",), (-1,))
+        sems=2,
+    )
     above = move(band, ("row",), (1,))
     below = move(band, ("row",), (-1,))
-    w1_flat = weight_one.reshape(27 * chan, chan)
     (pay,) = call(
         silu_kernel,
         "hidden_and_act",
         16,
         [((peers, cells + cells // 2 + 5 * width, 128), BF)],
-        (above_edge, below_edge, xprev, gnext),
+        (above, below, xprev, gnext),
         [
-            ((16, WIDE, chan), F32),
+            ((16, cols, chan), BF),
             ((10, PITCH, chan), F32),
-            ((16, cols, 3 * chan), BF),
-            (x.shape, BF),
             (g.shape, BF),
-            (w1_flat.shape, BF),
+            (w1.shape, BF),
         ],
-        far=(x, g, w1_flat),
+        far=(x, g, w1),
         scalars=(lengths,),
-        sems=3,
+        sems=4,
     )
     got = lax.all_to_all(pay, "row", 0, 0)
     (tall,) = call(
@@ -399,18 +376,15 @@
         [((frames, rows + 2, cols, chan), BF)],
         (above, below, xprev, gnext),
         [
-            ((24, WIDE, chan), F32),
-            ((30, WIDE, chan), F32),
-            ((24, cols, 3 * chan), BF),
-            ((3, 30, cols, chan), BF),
-            (x.shape, BF),
+            ((24, cols, chan), BF),
+            ((30, cols, chan), BF),
             (g.shape, BF),
-            (w1_flat.shape, BF),
+            (w1.shape, BF),
             (w2.shape, BF),
         ],
-        far=(x, g, w1_flat, w2),
+        far=(x, g, w1, w2),
         scalars=(lengths,),
-        sems=4,
+        sems=5,
     )
     got, tall = lax.optimization_barrier((got, tall))
     after = move(tall, ("tm",), (-1,))
@@ -456,7 +430,7 @@
         16,
         [((frames, rows, cols, chan), F32)],
         (tall, after),
-        [((16, WIDE, chan), F32), ((3, 16, cols, chan), BF), (w1.shape, BF)],
+        [(w1.shape, BF)],
         far=(w1,),
         sems=1,
     )

time: 101 us -> 90.8 us (0.90)
  the two profiles are of different devices: /device:TPU:10 before, /device:TPU:8 now
where the time goes in v6:
time: 90.8 us; the launch traced here: 90.3 us
  starting transfers between devices  43 us (47%)
  waiting for transfers between devices  27.5 us (30%)
  Pallas kernels  17.5 us (19%)
  between operations  1.37 us (2%)
    pallas_call x7, Pallas kernels, call(): pl.pallas_call(body, name=name, out_shape=outs, in_specs=[pl.BlockSpec(me...  17.5 us
    all_to_all x1, starting transfers between devices, local(): by_step = lax.all_to_all(summed.reshape((steps,) + shape), 'tm', 0, 0)  14.4 us
    ppermute x5, starting transfers between devices, move(): lax.ppermute(value, axes if len(axes) > 1 else axes[0], route(sizes, steps))  11.5 us
    all_to_all x1, starting transfers between devices, local(): got = lax.all_to_all(pay, 'row', 0, 0)  10.6 us
    all_to_all x1, waiting for transfers between devices, local(): by_step = lax.all_to_all(summed.reshape((steps,) + shape), 'tm', 0, 0)  9.52 us
    all_to_all x1, waiting for transfers between devices, local(): got = lax.all_to_all(pay, 'row', 0, 0)  8.04 us
    all_to_all x1, starting transfers between devices, local(): lax.all_to_all(part.reshape((clips, steps * shape[0], shape[1])), 'clip',...  6.56 us
    ppermute x5, waiting for transfers between devices, move(): lax.ppermute(value, axes if len(axes) > 1 else axes[0], route(sizes, steps))  5.95 us
  transfers between devices with their start and end apart: 8, of which 7 were waited for; matrix products, arithmetic and copies ran while one was open for 0% of the time, Pallas kernels for 11%

profile of v6, /device:TPU:8, one launch (start us, length us, event | category | flops | bytes accessed | tf_op | source)
XLA Modules:
  0.0 90.3 jit_solution(10640273742640671608)
XLA Ops:
  0.6 0.9 slice_bitcast_fusion
  1.5 1.3 %collective-permute-start.1 = (bf16[2,2,48,192]{3,2,1,0:T(8,128)(2,1)S(1)}, bf16[2,2,48,192]{3,2,1,0:T(8,128)(2,1)S(1)}, u32[]{:S(2)}, u32[]{:S(2)}) collective-permute-start(bf16[2,2,48,192]{3,2,1,0:T(8,128)(2,1)S(1)} %slice_bitcast_fusion), channel_id=1, source_target_pairs={{1,0},{2,1},{3,2},{4,3},{5,4},{6,5},{7,6},{8,7},{9,8},{10,9},{11,1... | collective-permute-start | bytes 221192 | tf_op jit(solution)/shard_map/ppermute | solution.py:38
  2.8 4.6 %collective-permute-start = (bf16[2,2,48,192]{3,2,1,0:T(8,128)(2,1)}, bf16[2,2,48,192]{3,2,1,0:T(8,128)(2,1)S(1)}, u32[]{:S(2)}, u32[]{:S(2)}) collective-permute-start(bf16[2,2,48,192]{3,2,1,0:T(8,128)(2,1)} %bitcast.17), channel_id=1, source_target_pairs={{0,1},{1,2},{2,3},{3,4},{4,5},{5,6},{6,7},{7,8},{8,9},{9,10},{10,1... | collective-permute-start | bytes 221192 | tf_op jit(solution)/shard_map/ppermute | solution.py:38
  7.4 0.8 collective-permute-done.1.gnext
  8.1 1.8 %collective-permute-done.xprev = bf16[2,2,48,192]{3,2,1,0:T(8,128)(2,1)S(1)} collective-permute-done((bf16[2,2,48,192]{3,2,1,0:T(8,128)(2,1)}, bf16[2,2,48,192]{3,2,1,0:T(8,128)(2,1)S(1)}, u32[]{:S(2)}, u32[]{:S(2)}) %collective-permute-start) | collective-permute-done | bytes 73760 | tf_op jit(solution)/shard_map/ppermute | solution.py:38
  9.9 1.0 %band.1 = bf16[10,2,48,192]{3,2,1,0:T(8,128)(2,1)S(1)} custom-call(bf16[2,2,48,192]{3,2,1,0:T(8,128)(2,1)} %bitcast.18, bf16[4,2,48,192]{3,2,1,0:T(8,128)(2,1)} %bitcast.14, bf16[2,2,48,192]{3,2,1,0:T(8,128)(2,1)S(1)} %collective-permute-done.xprev, bf16[2,2,48,192]{3,2,1,0:T(8,128)(2,1)S(1)} %collective-permute-done.1.gnext), custom_call_target="tpu_custom_call" | custom-call | tf_op jit(solution)/shard_map/band/pallas_call | solution.py:318
  10.9 1.3 %collective-permute-start.3 = (bf16[10,2,48,192]{3,2,1,0:T(8,128)(2,1)S(1)}, bf16[10,2,48,192]{3,2,1,0:T(8,128)(2,1)S(1)}, u32[]{:S(2)}, u32[]{:S(2)}) collective-permute-start(bf16[10,2,48,192]{3,2,1,0:T(8,128)(2,1)S(1)} %band.1), channel_id=1, source_target_pairs={{16,0},{32,16},{48,32},{64,48},{80,64},{96,80},{112,96},{17,1},{33... | collective-permute-start | bytes 1105928 | tf_op jit(solution)/shard_map/ppermute | solution.py:38
  12.2 3.1 %collective-permute-start.2 = (bf16[10,2,48,192]{3,2,1,0:T(8,128)(2,1)S(1)}, bf16[10,2,48,192]{3,2,1,0:T(8,128)(2,1)S(1)}, u32[]{:S(2)}, u32[]{:S(2)}) collective-permute-start(bf16[10,2,48,192]{3,2,1,0:T(8,128)(2,1)S(1)} %band.1), channel_id=1, source_target_pairs={{0,16},{16,32},{32,48},{48,64},{64,80},{80,96},{96,112},{1,17},{17... | collective-permute-start | bytes 1105928 | tf_op jit(solution)/shard_map/ppermute | solution.py:38
  15.9 0.0 collective-permute-done.3.below
  15.9 0.8 collective-permute-done.2.above
  16.7 3.8 %hidden_and_act.1 = bf16[8,408,128]{2,1,0:T(8,128)(2,1)} custom-call(s32[1]{0:T(128)S(6)} %copy.7.lengths, bf16[2,2,48,192]{3,2,1,0:T(8,128)(2,1)} %bitcast.19, bf16[4,2,48,192]{3,2,1,0:T(8,128)(2,1)} %bitcast.15, bf16[27,192,192]{2,1,0:T(8,128)(2,1)} %bitcast.10, bf16[10,2,48,192]{3,2,1,0:T(8,128)(2,1)S(1)} %collective-permute-done.2.above, ...), custom_call_target="tpu_custom_call" | custom-call | tf_op jit(solution)/shard_map/hidden_and_act/pallas_call | solution.py:318
  20.5 10.6 %all-to-all-start = ((bf16[8,408,128]{2,1,0:T(8,128)(2,1)}), bf16[8,408,128]{2,1,0:T(8,128)(2,1)S(1)}, u32[]{:S(2)}, u32[]{:S(2)}) async-start(bf16[8,408,128]{2,1,0:T(8,128)(2,1)} %hidden_and_act.1), calls=%async_computation | async-start | bytes 1671168 | tf_op jit(solution)/shard_map/all_to_all | solution.py:371
  31.1 5.6 %hidden_grad.1.tall = bf16[2,4,48,192]{3,2,1,0:T(8,128)(2,1)S(1)} custom-call(s32[1]{0:T(128)S(6)} %copy.7.lengths, bf16[2,2,48,192]{3,2,1,0:T(8,128)(2,1)} %bitcast.20, bf16[4,2,48,192]{3,2,1,0:T(8,128)(2,1)} %bitcast.16, bf16[27,192,192]{2,1,0:T(8,128)(2,1)} %bitcast.11, bf16[27,192,192]{2,1,0:T(8,128)(2,1)} %bitcast.13, ...), custom_call_target="tpu_custom_call" | custom-call | tf_op jit(solution)/shard_map/hidden_grad/pallas_call | solution.py:318
  36.7 8.0 %all-to-all-done.got = bf16[8,408,128]{2,1,0:T(8,128)(2,1)S(1)} async-done(((bf16[8,408,128]{2,1,0:T(8,128)(2,1)}), bf16[8,408,128]{2,1,0:T(8,128)(2,1)S(1)}, u32[]{:S(2)}, u32[]{:S(2)}) %all-to-all-start) | async-done | bytes 835616 | tf_op jit(solution)/shard_map/all_to_all | solution.py:371
  44.8 2.4 %kernel_grad_part.1 = bf16[64,16,128]{2,1,0:T(8,128)(2,1)} custom-call(bf16[8,408,128]{2,1,0:T(8,128)(2,1)S(1)} %all-to-all-done.got), custom_call_target="tpu_custom_call" | custom-call | tf_op jit(solution)/shard_map/kernel_grad_part/pallas_call | solution.py:318
  47.2 6.6 %all-to-all-start.1 = ((bf16[4,256,128]{2,1,0:T(8,128)(2,1)}), bf16[4,256,128]{2,1,0:T(8,128)(2,1)S(1)}, u32[]{:S(2)}, u32[]{:S(2)}) async-start(bf16[4,256,128]{2,1,0:T(8,128)(2,1)} %bitcast.5), calls=%async_computation.1 | async-start | bytes 524288 | tf_op jit(solution)/shard_map/all_to_all | solution.py:407
  53.8 1.3 %collective-permute-start.4 = (bf16[2,4,48,192]{3,2,1,0:T(8,128)(2,1)S(1)}, bf16[2,4,48,192]{3,2,1,0:T(8,128)(2,1)S(1)}, u32[]{:S(2)}, u32[]{:S(2)}) collective-permute-start(bf16[2,4,48,192]{3,2,1,0:T(8,128)(2,1)S(1)} %hidden_grad.1.tall), channel_id=1, source_target_pairs={{1,0},{2,1},{3,2},{4,3},{5,4},{6,5},{7,6},{8,7},{9,8},{10,9},{11,1... | collective-permute-start | bytes 442376 | tf_op jit(solution)/shard_map/ppermute | solution.py:38
  55.0 4.0 %all-to-all-done.1.got = bf16[4,256,128]{2,1,0:T(8,128)(2,1)S(1)} async-done(((bf16[4,256,128]{2,1,0:T(8,128)(2,1)}), bf16[4,256,128]{2,1,0:T(8,128)(2,1)S(1)}, u32[]{:S(2)}, u32[]{:S(2)}) %all-to-all-start.1) | async-done | bytes 262176 | tf_op jit(solution)/shard_map/all_to_all | solution.py:407
  59.1 0.7 clip_sum.1
  59.7 2.7 %collective-permute-done.4.after = bf16[2,4,48,192]{3,2,1,0:T(8,128)(2,1)S(1)} collective-permute-done((bf16[2,4,48,192]{3,2,1,0:T(8,128)(2,1)S(1)}, bf16[2,4,48,192]{3,2,1,0:T(8,128)(2,1)S(1)}, u32[]{:S(2)}, u32[]{:S(2)}) %collective-permute-start.4) | collective-permute-done | bytes 147488 | tf_op jit(solution)/shard_map/ppermute | solution.py:38
  62.4 14.4 %all-to-all-start.2 = ((bf16[16,16,128]{2,1,0:T(8,128)(2,1)}), bf16[16,16,128]{2,1,0:T(8,128)(2,1)S(1)}, u32[]{:S(2)}, u32[]{:S(2)}) async-start(bf16[16,16,128]{2,1,0:T(8,128)(2,1)} %bitcast.7), calls=%async_computation.2 | async-start | bytes 131072 | tf_op jit(solution)/shard_map/all_to_all | solution.py:417
  76.7 3.3 %input_grad.1 = f32[2,2,48,192]{3,2,1,0:T(8,128)} custom-call(bf16[27,192,192]{2,1,0:T(8,128)(2,1)} %bitcast.12, bf16[2,4,48,192]{3,2,1,0:T(8,128)(2,1)S(1)} %hidden_grad.1.tall, bf16[2,4,48,192]{3,2,1,0:T(8,128)(2,1)S(1)} %collective-permute-done.4.after), custom_call_target="tpu_custom_call" | custom-call | tf_op jit(solution)/shard_map/input_grad/pallas_call | solution.py:318
  80.0 9.5 %all-to-all-done.2.got = bf16[16,16,128]{2,1,0:T(8,128)(2,1)S(1)} async-done(((bf16[16,16,128]{2,1,0:T(8,128)(2,1)}), bf16[16,16,128]{2,1,0:T(8,128)(2,1)S(1)}, u32[]{:S(2)}, u32[]{:S(2)}) %all-to-all-start.2) | async-done | bytes 65568 | tf_op jit(solution)/shard_map/all_to_all | solution.py:417
  89.6 0.7 kernel_grad_sum.1
Async XLA Ops:
  1.5 6.6 %collective-permute-start.1 = (bf16[2,2,48,192]{3,2,1,0:T(8,128)(2,1)S(1)}, bf16[2,2,48,192]{3,2,1,0:T(8,128)(2,1)S(1)}, u32[]{:S(2)}, u32[]{:S(2)}) collective-permute-start(bf16[2,2,48,192]{3,2,1,0:T(8,128)(2,1)S(1)} %slice_bitcast_fusion), channel_id=1, source_target_pairs={{1,0},{2,1},{3,2},{4,3},{5,4},{6,5},{7,6},{8,7},{9,8},{10,9},{11,1... | collective-permute-start | bytes 221192 | tf_op jit(solution)/shard_map/ppermute | solution.py:38
  2.8 7.1 %collective-permute-start = (bf16[2,2,48,192]{3,2,1,0:T(8,128)(2,1)}, bf16[2,2,48,192]{3,2,1,0:T(8,128)(2,1)S(1)}, u32[]{:S(2)}, u32[]{:S(2)}) collective-permute-start(bf16[2,2,48,192]{3,2,1,0:T(8,128)(2,1)} %bitcast.17), channel_id=1, source_target_pairs={{0,1},{1,2},{2,3},{3,4},{4,5},{5,6},{6,7},{7,8},{8,9},{9,10},{10,1... | collective-permute-start | bytes 221192 | tf_op jit(solution)/shard_map/ppermute | solution.py:38
  10.9 5.0 %collective-permute-start.3 = (bf16[10,2,48,192]{3,2,1,0:T(8,128)(2,1)S(1)}, bf16[10,2,48,192]{3,2,1,0:T(8,128)(2,1)S(1)}, u32[]{:S(2)}, u32[]{:S(2)}) collective-permute-start(bf16[10,2,48,192]{3,2,1,0:T(8,128)(2,1)S(1)} %band.1), channel_id=1, source_target_pairs={{16,0},{32,16},{48,32},{64,48},{80,64},{96,80},{112,96},{17,1},{33... | collective-permute-start | bytes 1105928 | tf_op jit(solution)/shard_map/ppermute | solution.py:38
  12.2 4.5 %collective-permute-start.2 = (bf16[10,2,48,192]{3,2,1,0:T(8,128)(2,1)S(1)}, bf16[10,2,48,192]{3,2,1,0:T(8,128)(2,1)S(1)}, u32[]{:S(2)}, u32[]{:S(2)}) collective-permute-start(bf16[10,2,48,192]{3,2,1,0:T(8,128)(2,1)S(1)} %band.1), channel_id=1, source_target_pairs={{0,16},{16,32},{32,48},{48,64},{64,80},{80,96},{96,112},{1,17},{17... | collective-permute-start | bytes 1105928 | tf_op jit(solution)/shard_map/ppermute | solution.py:38
  20.5 24.3 %all-to-all-start = ((bf16[8,408,128]{2,1,0:T(8,128)(2,1)}), bf16[8,408,128]{2,1,0:T(8,128)(2,1)S(1)}, u32[]{:S(2)}, u32[]{:S(2)}) async-start(bf16[8,408,128]{2,1,0:T(8,128)(2,1)} %hidden_and_act.1), calls=%async_computation | async-start | bytes 1671168 | tf_op jit(solution)/shard_map/all_to_all | solution.py:371
  47.2 11.9 %all-to-all-start.1 = ((bf16[4,256,128]{2,1,0:T(8,128)(2,1)}), bf16[4,256,128]{2,1,0:T(8,128)(2,1)S(1)}, u32[]{:S(2)}, u32[]{:S(2)}) async-start(bf16[4,256,128]{2,1,0:T(8,128)(2,1)} %bitcast.5), calls=%async_computation.1 | async-start | bytes 524288 | tf_op jit(solution)/shard_map/all_to_all | solution.py:407
  53.8 8.6 %collective-permute-start.4 = (bf16[2,4,48,192]{3,2,1,0:T(8,128)(2,1)S(1)}, bf16[2,4,48,192]{3,2,1,0:T(8,128)(2,1)S(1)}, u32[]{:S(2)}, u32[]{:S(2)}) collective-permute-start(bf16[2,4,48,192]{3,2,1,0:T(8,128)(2,1)S(1)} %hidden_grad.1.tall), channel_id=1, source_target_pairs={{1,0},{2,1},{3,2},{4,3},{5,4},{6,5},{7,6},{8,7},{9,8},{10,9},{11,1... | collective-permute-start | bytes 442376 | tf_op jit(solution)/shard_map/ppermute | solution.py:38
  62.4 27.2 %all-to-all-start.2 = ((bf16[16,16,128]{2,1,0:T(8,128)(2,1)}), bf16[16,16,128]{2,1,0:T(8,128)(2,1)S(1)}, u32[]{:S(2)}, u32[]{:S(2)}) async-start(bf16[16,16,128]{2,1,0:T(8,128)(2,1)} %bitcast.7), calls=%async_computation.2 | async-start | bytes 131072 | tf_op jit(solution)/shard_map/all_to_all | solution.py:417

commit v7 on v6

--- a/solution.py
+++ b/solution.py
@@ -386,8 +386,8 @@
         scalars=(lengths,),
         sems=5,
     )
-    got, tall = lax.optimization_barrier((got, tall))
     after = move(tall, ("tm",), (-1,))
+    got, after = lax.optimization_barrier((got, after))
 
     blocks = clips * steps
     span = 27 * chan // blocks
@@ -413,7 +413,6 @@
         (by_clip,),
         [],
     )
-    summed, after = lax.optimization_barrier((summed, after))
     by_step = lax.all_to_all(summed.reshape((steps,) + shape), "tm", 0, 0)
     total = clips * 2 * frames * steps * rows * peers * cols
     (kernel_grad,) = call(

time: 90.8 us -> 90.4 us (level)
  the two profiles are of different devices: /device:TPU:8 before, /device:TPU:2 now
where the time goes in v7:
time: 90.4 us; the launch traced here: 89.9 us
  waiting for transfers between devices  31.4 us (35%)
  starting transfers between devices  30.4 us (34%)
  Pallas kernels  16.8 us (19%)
  blocking collectives  9.07 us (10%)
  between operations  1.37 us (2%)
    ppermute x5, waiting for transfers between devices, move(): lax.ppermute(value, axes if len(axes) > 1 else axes[0], route(sizes, steps))  21.8 us
    pallas_call x7, Pallas kernels, call(): pl.pallas_call(body, name=name, out_shape=outs, in_specs=[pl.BlockSpec(me...  16.8 us
    all_to_all x1, starting transfers between devices, local(): by_step = lax.all_to_all(summed.reshape((steps,) + shape), 'tm', 0, 0)  15.4 us
    ppermute x5, starting transfers between devices, move(): lax.ppermute(value, axes if len(axes) > 1 else axes[0], route(sizes, steps))  11.5 us
    all_to_all x1, waiting for transfers between devices, local(): by_step = lax.all_to_all(summed.reshape((steps,) + shape), 'tm', 0, 0)  9.6 us
    all_to_all x1, blocking collectives, local(): lax.all_to_all(part.reshape((clips, steps * shape[0], shape[1])), 'clip',...  9.07 us
    all_to_all x1, starting transfers between devices, local(): got = lax.all_to_all(pay, 'row', 0, 0)  3.51 us
  transfers between devices with their start and end apart: 7, of which 6 were waited for; matrix products, arithmetic and copies ran while one was open for 0% of the time, Pallas kernels for 10%

profile of v7, /device:TPU:2, one launch (start us, length us, event | category | flops | bytes accessed | tf_op | source)
XLA Modules:
  0.0 89.9 jit_solution(11675520570543839065)
XLA Ops:
  0.6 0.9 %slice_bitcast_fusion = bf16[2,2,48,192]{3,2,1,0:T(8,128)(2,1)S(1)} fusion(bf16[1,4,2,48,192]{4,3,2,1,0:T(8,128)(2,1)} %param.6), kind=kLoop, calls=%fused_computation | loop fusion | bytes 147456 | tf_op jit(solution)/shard_map/slice | solution.py:342
  1.5 1.3 %collective-permute-start.1 = (bf16[2,2,48,192]{3,2,1,0:T(8,128)(2,1)S(1)}, bf16[2,2,48,192]{3,2,1,0:T(8,128)(2,1)S(1)}, u32[]{:S(2)}, u32[]{:S(2)}) collective-permute-start(bf16[2,2,48,192]{3,2,1,0:T(8,128)(2,1)S(1)} %slice_bitcast_fusion), channel_id=1, source_target_pairs={{1,0},{2,1},{3,2},{4,3},{5,4},{6,5},{7,6},{8,7},{9,8},{10,9},{11,1... | collective-permute-start | bytes 221192 | tf_op jit(solution)/shard_map/ppermute | solution.py:38
  2.8 4.6 %collective-permute-start = (bf16[2,2,48,192]{3,2,1,0:T(8,128)(2,1)}, bf16[2,2,48,192]{3,2,1,0:T(8,128)(2,1)S(1)}, u32[]{:S(2)}, u32[]{:S(2)}) collective-permute-start(bf16[2,2,48,192]{3,2,1,0:T(8,128)(2,1)} %bitcast.18), channel_id=1, source_target_pairs={{0,1},{1,2},{2,3},{3,4},{4,5},{5,6},{6,7},{7,8},{8,9},{9,10},{10,1... | collective-permute-start | bytes 221192 | tf_op jit(solution)/shard_map/ppermute | solution.py:38
  7.4 0.8 collective-permute-done.1.gnext
  8.1 1.8 %collective-permute-done.xprev = bf16[2,2,48,192]{3,2,1,0:T(8,128)(2,1)S(1)} collective-permute-done((bf16[2,2,48,192]{3,2,1,0:T(8,128)(2,1)}, bf16[2,2,48,192]{3,2,1,0:T(8,128)(2,1)S(1)}, u32[]{:S(2)}, u32[]{:S(2)}) %collective-permute-start) | collective-permute-done | bytes 73760 | tf_op jit(solution)/shard_map/ppermute | solution.py:38
  9.9 1.0 %band.1 = bf16[10,2,48,192]{3,2,1,0:T(8,128)(2,1)S(1)} custom-call(bf16[2,2,48,192]{3,2,1,0:T(8,128)(2,1)} %bitcast.19, bf16[4,2,48,192]{3,2,1,0:T(8,128)(2,1)} %bitcast.15, bf16[2,2,48,192]{3,2,1,0:T(8,128)(2,1)S(1)} %collective-permute-done.xprev, bf16[2,2,48,192]{3,2,1,0:T(8,128)(2,1)S(1)} %collective-permute-done.1.gnext), custom_call_target="tpu_custom_call" | custom-call | tf_op jit(solution)/shard_map/band/pallas_call | solution.py:318
  10.9 1.9 %collective-permute-start.3 = (bf16[10,2,48,192]{3,2,1,0:T(8,128)(2,1)S(1)}, bf16[10,2,48,192]{3,2,1,0:T(8,128)(2,1)S(1)}, u32[]{:S(2)}, u32[]{:S(2)}) collective-permute-start(bf16[10,2,48,192]{3,2,1,0:T(8,128)(2,1)S(1)} %band.1), channel_id=1, source_target_pairs={{16,0},{32,16},{48,32},{64,48},{80,64},{96,80},{112,96},{17,1},{33... | collective-permute-start | bytes 1105928 | tf_op jit(solution)/shard_map/ppermute | solution.py:38
  12.8 2.4 %collective-permute-start.2 = (bf16[10,2,48,192]{3,2,1,0:T(8,128)(2,1)S(1)}, bf16[10,2,48,192]{3,2,1,0:T(8,128)(2,1)S(1)}, u32[]{:S(2)}, u32[]{:S(2)}) collective-permute-start(bf16[10,2,48,192]{3,2,1,0:T(8,128)(2,1)S(1)} %band.1), channel_id=1, source_target_pairs={{0,16},{16,32},{32,48},{48,64},{64,80},{80,96},{96,112},{1,17},{17... | collective-permute-start | bytes 1105928 | tf_op jit(solution)/shard_map/ppermute | solution.py:38
  15.9 3.3 %collective-permute-done.3.below = bf16[10,2,48,192]{3,2,1,0:T(8,128)(2,1)S(1)} collective-permute-done((bf16[10,2,48,192]{3,2,1,0:T(8,128)(2,1)S(1)}, bf16[10,2,48,192]{3,2,1,0:T(8,128)(2,1)S(1)}, u32[]{:S(2)}, u32[]{:S(2)}) %collective-permute-start.3) | collective-permute-done | bytes 368672 | tf_op jit(solution)/shard_map/ppermute | solution.py:38
  19.1 8.1 %collective-permute-done.2.above = bf16[10,2,48,192]{3,2,1,0:T(8,128)(2,1)S(1)} collective-permute-done((bf16[10,2,48,192]{3,2,1,0:T(8,128)(2,1)S(1)}, bf16[10,2,48,192]{3,2,1,0:T(8,128)(2,1)S(1)}, u32[]{:S(2)}, u32[]{:S(2)}) %collective-permute-start.2) | collective-permute-done | bytes 368672 | tf_op jit(solution)/shard_map/ppermute | solution.py:38
  27.2 3.8 %hidden_and_act.1 = bf16[8,408,128]{2,1,0:T(8,128)(2,1)} custom-call(s32[1]{0:T(128)S(6)} %copy.7.lengths, bf16[2,2,48,192]{3,2,1,0:T(8,128)(2,1)} %bitcast.20, bf16[4,2,48,192]{3,2,1,0:T(8,128)(2,1)} %bitcast.16, bf16[27,192,192]{2,1,0:T(8,128)(2,1)} %bitcast.11, bf16[10,2,48,192]{3,2,1,0:T(8,128)(2,1)S(1)} %collective-permute-done.2.above, ...), custom_call_target="tpu_custom_call" | custom-call | tf_op jit(solution)/shard_map/hidden_and_act/pallas_call | solution.py:318
  31.0 3.5 %all-to-all-start = ((bf16[8,408,128]{2,1,0:T(8,128)(2,1)}), bf16[8,408,128]{2,1,0:T(8,128)(2,1)S(1)}, u32[]{:S(2)}, u32[]{:S(2)}) async-start(bf16[8,408,128]{2,1,0:T(8,128)(2,1)} %hidden_and_act.1), calls=%async_computation | async-start | bytes 1671168 | tf_op jit(solution)/shard_map/all_to_all | solution.py:371
  34.5 5.6 %hidden_grad.1.tall = bf16[2,4,48,192]{3,2,1,0:T(8,128)(2,1)S(1)} custom-call(s32[1]{0:T(128)S(6)} %copy.7.lengths, bf16[2,2,48,192]{3,2,1,0:T(8,128)(2,1)} %bitcast.21, bf16[4,2,48,192]{3,2,1,0:T(8,128)(2,1)} %bitcast.17, bf16[27,192,192]{2,1,0:T(8,128)(2,1)} %bitcast.12, bf16[27,192,192]{2,1,0:T(8,128)(2,1)} %bitcast.14, ...), custom_call_target="tpu_custom_call" | custom-call | tf_op jit(solution)/shard_map/hidden_grad/pallas_call | solution.py:318
  40.2 1.3 %collective-permute-start.4 = (bf16[2,4,48,192]{3,2,1,0:T(8,128)(2,1)S(1)}, bf16[2,4,48,192]{3,2,1,0:T(8,128)(2,1)S(1)}, u32[]{:S(2)}, u32[]{:S(2)}) collective-permute-start(bf16[2,4,48,192]{3,2,1,0:T(8,128)(2,1)S(1)} %hidden_grad.1.tall), channel_id=1, source_target_pairs={{1,0},{2,1},{3,2},{4,3},{5,4},{6,5},{7,6},{8,7},{9,8},{10,9},{11,1... | collective-permute-start | bytes 442376 | tf_op jit(solution)/shard_map/ppermute | solution.py:38
  41.5 7.9 %collective-permute-done.4.after = bf16[2,4,48,192]{3,2,1,0:T(8,128)(2,1)S(1)} collective-permute-done((bf16[2,4,48,192]{3,2,1,0:T(8,128)(2,1)S(1)}, bf16[2,4,48,192]{3,2,1,0:T(8,128)(2,1)S(1)}, u32[]{:S(2)}, u32[]{:S(2)}) %collective-permute-start.4) | collective-permute-done | bytes 147488 | tf_op jit(solution)/shard_map/ppermute | solution.py:38
  49.4 0.0 all-to-all-done.got
  49.4 1.7 %kernel_grad_part.1 = bf16[64,16,128]{2,1,0:T(8,128)(2,1)S(1)} custom-call(bf16[8,408,128]{2,1,0:T(8,128)(2,1)S(1)} %all-to-all-done.got), custom_call_target="tpu_custom_call" | custom-call | tf_op jit(solution)/shard_map/kernel_grad_part/pallas_call | solution.py:318
  51.1 9.1 %all_to_all.15.got = bf16[4,256,128]{2,1,0:T(8,128)(2,1)S(1)} all-to-all(bf16[4,256,128]{2,1,0:T(8,128)(2,1)S(1)} %bitcast.10), channel_id=1, replica_groups=mesh['clip'=4,'row'=8,'tm'=16] {'clip'}, dimensions={0} | all-to-all | bytes 524288 | tf_op jit(solution)/shard_map/all_to_all | solution.py:407
  60.2 0.7 clip_sum.1
  60.9 15.4 %all-to-all-start.2 = ((bf16[16,16,128]{2,1,0:T(8,128)(2,1)}), bf16[16,16,128]{2,1,0:T(8,128)(2,1)S(1)}, u32[]{:S(2)}, u32[]{:S(2)}) async-start(bf16[16,16,128]{2,1,0:T(8,128)(2,1)} %bitcast.7), calls=%async_computation.2 | async-start | bytes 131072 | tf_op jit(solution)/shard_map/all_to_all | solution.py:416
  76.3 3.3 %input_grad.1 = f32[2,2,48,192]{3,2,1,0:T(8,128)} custom-call(bf16[27,192,192]{2,1,0:T(8,128)(2,1)} %bitcast.13, bf16[2,4,48,192]{3,2,1,0:T(8,128)(2,1)S(1)} %hidden_grad.1.tall, bf16[2,4,48,192]{3,2,1,0:T(8,128)(2,1)S(1)} %collective-permute-done.4.after), custom_call_target="tpu_custom_call" | custom-call | tf_op jit(solution)/shard_map/input_grad/pallas_call | solution.py:318
  79.6 9.6 %all-to-all-done.2.got = bf16[16,16,128]{2,1,0:T(8,128)(2,1)S(1)} async-done(((bf16[16,16,128]{2,1,0:T(8,128)(2,1)}), bf16[16,16,128]{2,1,0:T(8,128)(2,1)S(1)}, u32[]{:S(2)}, u32[]{:S(2)}) %all-to-all-start.2) | async-done | bytes 65568 | tf_op jit(solution)/shard_map/all_to_all | solution.py:416
  89.2 0.7 kernel_grad_sum.1
Async XLA Ops:
  1.5 6.6 %collective-permute-start.1 = (bf16[2,2,48,192]{3,2,1,0:T(8,128)(2,1)S(1)}, bf16[2,2,48,192]{3,2,1,0:T(8,128)(2,1)S(1)}, u32[]{:S(2)}, u32[]{:S(2)}) collective-permute-start(bf16[2,2,48,192]{3,2,1,0:T(8,128)(2,1)S(1)} %slice_bitcast_fusion), channel_id=1, source_target_pairs={{1,0},{2,1},{3,2},{4,3},{5,4},{6,5},{7,6},{8,7},{9,8},{10,9},{11,1... | collective-permute-start | bytes 221192 | tf_op jit(solution)/shard_map/ppermute | solution.py:38
  2.8 7.1 %collective-permute-start = (bf16[2,2,48,192]{3,2,1,0:T(8,128)(2,1)}, bf16[2,2,48,192]{3,2,1,0:T(8,128)(2,1)S(1)}, u32[]{:S(2)}, u32[]{:S(2)}) collective-permute-start(bf16[2,2,48,192]{3,2,1,0:T(8,128)(2,1)} %bitcast.18), channel_id=1, source_target_pairs={{0,1},{1,2},{2,3},{3,4},{4,5},{5,6},{6,7},{7,8},{8,9},{9,10},{10,1... | collective-permute-start | bytes 221192 | tf_op jit(solution)/shard_map/ppermute | solution.py:38
  10.9 8.3 %collective-permute-start.3 = (bf16[10,2,48,192]{3,2,1,0:T(8,128)(2,1)S(1)}, bf16[10,2,48,192]{3,2,1,0:T(8,128)(2,1)S(1)}, u32[]{:S(2)}, u32[]{:S(2)}) collective-permute-start(bf16[10,2,48,192]{3,2,1,0:T(8,128)(2,1)S(1)} %band.1), channel_id=1, source_target_pairs={{16,0},{32,16},{48,32},{64,48},{80,64},{96,80},{112,96},{17,1},{33... | collective-permute-start | bytes 1105928 | tf_op jit(solution)/shard_map/ppermute | solution.py:38
  12.8 14.4 %collective-permute-start.2 = (bf16[10,2,48,192]{3,2,1,0:T(8,128)(2,1)S(1)}, bf16[10,2,48,192]{3,2,1,0:T(8,128)(2,1)S(1)}, u32[]{:S(2)}, u32[]{:S(2)}) collective-permute-start(bf16[10,2,48,192]{3,2,1,0:T(8,128)(2,1)S(1)} %band.1), channel_id=1, source_target_pairs={{0,16},{16,32},{32,48},{48,64},{64,80},{80,96},{96,112},{1,17},{17... | collective-permute-start | bytes 1105928 | tf_op jit(solution)/shard_map/ppermute | solution.py:38
  31.0 18.4 %all-to-all-start = ((bf16[8,408,128]{2,1,0:T(8,128)(2,1)}), bf16[8,408,128]{2,1,0:T(8,128)(2,1)S(1)}, u32[]{:S(2)}, u32[]{:S(2)}) async-start(bf16[8,408,128]{2,1,0:T(8,128)(2,1)} %hidden_and_act.1), calls=%async_computation | async-start | bytes 1671168 | tf_op jit(solution)/shard_map/all_to_all | solution.py:371
  40.2 9.2 %collective-permute-start.4 = (bf16[2,4,48,192]{3,2,1,0:T(8,128)(2,1)S(1)}, bf16[2,4,48,192]{3,2,1,0:T(8,128)(2,1)S(1)}, u32[]{:S(2)}, u32[]{:S(2)}) collective-permute-start(bf16[2,4,48,192]{3,2,1,0:T(8,128)(2,1)S(1)} %hidden_grad.1.tall), channel_id=1, source_target_pairs={{1,0},{2,1},{3,2},{4,3},{5,4},{6,5},{7,6},{8,7},{9,8},{10,9},{11,1... | collective-permute-start | bytes 442376 | tf_op jit(solution)/shard_map/ppermute | solution.py:38
  60.9 28.4 %all-to-all-start.2 = ((bf16[16,16,128]{2,1,0:T(8,128)(2,1)}), bf16[16,16,128]{2,1,0:T(8,128)(2,1)S(1)}, u32[]{:S(2)}, u32[]{:S(2)}) async-start(bf16[16,16,128]{2,1,0:T(8,128)(2,1)} %bitcast.7), calls=%async_computation.2 | async-start | bytes 131072 | tf_op jit(solution)/shard_map/all_to_all | solution.py:416

commit v8 on v7

--- a/solution.py
+++ b/solution.py
@@ -80,54 +80,47 @@
     return copies
 
 
-def band_kernel(x, g, xprev, gnext, band, sem):
-    nx, ng = x.shape[0], g.shape[0]
-    copies = start_copies(((x, band.at[0:nx]), (g, band.at[2 * nx : 2 * nx + ng])), sem)
-    band[nx : 2 * nx] = xprev[...]
-    band[2 * nx + ng :] = gnext[...]
-    for copy in copies:
-        copy.wait()
+def band_kernel(lengths, x, g_far, xprev, gnext, band, g, sem):
+    frames = xprev.shape[0]
+    copies = start_copies(((g_far, g), (x, band.at[0:frames])), sem)
+    band[frames : 2 * frames] = xprev[...]
+    limit = 2 * lengths[0] - 2 * frames * lax.axis_index("tm")
+    copies[0].wait()
+    for r in range(2):
+        values = [g[f, r] for f in range(4)] + [gnext[f, r] for f in range(2)]
+        field = [jnp.where(f < limit, v.astype(F32), 0.0) for f, v in enumerate(values)]
+        for a in range(5):
+            band[2 * frames + a, r] = (field[a] + field[a + 1]).astype(BF)
+    copies[1].wait()
 
 
 def packed(width, span):
     return (width, span) == (24, 81)
 
 
-def masked_frames(values, limit):
-    return [jnp.where(f < limit, v.astype(F32), 0.0) for f, v in enumerate(values)]
-
-
-def silu_kernel(
-    lengths, x_far, g_far, w_far, above, below, xprev, gnext, pay, xe, ps, g, w, sem
-):
-    frames, rows, cols, chan = xprev.shape
+def silu_kernel(w_far, above, below, band, pay, xe, ps, w, sem):
+    _, rows, cols, chan = band.shape
+    frames = 2
     cells = frames * rows * cols
     peers = pay.shape[0]
     width = chan // peers
-    pairs = [(g_far, g), (w_far, w)]
-    pairs += [(x_far.at[f], xe.at[(2 + f) * 4 + 1 : (2 + f) * 4 + 3]) for f in range(2)]
-    copies = start_copies(pairs, sem)
-    for f in range(2):
-        xe[f * 4] = above[2 + f, 1]
-        xe[f * 4 + 1 : f * 4 + 3] = xprev[f]
-        xe[f * 4 + 3] = below[2 + f, 0]
-        xe[(2 + f) * 4] = above[f, 1]
-        xe[(2 + f) * 4 + 3] = below[f, 0]
-    limit = 2 * lengths[0] - 2 * frames * lax.axis_index("tm")
+    copies = start_copies([(w_far, w)], sem)
+    for f in range(2 * frames):
+        slot = (f + frames) % (2 * frames) * 4
+        xe[slot] = above[f, 1]
+        xe[slot + 1 : slot + 3] = band[f]
+        xe[slot + 3] = below[f, 0]
     ps[:, 0:EDGE, :] = jnp.zeros((10, EDGE, chan), F32)
-    copies[0].wait()
-    for r in range(2):
-        field = masked_frames([g[f, r] for f in range(4)] + [gnext[f, r] for f in range(2)], limit)
-        for a in range(5):
-            ps[a * 2 + r, EDGE : EDGE + cols, :] = field[a] + field[a + 1]
+    for a in range(5):
+        for r in range(2):
+            ps[a * 2 + r, EDGE : EDGE + cols, :] = band[4 + a, r].astype(F32)
     turned = [
         jnp.transpose(ps[2 * a : 2 * a + 2].reshape(2 * PITCH, chan)) for a in range(5)
     ]
     for p in range(peers):
         mine = jnp.concatenate([v[p * width : (p + 1) * width] for v in turned], axis=0)
         pay[p, cells + cells // 2 :, :] = mine.astype(BF)
-    for copy in copies[1:]:
-        copy.wait()
+    copies[0].wait()
 
     def patch(i, j):
         return blocks_of(xe, [(f + 2 - i) * 4 + j for f in range(2)], 2)
@@ -142,34 +135,16 @@
         pay[p, cells : cells + half, :] = high
 
 
-def hidden_grad_kernel(
-    lengths, x_far, g_far, w1_far, w2_far, above, below, xprev, gnext,
-    tall,
-    xe, pe, g, w1, w2, sem,
-):
-    frames, rows, cols, chan = xprev.shape
-    pairs = [(g_far, g), (w1_far, w1), (w2_far, w2)]
-    pairs += [(x_far.at[f], xe.at[(2 + f) * 6 + 2 : (2 + f) * 6 + 4]) for f in range(2)]
-    copies = start_copies(pairs, sem)
-    for f in range(2):
-        xe[f * 6 : f * 6 + 2] = above[2 + f]
-        xe[f * 6 + 2 : f * 6 + 4] = xprev[f]
-        xe[f * 6 + 4 : f * 6 + 6] = below[2 + f]
-        xe[(2 + f) * 6 : (2 + f) * 6 + 2] = above[f]
-        xe[(2 + f) * 6 + 4 : (2 + f) * 6 + 6] = below[f]
-    limit = 2 * lengths[0] - 2 * frames * lax.axis_index("tm")
-    copies[0].wait()
-    for r in range(6):
-        if r < 2:
-            values = [above[4 + f, r] for f in range(6)]
-        elif r > 3:
-            values = [below[4 + f, r - 4] for f in range(6)]
-        else:
-            values = [g[f, r - 2] for f in range(4)] + [gnext[f, r - 2] for f in range(2)]
-        field = masked_frames(values, limit)
-        for a in range(5):
-            pe[a * 6 + r] = (field[a] + field[a + 1]).astype(BF)
-    for copy in copies[1:]:
+def hidden_grad_kernel(w1_far, w2_far, above, below, own, tall, xe, pe, w1, w2, sem):
+    _, rows, cols, chan = own.shape
+    frames = 2
+    copies = start_copies([(w1_far, w1), (w2_far, w2)], sem)
+    for f in range(2 * frames + 5):
+        target, slot = (xe, (f + frames) % (2 * frames) * 6) if f < 4 else (pe, (f - 4) * 6)
+        target[slot : slot + 2] = above[f]
+        target[slot + 2 : slot + 4] = own[f]
+        target[slot + 4 : slot + 6] = below[f]
+    for copy in copies:
         copy.wait()
 
     def patch(i, j):
@@ -344,10 +319,11 @@
         band_kernel,
         "band",
         4,
-        [((5 * frames, rows, cols, chan), BF)],
+        [((2 * frames + 5, rows, cols, chan), BF)],
         (xprev, gnext),
-        [],
+        [(g.shape, BF)],
         far=(x, g),
+        scalars=(lengths,),
         sems=2,
     )
     above = move(band, ("row",), (1,))
@@ -357,16 +333,10 @@
         "hidden_and_act",
         16,
         [((peers, cells + cells // 2 + 5 * width, 128), BF)],
-        (above, below, xprev, gnext),
-        [
-            ((16, cols, chan), BF),
-            ((10, PITCH, chan), F32),
-            (g.shape, BF),
-            (w1.shape, BF),
-        ],
-        far=(x, g, w1),
-        scalars=(lengths,),
-        sems=4,
+        (above, below, band),
+        [((16, cols, chan), BF), ((10, PITCH, chan), F32), (w1.shape, BF)],
+        far=(w1,),
+        sems=1,
     )
     got = lax.all_to_all(pay, "row", 0, 0)
     (tall,) = call(
@@ -374,20 +344,17 @@
         "hidden_grad",
         28,
         [((frames, rows + 2, cols, chan), BF)],
-        (above, below, xprev, gnext),
+        (above, below, band),
         [
             ((24, cols, chan), BF),
             ((30, cols, chan), BF),
-            (g.shape, BF),
             (w1.shape, BF),
             (w2.shape, BF),
         ],
-        far=(x, g, w1, w2),
-        scalars=(lengths,),
-        sems=5,
+        far=(w1, w2),
+        sems=2,
     )
     after = move(tall, ("tm",), (-1,))
-    got, after = lax.optimization_barrier((got, after))
 
     blocks = clips * steps
     span = 27 * chan // blocks
@@ -404,6 +371,7 @@
             ((27 * width, 256), F32),
         ],
     )
+    part, after = lax.optimization_barrier((part, after))
     by_clip = lax.all_to_all(part.reshape((clips, steps * shape[0], shape[1])), "clip", 0, 0)
     (summed,) = call(
         clip_kernel,

time: 90.4 us -> 87.9 us (0.972)
  waiting for transfers between devices: 31.4 us -> 29.1 us
    ppermute x5, waiting for transfers between devices: 21.8 us -> 14.3 us  [move(): lax.ppermute(value, axes if len(axes) > 1 else axes[0], route(sizes, steps))]
    all_to_all x1, waiting for transfers between devices: 0.01 us -> 5.21 us  [local(): got = lax.all_to_all(pay, 'row', 0, 0)]
  transfers between devices with their start and end apart: 7 -> 7, of which waited for: 6 -> 7; matrix products, arithmetic and copies ran while one was open for 0% -> 0% of each run, Pallas kernels for 10% -> 12%
where the time goes in v8:
time: 87.9 us; the launch traced here: 87.4 us
  starting transfers between devices  30.4 us (35%)
  waiting for transfers between devices  29.1 us (33%)
  Pallas kernels  16.6 us (19%)
  blocking collectives  9.05 us (10%)
  between operations  1.37 us (2%)
  local copies, waits for them, and re-layouts  0.9 us (1%)
    pallas_call x7, Pallas kernels, call(): pl.pallas_call(body, name=name, out_shape=outs, in_specs=[pl.BlockSpec(me...  16.6 us
    all_to_all x1, starting transfers between devices, local(): by_step = lax.all_to_all(summed.reshape((steps,) + shape), 'tm', 0, 0)  15.4 us
    ppermute x5, waiting for transfers between devices, move(): lax.ppermute(value, axes if len(axes) > 1 else axes[0], route(sizes, steps))  14.3 us
    ppermute x5, starting transfers between devices, move(): lax.ppermute(value, axes if len(axes) > 1 else axes[0], route(sizes, steps))  11.5 us
    all_to_all x1, waiting for transfers between devices, local(): by_step = lax.all_to_all(summed.reshape((steps,) + shape), 'tm', 0, 0)  9.61 us
    all_to_all x1, blocking collectives, local(): lax.all_to_all(part.reshape((clips, steps * shape[0], shape[1])), 'clip',...  9.05 us
    all_to_all x1, waiting for transfers between devices, local(): got = lax.all_to_all(pay, 'row', 0, 0)  5.21 us
    all_to_all x1, starting transfers between devices, local(): got = lax.all_to_all(pay, 'row', 0, 0)  3.51 us
  transfers between devices with their start and end apart: 7, of which 7 were waited for; matrix products, arithmetic and copies ran while one was open for 0% of the time, Pallas kernels for 12%

profile of v8, /device:TPU:2, one launch (start us, length us, event | category | flops | bytes accessed | tf_op | source)
XLA Modules:
  0.0 87.4 jit_solution(4730273302745521656)
XLA Ops:
  0.6 0.9 %slice_bitcast_fusion = bf16[2,2,48,192]{3,2,1,0:T(8,128)(2,1)S(1)} fusion(bf16[1,4,2,48,192]{4,3,2,1,0:T(8,128)(2,1)} %param.6), kind=kLoop, calls=%fused_computation | loop fusion | bytes 147456 | tf_op jit(solution)/shard_map/slice | solution.py:317
  1.5 1.3 %collective-permute-start.1 = (bf16[2,2,48,192]{3,2,1,0:T(8,128)(2,1)S(1)}, bf16[2,2,48,192]{3,2,1,0:T(8,128)(2,1)S(1)}, u32[]{:S(2)}, u32[]{:S(2)}) collective-permute-start(bf16[2,2,48,192]{3,2,1,0:T(8,128)(2,1)S(1)} %slice_bitcast_fusion), channel_id=1, source_target_pairs={{1,0},{2,1},{3,2},{4,3},{5,4},{6,5},{7,6},{8,7},{9,8},{10,9},{11,1... | collective-permute-start | bytes 221192 | tf_op jit(solution)/shard_map/ppermute | solution.py:38
  2.8 4.6 %collective-permute-start = (bf16[2,2,48,192]{3,2,1,0:T(8,128)(2,1)}, bf16[2,2,48,192]{3,2,1,0:T(8,128)(2,1)S(1)}, u32[]{:S(2)}, u32[]{:S(2)}) collective-permute-start(bf16[2,2,48,192]{3,2,1,0:T(8,128)(2,1)} %bitcast.17), channel_id=1, source_target_pairs={{0,1},{1,2},{2,3},{3,4},{4,5},{5,6},{6,7},{7,8},{8,9},{9,10},{10,1... | collective-permute-start | bytes 221192 | tf_op jit(solution)/shard_map/ppermute | solution.py:38
  8.0 0.1 collective-permute-done.1.gnext
  8.1 1.8 %collective-permute-done.xprev = bf16[2,2,48,192]{3,2,1,0:T(8,128)(2,1)S(1)} collective-permute-done((bf16[2,2,48,192]{3,2,1,0:T(8,128)(2,1)}, bf16[2,2,48,192]{3,2,1,0:T(8,128)(2,1)S(1)}, u32[]{:S(2)}, u32[]{:S(2)}) %collective-permute-start) | collective-permute-done | bytes 73760 | tf_op jit(solution)/shard_map/ppermute | solution.py:38
  9.9 1.0 %band.1.own = bf16[9,2,48,192]{3,2,1,0:T(8,128)(2,1)S(1)} custom-call(s32[1]{0:T(128)S(6)} %copy.7.lengths, bf16[2,2,48,192]{3,2,1,0:T(8,128)(2,1)} %bitcast.18, bf16[4,2,48,192]{3,2,1,0:T(8,128)(2,1)} %bitcast.15, bf16[2,2,48,192]{3,2,1,0:T(8,128)(2,1)S(1)} %collective-permute-done.xprev, bf16[2,2,48,192]{3,2,1,0:T(8,128)(2,1)S(1)} %collective-permute-done.1.gnext), custom_call_target="tpu_custom_call" | custom-call | tf_op jit(solution)/shard_map/band/pallas_call | solution.py:293
  10.9 1.9 %collective-permute-start.3 = (bf16[9,2,48,192]{3,2,1,0:T(8,128)(2,1)S(1)}, bf16[9,2,48,192]{3,2,1,0:T(8,128)(2,1)S(1)}, u32[]{:S(2)}, u32[]{:S(2)}) collective-permute-start(bf16[9,2,48,192]{3,2,1,0:T(8,128)(2,1)S(1)} %band.1.own), channel_id=1, source_target_pairs={{16,0},{32,16},{48,32},{64,48},{80,64},{96,80},{112,96},{17,1},{33... | collective-permute-start | bytes 995336 | tf_op jit(solution)/shard_map/ppermute | solution.py:38
  12.8 2.4 %collective-permute-start.2 = (bf16[9,2,48,192]{3,2,1,0:T(8,128)(2,1)S(1)}, bf16[9,2,48,192]{3,2,1,0:T(8,128)(2,1)S(1)}, u32[]{:S(2)}, u32[]{:S(2)}) collective-permute-start(bf16[9,2,48,192]{3,2,1,0:T(8,128)(2,1)S(1)} %band.1.own), channel_id=1, source_target_pairs={{0,16},{16,32},{32,48},{48,64},{64,80},{80,96},{96,112},{1,17},{17... | collective-permute-start | bytes 995336 | tf_op jit(solution)/shard_map/ppermute | solution.py:38
  15.3 3.4 %collective-permute-done.3.below = bf16[9,2,48,192]{3,2,1,0:T(8,128)(2,1)S(1)} collective-permute-done((bf16[9,2,48,192]{3,2,1,0:T(8,128)(2,1)S(1)}, bf16[9,2,48,192]{3,2,1,0:T(8,128)(2,1)S(1)}, u32[]{:S(2)}, u32[]{:S(2)}) %collective-permute-start.3) | collective-permute-done | bytes 331808 | tf_op jit(solution)/shard_map/ppermute | solution.py:38
  18.6 8.1 %collective-permute-done.2.above = bf16[9,2,48,192]{3,2,1,0:T(8,128)(2,1)S(1)} collective-permute-done((bf16[9,2,48,192]{3,2,1,0:T(8,128)(2,1)S(1)}, bf16[9,2,48,192]{3,2,1,0:T(8,128)(2,1)S(1)}, u32[]{:S(2)}, u32[]{:S(2)}) %collective-permute-start.2) | collective-permute-done | bytes 331808 | tf_op jit(solution)/shard_map/ppermute | solution.py:38
  26.7 3.7 %hidden_and_act.1 = bf16[8,408,128]{2,1,0:T(8,128)(2,1)} custom-call(bf16[27,192,192]{2,1,0:T(8,128)(2,1)} %bitcast.11, bf16[9,2,48,192]{3,2,1,0:T(8,128)(2,1)S(1)} %collective-permute-done.2.above, bf16[9,2,48,192]{3,2,1,0:T(8,128)(2,1)S(1)} %collective-permute-done.3.below, bf16[9,2,48,192]{3,2,1,0:T(8,128)(2,1)S(1)} %band.1.own), custom_call_target="tpu_custom_call" | custom-call | tf_op jit(solution)/shard_map/hidden_and_act/pallas_call | solution.py:293
  30.4 3.5 %all-to-all-start = ((bf16[8,408,128]{2,1,0:T(8,128)(2,1)}), bf16[8,408,128]{2,1,0:T(8,128)(2,1)S(1)}, u32[]{:S(2)}, u32[]{:S(2)}) async-start(bf16[8,408,128]{2,1,0:T(8,128)(2,1)} %hidden_and_act.1), calls=%async_computation | async-start | bytes 1671168 | tf_op jit(solution)/shard_map/all_to_all | solution.py:341
  33.9 5.5 %hidden_grad.1.tall = bf16[2,4,48,192]{3,2,1,0:T(8,128)(2,1)S(1)} custom-call(bf16[27,192,192]{2,1,0:T(8,128)(2,1)} %bitcast.12, bf16[27,192,192]{2,1,0:T(8,128)(2,1)} %bitcast.14, bf16[9,2,48,192]{3,2,1,0:T(8,128)(2,1)S(1)} %collective-permute-done.2.above, bf16[9,2,48,192]{3,2,1,0:T(8,128)(2,1)S(1)} %collective-permute-done.3.below, ...), custom_call_target="tpu_custom_call" | custom-call | tf_op jit(solution)/shard_map/hidden_grad/pallas_call | solution.py:293
  39.4 1.3 %collective-permute-start.4 = (bf16[2,4,48,192]{3,2,1,0:T(8,128)(2,1)S(1)}, bf16[2,4,48,192]{3,2,1,0:T(8,128)(2,1)S(1)}, u32[]{:S(2)}, u32[]{:S(2)}) collective-permute-start(bf16[2,4,48,192]{3,2,1,0:T(8,128)(2,1)S(1)} %hidden_grad.1.tall), channel_id=1, source_target_pairs={{1,0},{2,1},{3,2},{4,3},{5,4},{6,5},{7,6},{8,7},{9,8},{10,9},{11,1... | collective-permute-start | bytes 442376 | tf_op jit(solution)/shard_map/ppermute | solution.py:38
  40.7 5.2 %all-to-all-done.got = bf16[8,408,128]{2,1,0:T(8,128)(2,1)S(1)} async-done(((bf16[8,408,128]{2,1,0:T(8,128)(2,1)}), bf16[8,408,128]{2,1,0:T(8,128)(2,1)S(1)}, u32[]{:S(2)}, u32[]{:S(2)}) %all-to-all-start) | async-done | bytes 835616 | tf_op jit(solution)/shard_map/all_to_all | solution.py:341
  45.9 1.7 %kernel_grad_part.1 = bf16[64,16,128]{2,1,0:T(8,128)(2,1)S(1)} custom-call(bf16[8,408,128]{2,1,0:T(8,128)(2,1)S(1)} %all-to-all-done.got), custom_call_target="tpu_custom_call" | custom-call | tf_op jit(solution)/shard_map/kernel_grad_part/pallas_call | solution.py:293
  47.7 1.0 %collective-permute-done.4.after = bf16[2,4,48,192]{3,2,1,0:T(8,128)(2,1)S(1)} collective-permute-done((bf16[2,4,48,192]{3,2,1,0:T(8,128)(2,1)S(1)}, bf16[2,4,48,192]{3,2,1,0:T(8,128)(2,1)S(1)}, u32[]{:S(2)}, u32[]{:S(2)}) %collective-permute-start.4) | collective-permute-done | bytes 147488 | tf_op jit(solution)/shard_map/ppermute | solution.py:38
  48.6 9.1 %all_to_all.15.got = bf16[4,256,128]{2,1,0:T(8,128)(2,1)S(1)} all-to-all(bf16[4,256,128]{2,1,0:T(8,128)(2,1)S(1)} %bitcast.10), channel_id=1, replica_groups=mesh['clip'=4,'row'=8,'tm'=16] {'clip'}, dimensions={0} | all-to-all | bytes 524288 | tf_op jit(solution)/shard_map/all_to_all | solution.py:375
  57.7 0.7 clip_sum.1
  58.3 15.4 %all-to-all-start.2 = ((bf16[16,16,128]{2,1,0:T(8,128)(2,1)}), bf16[16,16,128]{2,1,0:T(8,128)(2,1)S(1)}, u32[]{:S(2)}, u32[]{:S(2)}) async-start(bf16[16,16,128]{2,1,0:T(8,128)(2,1)} %bitcast.7), calls=%async_computation.2 | async-start | bytes 131072 | tf_op jit(solution)/shard_map/all_to_all | solution.py:384
  73.8 3.3 %input_grad.1 = f32[2,2,48,192]{3,2,1,0:T(8,128)} custom-call(bf16[27,192,192]{2,1,0:T(8,128)(2,1)} %bitcast.13, bf16[2,4,48,192]{3,2,1,0:T(8,128)(2,1)S(1)} %hidden_grad.1.tall, bf16[2,4,48,192]{3,2,1,0:T(8,128)(2,1)S(1)} %collective-permute-done.4.after), custom_call_target="tpu_custom_call" | custom-call | tf_op jit(solution)/shard_map/input_grad/pallas_call | solution.py:293
  77.1 9.6 %all-to-all-done.2.got = bf16[16,16,128]{2,1,0:T(8,128)(2,1)S(1)} async-done(((bf16[16,16,128]{2,1,0:T(8,128)(2,1)}), bf16[16,16,128]{2,1,0:T(8,128)(2,1)S(1)}, u32[]{:S(2)}, u32[]{:S(2)}) %all-to-all-start.2) | async-done | bytes 65568 | tf_op jit(solution)/shard_map/all_to_all | solution.py:384
  86.7 0.7 kernel_grad_sum.1
Async XLA Ops:
  1.5 6.6 %collective-permute-start.1 = (bf16[2,2,48,192]{3,2,1,0:T(8,128)(2,1)S(1)}, bf16[2,2,48,192]{3,2,1,0:T(8,128)(2,1)S(1)}, u32[]{:S(2)}, u32[]{:S(2)}) collective-permute-start(bf16[2,2,48,192]{3,2,1,0:T(8,128)(2,1)S(1)} %slice_bitcast_fusion), channel_id=1, source_target_pairs={{1,0},{2,1},{3,2},{4,3},{5,4},{6,5},{7,6},{8,7},{9,8},{10,9},{11,1... | collective-permute-start | bytes 221192 | tf_op jit(solution)/shard_map/ppermute | solution.py:38
  2.8 7.1 %collective-permute-start = (bf16[2,2,48,192]{3,2,1,0:T(8,128)(2,1)}, bf16[2,2,48,192]{3,2,1,0:T(8,128)(2,1)S(1)}, u32[]{:S(2)}, u32[]{:S(2)}) collective-permute-start(bf16[2,2,48,192]{3,2,1,0:T(8,128)(2,1)} %bitcast.17), channel_id=1, source_target_pairs={{0,1},{1,2},{2,3},{3,4},{4,5},{5,6},{6,7},{7,8},{8,9},{9,10},{10,1... | collective-permute-start | bytes 221192 | tf_op jit(solution)/shard_map/ppermute | solution.py:38
  10.9 7.7 %collective-permute-start.3 = (bf16[9,2,48,192]{3,2,1,0:T(8,128)(2,1)S(1)}, bf16[9,2,48,192]{3,2,1,0:T(8,128)(2,1)S(1)}, u32[]{:S(2)}, u32[]{:S(2)}) collective-permute-start(bf16[9,2,48,192]{3,2,1,0:T(8,128)(2,1)S(1)} %band.1.own), channel_id=1, source_target_pairs={{16,0},{32,16},{48,32},{64,48},{80,64},{96,80},{112,96},{17,1},{33... | collective-permute-start | bytes 995336 | tf_op jit(solution)/shard_map/ppermute | solution.py:38
  12.8 13.9 %collective-permute-start.2 = (bf16[9,2,48,192]{3,2,1,0:T(8,128)(2,1)S(1)}, bf16[9,2,48,192]{3,2,1,0:T(8,128)(2,1)S(1)}, u32[]{:S(2)}, u32[]{:S(2)}) collective-permute-start(bf16[9,2,48,192]{3,2,1,0:T(8,128)(2,1)S(1)} %band.1.own), channel_id=1, source_target_pairs={{0,16},{16,32},{32,48},{48,64},{64,80},{80,96},{96,112},{1,17},{17... | collective-permute-start | bytes 995336 | tf_op jit(solution)/shard_map/ppermute | solution.py:38
  30.4 15.5 %all-to-all-start = ((bf16[8,408,128]{2,1,0:T(8,128)(2,1)}), bf16[8,408,128]{2,1,0:T(8,128)(2,1)S(1)}, u32[]{:S(2)}, u32[]{:S(2)}) async-start(bf16[8,408,128]{2,1,0:T(8,128)(2,1)} %hidden_and_act.1), calls=%async_computation | async-start | bytes 1671168 | tf_op jit(solution)/shard_map/all_to_all | solution.py:341
  39.4 9.2 %collective-permute-start.4 = (bf16[2,4,48,192]{3,2,1,0:T(8,128)(2,1)S(1)}, bf16[2,4,48,192]{3,2,1,0:T(8,128)(2,1)S(1)}, u32[]{:S(2)}, u32[]{:S(2)}) collective-permute-start(bf16[2,4,48,192]{3,2,1,0:T(8,128)(2,1)S(1)} %hidden_grad.1.tall), channel_id=1, source_target_pairs={{1,0},{2,1},{3,2},{4,3},{5,4},{6,5},{7,6},{8,7},{9,8},{10,9},{11,1... | collective-permute-start | bytes 442376 | tf_op jit(solution)/shard_map/ppermute | solution.py:38
  58.3 28.3 %all-to-all-start.2 = ((bf16[16,16,128]{2,1,0:T(8,128)(2,1)}), bf16[16,16,128]{2,1,0:T(8,128)(2,1)S(1)}, u32[]{:S(2)}, u32[]{:S(2)}) async-start(bf16[16,16,128]{2,1,0:T(8,128)(2,1)} %bitcast.7), calls=%async_computation.2 | async-start | bytes 131072 | tf_op jit(solution)/shard_map/all_to_all | solution.py:384

commit v9 on v8

--- a/solution.py
+++ b/solution.py
@@ -54,12 +54,12 @@
     return moved.reshape(cells, chan)
 
 
-def conv(patch, weight, dot, first_shift, cols):
+def conv(patch, weight, dot, first_shift, cols, row_taps=(0, 1, 2)):
     total = None
     for k in (1, 0, 2):
         part = None
         for i in range(3):
-            for j in range(3):
+            for j in row_taps:
                 term = dot(patch(i, j), weight[i * 9 + j * 3 + k])
                 part = term if part is None else part + term
         if k != 1:
@@ -98,47 +98,68 @@
     return (width, span) == (24, 81)
 
 
-def silu_kernel(w_far, above, below, band, pay, xe, ps, w, sem):
+def own_kernel(w_far, band, turned, part, w, xe, ps, sem):
     _, rows, cols, chan = band.shape
     frames = 2
-    cells = frames * rows * cols
-    peers = pay.shape[0]
+    peers = turned.shape[0]
     width = chan // peers
     copies = start_copies([(w_far, w)], sem)
+    none = jnp.zeros((cols, chan), BF)
     for f in range(2 * frames):
         slot = (f + frames) % (2 * frames) * 4
-        xe[slot] = above[f, 1]
+        xe[slot] = none
         xe[slot + 1 : slot + 3] = band[f]
-        xe[slot + 3] = below[f, 0]
+        xe[slot + 3] = none
     ps[:, 0:EDGE, :] = jnp.zeros((10, EDGE, chan), F32)
     for a in range(5):
         for r in range(2):
             ps[a * 2 + r, EDGE : EDGE + cols, :] = band[4 + a, r].astype(F32)
-    turned = [
-        jnp.transpose(ps[2 * a : 2 * a + 2].reshape(2 * PITCH, chan)) for a in range(5)
-    ]
+    fields = [jnp.transpose(ps[2 * a : 2 * a + 2].reshape(2 * PITCH, chan)) for a in range(5)]
     for p in range(peers):
-        mine = jnp.concatenate([v[p * width : (p + 1) * width] for v in turned], axis=0)
-        pay[p, cells + cells // 2 :, :] = mine.astype(BF)
+        mine = jnp.concatenate([v[p * width : (p + 1) * width] for v in fields], axis=0)
+        turned[p] = mine.astype(BF)
     copies[0].wait()
 
     def patch(i, j):
         return blocks_of(xe, [(f + 2 - i) * 4 + j for f in range(2)], 2)
 
-    hidden = conv(patch, w, plain_dot, 1, cols)
+    part[...] = conv(patch, w, plain_dot, 1, cols)
+
+
+def silu_kernel(turned, w, part, above, below, pay, own, sem):
+    _, rows, cols, chan = above.shape
+    frames = 2
+    cells = frames * rows * cols
+    half = cells // 2
+    peers = pay.shape[0]
+    copies = [pltpu.make_async_copy(turned, pay.at[:, cells + half :], sem.at[peers])]
+    copies[0].start()
+
+    def top_patch(i, j):
+        frame = [above[(f + 2 - i + frames) % (2 * frames), 1] for f in range(2)]
+        return jnp.concatenate(frame, axis=0)
+
+    def bottom_patch(i, j):
+        frame = [below[(f + 2 - i + frames) % (2 * frames), 0] for f in range(2)]
+        return jnp.concatenate(frame, axis=0)
+
+    top = conv(top_patch, w, plain_dot, 1, cols, (0,)).reshape(frames, 1, cols, chan)
+    bottom = conv(bottom_patch, w, plain_dot, 1, cols, (2,)).reshape(frames, 1, cols, chan)
+    hidden = part[...] + jnp.concatenate([top, bottom], axis=1).reshape(cells, chan)
     act = hidden / (1.0 + jnp.exp(-hidden))
-    half = cells // 2
-    low = act[:, :128].astype(BF)
-    high = jnp.concatenate([act[:half, 128:], act[half:, 128:]], axis=1).astype(BF)
+    own[0:cells] = act[:, :128].astype(BF)
+    own[cells:] = jnp.concatenate([act[:half, 128:], act[half:, 128:]], axis=1).astype(BF)
     for p in range(peers):
-        pay[p, 0:cells, :] = low
-        pay[p, cells : cells + half, :] = high
-
-
-def hidden_grad_kernel(w1_far, w2_far, above, below, own, tall, xe, pe, w1, w2, sem):
+        copies.append(pltpu.make_async_copy(own, pay.at[p, 0 : cells + half], sem.at[p]))
+        copies[-1].start()
+    for copy in copies:
+        copy.wait()
+
+
+def hidden_grad_kernel(w2_far, w1, above, below, own, tall, xe, pe, w2, sem):
     _, rows, cols, chan = own.shape
     frames = 2
-    copies = start_copies([(w1_far, w1), (w2_far, w2)], sem)
+    copies = start_copies([(w2_far, w2)], sem)
     for f in range(2 * frames + 5):
         target, slot = (xe, (f + frames) % (2 * frames) * 6) if f < 4 else (pe, (f - 4) * 6)
         target[slot : slot + 2] = above[f]
@@ -283,10 +304,11 @@
     grad[...] = conv(patch, w1, transposed_dot, -1, cols).reshape(grad.shape)
 
 
-def call(body, name, limit, shapes, args, scratch, far=(), scalars=(), sems=0):
+def call(body, name, limit, shapes, args, scratch, far=(), scalars=(), sems=0, out_far=False):
     spaces = [pltpu.SMEM] * len(scalars) + [pltpu.HBM] * len(far) + [pltpu.VMEM] * len(args)
     far = [pltpu.with_memory_space_constraint(value, pltpu.HBM) for value in far]
-    outs = [jax.ShapeDtypeStruct(shape, kind) for shape, kind in shapes]
+    made = pltpu.HBM if out_far else jax.ShapeDtypeStruct
+    outs = [made(shape, kind) for shape, kind in shapes]
     buffers = [pltpu.VMEM(shape, kind) for shape, kind in scratch]
     if sems:
         buffers.append(pltpu.SemaphoreType.DMA((sems,)))
@@ -295,7 +317,7 @@
         name=name,
         out_shape=outs,
         in_specs=[pl.BlockSpec(memory_space=space) for space in spaces],
-        out_specs=[pl.BlockSpec(memory_space=pltpu.VMEM)] * len(outs),
+        out_specs=[pl.BlockSpec(memory_space=pltpu.HBM if out_far else pltpu.VMEM)] * len(outs),
         scratch_shapes=buffers,
         compiler_params=pltpu.CompilerParams(vmem_limit_bytes=limit * MIB),
     )(*scalars, *far, *args)
@@ -328,31 +350,36 @@
     )
     above = move(band, ("row",), (1,))
     below = move(band, ("row",), (-1,))
+    turned, own_part, w1_near = call(
+        own_kernel,
+        "own_rows",
+        8,
+        [((peers, 5 * width, 128), BF), ((cells, chan), F32), (w1.shape, BF)],
+        (band,),
+        [((16, cols, chan), BF), ((10, PITCH, chan), F32)],
+        far=(w1,),
+        sems=1,
+    )
     (pay,) = call(
         silu_kernel,
         "hidden_and_act",
-        16,
+        4,
         [((peers, cells + cells // 2 + 5 * width, 128), BF)],
-        (above, below, band),
-        [((16, cols, chan), BF), ((10, PITCH, chan), F32), (w1.shape, BF)],
-        far=(w1,),
-        sems=1,
+        (turned, w1_near, own_part, above, below),
+        [((cells + cells // 2, 128), BF)],
+        sems=peers + 1,
+        out_far=True,
     )
     got = lax.all_to_all(pay, "row", 0, 0)
     (tall,) = call(
         hidden_grad_kernel,
         "hidden_grad",
-        28,
+        14,
         [((frames, rows + 2, cols, chan), BF)],
-        (above, below, band),
-        [
-            ((24, cols, chan), BF),
-            ((30, cols, chan), BF),
-            (w1.shape, BF),
-            (w2.shape, BF),
-        ],
-        far=(w1, w2),
-        sems=2,
+        (w1_near, above, below, band),
+        [((24, cols, chan), BF), ((30, cols, chan), BF), (w2.shape, BF)],
+        far=(w2,),
+        sems=1,
     )
     after = move(tall, ("tm",), (-1,))
 
@@ -362,7 +389,7 @@
     (part,) = call(
         functools.partial(second_kernel, span),
         "kernel_grad_part",
-        16,
+        13,
         [((blocks,) + shape, BF)],
         (got,),
         [
@@ -394,7 +421,7 @@
     (input_grad,) = call(
         grad_kernel,
         "input_grad",
-        16,
+        8,
         [((frames, rows, cols, chan), F32)],
         (tall, after),
         [(w1.shape, BF)],

time: 87.9 us -> 87.7 us (level)
  waiting for transfers between devices: 29.1 us -> 23.9 us
  Pallas kernels: 16.6 us -> 18.9 us
  local copies, waits for them, and re-layouts: 0.9 us -> 2.68 us
    ppermute x5, waiting for transfers between devices: 14.3 us -> 11.5 us  [move(): lax.ppermute(value, axes if len(axes) > 1 else axes[0], route(sizes, steps))]
    pallas_call x7 -> x8, Pallas kernels: 16.6 us -> 18.9 us  [call(): pl.pallas_call(body, name=name, out_shape=outs, in_specs=[pl.BlockSpec(me...]
    unnamed x0 -> x4, local copies, waits for them, and re-layouts: none -> 1.78 us
    all_to_all x1, waiting for transfers between devices: 5.21 us -> 3.76 us  [local(): got = lax.all_to_all(pay, 'row', 0, 0)]
    all_to_all x1, waiting for transfers between devices: 9.61 us -> 8.69 us  [local(): by_step = lax.all_to_all(summed.reshape((steps,) + shape), 'tm', 0, 0)]
  transfers between devices with their start and end apart: 7 -> 7, of which waited for: 7 -> 7; matrix products, arithmetic and copies ran while one was open for 0% -> 0% of each run, Pallas kernels for 12% -> 17%
where the time goes in v9:
time: 87.7 us; the launch traced here: 87 us
  starting transfers between devices  31 us (35%)
  waiting for transfers between devices  23.9 us (27%)
  Pallas kernels  18.9 us (22%)
  blocking collectives  9.05 us (10%)
  local copies, waits for them, and re-layouts  2.68 us (3%)
  between operations  1.4 us (2%)
    pallas_call x8, Pallas kernels, call(): pl.pallas_call(body, name=name, out_shape=outs, in_specs=[pl.BlockSpec(me...  18.9 us
    all_to_all x1, starting transfers between devices, local(): by_step = lax.all_to_all(summed.reshape((steps,) + shape), 'tm', 0, 0)  15.4 us
    ppermute x5, waiting for transfers between devices, move(): lax.ppermute(value, axes if len(axes) > 1 else axes[0], route(sizes, steps))  11.5 us
    ppermute x5, starting transfers between devices, move(): lax.ppermute(value, axes if len(axes) > 1 else axes[0], route(sizes, steps))  11.5 us
    all_to_all x1, blocking collectives, local(): lax.all_to_all(part.reshape((clips, steps * shape[0], shape[1])), 'clip',...  9.05 us
    all_to_all x1, waiting for transfers between devices, local(): by_step = lax.all_to_all(summed.reshape((steps,) + shape), 'tm', 0, 0)  8.69 us
    all_to_all x1, starting transfers between devices, local(): got = lax.all_to_all(pay, 'row', 0, 0)  4.17 us
    all_to_all x1, waiting for transfers between devices, local(): got = lax.all_to_all(pay, 'row', 0, 0)  3.76 us
  transfers between devices with their start and end apart: 7, of which 7 were waited for; matrix products, arithmetic and copies ran while one was open for 0% of the time, Pallas kernels for 17%

profile of v9, /device:TPU:2, one launch (start us, length us, event | category | flops | bytes accessed | tf_op | source)
XLA Modules:
  0.0 87.0 jit_solution(8513791890338639596)
XLA Ops:
  0.6 0.9 %slice_bitcast_fusion = bf16[2,2,48,192]{3,2,1,0:T(8,128)(2,1)S(1)} fusion(bf16[1,4,2,48,192]{4,3,2,1,0:T(8,128)(2,1)} %param.6), kind=kLoop, calls=%fused_computation | loop fusion | bytes 147456 | tf_op jit(solution)/shard_map/slice | solution.py:339
  1.5 1.3 %collective-permute-start.1 = (bf16[2,2,48,192]{3,2,1,0:T(8,128)(2,1)S(1)}, bf16[2,2,48,192]{3,2,1,0:T(8,128)(2,1)S(1)}, u32[]{:S(2)}, u32[]{:S(2)}) collective-permute-start(bf16[2,2,48,192]{3,2,1,0:T(8,128)(2,1)S(1)} %slice_bitcast_fusion), channel_id=1, source_target_pairs={{1,0},{2,1},{3,2},{4,3},{5,4},{6,5},{7,6},{8,7},{9,8},{10,9},{11,1... | collective-permute-start | bytes 221192 | tf_op jit(solution)/shard_map/ppermute | solution.py:38
  2.8 4.6 %collective-permute-start = (bf16[2,2,48,192]{3,2,1,0:T(8,128)(2,1)}, bf16[2,2,48,192]{3,2,1,0:T(8,128)(2,1)S(1)}, u32[]{:S(2)}, u32[]{:S(2)}) collective-permute-start(bf16[2,2,48,192]{3,2,1,0:T(8,128)(2,1)} %bitcast.16), channel_id=1, source_target_pairs={{0,1},{1,2},{2,3},{3,4},{4,5},{5,6},{6,7},{7,8},{8,9},{9,10},{10,1... | collective-permute-start | bytes 221192 | tf_op jit(solution)/shard_map/ppermute | solution.py:38
  8.0 0.1 collective-permute-done.1.gnext
  8.1 1.8 %collective-permute-done.xprev = bf16[2,2,48,192]{3,2,1,0:T(8,128)(2,1)S(1)} collective-permute-done((bf16[2,2,48,192]{3,2,1,0:T(8,128)(2,1)}, bf16[2,2,48,192]{3,2,1,0:T(8,128)(2,1)S(1)}, u32[]{:S(2)}, u32[]{:S(2)}) %collective-permute-start) | collective-permute-done | bytes 73760 | tf_op jit(solution)/shard_map/ppermute | solution.py:38
  9.9 1.0 %band.1.own = bf16[9,2,48,192]{3,2,1,0:T(8,128)(2,1)S(1)} custom-call(s32[1]{0:T(128)S(6)} %copy.7.lengths, bf16[2,2,48,192]{3,2,1,0:T(8,128)(2,1)} %bitcast.17, bf16[4,2,48,192]{3,2,1,0:T(8,128)(2,1)} %bitcast.14, bf16[2,2,48,192]{3,2,1,0:T(8,128)(2,1)S(1)} %collective-permute-done.xprev, bf16[2,2,48,192]{3,2,1,0:T(8,128)(2,1)S(1)} %collective-permute-done.1.gnext), custom_call_target="tpu_custom_call" | custom-call | tf_op jit(solution)/shard_map/band/pallas_call | solution.py:315
  10.9 1.9 %collective-permute-start.3 = (bf16[9,2,48,192]{3,2,1,0:T(8,128)(2,1)S(1)}, bf16[9,2,48,192]{3,2,1,0:T(8,128)(2,1)S(1)}, u32[]{:S(2)}, u32[]{:S(2)}) collective-permute-start(bf16[9,2,48,192]{3,2,1,0:T(8,128)(2,1)S(1)} %band.1.own), channel_id=1, source_target_pairs={{16,0},{32,16},{48,32},{64,48},{80,64},{96,80},{112,96},{17,1},{33... | collective-permute-start | bytes 995336 | tf_op jit(solution)/shard_map/ppermute | solution.py:38
  12.8 2.4 %collective-permute-start.2 = (bf16[9,2,48,192]{3,2,1,0:T(8,128)(2,1)S(1)}, bf16[9,2,48,192]{3,2,1,0:T(8,128)(2,1)S(1)}, u32[]{:S(2)}, u32[]{:S(2)}) collective-permute-start(bf16[9,2,48,192]{3,2,1,0:T(8,128)(2,1)S(1)} %band.1.own), channel_id=1, source_target_pairs={{0,16},{16,32},{32,48},{48,64},{64,80},{80,96},{96,112},{1,17},{17... | collective-permute-start | bytes 995336 | tf_op jit(solution)/shard_map/ppermute | solution.py:38
  15.3 2.6 %own_rows.1 = (bf16[8,120,128]{2,1,0:T(8,128)(2,1)S(1)}, f32[192,192]{1,0:T(8,128)S(1)}, bf16[27,192,192]{2,1,0:T(8,128)(2,1)S(1)}) custom-call(bf16[27,192,192]{2,1,0:T(8,128)(2,1)} %bitcast.11, bf16[9,2,48,192]{3,2,1,0:T(8,128)(2,1)S(1)} %band.1.own), custom_call_target="tpu_custom_call" | custom-call | tf_op jit(solution)/shard_map/own_rows/pallas_call | solution.py:315
  17.9 0.8 collective-permute-done.3.below
  18.6 8.1 %collective-permute-done.2.above = bf16[9,2,48,192]{3,2,1,0:T(8,128)(2,1)S(1)} collective-permute-done((bf16[9,2,48,192]{3,2,1,0:T(8,128)(2,1)S(1)}, bf16[9,2,48,192]{3,2,1,0:T(8,128)(2,1)S(1)}, u32[]{:S(2)}, u32[]{:S(2)}) %collective-permute-start.2) | collective-permute-done | bytes 331808 | tf_op jit(solution)/shard_map/ppermute | solution.py:38
  26.7 1.4 %hidden_and_act.1 = bf16[8,408,128]{2,1,0:T(8,128)(2,1)} custom-call(bf16[8,120,128]{2,1,0:T(8,128)(2,1)S(1)} %get-tuple-element.8.turned, bf16[27,192,192]{2,1,0:T(8,128)(2,1)S(1)} %get-tuple-element.7.w1.w, f32[192,192]{1,0:T(8,128)S(1)} %get-tuple-element.9.part, bf16[9,2,48,192]{3,2,1,0:T(8,128)(2,1)S(1)} %collective-permute-done.2.above, ...), custom_call_target="tpu_custom_call" | custom-call | tf_op jit(solution)/shard_map/hidden_and_act/pallas_call | solution.py:315
  28.2 0.0 copy-start
  28.2 0.8 copy-done
  28.9 4.2 %all-to-all-start = ((bf16[8,408,128]{2,1,0:T(8,128)(2,1)}), bf16[8,408,128]{2,1,0:T(8,128)(2,1)}, u32[]{:S(2)}, u32[]{:S(2)}) async-start(bf16[8,408,128]{2,1,0:T(8,128)(2,1)} %hidden_and_act.1), calls=%async_computation | async-start | bytes 1671168 | tf_op jit(solution)/shard_map/all_to_all | solution.py:373
  33.1 0.0 copy-start.1
  33.1 1.0 %copy-done.1 = bf16[9,2,48,192]{3,2,1,0:T(8,128)(2,1)S(1)} copy-done((bf16[9,2,48,192]{3,2,1,0:T(8,128)(2,1)S(1)}, bf16[9,2,48,192]{3,2,1,0:T(8,128)(2,1)}, u32[]{:S(2)}) %copy-start.1) | copy-done | bytes 331800
  34.1 5.4 %hidden_grad.1.tall = bf16[2,4,48,192]{3,2,1,0:T(8,128)(2,1)} custom-call(bf16[27,192,192]{2,1,0:T(8,128)(2,1)} %bitcast.13, bf16[27,192,192]{2,1,0:T(8,128)(2,1)S(1)} %get-tuple-element.7.w1.w, bf16[9,2,48,192]{3,2,1,0:T(8,128)(2,1)S(1)} %copy-done.1, bf16[9,2,48,192]{3,2,1,0:T(8,128)(2,1)S(1)} %collective-permute-done.3.below, ...), custom_call_target="tpu_custom_call" | custom-call | tf_op jit(solution)/shard_map/hidden_grad/pallas_call | solution.py:315
  39.5 1.3 %collective-permute-start.4 = (bf16[2,4,48,192]{3,2,1,0:T(8,128)(2,1)}, bf16[2,4,48,192]{3,2,1,0:T(8,128)(2,1)S(1)}, u32[]{:S(2)}, u32[]{:S(2)}) collective-permute-start(bf16[2,4,48,192]{3,2,1,0:T(8,128)(2,1)} %hidden_grad.1.tall), channel_id=1, source_target_pairs={{1,0},{2,1},{3,2},{4,3},{5,4},{6,5},{7,6},{8,7},{9,8},{10,9},{11,1... | collective-permute-start | bytes 442376 | tf_op jit(solution)/shard_map/ppermute | solution.py:38
  40.8 3.8 %all-to-all-done.got = bf16[8,408,128]{2,1,0:T(8,128)(2,1)} async-done(((bf16[8,408,128]{2,1,0:T(8,128)(2,1)}), bf16[8,408,128]{2,1,0:T(8,128)(2,1)}, u32[]{:S(2)}, u32[]{:S(2)}) %all-to-all-start) | async-done | bytes 835616 | tf_op jit(solution)/shard_map/all_to_all | solution.py:373
  44.6 2.9 %kernel_grad_part.1 = bf16[64,16,128]{2,1,0:T(8,128)(2,1)S(1)} custom-call(bf16[8,408,128]{2,1,0:T(8,128)(2,1)} %all-to-all-done.got), custom_call_target="tpu_custom_call" | custom-call | tf_op jit(solution)/shard_map/kernel_grad_part/pallas_call | solution.py:315
  47.5 0.8 collective-permute-done.4.after
  48.3 9.1 %all_to_all.15.got = bf16[4,256,128]{2,1,0:T(8,128)(2,1)S(1)} all-to-all(bf16[4,256,128]{2,1,0:T(8,128)(2,1)S(1)} %bitcast.10), channel_id=1, replica_groups=mesh['clip'=4,'row'=8,'tm'=16] {'clip'}, dimensions={0} | all-to-all | bytes 524288 | tf_op jit(solution)/shard_map/all_to_all | solution.py:402
  57.3 0.7 clip_sum.1
  58.0 15.4 %all-to-all-start.2 = ((bf16[16,16,128]{2,1,0:T(8,128)(2,1)}), bf16[16,16,128]{2,1,0:T(8,128)(2,1)S(1)}, u32[]{:S(2)}, u32[]{:S(2)}) async-start(bf16[16,16,128]{2,1,0:T(8,128)(2,1)} %bitcast.7), calls=%async_computation.2 | async-start | bytes 131072 | tf_op jit(solution)/shard_map/all_to_all | solution.py:411
  73.4 4.2 %input_grad.1 = f32[2,2,48,192]{3,2,1,0:T(8,128)} custom-call(bf16[27,192,192]{2,1,0:T(8,128)(2,1)} %bitcast.12, bf16[2,4,48,192]{3,2,1,0:T(8,128)(2,1)} %hidden_grad.1.tall, bf16[2,4,48,192]{3,2,1,0:T(8,128)(2,1)S(1)} %collective-permute-done.4.after), custom_call_target="tpu_custom_call" | custom-call | tf_op jit(solution)/shard_map/input_grad/pallas_call | solution.py:315
  77.6 8.7 %all-to-all-done.2.got = bf16[16,16,128]{2,1,0:T(8,128)(2,1)S(1)} async-done(((bf16[16,16,128]{2,1,0:T(8,128)(2,1)}), bf16[16,16,128]{2,1,0:T(8,128)(2,1)S(1)}, u32[]{:S(2)}, u32[]{:S(2)}) %all-to-all-start.2) | async-done | bytes 65568 | tf_op jit(solution)/shard_map/all_to_all | solution.py:411
  86.3 0.7 kernel_grad_sum.1
Async XLA Ops:
  1.5 6.6 %collective-permute-start.1 = (bf16[2,2,48,192]{3,2,1,0:T(8,128)(2,1)S(1)}, bf16[2,2,48,192]{3,2,1,0:T(8,128)(2,1)S(1)}, u32[]{:S(2)}, u32[]{:S(2)}) collective-permute-start(bf16[2,2,48,192]{3,2,1,0:T(8,128)(2,1)S(1)} %slice_bitcast_fusion), channel_id=1, source_target_pairs={{1,0},{2,1},{3,2},{4,3},{5,4},{6,5},{7,6},{8,7},{9,8},{10,9},{11,1... | collective-permute-start | bytes 221192 | tf_op jit(solution)/shard_map/ppermute | solution.py:38
  2.8 7.1 %collective-permute-start = (bf16[2,2,48,192]{3,2,1,0:T(8,128)(2,1)}, bf16[2,2,48,192]{3,2,1,0:T(8,128)(2,1)S(1)}, u32[]{:S(2)}, u32[]{:S(2)}) collective-permute-start(bf16[2,2,48,192]{3,2,1,0:T(8,128)(2,1)} %bitcast.16), channel_id=1, source_target_pairs={{0,1},{1,2},{2,3},{3,4},{4,5},{5,6},{6,7},{7,8},{8,9},{9,10},{10,1... | collective-permute-start | bytes 221192 | tf_op jit(solution)/shard_map/ppermute | solution.py:38
  10.9 7.7 %collective-permute-start.3 = (bf16[9,2,48,192]{3,2,1,0:T(8,128)(2,1)S(1)}, bf16[9,2,48,192]{3,2,1,0:T(8,128)(2,1)S(1)}, u32[]{:S(2)}, u32[]{:S(2)}) collective-permute-start(bf16[9,2,48,192]{3,2,1,0:T(8,128)(2,1)S(1)} %band.1.own), channel_id=1, source_target_pairs={{16,0},{32,16},{48,32},{64,48},{80,64},{96,80},{112,96},{17,1},{33... | collective-permute-start | bytes 995336 | tf_op jit(solution)/shard_map/ppermute | solution.py:38
  12.8 13.9 %collective-permute-start.2 = (bf16[9,2,48,192]{3,2,1,0:T(8,128)(2,1)S(1)}, bf16[9,2,48,192]{3,2,1,0:T(8,128)(2,1)S(1)}, u32[]{:S(2)}, u32[]{:S(2)}) collective-permute-start(bf16[9,2,48,192]{3,2,1,0:T(8,128)(2,1)S(1)} %band.1.own), channel_id=1, source_target_pairs={{0,16},{16,32},{32,48},{48,64},{64,80},{80,96},{96,112},{1,17},{17... | collective-permute-start | bytes 995336 | tf_op jit(solution)/shard_map/ppermute | solution.py:38
  28.2 0.8 copy-start
  28.9 15.6 %all-to-all-start = ((bf16[8,408,128]{2,1,0:T(8,128)(2,1)}), bf16[8,408,128]{2,1,0:T(8,128)(2,1)}, u32[]{:S(2)}, u32[]{:S(2)}) async-start(bf16[8,408,128]{2,1,0:T(8,128)(2,1)} %hidden_and_act.1), calls=%async_computation | async-start | bytes 1671168 | tf_op jit(solution)/shard_map/all_to_all | solution.py:373
  33.1 1.0 %copy-start.1 = (bf16[9,2,48,192]{3,2,1,0:T(8,128)(2,1)S(1)}, bf16[9,2,48,192]{3,2,1,0:T(8,128)(2,1)}, u32[]{:S(2)}) copy-start(bf16[9,2,48,192]{3,2,1,0:T(8,128)(2,1)} %copy-done) | copy-start | bytes 995332
  39.5 8.7 %collective-permute-start.4 = (bf16[2,4,48,192]{3,2,1,0:T(8,128)(2,1)}, bf16[2,4,48,192]{3,2,1,0:T(8,128)(2,1)S(1)}, u32[]{:S(2)}, u32[]{:S(2)}) collective-permute-start(bf16[2,4,48,192]{3,2,1,0:T(8,128)(2,1)} %hidden_grad.1.tall), channel_id=1, source_target_pairs={{1,0},{2,1},{3,2},{4,3},{5,4},{6,5},{7,6},{8,7},{9,8},{10,9},{11,1... | collective-permute-start | bytes 442376 | tf_op jit(solution)/shard_map/ppermute | solution.py:38
  58.0 28.4 %all-to-all-start.2 = ((bf16[16,16,128]{2,1,0:T(8,128)(2,1)}), bf16[16,16,128]{2,1,0:T(8,128)(2,1)S(1)}, u32[]{:S(2)}, u32[]{:S(2)}) async-start(bf16[16,16,128]{2,1,0:T(8,128)(2,1)} %bitcast.7), calls=%async_computation.2 | async-start | bytes 131072 | tf_op jit(solution)/shard_map/all_to_all | solution.py:411

commit v10 on v9

--- a/solution.py
+++ b/solution.py
@@ -156,10 +156,10 @@
         copy.wait()
 
 
-def hidden_grad_kernel(w2_far, w1, above, below, own, tall, xe, pe, w2, sem):
+def hidden_grad_kernel(w1_far, w2_far, above, below, own, tall, xe, pe, w1, w2, sem):
     _, rows, cols, chan = own.shape
     frames = 2
-    copies = start_copies([(w2_far, w2)], sem)
+    copies = start_copies([(w1_far, w1), (w2_far, w2)], sem)
     for f in range(2 * frames + 5):
         target, slot = (xe, (f + frames) % (2 * frames) * 6) if f < 4 else (pe, (f - 4) * 6)
         target[slot : slot + 2] = above[f]
@@ -376,10 +376,15 @@
         "hidden_grad",
         14,
         [((frames, rows + 2, cols, chan), BF)],
-        (w1_near, above, below, band),
-        [((24, cols, chan), BF), ((30, cols, chan), BF), (w2.shape, BF)],
-        far=(w2,),
-        sems=1,
+        (above, below, band),
+        [
+            ((24, cols, chan), BF),
+            ((30, cols, chan), BF),
+            (w1.shape, BF),
+            (w2.shape, BF),
+        ],
+        far=(w1, w2),
+        sems=2,
     )
     after = move(tall, ("tm",), (-1,))
 

time: 87.7 us -> 87.8 us (level)
  starting transfers between devices: 31 us -> 34 us
  Pallas kernels: 18.9 us -> 16.9 us
  blocking collectives: 9.05 us -> 10.9 us
  local copies, waits for them, and re-layouts: 2.68 us -> 0.9 us
    ppermute x5, waiting for transfers between devices: 11.5 us -> 8.32 us  [move(): lax.ppermute(value, axes if len(axes) > 1 else axes[0], route(sizes, steps))]
    pallas_call x8, Pallas kernels: 18.9 us -> 16.9 us  [call(): pl.pallas_call(body, name=name, out_shape=outs, in_specs=[pl.BlockSpec(me...]
    all_to_all x1, blocking collectives: 9.05 us -> 10.9 us  [local(): lax.all_to_all(part.reshape((clips, steps * shape[0], shape[1])), 'clip',...]
    unnamed x4 -> x0, local copies, waits for them, and re-layouts: 1.78 us -> none
    all_to_all x1, starting transfers between devices: 4.17 us -> 5.92 us  [local(): got = lax.all_to_all(pay, 'row', 0, 0)]
    all_to_all x1, waiting for transfers between devices: 3.76 us -> 5.42 us  [local(): got = lax.all_to_all(pay, 'row', 0, 0)]
  transfers between devices with their start and end apart: 7 -> 7, of which waited for: 7 -> 6; matrix products, arithmetic and copies ran while one was open for 0% -> 1% of each run, Pallas kernels for 17% -> 15%
where the time goes in v10:
time: 87.8 us; the launch traced here: 87.3 us
  starting transfers between devices  34 us (39%)
  waiting for transfers between devices  23.2 us (26%)
  Pallas kernels  16.9 us (19%)
  blocking collectives  10.9 us (12%)
  between operations  1.38 us (2%)
  local copies, waits for them, and re-layouts  0.9 us (1%)
    pallas_call x8, Pallas kernels, call(): pl.pallas_call(body, name=name, out_shape=outs, in_specs=[pl.BlockSpec(me...  16.9 us
    all_to_all x1, starting transfers between devices, local(): by_step = lax.all_to_all(summed.reshape((steps,) + shape), 'tm', 0, 0)  16.1 us
    ppermute x5, starting transfers between devices, move(): lax.ppermute(value, axes if len(axes) > 1 else axes[0], route(sizes, steps))  12 us
    all_to_all x1, blocking collectives, local(): lax.all_to_all(part.reshape((clips, steps * shape[0], shape[1])), 'clip',...  10.9 us
    all_to_all x1, waiting for transfers between devices, local(): by_step = lax.all_to_all(summed.reshape((steps,) + shape), 'tm', 0, 0)  9.5 us
    ppermute x5, waiting for transfers between devices, move(): lax.ppermute(value, axes if len(axes) > 1 else axes[0], route(sizes, steps))  8.32 us
    all_to_all x1, starting transfers between devices, local(): got = lax.all_to_all(pay, 'row', 0, 0)  5.92 us
    all_to_all x1, waiting for transfers between devices, local(): got = lax.all_to_all(pay, 'row', 0, 0)  5.42 us
  transfers between devices with their start and end apart: 7, of which 6 were waited for; matrix products, arithmetic and copies ran while one was open for 1% of the time, Pallas kernels for 15%

profile of v10, /device:TPU:2, one launch (start us, length us, event | category | flops | bytes accessed | tf_op | source)
XLA Modules:
  0.0 87.3 jit_solution(8526520342271529270)
XLA Ops:
  0.6 3.8 %collective-permute-start = (bf16[2,2,48,192]{3,2,1,0:T(8,128)(2,1)}, bf16[2,2,48,192]{3,2,1,0:T(8,128)(2,1)S(1)}, u32[]{:S(2)}, u32[]{:S(2)}) collective-permute-start(bf16[2,2,48,192]{3,2,1,0:T(8,128)(2,1)} %bitcast.17), channel_id=1, source_target_pairs={{0,1},{1,2},{2,3},{3,4},{4,5},{5,6},{6,7},{7,8},{8,9},{9,10},{10,1... | collective-permute-start | bytes 221192 | tf_op jit(solution)/shard_map/ppermute | solution.py:38
  4.5 0.9 %slice_bitcast_fusion = bf16[2,2,48,192]{3,2,1,0:T(8,128)(2,1)S(1)} fusion(bf16[1,4,2,48,192]{4,3,2,1,0:T(8,128)(2,1)} %param.6), kind=kLoop, calls=%fused_computation | loop fusion | bytes 147456 | tf_op jit(solution)/shard_map/slice | solution.py:339
  5.4 1.3 %collective-permute-start.1 = (bf16[2,2,48,192]{3,2,1,0:T(8,128)(2,1)S(1)}, bf16[2,2,48,192]{3,2,1,0:T(8,128)(2,1)S(1)}, u32[]{:S(2)}, u32[]{:S(2)}) collective-permute-start(bf16[2,2,48,192]{3,2,1,0:T(8,128)(2,1)S(1)} %slice_bitcast_fusion), channel_id=1, source_target_pairs={{1,0},{2,1},{3,2},{4,3},{5,4},{6,5},{7,6},{8,7},{9,8},{10,9},{11,1... | collective-permute-start | bytes 221192 | tf_op jit(solution)/shard_map/ppermute | solution.py:38
  7.3 0.0 collective-permute-done.xprev
  7.3 4.6 %collective-permute-done.1.gnext = bf16[2,2,48,192]{3,2,1,0:T(8,128)(2,1)S(1)} collective-permute-done((bf16[2,2,48,192]{3,2,1,0:T(8,128)(2,1)S(1)}, bf16[2,2,48,192]{3,2,1,0:T(8,128)(2,1)S(1)}, u32[]{:S(2)}, u32[]{:S(2)}) %collective-permute-start.1) | collective-permute-done | bytes 73760 | tf_op jit(solution)/shard_map/ppermute | solution.py:38
  11.9 1.0 %band.1.own = bf16[9,2,48,192]{3,2,1,0:T(8,128)(2,1)S(1)} custom-call(s32[1]{0:T(128)S(6)} %copy.7.lengths, bf16[2,2,48,192]{3,2,1,0:T(8,128)(2,1)} %bitcast.18, bf16[4,2,48,192]{3,2,1,0:T(8,128)(2,1)} %bitcast.15, bf16[2,2,48,192]{3,2,1,0:T(8,128)(2,1)S(1)} %collective-permute-done.xprev, bf16[2,2,48,192]{3,2,1,0:T(8,128)(2,1)S(1)} %collective-permute-done.1.gnext), custom_call_target="tpu_custom_call" | custom-call | tf_op jit(solution)/shard_map/band/pallas_call | solution.py:315
  12.9 1.9 %collective-permute-start.2 = (bf16[9,2,48,192]{3,2,1,0:T(8,128)(2,1)S(1)}, bf16[9,2,48,192]{3,2,1,0:T(8,128)(2,1)S(1)}, u32[]{:S(2)}, u32[]{:S(2)}) collective-permute-start(bf16[9,2,48,192]{3,2,1,0:T(8,128)(2,1)S(1)} %band.1.own), channel_id=1, source_target_pairs={{0,16},{16,32},{32,48},{48,64},{64,80},{80,96},{96,112},{1,17},{17... | collective-permute-start | bytes 995336 | tf_op jit(solution)/shard_map/ppermute | solution.py:38
  14.8 3.6 %collective-permute-start.3 = (bf16[9,2,48,192]{3,2,1,0:T(8,128)(2,1)S(1)}, bf16[9,2,48,192]{3,2,1,0:T(8,128)(2,1)S(1)}, u32[]{:S(2)}, u32[]{:S(2)}) collective-permute-start(bf16[9,2,48,192]{3,2,1,0:T(8,128)(2,1)S(1)} %band.1.own), channel_id=1, source_target_pairs={{16,0},{32,16},{48,32},{64,48},{80,64},{96,80},{112,96},{17,1},{33... | collective-permute-start | bytes 995336 | tf_op jit(solution)/shard_map/ppermute | solution.py:38
  18.5 2.6 %own_rows.1 = (bf16[8,120,128]{2,1,0:T(8,128)(2,1)S(1)}, f32[192,192]{1,0:T(8,128)S(1)}, bf16[27,192,192]{2,1,0:T(8,128)(2,1)S(1)}) custom-call(bf16[27,192,192]{2,1,0:T(8,128)(2,1)} %bitcast.11, bf16[9,2,48,192]{3,2,1,0:T(8,128)(2,1)S(1)} %band.1.own), custom_call_target="tpu_custom_call" | custom-call | tf_op jit(solution)/shard_map/own_rows/pallas_call | solution.py:315
  21.1 1.4 %collective-permute-done.2.above = bf16[9,2,48,192]{3,2,1,0:T(8,128)(2,1)S(1)} collective-permute-done((bf16[9,2,48,192]{3,2,1,0:T(8,128)(2,1)S(1)}, bf16[9,2,48,192]{3,2,1,0:T(8,128)(2,1)S(1)}, u32[]{:S(2)}, u32[]{:S(2)}) %collective-permute-start.2) | collective-permute-done | bytes 331808 | tf_op jit(solution)/shard_map/ppermute | solution.py:38
  22.5 1.8 %collective-permute-done.3.below = bf16[9,2,48,192]{3,2,1,0:T(8,128)(2,1)S(1)} collective-permute-done((bf16[9,2,48,192]{3,2,1,0:T(8,128)(2,1)S(1)}, bf16[9,2,48,192]{3,2,1,0:T(8,128)(2,1)S(1)}, u32[]{:S(2)}, u32[]{:S(2)}) %collective-permute-start.3) | collective-permute-done | bytes 331808 | tf_op jit(solution)/shard_map/ppermute | solution.py:38
  24.3 1.4 %hidden_and_act.1 = bf16[8,408,128]{2,1,0:T(8,128)(2,1)} custom-call(bf16[8,120,128]{2,1,0:T(8,128)(2,1)S(1)} %get-tuple-element.7.turned, bf16[27,192,192]{2,1,0:T(8,128)(2,1)S(1)} %get-tuple-element.8.w, f32[192,192]{1,0:T(8,128)S(1)} %get-tuple-element.9.part, bf16[9,2,48,192]{3,2,1,0:T(8,128)(2,1)S(1)} %collective-permute-done.2.above, ...), custom_call_target="tpu_custom_call" | custom-call | tf_op jit(solution)/shard_map/hidden_and_act/pallas_call | solution.py:315
  25.7 5.9 %all-to-all-start = ((bf16[8,408,128]{2,1,0:T(8,128)(2,1)}), bf16[8,408,128]{2,1,0:T(8,128)(2,1)S(1)}, u32[]{:S(2)}, u32[]{:S(2)}) async-start(bf16[8,408,128]{2,1,0:T(8,128)(2,1)} %hidden_and_act.1), calls=%async_computation | async-start | bytes 1671168 | tf_op jit(solution)/shard_map/all_to_all | solution.py:373
  31.6 5.5 %hidden_grad.1.tall = bf16[2,4,48,192]{3,2,1,0:T(8,128)(2,1)S(1)} custom-call(bf16[27,192,192]{2,1,0:T(8,128)(2,1)} %bitcast.12, bf16[27,192,192]{2,1,0:T(8,128)(2,1)} %bitcast.14, bf16[9,2,48,192]{3,2,1,0:T(8,128)(2,1)S(1)} %collective-permute-done.2.above, bf16[9,2,48,192]{3,2,1,0:T(8,128)(2,1)S(1)} %collective-permute-done.3.below, ...), custom_call_target="tpu_custom_call" | custom-call | tf_op jit(solution)/shard_map/hidden_grad/pallas_call | solution.py:315
  37.1 1.3 %collective-permute-start.4 = (bf16[2,4,48,192]{3,2,1,0:T(8,128)(2,1)S(1)}, bf16[2,4,48,192]{3,2,1,0:T(8,128)(2,1)S(1)}, u32[]{:S(2)}, u32[]{:S(2)}) collective-permute-start(bf16[2,4,48,192]{3,2,1,0:T(8,128)(2,1)S(1)} %hidden_grad.1.tall), channel_id=1, source_target_pairs={{1,0},{2,1},{3,2},{4,3},{5,4},{6,5},{7,6},{8,7},{9,8},{10,9},{11,1... | collective-permute-start | bytes 442376 | tf_op jit(solution)/shard_map/ppermute | solution.py:38
  38.4 5.4 %all-to-all-done.got = bf16[8,408,128]{2,1,0:T(8,128)(2,1)S(1)} async-done(((bf16[8,408,128]{2,1,0:T(8,128)(2,1)}), bf16[8,408,128]{2,1,0:T(8,128)(2,1)S(1)}, u32[]{:S(2)}, u32[]{:S(2)}) %all-to-all-start) | async-done | bytes 835616 | tf_op jit(solution)/shard_map/all_to_all | solution.py:373
  43.8 1.7 %kernel_grad_part.1 = bf16[64,16,128]{2,1,0:T(8,128)(2,1)S(1)} custom-call(bf16[8,408,128]{2,1,0:T(8,128)(2,1)S(1)} %all-to-all-done.got), custom_call_target="tpu_custom_call" | custom-call | tf_op jit(solution)/shard_map/kernel_grad_part/pallas_call | solution.py:315
  45.5 0.6 collective-permute-done.4.after
  46.1 10.9 %all_to_all.15.got = bf16[4,256,128]{2,1,0:T(8,128)(2,1)S(1)} all-to-all(bf16[4,256,128]{2,1,0:T(8,128)(2,1)S(1)} %bitcast.10), channel_id=1, replica_groups=mesh['clip'=4,'row'=8,'tm'=16] {'clip'}, dimensions={0} | all-to-all | bytes 524288 | tf_op jit(solution)/shard_map/all_to_all | solution.py:407
  57.1 0.7 clip_sum.1
  57.7 16.1 %all-to-all-start.2 = ((bf16[16,16,128]{2,1,0:T(8,128)(2,1)}), bf16[16,16,128]{2,1,0:T(8,128)(2,1)S(1)}, u32[]{:S(2)}, u32[]{:S(2)}) async-start(bf16[16,16,128]{2,1,0:T(8,128)(2,1)} %bitcast.7), calls=%async_computation.2 | async-start | bytes 131072 | tf_op jit(solution)/shard_map/all_to_all | solution.py:416
  73.8 3.3 %input_grad.1 = f32[2,2,48,192]{3,2,1,0:T(8,128)} custom-call(bf16[27,192,192]{2,1,0:T(8,128)(2,1)} %bitcast.13, bf16[2,4,48,192]{3,2,1,0:T(8,128)(2,1)S(1)} %hidden_grad.1.tall, bf16[2,4,48,192]{3,2,1,0:T(8,128)(2,1)S(1)} %collective-permute-done.4.after), custom_call_target="tpu_custom_call" | custom-call | tf_op jit(solution)/shard_map/input_grad/pallas_call | solution.py:315
  77.1 9.5 %all-to-all-done.2.got = bf16[16,16,128]{2,1,0:T(8,128)(2,1)S(1)} async-done(((bf16[16,16,128]{2,1,0:T(8,128)(2,1)}), bf16[16,16,128]{2,1,0:T(8,128)(2,1)S(1)}, u32[]{:S(2)}, u32[]{:S(2)}) %all-to-all-start.2) | async-done | bytes 65568 | tf_op jit(solution)/shard_map/all_to_all | solution.py:416
  86.6 0.7 kernel_grad_sum.1
Async XLA Ops:
  0.6 6.7 %collective-permute-start = (bf16[2,2,48,192]{3,2,1,0:T(8,128)(2,1)}, bf16[2,2,48,192]{3,2,1,0:T(8,128)(2,1)S(1)}, u32[]{:S(2)}, u32[]{:S(2)}) collective-permute-start(bf16[2,2,48,192]{3,2,1,0:T(8,128)(2,1)} %bitcast.17), channel_id=1, source_target_pairs={{0,1},{1,2},{2,3},{3,4},{4,5},{5,6},{6,7},{7,8},{8,9},{9,10},{10,1... | collective-permute-start | bytes 221192 | tf_op jit(solution)/shard_map/ppermute | solution.py:38
  5.4 6.5 %collective-permute-start.1 = (bf16[2,2,48,192]{3,2,1,0:T(8,128)(2,1)S(1)}, bf16[2,2,48,192]{3,2,1,0:T(8,128)(2,1)S(1)}, u32[]{:S(2)}, u32[]{:S(2)}) collective-permute-start(bf16[2,2,48,192]{3,2,1,0:T(8,128)(2,1)S(1)} %slice_bitcast_fusion), channel_id=1, source_target_pairs={{1,0},{2,1},{3,2},{4,3},{5,4},{6,5},{7,6},{8,7},{9,8},{10,9},{11,1... | collective-permute-start | bytes 221192 | tf_op jit(solution)/shard_map/ppermute | solution.py:38
  12.9 9.6 %collective-permute-start.2 = (bf16[9,2,48,192]{3,2,1,0:T(8,128)(2,1)S(1)}, bf16[9,2,48,192]{3,2,1,0:T(8,128)(2,1)S(1)}, u32[]{:S(2)}, u32[]{:S(2)}) collective-permute-start(bf16[9,2,48,192]{3,2,1,0:T(8,128)(2,1)S(1)} %band.1.own), channel_id=1, source_target_pairs={{0,16},{16,32},{32,48},{48,64},{64,80},{80,96},{96,112},{1,17},{17... | collective-permute-start | bytes 995336 | tf_op jit(solution)/shard_map/ppermute | solution.py:38
  14.8 9.4 %collective-permute-start.3 = (bf16[9,2,48,192]{3,2,1,0:T(8,128)(2,1)S(1)}, bf16[9,2,48,192]{3,2,1,0:T(8,128)(2,1)S(1)}, u32[]{:S(2)}, u32[]{:S(2)}) collective-permute-start(bf16[9,2,48,192]{3,2,1,0:T(8,128)(2,1)S(1)} %band.1.own), channel_id=1, source_target_pairs={{16,0},{32,16},{48,32},{64,48},{80,64},{96,80},{112,96},{17,1},{33... | collective-permute-start | bytes 995336 | tf_op jit(solution)/shard_map/ppermute | solution.py:38
  25.7 18.1 %all-to-all-start = ((bf16[8,408,128]{2,1,0:T(8,128)(2,1)}), bf16[8,408,128]{2,1,0:T(8,128)(2,1)S(1)}, u32[]{:S(2)}, u32[]{:S(2)}) async-start(bf16[8,408,128]{2,1,0:T(8,128)(2,1)} %hidden_and_act.1), calls=%async_computation | async-start | bytes 1671168 | tf_op jit(solution)/shard_map/all_to_all | solution.py:373
  37.1 9.0 %collective-permute-start.4 = (bf16[2,4,48,192]{3,2,1,0:T(8,128)(2,1)S(1)}, bf16[2,4,48,192]{3,2,1,0:T(8,128)(2,1)S(1)}, u32[]{:S(2)}, u32[]{:S(2)}) collective-permute-start(bf16[2,4,48,192]{3,2,1,0:T(8,128)(2,1)S(1)} %hidden_grad.1.tall), channel_id=1, source_target_pairs={{1,0},{2,1},{3,2},{4,3},{5,4},{6,5},{7,6},{8,7},{9,8},{10,9},{11,1... | collective-permute-start | bytes 442376 | tf_op jit(solution)/shard_map/ppermute | solution.py:38
  57.7 28.9 %all-to-all-start.2 = ((bf16[16,16,128]{2,1,0:T(8,128)(2,1)}), bf16[16,16,128]{2,1,0:T(8,128)(2,1)S(1)}, u32[]{:S(2)}, u32[]{:S(2)}) async-start(bf16[16,16,128]{2,1,0:T(8,128)(2,1)} %bitcast.7), calls=%async_computation.2 | async-start | bytes 131072 | tf_op jit(solution)/shard_map/all_to_all | solution.py:416

commit v11 on v10

--- a/solution.py
+++ b/solution.py
@@ -386,7 +386,7 @@
         far=(w1, w2),
         sems=2,
     )
-    after = move(tall, ("tm",), (-1,))
+    got, tall = lax.optimization_barrier((got, tall))
 
     blocks = clips * steps
     span = 27 * chan // blocks
@@ -403,7 +403,6 @@
             ((27 * width, 256), F32),
         ],
     )
-    part, after = lax.optimization_barrier((part, after))
     by_clip = lax.all_to_all(part.reshape((clips, steps * shape[0], shape[1])), "clip", 0, 0)
     (summed,) = call(
         clip_kernel,
@@ -413,6 +412,7 @@
         (by_clip,),
         [],
     )
+    after = move(tall, ("tm",), (-1,))
     by_step = lax.all_to_all(summed.reshape((steps,) + shape), "tm", 0, 0)
     total = clips * 2 * frames * steps * rows * peers * cols
     (kernel_grad,) = call(

time: 87.8 us -> 85.3 us (0.972)
  the two profiles are of different devices: /device:TPU:2 before, /device:TPU:32 now
where the time goes in v11:
time: 85.3 us; the launch traced here: 84.8 us
  starting transfers between devices  37.4 us (44%)
  waiting for transfers between devices  19.1 us (22%)
  Pallas kernels  16.9 us (20%)
  blocking collectives  9.14 us (11%)
  between operations  1.39 us (2%)
  local copies, waits for them, and re-layouts  0.9 us (1%)
    pallas_call x8, Pallas kernels, call(): pl.pallas_call(body, name=name, out_shape=outs, in_specs=[pl.BlockSpec(me...  16.9 us
    ppermute x5, starting transfers between devices, move(): lax.ppermute(value, axes if len(axes) > 1 else axes[0], route(sizes, steps))  15.7 us
    all_to_all x1, starting transfers between devices, local(): by_step = lax.all_to_all(summed.reshape((steps,) + shape), 'tm', 0, 0)  15.5 us
    ppermute x5, waiting for transfers between devices, move(): lax.ppermute(value, axes if len(axes) > 1 else axes[0], route(sizes, steps))  10.3 us
    all_to_all x1, blocking collectives, local(): lax.all_to_all(part.reshape((clips, steps * shape[0], shape[1])), 'clip',...  9.14 us
    all_to_all x1, waiting for transfers between devices, local(): got = lax.all_to_all(pay, 'row', 0, 0)  8.18 us
    all_to_all x1, starting transfers between devices, local(): got = lax.all_to_all(pay, 'row', 0, 0)  6.22 us
  transfers between devices with their start and end apart: 7, of which 4 were waited for; matrix products, arithmetic and copies ran while one was open for 0% of the time, Pallas kernels for 13%

profile of v11, /device:TPU:32, one launch (start us, length us, event | category | flops | bytes accessed | tf_op | source)
XLA Modules:
  0.0 84.8 jit_solution(18304427738387595678)
XLA Ops:
  0.6 0.9 %slice_bitcast_fusion = bf16[2,2,48,192]{3,2,1,0:T(8,128)(2,1)S(1)} fusion(bf16[1,4,2,48,192]{4,3,2,1,0:T(8,128)(2,1)} %param.6), kind=kLoop, calls=%fused_computation | loop fusion | bytes 147456 | tf_op jit(solution)/shard_map/slice | solution.py:339
  1.5 7.4 %collective-permute-start.1 = (bf16[2,2,48,192]{3,2,1,0:T(8,128)(2,1)S(1)}, bf16[2,2,48,192]{3,2,1,0:T(8,128)(2,1)S(1)}, u32[]{:S(2)}, u32[]{:S(2)}) collective-permute-start(bf16[2,2,48,192]{3,2,1,0:T(8,128)(2,1)S(1)} %slice_bitcast_fusion), channel_id=1, source_target_pairs={{1,0},{2,1},{3,2},{4,3},{5,4},{6,5},{7,6},{8,7},{9,8},{10,9},{11,1... | collective-permute-start | bytes 221192 | tf_op jit(solution)/shard_map/ppermute | solution.py:38
  8.9 1.9 %collective-permute-start = (bf16[2,2,48,192]{3,2,1,0:T(8,128)(2,1)}, bf16[2,2,48,192]{3,2,1,0:T(8,128)(2,1)S(1)}, u32[]{:S(2)}, u32[]{:S(2)}) collective-permute-start(bf16[2,2,48,192]{3,2,1,0:T(8,128)(2,1)} %bitcast.17), channel_id=1, source_target_pairs={{0,1},{1,2},{2,3},{3,4},{4,5},{5,6},{6,7},{7,8},{8,9},{9,10},{10,1... | collective-permute-start | bytes 221192 | tf_op jit(solution)/shard_map/ppermute | solution.py:38
  11.5 0.0 collective-permute-done.1.gnext
  11.5 4.1 %collective-permute-done.xprev = bf16[2,2,48,192]{3,2,1,0:T(8,128)(2,1)S(1)} collective-permute-done((bf16[2,2,48,192]{3,2,1,0:T(8,128)(2,1)}, bf16[2,2,48,192]{3,2,1,0:T(8,128)(2,1)S(1)}, u32[]{:S(2)}, u32[]{:S(2)}) %collective-permute-start) | collective-permute-done | bytes 73760 | tf_op jit(solution)/shard_map/ppermute | solution.py:38
  15.6 1.0 %band.1.own = bf16[9,2,48,192]{3,2,1,0:T(8,128)(2,1)S(1)} custom-call(s32[1]{0:T(128)S(6)} %copy.7.lengths, bf16[2,2,48,192]{3,2,1,0:T(8,128)(2,1)} %bitcast.18, bf16[4,2,48,192]{3,2,1,0:T(8,128)(2,1)} %bitcast.15, bf16[2,2,48,192]{3,2,1,0:T(8,128)(2,1)S(1)} %collective-permute-done.xprev, bf16[2,2,48,192]{3,2,1,0:T(8,128)(2,1)S(1)} %collective-permute-done.1.gnext), custom_call_target="tpu_custom_call" | custom-call | tf_op jit(solution)/shard_map/band/pallas_call | solution.py:315
  16.7 1.3 %collective-permute-start.3 = (bf16[9,2,48,192]{3,2,1,0:T(8,128)(2,1)S(1)}, bf16[9,2,48,192]{3,2,1,0:T(8,128)(2,1)S(1)}, u32[]{:S(2)}, u32[]{:S(2)}) collective-permute-start(bf16[9,2,48,192]{3,2,1,0:T(8,128)(2,1)S(1)} %band.1.own), channel_id=1, source_target_pairs={{16,0},{32,16},{48,32},{64,48},{80,64},{96,80},{112,96},{17,1},{33... | collective-permute-start | bytes 995336 | tf_op jit(solution)/shard_map/ppermute | solution.py:38
  18.0 3.1 %collective-permute-start.2 = (bf16[9,2,48,192]{3,2,1,0:T(8,128)(2,1)S(1)}, bf16[9,2,48,192]{3,2,1,0:T(8,128)(2,1)S(1)}, u32[]{:S(2)}, u32[]{:S(2)}) collective-permute-start(bf16[9,2,48,192]{3,2,1,0:T(8,128)(2,1)S(1)} %band.1.own), channel_id=1, source_target_pairs={{0,16},{16,32},{32,48},{48,64},{64,80},{80,96},{96,112},{1,17},{17... | collective-permute-start | bytes 995336 | tf_op jit(solution)/shard_map/ppermute | solution.py:38
  21.0 2.6 %own_rows.1 = (bf16[8,120,128]{2,1,0:T(8,128)(2,1)S(1)}, f32[192,192]{1,0:T(8,128)S(1)}, bf16[27,192,192]{2,1,0:T(8,128)(2,1)S(1)}) custom-call(bf16[27,192,192]{2,1,0:T(8,128)(2,1)} %bitcast.11, bf16[9,2,48,192]{3,2,1,0:T(8,128)(2,1)S(1)} %band.1.own), custom_call_target="tpu_custom_call" | custom-call | tf_op jit(solution)/shard_map/own_rows/pallas_call | solution.py:315
  23.6 0.0 collective-permute-done.3.below
  23.7 0.0 collective-permute-done.2.above
  23.7 1.4 %hidden_and_act.1 = bf16[8,408,128]{2,1,0:T(8,128)(2,1)} custom-call(bf16[8,120,128]{2,1,0:T(8,128)(2,1)S(1)} %get-tuple-element.7.turned, bf16[27,192,192]{2,1,0:T(8,128)(2,1)S(1)} %get-tuple-element.8.w, f32[192,192]{1,0:T(8,128)S(1)} %get-tuple-element.9.part, bf16[9,2,48,192]{3,2,1,0:T(8,128)(2,1)S(1)} %collective-permute-done.2.above, ...), custom_call_target="tpu_custom_call" | custom-call | tf_op jit(solution)/shard_map/hidden_and_act/pallas_call | solution.py:315
  25.1 6.2 %all-to-all-start = ((bf16[8,408,128]{2,1,0:T(8,128)(2,1)}), bf16[8,408,128]{2,1,0:T(8,128)(2,1)S(1)}, u32[]{:S(2)}, u32[]{:S(2)}) async-start(bf16[8,408,128]{2,1,0:T(8,128)(2,1)} %hidden_and_act.1), calls=%async_computation | async-start | bytes 1671168 | tf_op jit(solution)/shard_map/all_to_all | solution.py:373
  31.3 5.5 %hidden_grad.1.tall = bf16[2,4,48,192]{3,2,1,0:T(8,128)(2,1)S(1)} custom-call(bf16[27,192,192]{2,1,0:T(8,128)(2,1)} %bitcast.12, bf16[27,192,192]{2,1,0:T(8,128)(2,1)} %bitcast.14, bf16[9,2,48,192]{3,2,1,0:T(8,128)(2,1)S(1)} %collective-permute-done.2.above, bf16[9,2,48,192]{3,2,1,0:T(8,128)(2,1)S(1)} %collective-permute-done.3.below, ...), custom_call_target="tpu_custom_call" | custom-call | tf_op jit(solution)/shard_map/hidden_grad/pallas_call | solution.py:315
  36.8 8.2 %all-to-all-done.got = bf16[8,408,128]{2,1,0:T(8,128)(2,1)S(1)} async-done(((bf16[8,408,128]{2,1,0:T(8,128)(2,1)}), bf16[8,408,128]{2,1,0:T(8,128)(2,1)S(1)}, u32[]{:S(2)}, u32[]{:S(2)}) %all-to-all-start) | async-done | bytes 835616 | tf_op jit(solution)/shard_map/all_to_all | solution.py:373
  45.0 1.7 %kernel_grad_part.1 = bf16[64,16,128]{2,1,0:T(8,128)(2,1)S(1)} custom-call(bf16[8,408,128]{2,1,0:T(8,128)(2,1)S(1)} %all-to-all-done.got), custom_call_target="tpu_custom_call" | custom-call | tf_op jit(solution)/shard_map/kernel_grad_part/pallas_call | solution.py:315
  46.7 9.1 %all_to_all.15.got = bf16[4,256,128]{2,1,0:T(8,128)(2,1)S(1)} all-to-all(bf16[4,256,128]{2,1,0:T(8,128)(2,1)S(1)} %bitcast.10), channel_id=1, replica_groups=mesh['clip'=4,'row'=8,'tm'=16] {'clip'}, dimensions={0} | all-to-all | bytes 524288 | tf_op jit(solution)/shard_map/all_to_all | solution.py:406
  55.9 0.7 clip_sum.1
  56.5 15.5 %all-to-all-start.2 = ((bf16[16,16,128]{2,1,0:T(8,128)(2,1)}), bf16[16,16,128]{2,1,0:T(8,128)(2,1)S(1)}, u32[]{:S(2)}, u32[]{:S(2)}) async-start(bf16[16,16,128]{2,1,0:T(8,128)(2,1)} %bitcast.7), calls=%async_computation.2 | async-start | bytes 131072 | tf_op jit(solution)/shard_map/all_to_all | solution.py:416
  72.0 2.0 %collective-permute-start.4 = (bf16[2,4,48,192]{3,2,1,0:T(8,128)(2,1)S(1)}, bf16[2,4,48,192]{3,2,1,0:T(8,128)(2,1)S(1)}, u32[]{:S(2)}, u32[]{:S(2)}) collective-permute-start(bf16[2,4,48,192]{3,2,1,0:T(8,128)(2,1)S(1)} %hidden_grad.1.tall), channel_id=1, source_target_pairs={{1,0},{2,1},{3,2},{4,3},{5,4},{6,5},{7,6},{8,7},{9,8},{10,9},{11,1... | collective-permute-start | bytes 442376 | tf_op jit(solution)/shard_map/ppermute | solution.py:38
  74.0 6.2 %collective-permute-done.4.after = bf16[2,4,48,192]{3,2,1,0:T(8,128)(2,1)S(1)} collective-permute-done((bf16[2,4,48,192]{3,2,1,0:T(8,128)(2,1)S(1)}, bf16[2,4,48,192]{3,2,1,0:T(8,128)(2,1)S(1)}, u32[]{:S(2)}, u32[]{:S(2)}) %collective-permute-start.4) | collective-permute-done | bytes 147488 | tf_op jit(solution)/shard_map/ppermute | solution.py:38
  80.2 3.3 %input_grad.1 = f32[2,2,48,192]{3,2,1,0:T(8,128)} custom-call(bf16[27,192,192]{2,1,0:T(8,128)(2,1)} %bitcast.13, bf16[2,4,48,192]{3,2,1,0:T(8,128)(2,1)S(1)} %hidden_grad.1.tall, bf16[2,4,48,192]{3,2,1,0:T(8,128)(2,1)S(1)} %collective-permute-done.4.after), custom_call_target="tpu_custom_call" | custom-call | tf_op jit(solution)/shard_map/input_grad/pallas_call | solution.py:315
  83.5 0.6 all-to-all-done.2.got
  84.1 0.7 kernel_grad_sum.1
Async XLA Ops:
  1.5 10.0 %collective-permute-start.1 = (bf16[2,2,48,192]{3,2,1,0:T(8,128)(2,1)S(1)}, bf16[2,2,48,192]{3,2,1,0:T(8,128)(2,1)S(1)}, u32[]{:S(2)}, u32[]{:S(2)}) collective-permute-start(bf16[2,2,48,192]{3,2,1,0:T(8,128)(2,1)S(1)} %slice_bitcast_fusion), channel_id=1, source_target_pairs={{1,0},{2,1},{3,2},{4,3},{5,4},{6,5},{7,6},{8,7},{9,8},{10,9},{11,1... | collective-permute-start | bytes 221192 | tf_op jit(solution)/shard_map/ppermute | solution.py:38
  8.9 6.7 %collective-permute-start = (bf16[2,2,48,192]{3,2,1,0:T(8,128)(2,1)}, bf16[2,2,48,192]{3,2,1,0:T(8,128)(2,1)S(1)}, u32[]{:S(2)}, u32[]{:S(2)}) collective-permute-start(bf16[2,2,48,192]{3,2,1,0:T(8,128)(2,1)} %bitcast.17), channel_id=1, source_target_pairs={{0,1},{1,2},{2,3},{3,4},{4,5},{5,6},{6,7},{7,8},{8,9},{9,10},{10,1... | collective-permute-start | bytes 221192 | tf_op jit(solution)/shard_map/ppermute | solution.py:38
  16.7 7.0 %collective-permute-start.3 = (bf16[9,2,48,192]{3,2,1,0:T(8,128)(2,1)S(1)}, bf16[9,2,48,192]{3,2,1,0:T(8,128)(2,1)S(1)}, u32[]{:S(2)}, u32[]{:S(2)}) collective-permute-start(bf16[9,2,48,192]{3,2,1,0:T(8,128)(2,1)S(1)} %band.1.own), channel_id=1, source_target_pairs={{16,0},{32,16},{48,32},{64,48},{80,64},{96,80},{112,96},{17,1},{33... | collective-permute-start | bytes 995336 | tf_op jit(solution)/shard_map/ppermute | solution.py:38
  18.0 5.7 %collective-permute-start.2 = (bf16[9,2,48,192]{3,2,1,0:T(8,128)(2,1)S(1)}, bf16[9,2,48,192]{3,2,1,0:T(8,128)(2,1)S(1)}, u32[]{:S(2)}, u32[]{:S(2)}) collective-permute-start(bf16[9,2,48,192]{3,2,1,0:T(8,128)(2,1)S(1)} %band.1.own), channel_id=1, source_target_pairs={{0,16},{16,32},{32,48},{48,64},{64,80},{80,96},{96,112},{1,17},{17... | collective-permute-start | bytes 995336 | tf_op jit(solution)/shard_map/ppermute | solution.py:38
  25.1 19.9 %all-to-all-start = ((bf16[8,408,128]{2,1,0:T(8,128)(2,1)}), bf16[8,408,128]{2,1,0:T(8,128)(2,1)S(1)}, u32[]{:S(2)}, u32[]{:S(2)}) async-start(bf16[8,408,128]{2,1,0:T(8,128)(2,1)} %hidden_and_act.1), calls=%async_computation | async-start | bytes 1671168 | tf_op jit(solution)/shard_map/all_to_all | solution.py:373
  56.5 27.6 %all-to-all-start.2 = ((bf16[16,16,128]{2,1,0:T(8,128)(2,1)}), bf16[16,16,128]{2,1,0:T(8,128)(2,1)S(1)}, u32[]{:S(2)}, u32[]{:S(2)}) async-start(bf16[16,16,128]{2,1,0:T(8,128)(2,1)} %bitcast.7), calls=%async_computation.2 | async-start | bytes 131072 | tf_op jit(solution)/shard_map/all_to_all | solution.py:416
  72.0 8.2 %collective-permute-start.4 = (bf16[2,4,48,192]{3,2,1,0:T(8,128)(2,1)S(1)}, bf16[2,4,48,192]{3,2,1,0:T(8,128)(2,1)S(1)}, u32[]{:S(2)}, u32[]{:S(2)}) collective-permute-start(bf16[2,4,48,192]{3,2,1,0:T(8,128)(2,1)S(1)} %hidden_grad.1.tall), channel_id=1, source_target_pairs={{1,0},{2,1},{3,2},{4,3},{5,4},{6,5},{7,6},{8,7},{9,8},{10,9},{11,1... | collective-permute-start | bytes 442376 | tf_op jit(solution)/shard_map/ppermute | solution.py:38

commit v12 on v11

--- a/solution.py
+++ b/solution.py
@@ -80,7 +80,7 @@
     return copies
 
 
-def band_kernel(lengths, x, g_far, xprev, gnext, band, g, sem):
+def band_kernel(lengths, x, g_far, xprev, gnext, band, top, bot, g, sem):
     frames = xprev.shape[0]
     copies = start_copies(((g_far, g), (x, band.at[0:frames])), sem)
     band[frames : 2 * frames] = xprev[...]
@@ -92,6 +92,8 @@
         for a in range(5):
             band[2 * frames + a, r] = (field[a] + field[a + 1]).astype(BF)
     copies[1].wait()
+    top[...] = band[:, 0]
+    bot[...] = band[:, 1]
 
 
 def packed(width, span):
@@ -127,20 +129,20 @@
 
 
 def silu_kernel(turned, w, part, above, below, pay, own, sem):
-    _, rows, cols, chan = above.shape
+    _, cols, chan = above.shape
     frames = 2
-    cells = frames * rows * cols
+    cells = part.shape[0]
     half = cells // 2
     peers = pay.shape[0]
     copies = [pltpu.make_async_copy(turned, pay.at[:, cells + half :], sem.at[peers])]
     copies[0].start()
 
     def top_patch(i, j):
-        frame = [above[(f + 2 - i + frames) % (2 * frames), 1] for f in range(2)]
+        frame = [above[(f + 2 - i + frames) % (2 * frames)] for f in range(2)]
         return jnp.concatenate(frame, axis=0)
 
     def bottom_patch(i, j):
-        frame = [below[(f + 2 - i + frames) % (2 * frames), 0] for f in range(2)]
+        frame = [below[(f + 2 - i + frames) % (2 * frames)] for f in range(2)]
         return jnp.concatenate(frame, axis=0)
 
     top = conv(top_patch, w, plain_dot, 1, cols, (0,)).reshape(frames, 1, cols, chan)
@@ -156,35 +158,40 @@
         copy.wait()
 
 
-def hidden_grad_kernel(w1_far, w2_far, above, below, own, tall, xe, pe, w1, w2, sem):
+def hidden_grad_kernel(
+    w1_far, w2_far, above, below, own, grad, top, bot, xe, pe, w1, w2, sem
+):
     _, rows, cols, chan = own.shape
     frames = 2
     copies = start_copies([(w1_far, w1), (w2_far, w2)], sem)
     for f in range(2 * frames + 5):
-        target, slot = (xe, (f + frames) % (2 * frames) * 6) if f < 4 else (pe, (f - 4) * 6)
-        target[slot : slot + 2] = above[f]
-        target[slot + 2 : slot + 4] = own[f]
-        target[slot + 4 : slot + 6] = below[f]
+        target, slot = (xe, (f + frames) % (2 * frames) * 4) if f < 4 else (pe, (f - 4) * 4)
+        target[slot] = above[f]
+        target[slot + 1 : slot + 3] = own[f]
+        target[slot + 3] = below[f]
     for copy in copies:
         copy.wait()
 
     def patch(i, j):
-        return blocks_of(xe, [(f + 2 - i) * 6 + j for f in range(2)], 4)
+        return blocks_of(xe, [(f + 2 - i) * 4 + j for f in range(2)], 2)
 
     def pair_patch(i, j):
-        return blocks_of(pe, [(2 * t + i) * 6 + 2 - j for t in range(2)], 4)
+        return blocks_of(pe, [(2 * t + i) * 4 + 2 - j for t in range(2)], 2)
 
     hidden = conv(patch, w1, plain_dot, 1, cols)
     pair = conv(pair_patch, w2, transposed_dot, -1, cols)
     sigma = 1.0 / (1.0 + jnp.exp(-hidden))
-    grad = pair * sigma * (1.0 + hidden * (1.0 - sigma))
-    grad = grad.reshape(frames, rows + 2, cols, chan)
-    band = lax.axis_index("row")
-    none = jnp.zeros((frames, cols, chan), F32)
-    tall[:, 0] = jnp.where(band > 0, grad[:, 0], none).astype(BF)
-    tall[:, 1 : 1 + rows] = grad[:, 1 : 1 + rows].astype(BF)
-    last = band == lax.axis_size("row") - 1
-    tall[:, 1 + rows] = jnp.where(last, none, grad[:, 1 + rows]).astype(BF)
+    value = (pair * sigma * (1.0 + hidden * (1.0 - sigma))).astype(BF)
+    value = value.reshape(frames, rows, cols, chan)
+    grad[...] = value
+    top[...] = value[:, 0]
+    bot[...] = value[:, 1]
+
+
+def tall_kernel(grad, above, below, tall):
+    tall[:, 0] = above[...]
+    tall[:, 1:3] = grad[...]
+    tall[:, 3] = below[...]
 
 
 def second_kernel(span, got, out, field, left, prod):
@@ -337,19 +344,20 @@
 
     xprev = move(x, ("tm",), (1,))
     gnext = move(g[:frames], ("tm",), (-1,))
-    (band,) = call(
+    held = 2 * frames + 5
+    band, top, bot = call(
         band_kernel,
         "band",
         4,
-        [((2 * frames + 5, rows, cols, chan), BF)],
+        [((held, rows, cols, chan), BF)] + [((held, cols, chan), BF)] * 2,
         (xprev, gnext),
         [(g.shape, BF)],
         far=(x, g),
         scalars=(lengths,),
         sems=2,
     )
-    above = move(band, ("row",), (1,))
-    below = move(band, ("row",), (-1,))
+    above = move(bot, ("row",), (1,))
+    below = move(top, ("row",), (-1,))
     turned, own_part, w1_near = call(
         own_kernel,
         "own_rows",
@@ -371,20 +379,31 @@
         out_far=True,
     )
     got = lax.all_to_all(pay, "row", 0, 0)
-    (tall,) = call(
+    edge = (frames, cols, chan)
+    grad, grad_top, grad_bot = call(
         hidden_grad_kernel,
         "hidden_grad",
         14,
-        [((frames, rows + 2, cols, chan), BF)],
+        [((frames, rows, cols, chan), BF), (edge, BF), (edge, BF)],
         (above, below, band),
         [
-            ((24, cols, chan), BF),
-            ((30, cols, chan), BF),
+            ((16, cols, chan), BF),
+            ((20, cols, chan), BF),
             (w1.shape, BF),
             (w2.shape, BF),
         ],
         far=(w1, w2),
         sems=2,
+    )
+    above_grad = move(grad_bot, ("row",), (1,))
+    below_grad = move(grad_top, ("row",), (-1,))
+    (tall,) = call(
+        tall_kernel,
+        "tall_band",
+        4,
+        [((frames, rows + 2, cols, chan), BF)],
+        (grad, above_grad, below_grad),
+        [],
     )
     got, tall = lax.optimization_barrier((got, tall))
 

time: 85.3 us -> 85.2 us (level)
  the two profiles are of different devices: /device:TPU:32 before, /device:TPU:2 now
where the time goes in v12:
time: 85.2 us; the launch traced here: 84.7 us
  starting transfers between devices  41 us (48%)
  Pallas kernels  15.6 us (18%)
  waiting for transfers between devices  13.9 us (16%)
  blocking collectives  11.9 us (14%)
  between operations  1.41 us (2%)
  local copies, waits for them, and re-layouts  0.9 us (1%)
    ppermute x7, starting transfers between devices, move(): lax.ppermute(value, axes if len(axes) > 1 else axes[0], route(sizes, steps))  18.3 us
    all_to_all x1, starting transfers between devices, local(): by_step = lax.all_to_all(summed.reshape((steps,) + shape), 'tm', 0, 0)  16.8 us
    pallas_call x9, Pallas kernels, call(): pl.pallas_call(body, name=name, out_shape=outs, in_specs=[pl.BlockSpec(me...  15.6 us
    ppermute x7, waiting for transfers between devices, move(): lax.ppermute(value, axes if len(axes) > 1 else axes[0], route(sizes, steps))  13.1 us
    all_to_all x1, blocking collectives, local(): lax.all_to_all(part.reshape((clips, steps * shape[0], shape[1])), 'clip',...  11.9 us
    all_to_all x1, starting transfers between devices, local(): got = lax.all_to_all(pay, 'row', 0, 0)  5.92 us
  transfers between devices with their start and end apart: 9, of which 7 were waited for; matrix products, arithmetic and copies ran while one was open for 0% of the time, Pallas kernels for 12%

profile of v12, /device:TPU:2, one launch (start us, length us, event | category | flops | bytes accessed | tf_op | source)
XLA Modules:
  0.0 84.7 jit_solution(14284814340657924605)
XLA Ops:
  0.6 0.9 %slice_bitcast_fusion = bf16[2,2,48,192]{3,2,1,0:T(8,128)(2,1)S(1)} fusion(bf16[1,4,2,48,192]{4,3,2,1,0:T(8,128)(2,1)} %param.6), kind=kLoop, calls=%fused_computation | loop fusion | bytes 147456 | tf_op jit(solution)/shard_map/slice | solution.py:346
  1.5 1.3 %collective-permute-start.1 = (bf16[2,2,48,192]{3,2,1,0:T(8,128)(2,1)S(1)}, bf16[2,2,48,192]{3,2,1,0:T(8,128)(2,1)S(1)}, u32[]{:S(2)}, u32[]{:S(2)}) collective-permute-start(bf16[2,2,48,192]{3,2,1,0:T(8,128)(2,1)S(1)} %slice_bitcast_fusion), channel_id=1, source_target_pairs={{1,0},{2,1},{3,2},{4,3},{5,4},{6,5},{7,6},{8,7},{9,8},{10,9},{11,1... | collective-permute-start | bytes 221192 | tf_op jit(solution)/shard_map/ppermute | solution.py:38
  2.8 4.6 %collective-permute-start = (bf16[2,2,48,192]{3,2,1,0:T(8,128)(2,1)}, bf16[2,2,48,192]{3,2,1,0:T(8,128)(2,1)S(1)}, u32[]{:S(2)}, u32[]{:S(2)}) collective-permute-start(bf16[2,2,48,192]{3,2,1,0:T(8,128)(2,1)} %bitcast.17), channel_id=1, source_target_pairs={{0,1},{1,2},{2,3},{3,4},{4,5},{5,6},{6,7},{7,8},{8,9},{9,10},{10,1... | collective-permute-start | bytes 221192 | tf_op jit(solution)/shard_map/ppermute | solution.py:38
  8.0 0.1 collective-permute-done.1.gnext
  8.1 1.8 %collective-permute-done.xprev = bf16[2,2,48,192]{3,2,1,0:T(8,128)(2,1)S(1)} collective-permute-done((bf16[2,2,48,192]{3,2,1,0:T(8,128)(2,1)}, bf16[2,2,48,192]{3,2,1,0:T(8,128)(2,1)S(1)}, u32[]{:S(2)}, u32[]{:S(2)}) %collective-permute-start) | collective-permute-done | bytes 73760 | tf_op jit(solution)/shard_map/ppermute | solution.py:38
  9.9 1.0 %band.1 = (bf16[9,2,48,192]{3,2,1,0:T(8,128)(2,1)S(1)}, bf16[9,48,192]{2,1,0:T(8,128)(2,1)S(1)}, bf16[9,48,192]{2,1,0:T(8,128)(2,1)S(1)}) custom-call(s32[1]{0:T(128)S(6)} %copy.7.lengths, bf16[2,2,48,192]{3,2,1,0:T(8,128)(2,1)} %bitcast.18, bf16[4,2,48,192]{3,2,1,0:T(8,128)(2,1)} %bitcast.15, bf16[2,2,48,192]{3,2,1,0:T(8,128)(2,1)S(1)} %collective-permute-done.xprev, ...), custom_call_target="tpu_custom_call" | custom-call | tf_op jit(solution)/shard_map/band/pallas_call | solution.py:322
  10.9 1.9 %collective-permute-start.2 = (bf16[9,48,192]{2,1,0:T(8,128)(2,1)S(1)}, bf16[9,48,192]{2,1,0:T(8,128)(2,1)S(1)}, u32[]{:S(2)}, u32[]{:S(2)}) collective-permute-start(bf16[9,48,192]{2,1,0:T(8,128)(2,1)S(1)} %get-tuple-element.17), channel_id=1, source_target_pairs={{0,16},{16,32},{32,48},{48,64},{64,80},{80,96},{96,112},{1,17},{17... | collective-permute-start | bytes 497672 | tf_op jit(solution)/shard_map/ppermute | solution.py:38
  12.9 3.6 %collective-permute-start.3 = (bf16[9,48,192]{2,1,0:T(8,128)(2,1)S(1)}, bf16[9,48,192]{2,1,0:T(8,128)(2,1)S(1)}, u32[]{:S(2)}, u32[]{:S(2)}) collective-permute-start(bf16[9,48,192]{2,1,0:T(8,128)(2,1)S(1)} %get-tuple-element.18), channel_id=1, source_target_pairs={{16,0},{32,16},{48,32},{64,48},{80,64},{96,80},{112,96},{17,1},{33... | collective-permute-start | bytes 497672 | tf_op jit(solution)/shard_map/ppermute | solution.py:38
  16.5 2.6 %own_rows.1 = (bf16[8,120,128]{2,1,0:T(8,128)(2,1)S(1)}, f32[192,192]{1,0:T(8,128)S(1)}, bf16[27,192,192]{2,1,0:T(8,128)(2,1)S(1)}) custom-call(bf16[27,192,192]{2,1,0:T(8,128)(2,1)} %bitcast.11, bf16[9,2,48,192]{3,2,1,0:T(8,128)(2,1)S(1)} %get-tuple-element.13.band.own), custom_call_target="tpu_custom_call" | custom-call | tf_op jit(solution)/shard_map/own_rows/pallas_call | solution.py:322
  19.1 0.0 collective-permute-done.2.above
  19.1 0.8 collective-permute-done.3.below
  19.9 1.4 %hidden_and_act.1 = bf16[8,408,128]{2,1,0:T(8,128)(2,1)} custom-call(bf16[8,120,128]{2,1,0:T(8,128)(2,1)S(1)} %get-tuple-element.14.turned, bf16[27,192,192]{2,1,0:T(8,128)(2,1)S(1)} %get-tuple-element.15.w, f32[192,192]{1,0:T(8,128)S(1)} %get-tuple-element.16.part, bf16[9,48,192]{2,1,0:T(8,128)(2,1)S(1)} %collective-permute-done.2.above, ...), custom_call_target="tpu_custom_call" | custom-call | tf_op jit(solution)/shard_map/hidden_and_act/pallas_call | solution.py:322
  21.4 5.9 %all-to-all-start = ((bf16[8,408,128]{2,1,0:T(8,128)(2,1)}), bf16[8,408,128]{2,1,0:T(8,128)(2,1)S(1)}, u32[]{:S(2)}, u32[]{:S(2)}) async-start(bf16[8,408,128]{2,1,0:T(8,128)(2,1)} %hidden_and_act.1), calls=%async_computation | async-start | bytes 1671168 | tf_op jit(solution)/shard_map/all_to_all | solution.py:381
  27.3 4.1 %hidden_grad.1 = (bf16[2,2,48,192]{3,2,1,0:T(8,128)(2,1)S(1)}, bf16[2,48,192]{2,1,0:T(8,128)(2,1)S(1)}, bf16[2,48,192]{2,1,0:T(8,128)(2,1)S(1)}) custom-call(bf16[27,192,192]{2,1,0:T(8,128)(2,1)} %bitcast.12, bf16[27,192,192]{2,1,0:T(8,128)(2,1)} %bitcast.14, bf16[9,48,192]{2,1,0:T(8,128)(2,1)S(1)} %collective-permute-done.2.above, ...), custom_call_target="tpu_custom_call" | custom-call | tf_op jit(solution)/shard_map/hidden_grad/pallas_call | solution.py:322
  31.4 2.1 %collective-permute-start.4 = (bf16[2,48,192]{2,1,0:T(8,128)(2,1)S(1)}, bf16[2,48,192]{2,1,0:T(8,128)(2,1)S(1)}, u32[]{:S(2)}, u32[]{:S(2)}) collective-permute-start(bf16[2,48,192]{2,1,0:T(8,128)(2,1)S(1)} %get-tuple-element.20), channel_id=1, source_target_pairs={{0,16},{16,32},{32,48},{48,64},{64,80},{80,96},{96,112},{1,17},{17... | collective-permute-start | bytes 110600 | tf_op jit(solution)/shard_map/ppermute | solution.py:38
  33.5 3.5 %collective-permute-start.5 = (bf16[2,48,192]{2,1,0:T(8,128)(2,1)S(1)}, bf16[2,48,192]{2,1,0:T(8,128)(2,1)S(1)}, u32[]{:S(2)}, u32[]{:S(2)}) collective-permute-start(bf16[2,48,192]{2,1,0:T(8,128)(2,1)S(1)} %get-tuple-element.21), channel_id=1, source_target_pairs={{16,0},{32,16},{48,32},{64,48},{80,64},{96,80},{112,96},{17,1},{33... | collective-permute-start | bytes 110600 | tf_op jit(solution)/shard_map/ppermute | solution.py:38
  37.0 1.6 %collective-permute-done.4.above = bf16[2,48,192]{2,1,0:T(8,128)(2,1)S(1)} collective-permute-done((bf16[2,48,192]{2,1,0:T(8,128)(2,1)S(1)}, bf16[2,48,192]{2,1,0:T(8,128)(2,1)S(1)}, u32[]{:S(2)}, u32[]{:S(2)}) %collective-permute-start.4) | collective-permute-done | bytes 36896 | tf_op jit(solution)/shard_map/ppermute | solution.py:38
  38.6 0.2 collective-permute-done.5.below
  38.8 0.8 all-to-all-done.got
  39.6 1.7 %kernel_grad_part.1 = bf16[64,16,128]{2,1,0:T(8,128)(2,1)S(1)} custom-call(bf16[8,408,128]{2,1,0:T(8,128)(2,1)S(1)} %all-to-all-done.got), custom_call_target="tpu_custom_call" | custom-call | tf_op jit(solution)/shard_map/kernel_grad_part/pallas_call | solution.py:322
  41.3 11.9 %all_to_all.15.got = bf16[4,256,128]{2,1,0:T(8,128)(2,1)S(1)} all-to-all(bf16[4,256,128]{2,1,0:T(8,128)(2,1)S(1)} %bitcast.10), channel_id=1, replica_groups=mesh['clip'=4,'row'=8,'tm'=16] {'clip'}, dimensions={0} | all-to-all | bytes 524288 | tf_op jit(solution)/shard_map/all_to_all | solution.py:425
  53.2 0.7 clip_sum.1
  53.9 16.8 %all-to-all-start.2 = ((bf16[16,16,128]{2,1,0:T(8,128)(2,1)}), bf16[16,16,128]{2,1,0:T(8,128)(2,1)S(1)}, u32[]{:S(2)}, u32[]{:S(2)}) async-start(bf16[16,16,128]{2,1,0:T(8,128)(2,1)} %bitcast.7), calls=%async_computation.2 | async-start | bytes 131072 | tf_op jit(solution)/shard_map/all_to_all | solution.py:435
  70.7 1.3 %collective-permute-start.6 = (bf16[2,4,48,192]{3,2,1,0:T(8,128)(2,1)S(1)}, bf16[2,4,48,192]{3,2,1,0:T(8,128)(2,1)S(1)}, u32[]{:S(2)}, u32[]{:S(2)}) collective-permute-start(bf16[2,4,48,192]{3,2,1,0:T(8,128)(2,1)S(1)} %tall_band.1.tall), channel_id=1, source_target_pairs={{1,0},{2,1},{3,2},{4,3},{5,4},{6,5},{7,6},{8,7},{9,8},{10,9},{11,1... | collective-permute-start | bytes 442376 | tf_op jit(solution)/shard_map/ppermute | solution.py:38
  72.0 8.7 %collective-permute-done.6.after = bf16[2,4,48,192]{3,2,1,0:T(8,128)(2,1)S(1)} collective-permute-done((bf16[2,4,48,192]{3,2,1,0:T(8,128)(2,1)S(1)}, bf16[2,4,48,192]{3,2,1,0:T(8,128)(2,1)S(1)}, u32[]{:S(2)}, u32[]{:S(2)}) %collective-permute-start.6) | collective-permute-done | bytes 147488 | tf_op jit(solution)/shard_map/ppermute | solution.py:38
  80.6 3.3 %input_grad.1 = f32[2,2,48,192]{3,2,1,0:T(8,128)} custom-call(bf16[27,192,192]{2,1,0:T(8,128)(2,1)} %bitcast.13, bf16[2,4,48,192]{3,2,1,0:T(8,128)(2,1)S(1)} %tall_band.1.tall, bf16[2,4,48,192]{3,2,1,0:T(8,128)(2,1)S(1)} %collective-permute-done.6.after), custom_call_target="tpu_custom_call" | custom-call | tf_op jit(solution)/shard_map/input_grad/pallas_call | solution.py:322
  84.0 0.0 all-to-all-done.2.got
  84.0 0.7 kernel_grad_sum.1
  (1 shorter events, 0.0 us)
Async XLA Ops:
  1.5 6.6 %collective-permute-start.1 = (bf16[2,2,48,192]{3,2,1,0:T(8,128)(2,1)S(1)}, bf16[2,2,48,192]{3,2,1,0:T(8,128)(2,1)S(1)}, u32[]{:S(2)}, u32[]{:S(2)}) collective-permute-start(bf16[2,2,48,192]{3,2,1,0:T(8,128)(2,1)S(1)} %slice_bitcast_fusion), channel_id=1, source_target_pairs={{1,0},{2,1},{3,2},{4,3},{5,4},{6,5},{7,6},{8,7},{9,8},{10,9},{11,1... | collective-permute-start | bytes 221192 | tf_op jit(solution)/shard_map/ppermute | solution.py:38
  2.8 7.1 %collective-permute-start = (bf16[2,2,48,192]{3,2,1,0:T(8,128)(2,1)}, bf16[2,2,48,192]{3,2,1,0:T(8,128)(2,1)S(1)}, u32[]{:S(2)}, u32[]{:S(2)}) collective-permute-start(bf16[2,2,48,192]{3,2,1,0:T(8,128)(2,1)} %bitcast.17), channel_id=1, source_target_pairs={{0,1},{1,2},{2,3},{3,4},{4,5},{5,6},{6,7},{7,8},{8,9},{9,10},{10,1... | collective-permute-start | bytes 221192 | tf_op jit(solution)/shard_map/ppermute | solution.py:38
  10.9 8.2 %collective-permute-start.2 = (bf16[9,48,192]{2,1,0:T(8,128)(2,1)S(1)}, bf16[9,48,192]{2,1,0:T(8,128)(2,1)S(1)}, u32[]{:S(2)}, u32[]{:S(2)}) collective-permute-start(bf16[9,48,192]{2,1,0:T(8,128)(2,1)S(1)} %get-tuple-element.17), channel_id=1, source_target_pairs={{0,16},{16,32},{32,48},{48,64},{64,80},{80,96},{96,112},{1,17},{17... | collective-permute-start | bytes 497672 | tf_op jit(solution)/shard_map/ppermute | solution.py:38
  12.9 7.1 %collective-permute-start.3 = (bf16[9,48,192]{2,1,0:T(8,128)(2,1)S(1)}, bf16[9,48,192]{2,1,0:T(8,128)(2,1)S(1)}, u32[]{:S(2)}, u32[]{:S(2)}) collective-permute-start(bf16[9,48,192]{2,1,0:T(8,128)(2,1)S(1)} %get-tuple-element.18), channel_id=1, source_target_pairs={{16,0},{32,16},{48,32},{64,48},{80,64},{96,80},{112,96},{17,1},{33... | collective-permute-start | bytes 497672 | tf_op jit(solution)/shard_map/ppermute | solution.py:38
  21.4 18.1 %all-to-all-start = ((bf16[8,408,128]{2,1,0:T(8,128)(2,1)}), bf16[8,408,128]{2,1,0:T(8,128)(2,1)S(1)}, u32[]{:S(2)}, u32[]{:S(2)}) async-start(bf16[8,408,128]{2,1,0:T(8,128)(2,1)} %hidden_and_act.1), calls=%async_computation | async-start | bytes 1671168 | tf_op jit(solution)/shard_map/all_to_all | solution.py:381
  31.4 7.2 %collective-permute-start.4 = (bf16[2,48,192]{2,1,0:T(8,128)(2,1)S(1)}, bf16[2,48,192]{2,1,0:T(8,128)(2,1)S(1)}, u32[]{:S(2)}, u32[]{:S(2)}) collective-permute-start(bf16[2,48,192]{2,1,0:T(8,128)(2,1)S(1)} %get-tuple-element.20), channel_id=1, source_target_pairs={{0,16},{16,32},{32,48},{48,64},{64,80},{80,96},{96,112},{1,17},{17... | collective-permute-start | bytes 110600 | tf_op jit(solution)/shard_map/ppermute | solution.py:38
  33.5 5.2 %collective-permute-start.5 = (bf16[2,48,192]{2,1,0:T(8,128)(2,1)S(1)}, bf16[2,48,192]{2,1,0:T(8,128)(2,1)S(1)}, u32[]{:S(2)}, u32[]{:S(2)}) collective-permute-start(bf16[2,48,192]{2,1,0:T(8,128)(2,1)S(1)} %get-tuple-element.21), channel_id=1, source_target_pairs={{16,0},{32,16},{48,32},{64,48},{80,64},{96,80},{112,96},{17,1},{33... | collective-permute-start | bytes 110600 | tf_op jit(solution)/shard_map/ppermute | solution.py:38
  53.9 30.1 %all-to-all-start.2 = ((bf16[16,16,128]{2,1,0:T(8,128)(2,1)}), bf16[16,16,128]{2,1,0:T(8,128)(2,1)S(1)}, u32[]{:S(2)}, u32[]{:S(2)}) async-start(bf16[16,16,128]{2,1,0:T(8,128)(2,1)} %bitcast.7), calls=%async_computation.2 | async-start | bytes 131072 | tf_op jit(solution)/shard_map/all_to_all | solution.py:435
  70.7 10.0 %collective-permute-start.6 = (bf16[2,4,48,192]{3,2,1,0:T(8,128)(2,1)S(1)}, bf16[2,4,48,192]{3,2,1,0:T(8,128)(2,1)S(1)}, u32[]{:S(2)}, u32[]{:S(2)}) collective-permute-start(bf16[2,4,48,192]{3,2,1,0:T(8,128)(2,1)S(1)} %tall_band.1.tall), channel_id=1, source_target_pairs={{1,0},{2,1},{3,2},{4,3},{5,4},{6,5},{7,6},{8,7},{9,8},{10,9},{11,1... | collective-permute-start | bytes 442376 | tf_op jit(solution)/shard_map/ppermute | solution.py:38

commit v13 on v12

--- a/solution.py
+++ b/solution.py
@@ -54,11 +54,11 @@
     return moved.reshape(cells, chan)
 
 
-def conv(patch, weight, dot, first_shift, cols, row_taps=(0, 1, 2)):
+def conv(patch, weight, dot, first_shift, cols, row_taps=(0, 1, 2), frame_taps=(0, 1, 2)):
     total = None
     for k in (1, 0, 2):
         part = None
-        for i in range(3):
+        for i in frame_taps:
             for j in row_taps:
                 term = dot(patch(i, j), weight[i * 9 + j * 3 + k])
                 part = term if part is None else part + term
@@ -298,17 +298,30 @@
         out[...] = total[:, :span]
 
 
-def grad_kernel(w1_far, tall, after, grad, w1, sem):
-    copies = start_copies([(w1_far, w1)], sem)
-    frames, rows, cols, chan = grad.shape
-    fields = [tall[0], tall[1], after[0], after[1]]
+def frame_conv(frames, weight, tap):
+    _, cols, chan = frames[0].shape
 
     def patch(i, j):
-        value = jnp.concatenate([fields[f + i][2 - j : 4 - j] for f in range(2)], axis=0)
-        return value.reshape(-1, chan)
-
+        return jnp.concatenate([f[2 - j : 4 - j] for f in frames], axis=0).reshape(-1, chan)
+
+    return conv(patch, weight, transposed_dot, -1, cols, frame_taps=(tap,))
+
+
+def own_grad_kernel(w_far, tall, part, w, sem):
+    copies = start_copies([(w_far, w)], sem)
+    half = part.shape[0] // 2
     copies[0].wait()
-    grad[...] = conv(patch, w1, transposed_dot, -1, cols).reshape(grad.shape)
+    both = frame_conv([tall[0], tall[1]], w, 0)
+    part[0:half] = both[0:half] + frame_conv([tall[1]], w, 1)
+    part[half:] = both[half:]
+
+
+def grad_kernel(w, part, after, grad):
+    half = part.shape[0] // 2
+    shape = grad.shape[1:]
+    both = part[...] + frame_conv([after[0], after[1]], w, 2)
+    grad[0] = both[0:half].reshape(shape)
+    grad[1] = (both[half:] + frame_conv([after[0]], w, 1)).reshape(shape)
 
 
 def call(body, name, limit, shapes, args, scratch, far=(), scalars=(), sems=0, out_far=False):
@@ -442,15 +455,23 @@
         (by_step,),
         [],
     )
+    grad_part, w1_again = call(
+        own_grad_kernel,
+        "own_input_grad",
+        5,
+        [((cells, chan), F32), (w1.shape, BF)],
+        (tall,),
+        [],
+        far=(w1,),
+        sems=1,
+    )
     (input_grad,) = call(
         grad_kernel,
         "input_grad",
-        8,
+        5,
         [((frames, rows, cols, chan), F32)],
-        (tall, after),
-        [(w1.shape, BF)],
-        far=(w1,),
-        sems=1,
+        (w1_again, grad_part, after),
+        [],
     )
     return (input_grad[None], kernel_grad.T)
 

time: 85.2 us -> 84.6 us (level)
  waiting for transfers between devices: 13.9 us -> 12.9 us
    ppermute x7, waiting for transfers between devices: 13.1 us -> 10.7 us  [move(): lax.ppermute(value, axes if len(axes) > 1 else axes[0], route(sizes, steps))]
    all_to_all x1, waiting for transfers between devices: 0.01 us -> 1.42 us  [local(): by_step = lax.all_to_all(summed.reshape((steps,) + shape), 'tm', 0, 0)]
    pallas_call x9 -> x10, Pallas kernels: 15.6 us -> 16 us  [call(): pl.pallas_call(body, name=name, out_shape=outs, in_specs=[pl.BlockSpec(me...]
  transfers between devices with their start and end apart: 9 -> 9, of which waited for: 7 -> 8; matrix products, arithmetic and copies ran while one was open for 0% -> 0% of each run, Pallas kernels for 12% -> 12%
where the time goes in v13:
time: 84.6 us; the launch traced here: 84 us
  starting transfers between devices  41 us (48%)
  Pallas kernels  16 us (19%)
  waiting for transfers between devices  12.9 us (15%)
  blocking collectives  11.9 us (14%)
  between operations  1.4 us (2%)
  local copies, waits for them, and re-layouts  0.9 us (1%)
    ppermute x7, starting transfers between devices, move(): lax.ppermute(value, axes if len(axes) > 1 else axes[0], route(sizes, steps))  18.3 us
    all_to_all x1, starting transfers between devices, local(): by_step = lax.all_to_all(summed.reshape((steps,) + shape), 'tm', 0, 0)  16.8 us
    pallas_call x10, Pallas kernels, call(): pl.pallas_call(body, name=name, out_shape=outs, in_specs=[pl.BlockSpec(me...  16 us
    all_to_all x1, blocking collectives, local(): lax.all_to_all(part.reshape((clips, steps * shape[0], shape[1])), 'clip',...  11.9 us
    ppermute x7, waiting for transfers between devices, move(): lax.ppermute(value, axes if len(axes) > 1 else axes[0], route(sizes, steps))  10.7 us
    all_to_all x1, starting transfers between devices, local(): got = lax.all_to_all(pay, 'row', 0, 0)  5.92 us
  transfers between devices with their start and end apart: 9, of which 8 were waited for; matrix products, arithmetic and copies ran while one was open for 0% of the time, Pallas kernels for 12%

profile of v13, /device:TPU:2, one launch (start us, length us, event | category | flops | bytes accessed | tf_op | source)
XLA Modules:
  0.0 84.0 jit_solution(9315017634377709567)
XLA Ops:
  0.6 0.9 %slice_bitcast_fusion = bf16[2,2,48,192]{3,2,1,0:T(8,128)(2,1)S(1)} fusion(bf16[1,4,2,48,192]{4,3,2,1,0:T(8,128)(2,1)} %param.6), kind=kLoop, calls=%fused_computation | loop fusion | bytes 147456 | tf_op jit(solution)/shard_map/slice | solution.py:359
  1.5 1.3 %collective-permute-start.1 = (bf16[2,2,48,192]{3,2,1,0:T(8,128)(2,1)S(1)}, bf16[2,2,48,192]{3,2,1,0:T(8,128)(2,1)S(1)}, u32[]{:S(2)}, u32[]{:S(2)}) collective-permute-start(bf16[2,2,48,192]{3,2,1,0:T(8,128)(2,1)S(1)} %slice_bitcast_fusion), channel_id=1, source_target_pairs={{1,0},{2,1},{3,2},{4,3},{5,4},{6,5},{7,6},{8,7},{9,8},{10,9},{11,1... | collective-permute-start | bytes 221192 | tf_op jit(solution)/shard_map/ppermute | solution.py:38
  2.8 4.6 %collective-permute-start = (bf16[2,2,48,192]{3,2,1,0:T(8,128)(2,1)}, bf16[2,2,48,192]{3,2,1,0:T(8,128)(2,1)S(1)}, u32[]{:S(2)}, u32[]{:S(2)}) collective-permute-start(bf16[2,2,48,192]{3,2,1,0:T(8,128)(2,1)} %bitcast.17), channel_id=1, source_target_pairs={{0,1},{1,2},{2,3},{3,4},{4,5},{5,6},{6,7},{7,8},{8,9},{9,10},{10,1... | collective-permute-start | bytes 221192 | tf_op jit(solution)/shard_map/ppermute | solution.py:38
  8.0 0.1 collective-permute-done.1.gnext
  8.1 1.8 %collective-permute-done.xprev = bf16[2,2,48,192]{3,2,1,0:T(8,128)(2,1)S(1)} collective-permute-done((bf16[2,2,48,192]{3,2,1,0:T(8,128)(2,1)}, bf16[2,2,48,192]{3,2,1,0:T(8,128)(2,1)S(1)}, u32[]{:S(2)}, u32[]{:S(2)}) %collective-permute-start) | collective-permute-done | bytes 73760 | tf_op jit(solution)/shard_map/ppermute | solution.py:38
  9.9 1.0 %band.1 = (bf16[9,2,48,192]{3,2,1,0:T(8,128)(2,1)S(1)}, bf16[9,48,192]{2,1,0:T(8,128)(2,1)S(1)}, bf16[9,48,192]{2,1,0:T(8,128)(2,1)S(1)}) custom-call(s32[1]{0:T(128)S(6)} %copy.7.lengths, bf16[2,2,48,192]{3,2,1,0:T(8,128)(2,1)} %bitcast.18, bf16[4,2,48,192]{3,2,1,0:T(8,128)(2,1)} %bitcast.15, bf16[2,2,48,192]{3,2,1,0:T(8,128)(2,1)S(1)} %collective-permute-done.xprev, ...), custom_call_target="tpu_custom_call" | custom-call | tf_op jit(solution)/shard_map/band/pallas_call | solution.py:335
  10.9 1.9 %collective-permute-start.2 = (bf16[9,48,192]{2,1,0:T(8,128)(2,1)S(1)}, bf16[9,48,192]{2,1,0:T(8,128)(2,1)S(1)}, u32[]{:S(2)}, u32[]{:S(2)}) collective-permute-start(bf16[9,48,192]{2,1,0:T(8,128)(2,1)S(1)} %get-tuple-element.19), channel_id=1, source_target_pairs={{0,16},{16,32},{32,48},{48,64},{64,80},{80,96},{96,112},{1,17},{17... | collective-permute-start | bytes 497672 | tf_op jit(solution)/shard_map/ppermute | solution.py:38
  12.9 3.6 %collective-permute-start.3 = (bf16[9,48,192]{2,1,0:T(8,128)(2,1)S(1)}, bf16[9,48,192]{2,1,0:T(8,128)(2,1)S(1)}, u32[]{:S(2)}, u32[]{:S(2)}) collective-permute-start(bf16[9,48,192]{2,1,0:T(8,128)(2,1)S(1)} %get-tuple-element.20), channel_id=1, source_target_pairs={{16,0},{32,16},{48,32},{64,48},{80,64},{96,80},{112,96},{17,1},{33... | collective-permute-start | bytes 497672 | tf_op jit(solution)/shard_map/ppermute | solution.py:38
  16.5 2.6 %own_rows.1 = (bf16[8,120,128]{2,1,0:T(8,128)(2,1)S(1)}, f32[192,192]{1,0:T(8,128)S(1)}, bf16[27,192,192]{2,1,0:T(8,128)(2,1)S(1)}) custom-call(bf16[27,192,192]{2,1,0:T(8,128)(2,1)} %bitcast.11, bf16[9,2,48,192]{3,2,1,0:T(8,128)(2,1)S(1)} %get-tuple-element.15.band.own), custom_call_target="tpu_custom_call" | custom-call | tf_op jit(solution)/shard_map/own_rows/pallas_call | solution.py:335
  19.1 0.0 collective-permute-done.2.above
  19.1 0.8 collective-permute-done.3.below
  19.9 1.4 %hidden_and_act.1 = bf16[8,408,128]{2,1,0:T(8,128)(2,1)} custom-call(bf16[8,120,128]{2,1,0:T(8,128)(2,1)S(1)} %get-tuple-element.16.turned, bf16[27,192,192]{2,1,0:T(8,128)(2,1)S(1)} %get-tuple-element.17.w, f32[192,192]{1,0:T(8,128)S(1)} %get-tuple-element.18.part, bf16[9,48,192]{2,1,0:T(8,128)(2,1)S(1)} %collective-permute-done.2.above, ...), custom_call_target="tpu_custom_call" | custom-call | tf_op jit(solution)/shard_map/hidden_and_act/pallas_call | solution.py:335
  21.4 5.9 %all-to-all-start = ((bf16[8,408,128]{2,1,0:T(8,128)(2,1)}), bf16[8,408,128]{2,1,0:T(8,128)(2,1)S(1)}, u32[]{:S(2)}, u32[]{:S(2)}) async-start(bf16[8,408,128]{2,1,0:T(8,128)(2,1)} %hidden_and_act.1), calls=%async_computation | async-start | bytes 1671168 | tf_op jit(solution)/shard_map/all_to_all | solution.py:394
  27.3 4.1 %hidden_grad.1 = (bf16[2,2,48,192]{3,2,1,0:T(8,128)(2,1)S(1)}, bf16[2,48,192]{2,1,0:T(8,128)(2,1)S(1)}, bf16[2,48,192]{2,1,0:T(8,128)(2,1)S(1)}) custom-call(bf16[27,192,192]{2,1,0:T(8,128)(2,1)} %bitcast.12, bf16[27,192,192]{2,1,0:T(8,128)(2,1)} %bitcast.14, bf16[9,48,192]{2,1,0:T(8,128)(2,1)S(1)} %collective-permute-done.2.above, ...), custom_call_target="tpu_custom_call" | custom-call | tf_op jit(solution)/shard_map/hidden_grad/pallas_call | solution.py:335
  31.4 2.1 %collective-permute-start.4 = (bf16[2,48,192]{2,1,0:T(8,128)(2,1)S(1)}, bf16[2,48,192]{2,1,0:T(8,128)(2,1)S(1)}, u32[]{:S(2)}, u32[]{:S(2)}) collective-permute-start(bf16[2,48,192]{2,1,0:T(8,128)(2,1)S(1)} %get-tuple-element.22), channel_id=1, source_target_pairs={{0,16},{16,32},{32,48},{48,64},{64,80},{80,96},{96,112},{1,17},{17... | collective-permute-start | bytes 110600 | tf_op jit(solution)/shard_map/ppermute | solution.py:38
  33.5 3.5 %collective-permute-start.5 = (bf16[2,48,192]{2,1,0:T(8,128)(2,1)S(1)}, bf16[2,48,192]{2,1,0:T(8,128)(2,1)S(1)}, u32[]{:S(2)}, u32[]{:S(2)}) collective-permute-start(bf16[2,48,192]{2,1,0:T(8,128)(2,1)S(1)} %get-tuple-element.23), channel_id=1, source_target_pairs={{16,0},{32,16},{48,32},{64,48},{80,64},{96,80},{112,96},{17,1},{33... | collective-permute-start | bytes 110600 | tf_op jit(solution)/shard_map/ppermute | solution.py:38
  37.0 1.6 %collective-permute-done.4.above = bf16[2,48,192]{2,1,0:T(8,128)(2,1)S(1)} collective-permute-done((bf16[2,48,192]{2,1,0:T(8,128)(2,1)S(1)}, bf16[2,48,192]{2,1,0:T(8,128)(2,1)S(1)}, u32[]{:S(2)}, u32[]{:S(2)}) %collective-permute-start.4) | collective-permute-done | bytes 36896 | tf_op jit(solution)/shard_map/ppermute | solution.py:38
  38.6 0.2 collective-permute-done.5.below
  38.7 0.8 all-to-all-done.got
  39.5 1.7 %kernel_grad_part.1 = bf16[64,16,128]{2,1,0:T(8,128)(2,1)S(1)} custom-call(bf16[8,408,128]{2,1,0:T(8,128)(2,1)S(1)} %all-to-all-done.got), custom_call_target="tpu_custom_call" | custom-call | tf_op jit(solution)/shard_map/kernel_grad_part/pallas_call | solution.py:335
  41.3 11.9 %all_to_all.15.got = bf16[4,256,128]{2,1,0:T(8,128)(2,1)S(1)} all-to-all(bf16[4,256,128]{2,1,0:T(8,128)(2,1)S(1)} %bitcast.10), channel_id=1, replica_groups=mesh['clip'=4,'row'=8,'tm'=16] {'clip'}, dimensions={0} | all-to-all | bytes 524288 | tf_op jit(solution)/shard_map/all_to_all | solution.py:438
  53.2 0.7 clip_sum.1
  53.8 16.8 %all-to-all-start.2 = ((bf16[16,16,128]{2,1,0:T(8,128)(2,1)}), bf16[16,16,128]{2,1,0:T(8,128)(2,1)S(1)}, u32[]{:S(2)}, u32[]{:S(2)}) async-start(bf16[16,16,128]{2,1,0:T(8,128)(2,1)} %bitcast.7), calls=%async_computation.2 | async-start | bytes 131072 | tf_op jit(solution)/shard_map/all_to_all | solution.py:448
  70.6 1.3 %collective-permute-start.6 = (bf16[2,4,48,192]{3,2,1,0:T(8,128)(2,1)S(1)}, bf16[2,4,48,192]{3,2,1,0:T(8,128)(2,1)S(1)}, u32[]{:S(2)}, u32[]{:S(2)}) collective-permute-start(bf16[2,4,48,192]{3,2,1,0:T(8,128)(2,1)S(1)} %tall_band.1.tall), channel_id=1, source_target_pairs={{1,0},{2,1},{3,2},{4,3},{5,4},{6,5},{7,6},{8,7},{9,8},{10,9},{11,1... | collective-permute-start | bytes 442376 | tf_op jit(solution)/shard_map/ppermute | solution.py:38
  71.9 2.4 %own_input_grad.1 = (f32[192,192]{1,0:T(8,128)S(1)}, bf16[27,192,192]{2,1,0:T(8,128)(2,1)S(1)}) custom-call(bf16[27,192,192]{2,1,0:T(8,128)(2,1)} %bitcast.13, bf16[2,4,48,192]{3,2,1,0:T(8,128)(2,1)S(1)} %tall_band.1.tall), custom_call_target="tpu_custom_call" | custom-call | tf_op jit(solution)/shard_map/own_input_grad/pallas_call | solution.py:335
  74.3 6.3 %collective-permute-done.6.after = bf16[2,4,48,192]{3,2,1,0:T(8,128)(2,1)S(1)} collective-permute-done((bf16[2,4,48,192]{3,2,1,0:T(8,128)(2,1)S(1)}, bf16[2,4,48,192]{3,2,1,0:T(8,128)(2,1)S(1)}, u32[]{:S(2)}, u32[]{:S(2)}) %collective-permute-start.6) | collective-permute-done | bytes 147488 | tf_op jit(solution)/shard_map/ppermute | solution.py:38
  80.6 1.3 %input_grad.1 = f32[2,2,48,192]{3,2,1,0:T(8,128)} custom-call(bf16[27,192,192]{2,1,0:T(8,128)(2,1)S(1)} %get-tuple-element.25.w, f32[192,192]{1,0:T(8,128)S(1)} %get-tuple-element.26.part, bf16[2,4,48,192]{3,2,1,0:T(8,128)(2,1)S(1)} %collective-permute-done.6.after), custom_call_target="tpu_custom_call" | custom-call | tf_op jit(solution)/shard_map/input_grad/pallas_call | solution.py:335
  81.9 1.4 %all-to-all-done.2.got = bf16[16,16,128]{2,1,0:T(8,128)(2,1)S(1)} async-done(((bf16[16,16,128]{2,1,0:T(8,128)(2,1)}), bf16[16,16,128]{2,1,0:T(8,128)(2,1)S(1)}, u32[]{:S(2)}, u32[]{:S(2)}) %all-to-all-start.2) | async-done | bytes 65568 | tf_op jit(solution)/shard_map/all_to_all | solution.py:448
  83.4 0.7 kernel_grad_sum.1
  (1 shorter events, 0.0 us)
Async XLA Ops:
  1.5 6.6 %collective-permute-start.1 = (bf16[2,2,48,192]{3,2,1,0:T(8,128)(2,1)S(1)}, bf16[2,2,48,192]{3,2,1,0:T(8,128)(2,1)S(1)}, u32[]{:S(2)}, u32[]{:S(2)}) collective-permute-start(bf16[2,2,48,192]{3,2,1,0:T(8,128)(2,1)S(1)} %slice_bitcast_fusion), channel_id=1, source_target_pairs={{1,0},{2,1},{3,2},{4,3},{5,4},{6,5},{7,6},{8,7},{9,8},{10,9},{11,1... | collective-permute-start | bytes 221192 | tf_op jit(solution)/shard_map/ppermute | solution.py:38
  2.8 7.1 %collective-permute-start = (bf16[2,2,48,192]{3,2,1,0:T(8,128)(2,1)}, bf16[2,2,48,192]{3,2,1,0:T(8,128)(2,1)S(1)}, u32[]{:S(2)}, u32[]{:S(2)}) collective-permute-start(bf16[2,2,48,192]{3,2,1,0:T(8,128)(2,1)} %bitcast.17), channel_id=1, source_target_pairs={{0,1},{1,2},{2,3},{3,4},{4,5},{5,6},{6,7},{7,8},{8,9},{9,10},{10,1... | collective-permute-start | bytes 221192 | tf_op jit(solution)/shard_map/ppermute | solution.py:38
  10.9 8.2 %collective-permute-start.2 = (bf16[9,48,192]{2,1,0:T(8,128)(2,1)S(1)}, bf16[9,48,192]{2,1,0:T(8,128)(2,1)S(1)}, u32[]{:S(2)}, u32[]{:S(2)}) collective-permute-start(bf16[9,48,192]{2,1,0:T(8,128)(2,1)S(1)} %get-tuple-element.19), channel_id=1, source_target_pairs={{0,16},{16,32},{32,48},{48,64},{64,80},{80,96},{96,112},{1,17},{17... | collective-permute-start | bytes 497672 | tf_op jit(solution)/shard_map/ppermute | solution.py:38
  12.9 7.1 %collective-permute-start.3 = (bf16[9,48,192]{2,1,0:T(8,128)(2,1)S(1)}, bf16[9,48,192]{2,1,0:T(8,128)(2,1)S(1)}, u32[]{:S(2)}, u32[]{:S(2)}) collective-permute-start(bf16[9,48,192]{2,1,0:T(8,128)(2,1)S(1)} %get-tuple-element.20), channel_id=1, source_target_pairs={{16,0},{32,16},{48,32},{64,48},{80,64},{96,80},{112,96},{17,1},{33... | collective-permute-start | bytes 497672 | tf_op jit(solution)/shard_map/ppermute | solution.py:38
  21.4 18.1 %all-to-all-start = ((bf16[8,408,128]{2,1,0:T(8,128)(2,1)}), bf16[8,408,128]{2,1,0:T(8,128)(2,1)S(1)}, u32[]{:S(2)}, u32[]{:S(2)}) async-start(bf16[8,408,128]{2,1,0:T(8,128)(2,1)} %hidden_and_act.1), calls=%async_computation | async-start | bytes 1671168 | tf_op jit(solution)/shard_map/all_to_all | solution.py:394
  31.4 7.2 %collective-permute-start.4 = (bf16[2,48,192]{2,1,0:T(8,128)(2,1)S(1)}, bf16[2,48,192]{2,1,0:T(8,128)(2,1)S(1)}, u32[]{:S(2)}, u32[]{:S(2)}) collective-permute-start(bf16[2,48,192]{2,1,0:T(8,128)(2,1)S(1)} %get-tuple-element.22), channel_id=1, source_target_pairs={{0,16},{16,32},{32,48},{48,64},{64,80},{80,96},{96,112},{1,17},{17... | collective-permute-start | bytes 110600 | tf_op jit(solution)/shard_map/ppermute | solution.py:38
  33.5 5.2 %collective-permute-start.5 = (bf16[2,48,192]{2,1,0:T(8,128)(2,1)S(1)}, bf16[2,48,192]{2,1,0:T(8,128)(2,1)S(1)}, u32[]{:S(2)}, u32[]{:S(2)}) collective-permute-start(bf16[2,48,192]{2,1,0:T(8,128)(2,1)S(1)} %get-tuple-element.23), channel_id=1, source_target_pairs={{16,0},{32,16},{48,32},{64,48},{80,64},{96,80},{112,96},{17,1},{33... | collective-permute-start | bytes 110600 | tf_op jit(solution)/shard_map/ppermute | solution.py:38
  53.8 29.5 %all-to-all-start.2 = ((bf16[16,16,128]{2,1,0:T(8,128)(2,1)}), bf16[16,16,128]{2,1,0:T(8,128)(2,1)S(1)}, u32[]{:S(2)}, u32[]{:S(2)}) async-start(bf16[16,16,128]{2,1,0:T(8,128)(2,1)} %bitcast.7), calls=%async_computation.2 | async-start | bytes 131072 | tf_op jit(solution)/shard_map/all_to_all | solution.py:448
  70.6 10.0 %collective-permute-start.6 = (bf16[2,4,48,192]{3,2,1,0:T(8,128)(2,1)S(1)}, bf16[2,4,48,192]{3,2,1,0:T(8,128)(2,1)S(1)}, u32[]{:S(2)}, u32[]{:S(2)}) collective-permute-start(bf16[2,4,48,192]{3,2,1,0:T(8,128)(2,1)S(1)} %tall_band.1.tall), channel_id=1, source_target_pairs={{1,0},{2,1},{3,2},{4,3},{5,4},{6,5},{7,6},{8,7},{9,8},{10,9},{11,1... | collective-permute-start | bytes 442376 | tf_op jit(solution)/shard_map/ppermute | solution.py:38

commit v14 on v13

--- a/solution.py
+++ b/solution.py
@@ -410,16 +410,6 @@
     )
     above_grad = move(grad_bot, ("row",), (1,))
     below_grad = move(grad_top, ("row",), (-1,))
-    (tall,) = call(
-        tall_kernel,
-        "tall_band",
-        4,
-        [((frames, rows + 2, cols, chan), BF)],
-        (grad, above_grad, below_grad),
-        [],
-    )
-    got, tall = lax.optimization_barrier((got, tall))
-
     blocks = clips * steps
     span = 27 * chan // blocks
     shape = (16, 128) if packed(width, span) else (width, (span + 127) // 128 * 128)
@@ -435,6 +425,15 @@
             ((27 * width, 256), F32),
         ],
     )
+    part, above_grad, below_grad = lax.optimization_barrier((part, above_grad, below_grad))
+    (tall,) = call(
+        tall_kernel,
+        "tall_band",
+        4,
+        [((frames, rows + 2, cols, chan), BF)],
+        (grad, above_grad, below_grad),
+        [],
+    )
     by_clip = lax.all_to_all(part.reshape((clips, steps * shape[0], shape[1])), "clip", 0, 0)
     (summed,) = call(
         clip_kernel,

time: 84.6 us -> 84.8 us (level)
  the two profiles are of different devices: /device:TPU:2 before, /device:TPU:32 now
where the time goes in v14:
time: 84.8 us; the launch traced here: 84.2 us
  starting transfers between devices  38.2 us (45%)
  waiting for transfers between devices  16.7 us (20%)
  Pallas kernels  16 us (19%)
  blocking collectives  10.9 us (13%)
  between operations  1.42 us (2%)
  local copies, waits for them, and re-layouts  0.9 us (1%)
    ppermute x7, starting transfers between devices, move(): lax.ppermute(value, axes if len(axes) > 1 else axes[0], route(sizes, steps))  18 us
    all_to_all x1, starting transfers between devices, local(): by_step = lax.all_to_all(summed.reshape((steps,) + shape), 'tm', 0, 0)  16.4 us
    pallas_call x10, Pallas kernels, call(): pl.pallas_call(body, name=name, out_shape=outs, in_specs=[pl.BlockSpec(me...  16 us
    all_to_all x1, blocking collectives, local(): lax.all_to_all(part.reshape((clips, steps * shape[0], shape[1])), 'clip',...  10.9 us
    ppermute x7, waiting for transfers between devices, move(): lax.ppermute(value, axes if len(axes) > 1 else axes[0], route(sizes, steps))  7.93 us
    all_to_all x1, waiting for transfers between devices, local(): got = lax.all_to_all(pay, 'row', 0, 0)  5.93 us
    all_to_all x1, starting transfers between devices, local(): got = lax.all_to_all(pay, 'row', 0, 0)  3.77 us
    all_to_all x1, waiting for transfers between devices, local(): by_step = lax.all_to_all(summed.reshape((steps,) + shape), 'tm', 0, 0)  2.87 us
  transfers between devices with their start and end apart: 9, of which 4 were waited for; matrix products, arithmetic and copies ran while one was open for 0% of the time, Pallas kernels for 14%

profile of v14, /device:TPU:32, one launch (start us, length us, event | category | flops | bytes accessed | tf_op | source)
XLA Modules:
  0.0 84.2 jit_solution(9421844983122718873)
XLA Ops:
  0.6 0.9 %slice_bitcast_fusion = bf16[2,2,48,192]{3,2,1,0:T(8,128)(2,1)S(1)} fusion(bf16[1,4,2,48,192]{4,3,2,1,0:T(8,128)(2,1)} %param.6), kind=kLoop, calls=%fused_computation | loop fusion | bytes 147456 | tf_op jit(solution)/shard_map/slice | solution.py:359
  1.5 7.4 %collective-permute-start.1 = (bf16[2,2,48,192]{3,2,1,0:T(8,128)(2,1)S(1)}, bf16[2,2,48,192]{3,2,1,0:T(8,128)(2,1)S(1)}, u32[]{:S(2)}, u32[]{:S(2)}) collective-permute-start(bf16[2,2,48,192]{3,2,1,0:T(8,128)(2,1)S(1)} %slice_bitcast_fusion), channel_id=1, source_target_pairs={{1,0},{2,1},{3,2},{4,3},{5,4},{6,5},{7,6},{8,7},{9,8},{10,9},{11,1... | collective-permute-start | bytes 221192 | tf_op jit(solution)/shard_map/ppermute | solution.py:38
  8.9 1.9 %collective-permute-start = (bf16[2,2,48,192]{3,2,1,0:T(8,128)(2,1)}, bf16[2,2,48,192]{3,2,1,0:T(8,128)(2,1)S(1)}, u32[]{:S(2)}, u32[]{:S(2)}) collective-permute-start(bf16[2,2,48,192]{3,2,1,0:T(8,128)(2,1)} %bitcast.17), channel_id=1, source_target_pairs={{0,1},{1,2},{2,3},{3,4},{4,5},{5,6},{6,7},{7,8},{8,9},{9,10},{10,1... | collective-permute-start | bytes 221192 | tf_op jit(solution)/shard_map/ppermute | solution.py:38
  11.5 0.0 collective-permute-done.1.gnext
  11.5 4.1 %collective-permute-done.xprev = bf16[2,2,48,192]{3,2,1,0:T(8,128)(2,1)S(1)} collective-permute-done((bf16[2,2,48,192]{3,2,1,0:T(8,128)(2,1)}, bf16[2,2,48,192]{3,2,1,0:T(8,128)(2,1)S(1)}, u32[]{:S(2)}, u32[]{:S(2)}) %collective-permute-start) | collective-permute-done | bytes 73760 | tf_op jit(solution)/shard_map/ppermute | solution.py:38
  15.6 1.0 %band.1 = (bf16[9,2,48,192]{3,2,1,0:T(8,128)(2,1)S(1)}, bf16[9,48,192]{2,1,0:T(8,128)(2,1)S(1)}, bf16[9,48,192]{2,1,0:T(8,128)(2,1)S(1)}) custom-call(s32[1]{0:T(128)S(6)} %copy.7.lengths, bf16[2,2,48,192]{3,2,1,0:T(8,128)(2,1)} %bitcast.18, bf16[4,2,48,192]{3,2,1,0:T(8,128)(2,1)} %bitcast.15, bf16[2,2,48,192]{3,2,1,0:T(8,128)(2,1)S(1)} %collective-permute-done.xprev, ...), custom_call_target="tpu_custom_call" | custom-call | tf_op jit(solution)/shard_map/band/pallas_call | solution.py:335
  16.7 1.3 %collective-permute-start.2 = (bf16[9,48,192]{2,1,0:T(8,128)(2,1)S(1)}, bf16[9,48,192]{2,1,0:T(8,128)(2,1)S(1)}, u32[]{:S(2)}, u32[]{:S(2)}) collective-permute-start(bf16[9,48,192]{2,1,0:T(8,128)(2,1)S(1)} %get-tuple-element.16), channel_id=1, source_target_pairs={{0,16},{16,32},{32,48},{48,64},{64,80},{80,96},{96,112},{1,17},{17... | collective-permute-start | bytes 497672 | tf_op jit(solution)/shard_map/ppermute | solution.py:38
  18.0 1.3 %collective-permute-start.3 = (bf16[9,48,192]{2,1,0:T(8,128)(2,1)S(1)}, bf16[9,48,192]{2,1,0:T(8,128)(2,1)S(1)}, u32[]{:S(2)}, u32[]{:S(2)}) collective-permute-start(bf16[9,48,192]{2,1,0:T(8,128)(2,1)S(1)} %get-tuple-element.17), channel_id=1, source_target_pairs={{16,0},{32,16},{48,32},{64,48},{80,64},{96,80},{112,96},{17,1},{33... | collective-permute-start | bytes 497672 | tf_op jit(solution)/shard_map/ppermute | solution.py:38
  19.3 2.6 %own_rows.1 = (bf16[8,120,128]{2,1,0:T(8,128)(2,1)S(1)}, f32[192,192]{1,0:T(8,128)S(1)}, bf16[27,192,192]{2,1,0:T(8,128)(2,1)S(1)}) custom-call(bf16[27,192,192]{2,1,0:T(8,128)(2,1)} %bitcast.11, bf16[9,2,48,192]{3,2,1,0:T(8,128)(2,1)S(1)} %get-tuple-element.18.own.band), custom_call_target="tpu_custom_call" | custom-call | tf_op jit(solution)/shard_map/own_rows/pallas_call | solution.py:335
  21.9 0.0 collective-permute-done.2.above
  21.9 0.0 collective-permute-done.3.below
  21.9 1.4 %hidden_and_act.1 = bf16[8,408,128]{2,1,0:T(8,128)(2,1)} custom-call(bf16[8,120,128]{2,1,0:T(8,128)(2,1)S(1)} %get-tuple-element.20.turned, bf16[27,192,192]{2,1,0:T(8,128)(2,1)S(1)} %get-tuple-element.21.w, f32[192,192]{1,0:T(8,128)S(1)} %get-tuple-element.22.part, bf16[9,48,192]{2,1,0:T(8,128)(2,1)S(1)} %collective-permute-done.2.above, ...), custom_call_target="tpu_custom_call" | custom-call | tf_op jit(solution)/shard_map/hidden_and_act/pallas_call | solution.py:335
  23.4 3.8 %all-to-all-start = ((bf16[8,408,128]{2,1,0:T(8,128)(2,1)}), bf16[8,408,128]{2,1,0:T(8,128)(2,1)S(1)}, u32[]{:S(2)}, u32[]{:S(2)}) async-start(bf16[8,408,128]{2,1,0:T(8,128)(2,1)} %hidden_and_act.1), calls=%async_computation | async-start | bytes 1671168 | tf_op jit(solution)/shard_map/all_to_all | solution.py:394
  27.1 4.1 %hidden_grad.1 = (bf16[2,2,48,192]{3,2,1,0:T(8,128)(2,1)S(1)}, bf16[2,48,192]{2,1,0:T(8,128)(2,1)S(1)}, bf16[2,48,192]{2,1,0:T(8,128)(2,1)S(1)}) custom-call(bf16[27,192,192]{2,1,0:T(8,128)(2,1)} %bitcast.12, bf16[27,192,192]{2,1,0:T(8,128)(2,1)} %bitcast.14, bf16[9,48,192]{2,1,0:T(8,128)(2,1)S(1)} %collective-permute-done.2.above, ...), custom_call_target="tpu_custom_call" | custom-call | tf_op jit(solution)/shard_map/hidden_grad/pallas_call | solution.py:335
  31.3 2.8 %collective-permute-start.4 = (bf16[2,48,192]{2,1,0:T(8,128)(2,1)S(1)}, bf16[2,48,192]{2,1,0:T(8,128)(2,1)S(1)}, u32[]{:S(2)}, u32[]{:S(2)}) collective-permute-start(bf16[2,48,192]{2,1,0:T(8,128)(2,1)S(1)} %get-tuple-element.23), channel_id=1, source_target_pairs={{0,16},{16,32},{32,48},{48,64},{64,80},{80,96},{96,112},{1,17},{17... | collective-permute-start | bytes 110600 | tf_op jit(solution)/shard_map/ppermute | solution.py:38
  34.1 1.3 %collective-permute-start.5 = (bf16[2,48,192]{2,1,0:T(8,128)(2,1)S(1)}, bf16[2,48,192]{2,1,0:T(8,128)(2,1)S(1)}, u32[]{:S(2)}, u32[]{:S(2)}) collective-permute-start(bf16[2,48,192]{2,1,0:T(8,128)(2,1)S(1)} %get-tuple-element.24), channel_id=1, source_target_pairs={{16,0},{32,16},{48,32},{64,48},{80,64},{96,80},{112,96},{17,1},{33... | collective-permute-start | bytes 110600 | tf_op jit(solution)/shard_map/ppermute | solution.py:38
  35.4 5.9 %all-to-all-done.got = bf16[8,408,128]{2,1,0:T(8,128)(2,1)S(1)} async-done(((bf16[8,408,128]{2,1,0:T(8,128)(2,1)}), bf16[8,408,128]{2,1,0:T(8,128)(2,1)S(1)}, u32[]{:S(2)}, u32[]{:S(2)}) %all-to-all-start) | async-done | bytes 835616 | tf_op jit(solution)/shard_map/all_to_all | solution.py:394
  41.3 1.7 %kernel_grad_part.1 = bf16[64,16,128]{2,1,0:T(8,128)(2,1)S(1)} custom-call(bf16[8,408,128]{2,1,0:T(8,128)(2,1)S(1)} %all-to-all-done.got), custom_call_target="tpu_custom_call" | custom-call | tf_op jit(solution)/shard_map/kernel_grad_part/pallas_call | solution.py:335
  43.0 0.0 collective-permute-done.4.above
  43.0 0.0 collective-permute-done.5.below
  43.1 10.9 %all_to_all.15.got = bf16[4,256,128]{2,1,0:T(8,128)(2,1)S(1)} all-to-all(bf16[4,256,128]{2,1,0:T(8,128)(2,1)S(1)} %bitcast.10), channel_id=1, replica_groups=mesh['clip'=4,'row'=8,'tm'=16] {'clip'}, dimensions={0} | all-to-all | bytes 524288 | tf_op jit(solution)/shard_map/all_to_all | solution.py:437
  54.0 0.7 clip_sum.1
  54.6 16.4 %all-to-all-start.2 = ((bf16[16,16,128]{2,1,0:T(8,128)(2,1)}), bf16[16,16,128]{2,1,0:T(8,128)(2,1)S(1)}, u32[]{:S(2)}, u32[]{:S(2)}) async-start(bf16[16,16,128]{2,1,0:T(8,128)(2,1)} %bitcast.7), calls=%async_computation.2 | async-start | bytes 131072 | tf_op jit(solution)/shard_map/all_to_all | solution.py:447
  71.1 2.0 %collective-permute-start.6 = (bf16[2,4,48,192]{3,2,1,0:T(8,128)(2,1)S(1)}, bf16[2,4,48,192]{3,2,1,0:T(8,128)(2,1)S(1)}, u32[]{:S(2)}, u32[]{:S(2)}) collective-permute-start(bf16[2,4,48,192]{3,2,1,0:T(8,128)(2,1)S(1)} %tall_band.1.tall), channel_id=1, source_target_pairs={{1,0},{2,1},{3,2},{4,3},{5,4},{6,5},{7,6},{8,7},{9,8},{10,9},{11,1... | collective-permute-start | bytes 442376 | tf_op jit(solution)/shard_map/ppermute | solution.py:38
  73.1 2.4 %own_input_grad.1 = (f32[192,192]{1,0:T(8,128)S(1)}, bf16[27,192,192]{2,1,0:T(8,128)(2,1)S(1)}) custom-call(bf16[27,192,192]{2,1,0:T(8,128)(2,1)} %bitcast.13, bf16[2,4,48,192]{3,2,1,0:T(8,128)(2,1)S(1)} %tall_band.1.tall), custom_call_target="tpu_custom_call" | custom-call | tf_op jit(solution)/shard_map/own_input_grad/pallas_call | solution.py:335
  75.5 3.8 %collective-permute-done.6.after = bf16[2,4,48,192]{3,2,1,0:T(8,128)(2,1)S(1)} collective-permute-done((bf16[2,4,48,192]{3,2,1,0:T(8,128)(2,1)S(1)}, bf16[2,4,48,192]{3,2,1,0:T(8,128)(2,1)S(1)}, u32[]{:S(2)}, u32[]{:S(2)}) %collective-permute-start.6) | collective-permute-done | bytes 147488 | tf_op jit(solution)/shard_map/ppermute | solution.py:38
  79.3 1.3 %input_grad.1 = f32[2,2,48,192]{3,2,1,0:T(8,128)} custom-call(bf16[27,192,192]{2,1,0:T(8,128)(2,1)S(1)} %get-tuple-element.27.w, f32[192,192]{1,0:T(8,128)S(1)} %get-tuple-element.28.part, bf16[2,4,48,192]{3,2,1,0:T(8,128)(2,1)S(1)} %collective-permute-done.6.after), custom_call_target="tpu_custom_call" | custom-call | tf_op jit(solution)/shard_map/input_grad/pallas_call | solution.py:335
  80.6 2.9 %all-to-all-done.2.got = bf16[16,16,128]{2,1,0:T(8,128)(2,1)S(1)} async-done(((bf16[16,16,128]{2,1,0:T(8,128)(2,1)}), bf16[16,16,128]{2,1,0:T(8,128)(2,1)S(1)}, u32[]{:S(2)}, u32[]{:S(2)}) %all-to-all-start.2) | async-done | bytes 65568 | tf_op jit(solution)/shard_map/all_to_all | solution.py:447
  83.5 0.7 kernel_grad_sum.1
  (1 shorter events, 0.0 us)
Async XLA Ops:
  1.5 10.0 %collective-permute-start.1 = (bf16[2,2,48,192]{3,2,1,0:T(8,128)(2,1)S(1)}, bf16[2,2,48,192]{3,2,1,0:T(8,128)(2,1)S(1)}, u32[]{:S(2)}, u32[]{:S(2)}) collective-permute-start(bf16[2,2,48,192]{3,2,1,0:T(8,128)(2,1)S(1)} %slice_bitcast_fusion), channel_id=1, source_target_pairs={{1,0},{2,1},{3,2},{4,3},{5,4},{6,5},{7,6},{8,7},{9,8},{10,9},{11,1... | collective-permute-start | bytes 221192 | tf_op jit(solution)/shard_map/ppermute | solution.py:38
  8.9 6.7 %collective-permute-start = (bf16[2,2,48,192]{3,2,1,0:T(8,128)(2,1)}, bf16[2,2,48,192]{3,2,1,0:T(8,128)(2,1)S(1)}, u32[]{:S(2)}, u32[]{:S(2)}) collective-permute-start(bf16[2,2,48,192]{3,2,1,0:T(8,128)(2,1)} %bitcast.17), channel_id=1, source_target_pairs={{0,1},{1,2},{2,3},{3,4},{4,5},{5,6},{6,7},{7,8},{8,9},{9,10},{10,1... | collective-permute-start | bytes 221192 | tf_op jit(solution)/shard_map/ppermute | solution.py:38
  16.7 5.2 %collective-permute-start.2 = (bf16[9,48,192]{2,1,0:T(8,128)(2,1)S(1)}, bf16[9,48,192]{2,1,0:T(8,128)(2,1)S(1)}, u32[]{:S(2)}, u32[]{:S(2)}) collective-permute-start(bf16[9,48,192]{2,1,0:T(8,128)(2,1)S(1)} %get-tuple-element.16), channel_id=1, source_target_pairs={{0,16},{16,32},{32,48},{48,64},{64,80},{80,96},{96,112},{1,17},{17... | collective-permute-start | bytes 497672 | tf_op jit(solution)/shard_map/ppermute | solution.py:38
  18.0 3.9 %collective-permute-start.3 = (bf16[9,48,192]{2,1,0:T(8,128)(2,1)S(1)}, bf16[9,48,192]{2,1,0:T(8,128)(2,1)S(1)}, u32[]{:S(2)}, u32[]{:S(2)}) collective-permute-start(bf16[9,48,192]{2,1,0:T(8,128)(2,1)S(1)} %get-tuple-element.17), channel_id=1, source_target_pairs={{16,0},{32,16},{48,32},{64,48},{80,64},{96,80},{112,96},{17,1},{33... | collective-permute-start | bytes 497672 | tf_op jit(solution)/shard_map/ppermute | solution.py:38
  23.4 17.9 %all-to-all-start = ((bf16[8,408,128]{2,1,0:T(8,128)(2,1)}), bf16[8,408,128]{2,1,0:T(8,128)(2,1)S(1)}, u32[]{:S(2)}, u32[]{:S(2)}) async-start(bf16[8,408,128]{2,1,0:T(8,128)(2,1)} %hidden_and_act.1), calls=%async_computation | async-start | bytes 1671168 | tf_op jit(solution)/shard_map/all_to_all | solution.py:394
  31.3 11.8 %collective-permute-start.4 = (bf16[2,48,192]{2,1,0:T(8,128)(2,1)S(1)}, bf16[2,48,192]{2,1,0:T(8,128)(2,1)S(1)}, u32[]{:S(2)}, u32[]{:S(2)}) collective-permute-start(bf16[2,48,192]{2,1,0:T(8,128)(2,1)S(1)} %get-tuple-element.23), channel_id=1, source_target_pairs={{0,16},{16,32},{32,48},{48,64},{64,80},{80,96},{96,112},{1,17},{17... | collective-permute-start | bytes 110600 | tf_op jit(solution)/shard_map/ppermute | solution.py:38
  34.1 9.0 %collective-permute-start.5 = (bf16[2,48,192]{2,1,0:T(8,128)(2,1)S(1)}, bf16[2,48,192]{2,1,0:T(8,128)(2,1)S(1)}, u32[]{:S(2)}, u32[]{:S(2)}) collective-permute-start(bf16[2,48,192]{2,1,0:T(8,128)(2,1)S(1)} %get-tuple-element.24), channel_id=1, source_target_pairs={{16,0},{32,16},{48,32},{64,48},{80,64},{96,80},{112,96},{17,1},{33... | collective-permute-start | bytes 110600 | tf_op jit(solution)/shard_map/ppermute | solution.py:38
  54.6 28.9 %all-to-all-start.2 = ((bf16[16,16,128]{2,1,0:T(8,128)(2,1)}), bf16[16,16,128]{2,1,0:T(8,128)(2,1)S(1)}, u32[]{:S(2)}, u32[]{:S(2)}) async-start(bf16[16,16,128]{2,1,0:T(8,128)(2,1)} %bitcast.7), calls=%async_computation.2 | async-start | bytes 131072 | tf_op jit(solution)/shard_map/all_to_all | solution.py:447
  71.1 8.2 %collective-permute-start.6 = (bf16[2,4,48,192]{3,2,1,0:T(8,128)(2,1)S(1)}, bf16[2,4,48,192]{3,2,1,0:T(8,128)(2,1)S(1)}, u32[]{:S(2)}, u32[]{:S(2)}) collective-permute-start(bf16[2,4,48,192]{3,2,1,0:T(8,128)(2,1)S(1)} %tall_band.1.tall), channel_id=1, source_target_pairs={{1,0},{2,1},{3,2},{4,3},{5,4},{6,5},{7,6},{8,7},{9,8},{10,9},{11,1... | collective-permute-start | bytes 442376 | tf_op jit(solution)/shard_map/ppermute | solution.py:38
